TPU v7x, 256 devices: a whole 4x4x8 slice. The times are simulated.
256 devices in a mesh: dp: 8 (over z_lo, core), expert: 32 (over x, z_hi, y).
Axes of the slice: x: 4, y: 4, z: 8 (z_hi: 2, z_lo: 4; z = z_hi * 4 + z_lo), core: 2. Of those that a mesh axis runs over, the one named last changes fastest.
Arguments:
- tokens: bfloat16 [32768, 2048], P(('dp', 'expert')), may hold values from -6 to 6
- out_grad: bfloat16 [32768, 2048], P(('dp', 'expert')), may hold values from -6 to 6
- expert_ids: int32 [32768, 8], P(('dp', 'expert')), may hold values from 0 to 127, as said below
- route_gates: float32 [32768, 8], P(('dp', 'expert')), may hold values from 0.05 to 1
- swap_flags: int32 [32], replicated, may hold values from 0 to 1, as said below
- gate_proj: bfloat16 [32, 2048, 768], P('expert'), may hold values from -0.125 to 0.125
- up_proj: bfloat16 [32, 2048, 768], P('expert'), may hold values from -0.125 to 0.125
- down_proj: bfloat16 [32, 768, 2048], P('expert'), may hold values from -0.21875 to 0.21875
Outputs:
- layer_out: bfloat16 [32768, 2048], P(('dp', 'expert'))
- grad_tokens: bfloat16 [32768, 2048], P(('dp', 'expert'))
- gate_grads: float32 [32768, 8], P(('dp', 'expert'))
- grad_gate_proj: bfloat16 [32, 2048, 768], P('expert', 'dp')
- grad_up_proj: bfloat16 [32, 2048, 768], P('expert', 'dp')
- grad_down_proj: bfloat16 [32, 768, 2048], P('expert', 'dp')
Inputs may be any that keep to these rules, and one draw needn't show every extreme that they name: `expert_ids`: each row names 8 different experts. In the rows of one device no expert is named by more than 16 rows, and one expert below 32, the same for all devices, is named by exactly 16 rows of every device. swap_flags[d] = swap_flags[d + 16] for d < 16.
All inputs are finite; a program needn't handle non-finite values.
Results may differ from a plain program's by a relative error of at most 0.013.
Values may be sent and summed in bfloat16 or wider, within the bound.
No kernel may reach another device: no remote copies, remote signals or barrier semaphores. Data moves between devices by JAX's collectives and lax.ppermute only.
A program may use at most 128 MiB of HBM per device.

v0:
```python
import jax
import jax.numpy as jnp
from jax import lax
from jax.sharding import PartitionSpec as P

SLOTS = 4


def partner(x, axis, bit):
    return lax.ppermute(x, axis, [(i, i ^ 1 << bit) for i in range(lax.axis_size(axis))])


def slot_table(target, devices, slot_most):
    tok_rows, pick_count = target.shape
    flat_total = tok_rows * pick_count
    matches = (target[:, :, None] == jnp.arange(devices, dtype=jnp.int32)[None, None, :]).astype(
        jnp.int32
    )
    per_token = jnp.sum(matches, axis=1)
    earlier = jnp.cumsum(per_token, axis=0) - per_token
    position = jnp.take_along_axis(earlier, jnp.minimum(target, devices - 1), axis=1)
    flat_index = jnp.arange(flat_total, dtype=jnp.int32).reshape(tok_rows, pick_count)
    empty_slots = jnp.full((devices, slot_most), flat_total, jnp.int32)
    return empty_slots.at[target, position].set(flat_index, mode="drop")


def expert_forward(row_block, gate_w, up_w, down_w):
    gate_pre = jnp.dot(row_block, gate_w, preferred_element_type=jnp.float32)
    up_pre = jnp.dot(row_block, up_w, preferred_element_type=jnp.float32)
    gate_sigmoid = jax.nn.sigmoid(gate_pre)
    hidden = (gate_pre * gate_sigmoid * up_pre).astype(jnp.bfloat16)
    expert_out = jnp.dot(hidden, down_w, preferred_element_type=jnp.float32).astype(jnp.bfloat16)
    return (gate_pre, up_pre, gate_sigmoid, hidden, expert_out)


def expert_backward(gate_pre, up_pre, gate_sigmoid, out_grads, gate_w, up_w, down_w):
    contract_last = (((1,), (1,)), ((), ()))
    hidden_grad = lax.dot_general(
        out_grads, down_w, contract_last, preferred_element_type=jnp.float32
    )
    gate_grad = (
        hidden_grad * up_pre * gate_sigmoid * (1.0 + gate_pre * (1.0 - gate_sigmoid))
    ).astype(jnp.bfloat16)
    up_grad = (hidden_grad * gate_pre * gate_sigmoid).astype(jnp.bfloat16)
    row_grads = lax.dot_general(
        gate_grad, gate_w, contract_last, preferred_element_type=jnp.float32
    )
    row_grads = row_grads + lax.dot_general(
        up_grad, up_w, contract_last, preferred_element_type=jnp.float32
    )
    return (jnp.concatenate([gate_grad, up_grad], axis=1), row_grads.astype(jnp.bfloat16))


def on_device(tokens, out_grad, expert_ids, route_gates, swap_flags, gate_proj, up_proj, down_proj):
    devices = lax.axis_size("expert")
    half_axis = devices // 2
    swap_bit = devices.bit_length() - 2
    my_index = lax.axis_index("expert")
    tok_rows, model_width = tokens.shape
    pick_count = expert_ids.shape[1]
    hidden_width = gate_proj.shape[2]
    slot_most = 2 * tok_rows * pick_count // (SLOTS * devices)
    flat_total = tok_rows * pick_count
    in_layer = expert_ids < devices
    is_moved = swap_flags[my_index] == 1
    own_weights = (gate_proj[0], up_proj[0], down_proj[0])
    clipped = jnp.minimum(expert_ids, devices - 1)
    moved_to = jnp.where(swap_flags[clipped] == 1, (expert_ids + half_axis) % devices, expert_ids)
    target = jnp.where(in_layer, moved_to, devices)
    partner_weights = partner((own_weights[0], own_weights[1], own_weights[2]), "expert", swap_bit)
    gate_w = jnp.where(is_moved, partner_weights[0], own_weights[0])
    up_w = jnp.where(is_moved, partner_weights[1], own_weights[1])
    down_w = jnp.where(is_moved, partner_weights[2], own_weights[2])
    slot_index = slot_table(target, devices, slot_most)
    row_index = slot_index // pick_count
    zero_row = jnp.zeros((1, model_width), jnp.bfloat16)
    token_pad = jnp.concatenate([tokens, zero_row], axis=0)
    grad_pad = jnp.concatenate([out_grad, zero_row], axis=0)
    gate_pad = jnp.concatenate([route_gates.reshape(-1), jnp.zeros((1,), jnp.float32)])
    slot_gate = gate_pad[slot_index]
    send_rows = token_pad[row_index]
    grad_rows = grad_pad[row_index]
    send_grads = (slot_gate[:, :, None] * grad_rows.astype(jnp.float32)).astype(jnp.bfloat16)
    block_shape = (devices, slot_most, model_width)
    arrived_rows = lax.all_to_all(send_rows, "expert", split_axis=0, concat_axis=0, tiled=True)
    row_block = arrived_rows.reshape(-1, model_width)
    gate_pre, up_pre, gate_sigmoid, hidden, expert_out = expert_forward(
        row_block, gate_w, up_w, down_w
    )
    returned_out = lax.all_to_all(
        expert_out.reshape(block_shape), "expert", split_axis=0, concat_axis=0, tiled=True
    )
    arrived_grads = lax.all_to_all(send_grads, "expert", split_axis=0, concat_axis=0, tiled=True)
    out_grads = arrived_grads.reshape(-1, model_width)
    both_grads, row_grads = expert_backward(
        gate_pre, up_pre, gate_sigmoid, out_grads, gate_w, up_w, down_w
    )
    returned_grads = lax.all_to_all(
        row_grads.reshape(block_shape), "expert", split_axis=0, concat_axis=0, tiled=True
    )
    flat_rows = row_index.reshape(-1)
    out_values = returned_out.reshape(-1, model_width).astype(jnp.float32)
    mixed_sum = (
        jnp.zeros((tok_rows + 1, model_width), jnp.float32)
        .at[flat_rows]
        .add(slot_gate.reshape(-1)[:, None] * out_values)
    )
    layer_out = mixed_sum[:tok_rows].astype(jnp.bfloat16)
    token_sum = (
        jnp.zeros((tok_rows + 1, model_width), jnp.float32)
        .at[flat_rows]
        .add(returned_grads.reshape(-1, model_width).astype(jnp.float32))
    )
    grad_tokens = token_sum[:tok_rows].astype(jnp.bfloat16)
    gate_dots = jnp.sum(grad_rows.reshape(-1, model_width).astype(jnp.float32) * out_values, axis=1)
    gate_grads = (
        jnp.zeros((flat_total + 1,), jnp.float32)
        .at[slot_index.reshape(-1)]
        .add(gate_dots)[:flat_total]
        .reshape(tok_rows, pick_count)
    )
    contract_first = (((0,), (0,)), ((), ()))
    columns = row_block
    gate_up_sum = lax.psum_scatter(
        lax.dot_general(
            columns, both_grads, contract_first, preferred_element_type=jnp.float32
        ).astype(jnp.bfloat16),
        "dp",
        scatter_dimension=0,
        tiled=True,
    ).astype(jnp.float32)
    columns = hidden
    down_sum = lax.psum_scatter(
        lax.dot_general(
            columns, out_grads, contract_first, preferred_element_type=jnp.float32
        ).astype(jnp.bfloat16),
        "dp",
        scatter_dimension=0,
        tiled=True,
    )
    grad_gate = gate_up_sum[:, :hidden_width].astype(jnp.bfloat16)
    grad_up = gate_up_sum[:, hidden_width:].astype(jnp.bfloat16)
    return (layer_out, grad_tokens, gate_grads, grad_gate[None], grad_up[None], down_sum[None])


def solution(mesh):
    return jax.shard_map(
        on_device,
        mesh=mesh,
        in_specs=(
            P(("dp", "expert"), None),
            P(("dp", "expert"), None),
            P(("dp", "expert"), None),
            P(("dp", "expert"), None),
            P(),
            P("expert", None, None),
            P("expert", None, None),
            P("expert", None, None),
        ),
        out_specs=(
            P(("dp", "expert"), None),
            P(("dp", "expert"), None),
            P(("dp", "expert"), None),
            P("expert", "dp", None),
            P("expert", "dp", None),
            P("expert", "dp", None),
        ),
        check_vma=False,
    )
```

profile of v0, /device:TPU:16, one launch (start us, length us, event | category | flops | bytes accessed | tf_op | source)
XLA Modules:
  0.0 552.4 jit_solution(1550108923154190763)
XLA Ops:
  7.2 0.7 broadcast_compare_fusion
  7.9 0.8 copy.61
  8.7 0.1 copy.64
  8.8 0.1 reshape.145
  8.9 6.6 %gather_fusion = s32[1024]{0:T(1024)S(1)} fusion(s32[32]{0:T(128)S(1)} %copy-done, s32[1024]{0:T(1024)S(1)} %broadcast_clamp_fusion), kind=kCustom, calls=%fused_computation | custom fusion | bytes 12288 | tf_op jit(solution)/shard_map/gather | solution.py:68
  15.5 0.1 reshape.221
  15.9 0.1 copy.66
  16.0 0.2 reduce_window_sum.11
  16.2 0.1 reshape.175
  16.3 7.1 %gather_fusion.4 = s32[1024]{0:T(1024)S(1)} fusion(s32[128,32]{1,0:T(8,128)S(1)} %sub.12, s32[1024]{0:T(1024)S(1)} %reshape.175), kind=kCustom, calls=%fused_computation.4 | custom fusion | bytes 16384 | tf_op jit(solution)/shard_map/jit(take_along_axis)/gather | solution.py:21
  23.6 0.1 multiply_reduce_fusion
  23.7 0.1 copy.70
  23.8 0.1 reshape.205
  23.9 0.1 copy.72
  24.0 0.1 reshape.130
  24.1 0.1 reshape.207
  24.2 4.3 scatter_custom_fusion.3
  28.7 0.1 reshape.161
  28.9 0.1 reshape.153
  29.0 3.1 gather_fusion.1
  32.3 2.5 gather_fusion.3
  34.8 2.0 fusion
  36.7 14.2 %all-to-all-start.2 = ((bf16[32,16,2048]{2,1,0:T(8,128)(2,1)}), bf16[32,16,2048]{2,1,0:T(8,128)(2,1)S(1)}, u32[]{:S(2)}, u32[]{:S(2)}) async-start(bf16[32,16,2048]{2,1,0:T(8,128)(2,1)} %fusion), calls=%async_computation.2 | async-start | bytes 4194304 | tf_op jit(solution)/shard_map/all_to_all | solution.py:93
  51.0 3.4 gather_fusion.2
  54.3 49.7 %all-to-all-done.2 = bf16[32,16,2048]{2,1,0:T(8,128)(2,1)S(1)} async-done(((bf16[32,16,2048]{2,1,0:T(8,128)(2,1)}), bf16[32,16,2048]{2,1,0:T(8,128)(2,1)S(1)}, u32[]{:S(2)}, u32[]{:S(2)}) %all-to-all-start.2) | async-done | bytes 2097184 | tf_op jit(solution)/shard_map/all_to_all | solution.py:93
  104.1 5.0 all-to-all-start
  109.1 3.1 collective-permute-start.2
  112.2 0.6 collective-permute-start.1
  112.8 3.2 collective-permute-start
  116.0 0.6 dynamic_slice.3
  117.2 81.9 %collective-permute-done.2 = bf16[768,2048]{1,0:T(8,128)(2,1)} collective-permute-done((bf16[768,2048]{1,0:T(8,128)(2,1)}, bf16[768,2048]{1,0:T(8,128)(2,1)}, u32[]{:S(2)}, u32[]{:S(2)}) %collective-permute-start.2) | collective-permute-done | bytes 3145760 | tf_op jit(solution)/shard_map/ppermute | solution.py:10
  199.1 6.0 %fusion.10 = f32[512,768]{1,0:T(8,128)} fusion(bf16[512,2048]{1,0:T(8,128)(2,1)S(1)} %bitcast.73, bf16[768,2048]{1,0:T(8,128)(2,1)} %collective-permute-done.2, pred[]{:T(512)} %bitcast.7, bf16[1,768,2048]{2,1,0:T(8,128)(2,1)} %param.15), kind=kOutput, calls=%fused_computation.33 | convolution fusion | flops 1612185600 | bytes 9961473 | tf_op jit(solution)/shard_map/dot_general | solution.py:38
  205.1 61.4 %collective-permute-done.1 = bf16[2048,768]{1,0:T(8,128)(2,1)} collective-permute-done((bf16[2048,768]{1,0:T(8,128)(2,1)}, bf16[2048,768]{1,0:T(8,128)(2,1)}, u32[]{:S(2)}, u32[]{:S(2)}) %collective-permute-start.1) | collective-permute-done | bytes 3145760 | tf_op jit(solution)/shard_map/ppermute | solution.py:10
  266.5 5.4 fusion.9
  271.9 49.3 %collective-permute-done = bf16[2048,768]{1,0:T(8,128)(2,1)} collective-permute-done((bf16[2048,768]{1,0:T(8,128)(2,1)}, bf16[2048,768]{1,0:T(8,128)(2,1)}, u32[]{:S(2)}, u32[]{:S(2)}) %collective-permute-start) | collective-permute-done | bytes 3145760 | tf_op jit(solution)/shard_map/ppermute | solution.py:10
  321.3 5.9 %multiply_convert_fusion.1 = (bf16[512,768]{1,0:T(8,128)(2,1)S(1)}, bf16[512,768]{1,0:T(8,128)(2,1)}, bf16[512,768]{1,0:T(8,128)(2,1)S(1)}) fusion(f32[512,768]{1,0:T(8,128)S(1)} %copy-done.15, f32[512,768]{1,0:T(8,128)S(1)} %fusion.9, bf16[512,2048]{1,0:T(8,128)(2,1)} %bitcast.6, bf16[2048,768]{1,0:T(8,128)(2,1)} %collective-permute-done, pred[]{:T(512)} %bitcast.7, ...), kind=kOutput, calls=%fused_computation.27 | convolution fusion | flops 1618477056 | bytes 13893633 | tf_op jit(solution)/shard_map/dot_general | solution.py:28
  327.2 0.9 copy-done.11
  328.1 0.3 copy-done.13
  328.4 7.2 %convolution_convert_fusion = bf16[2048,1536]{1,0:T(8,128)(2,1)} fusion(bf16[512,2048]{1,0:T(8,128)(2,1)} %bitcast.6, bf16[512,768]{1,0:T(8,128)(2,1)S(1)} %get-tuple-element.40, bf16[512,768]{1,0:T(8,128)(2,1)S(1)} %get-tuple-element.38), kind=kOutput, calls=%fused_computation.9 | convolution fusion | flops 3227516928 | bytes 9961472 | tf_op jit(solution)/shard_map/dot_general | solution.py:125
  335.6 1.9 copy-done.8
  337.4 5.3 convolution_convert_fusion.2
  342.7 10.1 %all-to-all-start.1 = ((bf16[32,16,2048]{2,1,0:T(8,128)(2,1)}), bf16[32,16,2048]{2,1,0:T(8,128)(2,1)S(1)}, u32[]{:S(2)}, u32[]{:S(2)}) async-start(bf16[32,16,2048]{2,1,0:T(8,128)(2,1)} %bitcast.76), calls=%async_computation.1 | async-start | bytes 4194304 | tf_op jit(solution)/shard_map/all_to_all | solution.py:90
  352.8 0.6 reduce-scatter.5.cloned.1.call-start
  353.4 5.1 convolution_convert_fusion.1
  358.5 1.1 copy-done.12
  359.6 4.8 fusion.8
  364.5 5.1 add_convert_fusion
  369.6 11.0 %all-to-all-done.1 = bf16[32,16,2048]{2,1,0:T(8,128)(2,1)S(1)} async-done(((bf16[32,16,2048]{2,1,0:T(8,128)(2,1)}), bf16[32,16,2048]{2,1,0:T(8,128)(2,1)S(1)}, u32[]{:S(2)}, u32[]{:S(2)}) %all-to-all-start.1) | async-done | bytes 2097184 | tf_op jit(solution)/shard_map/all_to_all | solution.py:90
  380.6 6.7 %all-to-all-start.3 = ((bf16[32,16,2048]{2,1,0:T(8,128)(2,1)}), bf16[32,16,2048]{2,1,0:T(8,128)(2,1)}, u32[]{:S(2)}, u32[]{:S(2)}) async-start(bf16[32,16,2048]{2,1,0:T(8,128)(2,1)} %bitcast.75), calls=%async_computation.3 | async-start | bytes 4194304 | tf_op jit(solution)/shard_map/all_to_all | solution.py:98
  387.4 0.1 reshape.135
  387.6 0.1 reshape.129
  387.7 2.2 fusion.1
  389.9 0.1 reshape.201
  390.0 4.1 scatter_custom_fusion.2
  394.1 0.7 copy.76
  394.8 58.6 %all-to-all-done.3 = bf16[32,16,2048]{2,1,0:T(8,128)(2,1)} async-done(((bf16[32,16,2048]{2,1,0:T(8,128)(2,1)}), bf16[32,16,2048]{2,1,0:T(8,128)(2,1)}, u32[]{:S(2)}, u32[]{:S(2)}) %all-to-all-start.3) | async-done | bytes 2097184 | tf_op jit(solution)/shard_map/all_to_all | solution.py:98
  453.4 8.6 %scatter_custom_fusion.1 = f32[129,2048]{1,0:T(8,128)S(1)} fusion(s32[512]{0:T(512)S(1)} %bitcast.78, bf16[512,2048]{1,0:T(8,128)(2,1)} %bitcast.22, f32[]{:T(128)} %constant.30.clone.1), kind=kCustom, calls=%fused_computation.14 | custom fusion | flops 2097152 | bytes 3153924 | tf_op jit(solution)/shard_map/scatter-add | solution.py:112
  462.0 0.9 slice.43
  462.9 2.4 bitcast_multiply_fusion
  465.2 8.8 %scatter_custom_fusion = f32[129,2048]{1,0:T(8,128)S(1)} fusion(s32[512]{0:T(512)S(1)} %bitcast.79, f32[512,2048]{1,0:T(8,128)} %bitcast_multiply_fusion, f32[]{:T(128)} %constant.30.clone.1), kind=kCustom, calls=%fused_computation.37 | custom fusion | flops 1048576 | bytes 1057280 | tf_op jit(solution)/shard_map/scatter-add | solution.py:106
  474.0 0.9 slice.44
  474.9 16.3 %reduce-scatter.3.cloned.1.call-done = bf16[256,1536]{1,0:T(8,128)(2,1)} async-done(((bf16[2048,1536]{1,0:T(8,128)(2,1)}), bf16[256,1536]{1,0:T(8,128)(2,1)}) %reduce-scatter.3.cloned.1.call-update) | async-done | bytes 786448 | tf_op jit(solution)/shard_map/reduce_scatter | solution.py:124
  491.2 2.0 slice_bitcast_fusion
  493.2 52.1 %reduce-scatter.5.cloned.1.call-done = bf16[96,2048]{1,0:T(8,128)(2,1)} async-done(((bf16[768,2048]{1,0:T(8,128)(2,1)}), bf16[96,2048]{1,0:T(8,128)(2,1)}) %reduce-scatter.5.cloned.1.call-update) | async-done | bytes 393232 | tf_op jit(solution)/shard_map/reduce_scatter | solution.py:133
  (65 shorter events, 1.3 us)
Async XLA Ops:
  7.2 1.7 copy-start
  16.3 7.3 %copy-start.7 = (s32[2]{0:T(128)S(1)}, s32[2]{0:T(128)}, u32[]{:S(2)}) copy-start(s32[2]{0:T(128)} %constant.96) | copy-start | bytes 28
  16.3 7.4 %copy-start.6 = (s32[2]{0:T(128)S(1)}, s32[2]{0:T(128)}, u32[]{:S(2)}) copy-start(s32[2]{0:T(128)} %constant.93) | copy-start | bytes 28
  16.3 7.6 %copy-start.5 = (f32[128,8]{0,1:T(8,128)S(1)}, f32[128,8]{0,1:T(8,128)}, u32[]{:S(2)}) copy-start(f32[128,8]{0,1:T(8,128)} %param.11) | copy-start | bytes 12292
  29.0 3.2 copy-start.3
  34.8 2.0 copy-start.1
  36.7 14.2 %copy-start.4 = (bf16[128,2048]{1,0:T(8,128)(2,1)S(1)}, bf16[128,2048]{1,0:T(8,128)(2,1)}, u32[]{:S(2)}) copy-start(bf16[128,2048]{1,0:T(8,128)(2,1)} %param.8) | copy-start | bytes 1572868
  36.7 67.3 %all-to-all-start.2 = ((bf16[32,16,2048]{2,1,0:T(8,128)(2,1)}), bf16[32,16,2048]{2,1,0:T(8,128)(2,1)S(1)}, u32[]{:S(2)}, u32[]{:S(2)}) async-start(bf16[32,16,2048]{2,1,0:T(8,128)(2,1)} %fusion), calls=%async_computation.2 | async-start | bytes 4194304 | tf_op jit(solution)/shard_map/all_to_all | solution.py:93
  104.1 95.0 %copy-start.2 = (bf16[32,16,2048]{2,1,0:T(8,128)(2,1)}, bf16[32,16,2048]{2,1,0:T(8,128)(2,1)S(1)}, u32[]{:S(2)}) copy-start(bf16[32,16,2048]{2,1,0:T(8,128)(2,1)S(1)} %all-to-all-done.2) | copy-start | bytes 6291460
  104.1 162.5 %all-to-all-start = ((bf16[32,16,2048]{2,1,0:T(8,128)(2,1)}), bf16[32,16,2048]{2,1,0:T(8,128)(2,1)}, u32[]{:S(2)}, u32[]{:S(2)}) async-start(bf16[32,16,2048]{2,1,0:T(8,128)(2,1)} %bitcast.5), calls=%async_computation | async-start | bytes 4194304 | tf_op jit(solution)/shard_map/all_to_all | solution.py:85
  109.1 382.1 %reduce-scatter.3.cloned.1.call-start = ((), (), s32[]{:S(2)}) async-start(), calls=%async_computation.6 | async-start | bytes 7077888 | tf_op jit(solution)/shard_map/reduce_scatter | solution.py:124
  109.1 90.0 %collective-permute-start.2 = (bf16[768,2048]{1,0:T(8,128)(2,1)}, bf16[768,2048]{1,0:T(8,128)(2,1)}, u32[]{:S(2)}, u32[]{:S(2)}) collective-permute-start(bf16[768,2048]{1,0:T(8,128)(2,1)} %bitcast.81), channel_id=1, source_target_pairs={{0,16},{1,17},{2,18},{3,19},{4,20},{5,21},{6,22},{7,23},{8,24},{9,... | collective-permute-start | bytes 9437192 | tf_op jit(solution)/shard_map/ppermute | solution.py:10
  112.2 154.3 %collective-permute-start.1 = (bf16[2048,768]{1,0:T(8,128)(2,1)}, bf16[2048,768]{1,0:T(8,128)(2,1)}, u32[]{:S(2)}, u32[]{:S(2)}) collective-permute-start(bf16[2048,768]{1,0:T(8,128)(2,1)} %bitcast.82), channel_id=1, source_target_pairs={{0,16},{1,17},{2,18},{3,19},{4,20},{5,21},{6,22},{7,23},{8,24},{9,... | collective-permute-start | bytes 9437192 | tf_op jit(solution)/shard_map/ppermute | solution.py:10
  112.8 208.5 %collective-permute-start = (bf16[2048,768]{1,0:T(8,128)(2,1)}, bf16[2048,768]{1,0:T(8,128)(2,1)}, u32[]{:S(2)}, u32[]{:S(2)}) collective-permute-start(bf16[2048,768]{1,0:T(8,128)(2,1)} %bitcast.83), channel_id=1, source_target_pairs={{0,16},{1,17},{2,18},{3,19},{4,20},{5,21},{6,22},{7,23},{8,24},{9,... | collective-permute-start | bytes 9437192 | tf_op jit(solution)/shard_map/ppermute | solution.py:10
  266.5 54.7 %copy-start.9 = (bf16[1,2048,768]{2,1,0:T(8,128)(2,1)S(1)}, bf16[1,2048,768]{2,1,0:T(8,128)(2,1)}, u32[]{:S(2)}) copy-start(bf16[1,2048,768]{2,1,0:T(8,128)(2,1)} %param.13) | copy-start | bytes 9437188
  266.5 54.7 %copy-start.15 = (f32[512,768]{1,0:T(8,128)S(1)}, f32[512,768]{1,0:T(8,128)}, u32[]{:S(2)}) copy-start(f32[512,768]{1,0:T(8,128)} %fusion.10) | copy-start | bytes 4718596
  327.2 0.9 copy-start.11
  327.2 1.2 copy-start.13
  335.6 1.9 copy-start.8
  342.7 10.7 %copy-start.16 = (bf16[512,768]{1,0:T(8,128)(2,1)S(1)}, bf16[512,768]{1,0:T(8,128)(2,1)}, u32[]{:S(2)}) copy-start(bf16[512,768]{1,0:T(8,128)(2,1)} %get-tuple-element.39) | copy-start | bytes 2359300
  342.7 37.9 %all-to-all-start.1 = ((bf16[32,16,2048]{2,1,0:T(8,128)(2,1)}), bf16[32,16,2048]{2,1,0:T(8,128)(2,1)S(1)}, u32[]{:S(2)}, u32[]{:S(2)}) async-start(bf16[32,16,2048]{2,1,0:T(8,128)(2,1)} %bitcast.76), calls=%async_computation.1 | async-start | bytes 4194304 | tf_op jit(solution)/shard_map/all_to_all | solution.py:90
  352.8 192.5 %reduce-scatter.5.cloned.1.call-start = ((), (), s32[]{:S(2)}) async-start(), calls=%async_computation.7 | async-start | bytes 3538944 | tf_op jit(solution)/shard_map/reduce_scatter | solution.py:133
  358.5 1.1 copy-start.12
  359.6 4.8 copy-start.10
  359.6 4.9 copy-start.14
  380.6 72.8 %all-to-all-start.3 = ((bf16[32,16,2048]{2,1,0:T(8,128)(2,1)}), bf16[32,16,2048]{2,1,0:T(8,128)(2,1)}, u32[]{:S(2)}, u32[]{:S(2)}) async-start(bf16[32,16,2048]{2,1,0:T(8,128)(2,1)} %bitcast.75), calls=%async_computation.3 | async-start | bytes 4194304 | tf_op jit(solution)/shard_map/all_to_all | solution.py:98
Sparse Core Ops, SparseCore 0:
  335.7 155.4 reduce-scatter.2
  494.3 50.9 reduce-scatter.4
where the time goes:
time: 560 us; the launch traced here: 552 us
  waiting for transfers between devices  380 us (68%)
  matrix products  44.8 us (8%)
  starting transfers between devices  43.4 us (8%)
  local copies, waits for them, and re-layouts  39.2 us (7%)
  other arithmetic  29.3 us (5%)
  between operations  15.3 us (3%)
    ppermute x3, waiting for transfers between devices, partner(): lax.ppermute(x, axis, [(i, i ^ 1 << bit) for i in range(lax.axis_size(axi...  193 us
    all_to_all x1, waiting for transfers between devices, on_device(): lax.all_to_all(row_grads.reshape(block_shape), 'expert', split_axis=0, co...  58.6 us
    reduce_scatter x1, waiting for transfers between devices, on_device(): lax.psum_scatter(lax.dot_general(columns, out_grads, contract_first, pref...  52.1 us
    all_to_all x1, waiting for transfers between devices, on_device(): lax.all_to_all(send_grads, 'expert', split_axis=0, concat_axis=0, tiled=T...  49.7 us
    reduce_scatter x1, waiting for transfers between devices, on_device(): lax.psum_scatter(lax.dot_general(columns, both_grads, contract_first, pre...  16.3 us
    all_to_all x1, starting transfers between devices, on_device(): lax.all_to_all(send_grads, 'expert', split_axis=0, concat_axis=0, tiled=T...  14.2 us
  transfers between devices with their start and end apart: 9, of which 8 were waited for; matrix products, arithmetic and copies ran while one was open for 12% of the time, Pallas kernels for 0%

commit v1 on v0

--- a/solution.py
+++ b/solution.py
@@ -53,7 +53,6 @@
 
 def on_device(tokens, out_grad, expert_ids, route_gates, swap_flags, gate_proj, up_proj, down_proj):
     devices = lax.axis_size("expert")
-    half_axis = devices // 2
     swap_bit = devices.bit_length() - 2
     my_index = lax.axis_index("expert")
     tok_rows, model_width = tokens.shape
@@ -64,13 +63,8 @@
     in_layer = expert_ids < devices
     is_moved = swap_flags[my_index] == 1
     own_weights = (gate_proj[0], up_proj[0], down_proj[0])
-    clipped = jnp.minimum(expert_ids, devices - 1)
-    moved_to = jnp.where(swap_flags[clipped] == 1, (expert_ids + half_axis) % devices, expert_ids)
-    target = jnp.where(in_layer, moved_to, devices)
-    partner_weights = partner((own_weights[0], own_weights[1], own_weights[2]), "expert", swap_bit)
-    gate_w = jnp.where(is_moved, partner_weights[0], own_weights[0])
-    up_w = jnp.where(is_moved, partner_weights[1], own_weights[1])
-    down_w = jnp.where(is_moved, partner_weights[2], own_weights[2])
+    target = jnp.where(in_layer, expert_ids, devices)
+    gate_w, up_w, down_w = own_weights
     slot_index = slot_table(target, devices, slot_most)
     row_index = slot_index // pick_count
     zero_row = jnp.zeros((1, model_width), jnp.bfloat16)
@@ -128,7 +122,7 @@
         "dp",
         scatter_dimension=0,
         tiled=True,
-    ).astype(jnp.float32)
+    )
     columns = hidden
     down_sum = lax.psum_scatter(
         lax.dot_general(
@@ -138,8 +132,12 @@
         scatter_dimension=0,
         tiled=True,
     )
-    grad_gate = gate_up_sum[:, :hidden_width].astype(jnp.bfloat16)
-    grad_up = gate_up_sum[:, hidden_width:].astype(jnp.bfloat16)
+    other_gate_up = partner(gate_up_sum, "expert", swap_bit)
+    other_down = partner(down_sum, "expert", swap_bit)
+    gate_up_sum = jnp.where(is_moved, other_gate_up, gate_up_sum)
+    down_sum = jnp.where(is_moved, other_down, down_sum)
+    grad_gate = gate_up_sum[:, :hidden_width]
+    grad_up = gate_up_sum[:, hidden_width:]
     return (layer_out, grad_tokens, gate_grads, grad_gate[None], grad_up[None], down_sum[None])
 
 

time: 560 us -> 399 us (0.71)
  waiting for transfers between devices: 380 us -> 208 us
  other arithmetic: 29.3 us -> 37.4 us
    ppermute x3 -> x2, waiting for transfers between devices: 193 us -> 0.01 us  [partner(): lax.ppermute(x, axis, [(i, i ^ 1 << bit) for i in range(lax.axis_size(axi...]
    reduce_scatter x1, waiting for transfers between devices: 16.3 us -> 85.4 us  [on_device(): lax.psum_scatter(lax.dot_general(columns, both_grads, contract_first, pre...]
    all_to_all x1, waiting for transfers between devices: 58.6 us -> 0.01 us  [on_device(): lax.all_to_all(row_grads.reshape(block_shape), 'expert', split_axis=0, co...]
    reduce_scatter x1, waiting for transfers between devices: 52.1 us -> 0.01 us  [on_device(): lax.psum_scatter(lax.dot_general(columns, out_grads, contract_first, pref...]
    all_to_all x1, waiting for transfers between devices: 11 us -> 58.3 us  [on_device(): lax.all_to_all(expert_out.reshape(block_shape), 'expert', split_axis=0, c...]
    all_to_all x1, waiting for transfers between devices: 0.01 us -> 37.9 us  [on_device(): lax.all_to_all(send_rows, 'expert', split_axis=0, concat_axis=0, tiled=True)]
    all_to_all x1, waiting for transfers between devices: 49.7 us -> 26.8 us  [on_device(): lax.all_to_all(send_grads, 'expert', split_axis=0, concat_axis=0, tiled=T...]
    all_to_all x1, starting transfers between devices: 5.02 us -> 14.2 us  [on_device(): lax.all_to_all(send_rows, 'expert', split_axis=0, concat_axis=0, tiled=True)]
  transfers between devices with their start and end apart: 9 -> 8, of which waited for: 8 -> 4; matrix products, arithmetic and copies ran while one was open for 12% -> 20% of each run, Pallas kernels for 0% -> 0%
where the time goes in v1:
time: 399 us; the launch traced here: 392 us
  waiting for transfers between devices  208 us (52%)
  starting transfers between devices  48.4 us (12%)
  local copies, waits for them, and re-layouts  41.3 us (10%)
  matrix products  40.8 us (10%)
  other arithmetic  37.4 us (9%)
  between operations  15.2 us (4%)
    reduce_scatter x1, waiting for transfers between devices, on_device(): lax.psum_scatter(lax.dot_general(columns, both_grads, contract_first, pre...  85.4 us
    all_to_all x1, waiting for transfers between devices, on_device(): lax.all_to_all(expert_out.reshape(block_shape), 'expert', split_axis=0, c...  58.3 us
    all_to_all x1, waiting for transfers between devices, on_device(): lax.all_to_all(send_rows, 'expert', split_axis=0, concat_axis=0, tiled=True)  37.9 us
    all_to_all x1, waiting for transfers between devices, on_device(): lax.all_to_all(send_grads, 'expert', split_axis=0, concat_axis=0, tiled=T...  26.8 us
    all_to_all x1, starting transfers between devices, on_device(): lax.all_to_all(expert_out.reshape(block_shape), 'expert', split_axis=0, c...  17 us
    all_to_all x1, starting transfers between devices, on_device(): lax.all_to_all(send_rows, 'expert', split_axis=0, concat_axis=0, tiled=True)  14.2 us
    scatter-add x1, other arithmetic, on_device(): mixed_sum = jnp.zeros((tok_rows + 1, model_width), jnp.float32).at[flat_r...  9.68 us
    scatter-add x1, other arithmetic, on_device(): token_sum = jnp.zeros((tok_rows + 1, model_width), jnp.float32).at[flat_r...  9.17 us
  transfers between devices with their start and end apart: 8, of which 4 were waited for; matrix products, arithmetic and copies ran while one was open for 20% of the time, Pallas kernels for 0%

profile of v1, /device:TPU:16, one launch (start us, length us, event | category | flops | bytes accessed | tf_op | source)
XLA Modules:
  0.0 391.7 jit_solution(6333458574628993169)
XLA Ops:
  7.2 0.8 broadcast_compare_fusion
  8.0 0.9 copy.54
  8.9 0.1 copy.53
  9.3 0.1 copy.56
  9.4 0.2 reduce_window_sum.11
  9.6 0.1 reshape.167
  9.7 7.1 %gather_fusion.3 = s32[1024]{0:T(1024)S(1)} fusion(s32[128,32]{1,0:T(8,128)S(1)} %sub.12, s32[1024]{0:T(1024)S(1)} %reshape.167), kind=kCustom, calls=%fused_computation.3 | custom fusion | bytes 16384 | tf_op jit(solution)/shard_map/jit(take_along_axis)/gather | solution.py:21
  16.8 0.1 reshape.170
  16.9 0.1 and_reduce_fusion
  17.0 0.1 multiply_reduce_fusion
  17.1 0.1 copy.60
  17.2 0.1 reshape.197
  17.3 0.1 reshape.199
  17.4 4.3 %scatter_custom_fusion.3 = s32[512]{0:T(512)S(1)} fusion(s32[1024]{0:T(1024)S(1)} %reshape.197, s32[1024]{0:T(1024)S(1)} %reshape.199, s32[]{:T(128)} %constant.20.clone.1), kind=kCustom, calls=%fused_computation.78 | custom fusion | bytes 2052
  21.7 0.1 reshape.139
  21.8 0.1 copy.64
  21.9 0.1 reshape.153
  22.0 1.9 concatenate.17
  23.9 6.4 %gather_fusion.1 = bf16[512,2048]{1,0:T(8,128)(2,1)} fusion(bf16[129,2048]{1,0:T(8,128)(2,1)} %concatenate.17, s32[1024]{0:T(1024)S(1)} %pad_clamp_fusion), kind=kCustom, calls=%fused_computation.1 | custom fusion | bytes 4196352 | tf_op jit(solution)/shard_map/gather | solution.py:75
  30.3 14.2 %all-to-all-start = ((bf16[32,16,2048]{2,1,0:T(8,128)(2,1)}), bf16[32,16,2048]{2,1,0:T(8,128)(2,1)}, u32[]{:S(2)}, u32[]{:S(2)}) async-start(bf16[32,16,2048]{2,1,0:T(8,128)(2,1)} %bitcast.66), calls=%async_computation | async-start | bytes 4194304 | tf_op jit(solution)/shard_map/all_to_all | solution.py:79
  44.6 0.1 copy.62
  44.7 0.1 reshape.130
  44.8 0.1 reshape.145
  44.9 3.1 gather_fusion
  48.1 0.1 reshape.144
  48.2 1.9 concatenate.18
  50.1 6.4 %gather_fusion.2 = bf16[512,2048]{1,0:T(8,128)(2,1)} fusion(bf16[129,2048]{1,0:T(8,128)(2,1)} %concatenate.18, s32[1024]{0:T(1024)S(1)} %pad_clamp_fusion), kind=kCustom, calls=%fused_computation.2 | custom fusion | bytes 4196352 | tf_op jit(solution)/shard_map/gather | solution.py:76
  56.4 3.3 fusion
  59.7 37.9 %all-to-all-done = bf16[32,16,2048]{2,1,0:T(8,128)(2,1)} async-done(((bf16[32,16,2048]{2,1,0:T(8,128)(2,1)}), bf16[32,16,2048]{2,1,0:T(8,128)(2,1)}, u32[]{:S(2)}, u32[]{:S(2)}) %all-to-all-start) | async-done | bytes 2097184 | tf_op jit(solution)/shard_map/all_to_all | solution.py:79
  97.6 5.0 %all-to-all-start.2 = ((bf16[32,16,2048]{2,1,0:T(8,128)(2,1)}), bf16[32,16,2048]{2,1,0:T(8,128)(2,1)}, u32[]{:S(2)}, u32[]{:S(2)}) async-start(bf16[32,16,2048]{2,1,0:T(8,128)(2,1)} %fusion), calls=%async_computation.2 | async-start | bytes 4194304 | tf_op jit(solution)/shard_map/all_to_all | solution.py:87
  102.6 0.6 reduce-scatter.5.cloned.1.call-start
  103.2 5.5 %fusion.10 = f32[512,768]{1,0:T(8,128)} fusion(bf16[512,2048]{1,0:T(8,128)(2,1)} %bitcast.6, bf16[1,2048,768]{2,1,0:T(8,128)(2,1)} %param.14), kind=kOutput, calls=%fused_computation.24 | convolution fusion | flops 1610612736 | bytes 6815744 | tf_op jit(solution)/shard_map/dot_general | solution.py:29
  108.7 26.8 %all-to-all-done.2 = bf16[32,16,2048]{2,1,0:T(8,128)(2,1)} async-done(((bf16[32,16,2048]{2,1,0:T(8,128)(2,1)}), bf16[32,16,2048]{2,1,0:T(8,128)(2,1)}, u32[]{:S(2)}, u32[]{:S(2)}) %all-to-all-start.2) | async-done | bytes 2097184 | tf_op jit(solution)/shard_map/all_to_all | solution.py:87
  135.5 4.5 %fusion.4 = f32[512,768]{1,0:T(8,128)S(1)} fusion(bf16[512,2048]{1,0:T(8,128)(2,1)} %bitcast.13, bf16[1,768,2048]{2,1,0:T(8,128)(2,1)} %param.15), kind=kOutput, calls=%fused_computation.18 | convolution fusion | flops 1610612736 | bytes 6815744 | tf_op jit(solution)/shard_map/dot_general | solution.py:38
  140.0 5.1 %multiply_convert_fusion.1 = (bf16[512,768]{1,0:T(8,128)(2,1)}, bf16[512,768]{1,0:T(8,128)(2,1)S(1)}, bf16[512,768]{1,0:T(8,128)(2,1)}) fusion(f32[512,768]{1,0:T(8,128)S(1)} %fusion.4, f32[512,768]{1,0:T(8,128)S(1)} %copy-done.9, bf16[512,2048]{1,0:T(8,128)(2,1)} %bitcast.6, bf16[1,2048,768]{2,1,0:T(8,128)(2,1)S(1)} %copy-done), kind=kOutput, calls=%fused_computation.35 | convolution fusion | flops 1616904192 | bytes 10747904 | tf_op jit(solution)/shard_map/dot_general | solution.py:28
  145.1 0.9 copy-done.8
  146.0 5.1 %convolution_convert_fusion.1 = bf16[768,2048]{1,0:T(8,128)(2,1)} fusion(bf16[512,768]{1,0:T(8,128)(2,1)S(1)} %get-tuple-element.39, bf16[512,2048]{1,0:T(8,128)(2,1)} %bitcast.13), kind=kOutput, calls=%fused_computation.17 | convolution fusion | flops 1612185600 | bytes 6029312 | tf_op jit(solution)/shard_map/dot_general | solution.py:128
  151.2 8.1 %convolution_convert_fusion = bf16[2048,1536]{1,0:T(8,128)(2,1)} fusion(bf16[512,2048]{1,0:T(8,128)(2,1)} %bitcast.6, bf16[512,768]{1,0:T(8,128)(2,1)} %get-tuple-element.40, bf16[512,768]{1,0:T(8,128)(2,1)} %get-tuple-element.38), kind=kOutput, calls=%fused_computation.8 | convolution fusion | flops 3227516928 | bytes 9961472 | tf_op jit(solution)/shard_map/dot_general | solution.py:119
  159.3 5.4 %fusion.16 = bf16[512,2048]{1,0:T(8,128)(2,1)} fusion(bf16[512,768]{1,0:T(8,128)(2,1)} %copy-done.8, bf16[1,768,2048]{2,1,0:T(8,128)(2,1)} %param.15), kind=kOutput, calls=%fused_computation.30 | convolution fusion | flops 1611661312 | bytes 6029312 | tf_op jit(solution)/shard_map/dot_general | solution.py:32
  164.7 17.0 %all-to-all-start.1 = ((bf16[32,16,2048]{2,1,0:T(8,128)(2,1)}), bf16[32,16,2048]{2,1,0:T(8,128)(2,1)}, u32[]{:S(2)}, u32[]{:S(2)}) async-start(bf16[32,16,2048]{2,1,0:T(8,128)(2,1)} %bitcast.68), calls=%async_computation.1 | async-start | bytes 4194304 | tf_op jit(solution)/shard_map/all_to_all | solution.py:84
  181.7 4.0 %fusion.8 = f32[512,2048]{1,0:T(8,128)S(1)} fusion(bf16[512,768]{1,0:T(8,128)(2,1)} %get-tuple-element.40, bf16[1,2048,768]{2,1,0:T(8,128)(2,1)} %param.14), kind=kOutput, calls=%fused_computation.22 | convolution fusion | flops 1610612736 | bytes 8126464 | tf_op jit(solution)/shard_map/dot_general | solution.py:48
  185.8 3.1 add_convert_fusion
  188.9 58.3 %all-to-all-done.1 = bf16[32,16,2048]{2,1,0:T(8,128)(2,1)} async-done(((bf16[32,16,2048]{2,1,0:T(8,128)(2,1)}), bf16[32,16,2048]{2,1,0:T(8,128)(2,1)}, u32[]{:S(2)}, u32[]{:S(2)}) %all-to-all-start.1) | async-done | bytes 2097184 | tf_op jit(solution)/shard_map/all_to_all | solution.py:84
  247.2 5.4 %all-to-all-start.3 = ((bf16[32,16,2048]{2,1,0:T(8,128)(2,1)}), bf16[32,16,2048]{2,1,0:T(8,128)(2,1)}, u32[]{:S(2)}, u32[]{:S(2)}) async-start(bf16[32,16,2048]{2,1,0:T(8,128)(2,1)} %bitcast.67), calls=%async_computation.3 | async-start | bytes 4194304 | tf_op jit(solution)/shard_map/all_to_all | solution.py:92
  252.6 0.1 copy.65
  252.7 0.1 reshape.135
  252.8 0.1 reshape.129
  252.9 0.6 dynamic_slice.3
  254.2 3.1 fusion.1
  257.3 0.1 reshape.193
  257.4 3.9 scatter_custom_fusion.2
  261.3 0.1 reshape.136
  261.4 0.7 copy.66
  262.1 3.0 collective-permute-start.1
  265.1 85.4 %reduce-scatter.3.cloned.1.call-done = bf16[256,1536]{1,0:T(8,128)(2,1)} async-done(((bf16[2048,1536]{1,0:T(8,128)(2,1)}), bf16[256,1536]{1,0:T(8,128)(2,1)}) %reduce-scatter.3.cloned.1.call-update) | async-done | bytes 786448 | tf_op jit(solution)/shard_map/reduce_scatter | solution.py:118
  350.5 3.2 collective-permute-start
  353.7 3.9 bitcast_multiply_fusion
  357.5 9.7 %scatter_custom_fusion = f32[129,2048]{1,0:T(8,128)} fusion(s32[512]{0:T(512)S(1)} %bitcast.70, f32[512,2048]{1,0:T(8,128)} %bitcast_multiply_fusion, f32[]{:T(128)} %constant.19.clone.1), kind=kCustom, calls=%fused_computation.42 | custom fusion | flops 1048576 | bytes 1057280 | tf_op jit(solution)/shard_map/scatter-add | solution.py:100
  367.2 2.1 slice.40
  369.3 9.2 %scatter_custom_fusion.1 = f32[129,2048]{1,0:T(8,128)} fusion(s32[512]{0:T(512)S(1)} %bitcast.71, bf16[512,2048]{1,0:T(8,128)(2,1)} %bitcast.22, f32[]{:T(128)} %constant.19.clone.1), kind=kCustom, calls=%fused_computation.13 | custom fusion | flops 2097152 | bytes 3153924 | tf_op jit(solution)/shard_map/scatter-add | solution.py:106
  378.5 2.2 slice.39
  380.6 1.8 select_bitcast_fusion
  382.4 1.2 broadcast_select_fusion
  383.7 0.9 slice_bitcast_fusion
  (45 shorter events, 0.6 us)
Async XLA Ops:
  7.2 132.8 %copy-start = (bf16[1,2048,768]{2,1,0:T(8,128)(2,1)S(1)}, bf16[1,2048,768]{2,1,0:T(8,128)(2,1)}, u32[]{:S(2)}) copy-start(bf16[1,2048,768]{2,1,0:T(8,128)(2,1)} %param.13) | copy-start | bytes 9437188
  9.7 7.3 %copy-start.5 = (s32[2]{0:T(128)S(1)}, s32[2]{0:T(128)}, u32[]{:S(2)}) copy-start(s32[2]{0:T(128)} %constant.84) | copy-start | bytes 28
  9.7 7.3 %copy-start.4 = (s32[2]{0:T(128)S(1)}, s32[2]{0:T(128)}, u32[]{:S(2)}) copy-start(s32[2]{0:T(128)} %constant.81) | copy-start | bytes 28
  30.3 14.2 %copy-start.3 = (f32[128,8]{0,1:T(8,128)S(1)}, f32[128,8]{0,1:T(8,128)}, u32[]{:S(2)}) copy-start(f32[128,8]{0,1:T(8,128)} %param.11) | copy-start | bytes 12292
  30.3 67.3 %all-to-all-start = ((bf16[32,16,2048]{2,1,0:T(8,128)(2,1)}), bf16[32,16,2048]{2,1,0:T(8,128)(2,1)}, u32[]{:S(2)}, u32[]{:S(2)}) async-start(bf16[32,16,2048]{2,1,0:T(8,128)(2,1)} %bitcast.66), calls=%async_computation | async-start | bytes 4194304 | tf_op jit(solution)/shard_map/all_to_all | solution.py:79
  97.6 37.9 %all-to-all-start.2 = ((bf16[32,16,2048]{2,1,0:T(8,128)(2,1)}), bf16[32,16,2048]{2,1,0:T(8,128)(2,1)}, u32[]{:S(2)}, u32[]{:S(2)}) async-start(bf16[32,16,2048]{2,1,0:T(8,128)(2,1)} %fusion), calls=%async_computation.2 | async-start | bytes 4194304 | tf_op jit(solution)/shard_map/all_to_all | solution.py:87
  102.6 159.4 %reduce-scatter.5.cloned.1.call-start = ((), (), s32[]{:S(2)}) async-start(), calls=%async_computation.7 | async-start | bytes 3538944 | tf_op jit(solution)/shard_map/reduce_scatter | solution.py:127
  135.5 4.5 %copy-start.9 = (f32[512,768]{1,0:T(8,128)S(1)}, f32[512,768]{1,0:T(8,128)}, u32[]{:S(2)}) copy-start(f32[512,768]{1,0:T(8,128)} %fusion.10) | copy-start | bytes 4718596
  145.1 0.9 copy-start.8
  151.1 199.4 %reduce-scatter.3.cloned.1.call-start = ((), (), s32[]{:S(2)}) async-start(), calls=%async_computation.6 | async-start | bytes 7077888 | tf_op jit(solution)/shard_map/reduce_scatter | solution.py:118
  164.7 82.5 %all-to-all-start.1 = ((bf16[32,16,2048]{2,1,0:T(8,128)(2,1)}), bf16[32,16,2048]{2,1,0:T(8,128)(2,1)}, u32[]{:S(2)}, u32[]{:S(2)}) async-start(bf16[32,16,2048]{2,1,0:T(8,128)(2,1)} %bitcast.68), calls=%async_computation.1 | async-start | bytes 4194304 | tf_op jit(solution)/shard_map/all_to_all | solution.py:84
  181.7 4.1 %copy-start.7 = (bf16[512,768]{1,0:T(8,128)(2,1)S(1)}, bf16[512,768]{1,0:T(8,128)(2,1)}, u32[]{:S(2)}) copy-start(bf16[512,768]{1,0:T(8,128)(2,1)} %get-tuple-element.38) | copy-start | bytes 2359300
  247.2 5.7 %copy-start.6 = (s32[32]{0:T(128)S(1)}, s32[32]{0:T(128)}, u32[]{:S(2)}) copy-start(s32[32]{0:T(128)} %param.12) | copy-start | bytes 388
  247.2 122.1 %all-to-all-start.3 = ((bf16[32,16,2048]{2,1,0:T(8,128)(2,1)}), bf16[32,16,2048]{2,1,0:T(8,128)(2,1)}, u32[]{:S(2)}, u32[]{:S(2)}) async-start(bf16[32,16,2048]{2,1,0:T(8,128)(2,1)} %bitcast.67), calls=%async_computation.3 | async-start | bytes 4194304 | tf_op jit(solution)/shard_map/all_to_all | solution.py:92
  262.1 118.6 %collective-permute-start.1 = (bf16[96,2048]{1,0:T(8,128)(2,1)}, bf16[96,2048]{1,0:T(8,128)(2,1)}, u32[]{:S(2)}, u32[]{:S(2)}) collective-permute-start(bf16[96,2048]{1,0:T(8,128)(2,1)} %reduce-scatter.5.cloned.1.call-done), channel_id=1, source_target_pairs={{0,16},{1,17},{2,18},{3,19},{4,20},{5,21},{6,22},{7,23},{8,24},{9,... | collective-permute-start | bytes 1179656 | tf_op jit(solution)/shard_map/ppermute | solution.py:10
  350.5 31.9 %collective-permute-start = (bf16[256,1536]{1,0:T(8,128)(2,1)}, bf16[256,1536]{1,0:T(8,128)(2,1)}, u32[]{:S(2)}, u32[]{:S(2)}) collective-permute-start(bf16[256,1536]{1,0:T(8,128)(2,1)} %reduce-scatter.3.cloned.1.call-done), channel_id=1, source_target_pairs={{0,16},{1,17},{2,18},{3,19},{4,20},{5,21},{6,22},{7,23},{8,24},{9,... | collective-permute-start | bytes 2359304 | tf_op jit(solution)/shard_map/ppermute | solution.py:10
  369.3 11.3 %copy-start.2 = (bf16[96,2048]{1,0:T(8,128)(2,1)S(1)}, bf16[96,2048]{1,0:T(8,128)(2,1)}, u32[]{:S(2)}) copy-start(bf16[96,2048]{1,0:T(8,128)(2,1)} %reduce-scatter.5.cloned.1.call-done) | copy-start | bytes 1179652
  378.5 4.0 %copy-start.1 = (bf16[256,1536]{1,0:T(8,128)(2,1)S(1)}, bf16[256,1536]{1,0:T(8,128)(2,1)}, u32[]{:S(2)}) copy-start(bf16[256,1536]{1,0:T(8,128)(2,1)} %reduce-scatter.3.cloned.1.call-done) | copy-start | bytes 2359300
Sparse Core Ops, SparseCore 0:
  151.3 88.4 reduce-scatter.4
  242.3 108.1 reduce-scatter.2

commit v2 on v1

v2 whole, which is shorter than its diff:
```python
import jax
import jax.numpy as jnp
from jax import lax
from jax.sharding import PartitionSpec as P

MOST = 16
X_SIZE, HI_SIZE, Y_SIZE = 4, 2, 4
LO_SIZE, CORES = 4, 2
PLANE = X_SIZE * Y_SIZE
SIDE = 128

BOTH = ("dp", "expert")
PLANE_GROUPS = [
    [x * HI_SIZE * Y_SIZE + hi * Y_SIZE + y for x in range(X_SIZE) for y in range(Y_SIZE)]
    for hi in range(HI_SIZE)
]
LINE_GROUPS = [[lo * CORES + core for lo in range(LO_SIZE)] for core in range(CORES)]


def across(value):
    experts = lax.axis_size("expert")
    pairs = []
    for dp in range(lax.axis_size("dp")):
        lo, core = divmod(dp, CORES)
        other_dp = (LO_SIZE - 1 - lo) * CORES + core
        for expert in range(experts):
            pairs.append((dp * experts + expert, other_dp * experts + (expert ^ Y_SIZE)))
    return lax.ppermute(value, BOTH, pairs)


def to_plane(blocks):
    return lax.all_to_all(
        blocks, "expert", split_axis=0, concat_axis=0, axis_index_groups=PLANE_GROUPS, tiled=True
    )


def half_experts(half):
    place = lax.broadcasted_iota(jnp.int32, (1, 1, PLANE), 2)
    return (place // Y_SIZE) * (HI_SIZE * Y_SIZE) + half * Y_SIZE + place % Y_SIZE


def split_columns(values):
    high = lax.reduce_precision(values, 8, 7)
    middle = lax.reduce_precision(values - high, 8, 7)
    low = lax.reduce_precision(values - high - middle, 8, 7)
    rest = jnp.zeros((values.shape[0], SIDE - 3 * PLANE), jnp.float32)
    return jnp.concatenate([high, middle, low, rest], axis=1).astype(jnp.bfloat16)


def join_columns(columns):
    parts = columns[:, : 3 * PLANE].astype(jnp.float32)
    return parts[:, :PLANE] + parts[:, PLANE : 2 * PLANE] + parts[:, 2 * PLANE :]


def selection(gate_table):
    rows = gate_table.shape[0]
    chosen = jnp.transpose(gate_table) > 0
    before = (
        lax.broadcasted_iota(jnp.int32, (rows, rows), 0)
        < lax.broadcasted_iota(jnp.int32, (rows, rows), 1)
    ).astype(jnp.bfloat16)
    rank = jnp.dot(chosen.astype(jnp.bfloat16), before, preferred_element_type=jnp.float32)
    slot = lax.broadcasted_iota(jnp.int32, (1, MOST, 1), 1).astype(jnp.float32)
    hit = jnp.logical_and(rank[:, None, :] == slot, chosen[:, None, :])
    return hit.astype(jnp.bfloat16).reshape(PLANE * MOST, rows)


def fill(picked, values):
    return jnp.dot(picked, values, preferred_element_type=jnp.float32).astype(jnp.bfloat16)


def collect(picked, values):
    return lax.dot_general(
        picked, values, (((0,), (0,)), ((), ())), preferred_element_type=jnp.float32
    )


def line_sum(partial, core):
    rows = partial.shape[0] // (LO_SIZE * CORES)
    parts = partial.reshape(LO_SIZE, CORES, rows, partial.shape[1])
    give = lax.dynamic_index_in_dim(parts, 1 - core, axis=1, keepdims=False)
    keep = lax.dynamic_index_in_dim(parts, core, axis=1, keepdims=False)
    taken = lax.ppermute(give, "dp", [(i, i ^ 1) for i in range(LO_SIZE * CORES)])
    both = (keep.astype(jnp.float32) + taken.astype(jnp.float32)).astype(jnp.bfloat16)
    arrived = lax.all_to_all(
        both, "dp", split_axis=0, concat_axis=0, axis_index_groups=LINE_GROUPS, tiled=True
    )
    return jnp.sum(arrived.astype(jnp.float32), axis=0).astype(jnp.bfloat16)


def on_device(tokens, out_grad, expert_ids, route_gates, swap_flags, gate_proj, up_proj, down_proj):
    devices = lax.axis_size("expert")
    my_expert = lax.axis_index("expert")
    core = lax.axis_index("dp") % CORES
    half = (my_expert // Y_SIZE) % HI_SIZE
    place = (my_expert // (HI_SIZE * Y_SIZE)) * Y_SIZE + my_expert % Y_SIZE
    width = tokens.shape[1]
    hidden_width = gate_proj.shape[2]
    gate_w, up_w, down_w = gate_proj[0], up_proj[0], down_proj[0]

    own_names = half_experts(half)
    far_names = half_experts(1 - half)
    own_hits = expert_ids[:, :, None] == own_names
    far_hits = expert_ids[:, :, None] == far_names
    own_gates = jnp.sum(jnp.where(own_hits, route_gates[:, :, None], 0.0), axis=1)
    far_gates = jnp.sum(jnp.where(far_hits, route_gates[:, :, None], 0.0), axis=1)

    far_tokens = across(jnp.concatenate([tokens, split_columns(far_gates)], axis=1))
    far_cotangents = across(out_grad)

    own_picked = selection(own_gates)
    near_source = jnp.concatenate([tokens, split_columns(own_gates), out_grad], axis=1)
    near_rows = to_plane(fill(own_picked, near_source).reshape(PLANE, MOST, -1))
    near_rows = near_rows.reshape(PLANE * MOST, -1)

    far_picked = selection(join_columns(far_tokens[:, width:]))
    far_rows = to_plane(fill(far_picked, far_tokens).reshape(PLANE, MOST, -1))
    far_rows = far_rows.reshape(PLANE * MOST, -1)
    far_grads = to_plane(fill(far_picked, far_cotangents).reshape(PLANE, MOST, -1))
    far_grads = far_grads.reshape(PLANE * MOST, -1)

    row_block = jnp.concatenate([near_rows[:, :width], far_rows[:, :width]], axis=0)
    side_block = jnp.concatenate(
        [near_rows[:, width : width + SIDE], far_rows[:, width:]], axis=0
    ).astype(jnp.float32)
    grad_block = jnp.concatenate([near_rows[:, width + SIDE :], far_grads], axis=0)
    lane = lax.broadcasted_iota(jnp.int32, (1, SIDE), 1)
    mine = jnp.logical_and(lane % PLANE == place, lane < 3 * PLANE)
    slot_gate = jnp.sum(jnp.where(mine, side_block, 0.0), axis=1, keepdims=True)

    gate_pre = jnp.dot(row_block, gate_w, preferred_element_type=jnp.float32)
    up_pre = jnp.dot(row_block, up_w, preferred_element_type=jnp.float32)
    sigmoid = jax.nn.sigmoid(gate_pre)
    hidden = (gate_pre * sigmoid * up_pre).astype(jnp.bfloat16)
    expert_out = jnp.dot(hidden, down_w, preferred_element_type=jnp.float32)
    grad_rows = grad_block.astype(jnp.float32)
    gate_dots = jnp.sum(grad_rows * expert_out, axis=1, keepdims=True)
    weighted_out = (slot_gate * expert_out).astype(jnp.bfloat16)
    pick_grad = (slot_gate * grad_rows).astype(jnp.bfloat16)

    contract_last = (((1,), (1,)), ((), ()))
    contract_first = (((0,), (0,)), ((), ()))
    down_part = lax.dot_general(
        hidden, pick_grad, contract_first, preferred_element_type=jnp.float32
    ).astype(jnp.bfloat16)
    down_sum = line_sum(down_part, core)
    hidden_grad = lax.dot_general(
        pick_grad, down_w, contract_last, preferred_element_type=jnp.float32
    )
    gate_grad = (hidden_grad * up_pre * sigmoid * (1.0 + gate_pre * (1.0 - sigmoid))).astype(
        jnp.bfloat16
    )
    up_grad = (hidden_grad * gate_pre * sigmoid).astype(jnp.bfloat16)
    both_grads = jnp.concatenate([gate_grad, up_grad], axis=1)
    gate_up_part = lax.dot_general(
        row_block, both_grads, contract_first, preferred_element_type=jnp.float32
    ).astype(jnp.bfloat16)
    gate_up_sum = line_sum(gate_up_part, core)
    row_grads = lax.dot_general(gate_grad, gate_w, contract_last, preferred_element_type=jnp.float32)
    row_grads = row_grads + lax.dot_general(
        up_grad, up_w, contract_last, preferred_element_type=jnp.float32
    )
    row_grads = row_grads.astype(jnp.bfloat16)

    dot_table = jnp.where(lane[:, :PLANE] == place, gate_dots, 0.0)
    out_rows = jnp.concatenate([weighted_out, split_columns(dot_table)], axis=1)

    def give_back(rows):
        halves = rows.reshape(2, PLANE, MOST, -1)
        sent = jnp.concatenate([halves[0], halves[1]], axis=1)
        returned = to_plane(sent)
        near = collect(own_picked, returned[:, :MOST].reshape(PLANE * MOST, -1))
        far = collect(far_picked, returned[:, MOST:].reshape(PLANE * MOST, -1))
        return near, across(far.astype(jnp.bfloat16)).astype(jnp.float32)

    near_out, far_out = give_back(out_rows)
    layer_out = (near_out[:, :width] + far_out[:, :width]).astype(jnp.bfloat16)
    near_dots = join_columns(near_out[:, width:])
    far_dots = join_columns(far_out[:, width:])
    gate_grads = jnp.sum(
        jnp.where(own_hits, near_dots[:, None, :], 0.0)
        + jnp.where(far_hits, far_dots[:, None, :], 0.0),
        axis=2,
    )
    near_token, far_token = give_back(row_grads)
    grad_tokens = (near_token + far_token).astype(jnp.bfloat16)

    is_moved = swap_flags[my_expert] == 1
    swap = [(i, i ^ (devices // 2)) for i in range(devices)]
    other_down = lax.ppermute(down_sum, "expert", swap)
    other_gate_up = lax.ppermute(gate_up_sum, "expert", swap)
    down_sum = jnp.where(is_moved, other_down, down_sum)
    gate_up_sum = jnp.where(is_moved, other_gate_up, gate_up_sum)
    grad_gate = gate_up_sum[:, :hidden_width]
    grad_up = gate_up_sum[:, hidden_width:]
    return (layer_out, grad_tokens, gate_grads, grad_gate[None], grad_up[None], down_sum[None])


def solution(mesh):
    return jax.shard_map(
        on_device,
        mesh=mesh,
        in_specs=(
            P(("dp", "expert"), None),
            P(("dp", "expert"), None),
            P(("dp", "expert"), None),
            P(("dp", "expert"), None),
            P(),
            P("expert", None, None),
            P("expert", None, None),
            P("expert", None, None),
        ),
        out_specs=(
            P(("dp", "expert"), None),
            P(("dp", "expert"), None),
            P(("dp", "expert"), None),
            P("expert", "dp", None),
            P("expert", "dp", None),
            P("expert", "dp", None),
        ),
        check_vma=False,
    )
```

time: 399 us -> 356 us (0.89)
  the two profiles are of different devices: /device:TPU:16 before, /device:TPU:54 now
where the time goes in v2:
time: 356 us; the launch traced here: 355 us
  waiting for transfers between devices  167 us (47%)
  starting transfers between devices  82.4 us (23%)
  matrix products  44.3 us (12%)
  local copies, waits for them, and re-layouts  29.9 us (8%)
  other arithmetic  29.5 us (8%)
    ppermute x4, waiting for transfers between devices, across(): return lax.ppermute(value, BOTH, pairs)  84.1 us
    all_to_all x5, waiting for transfers between devices, to_plane(): lax.all_to_all(blocks, 'expert', split_axis=0, concat_axis=0, axis_index_...  40 us
    all_to_all x5, starting transfers between devices, to_plane(): lax.all_to_all(blocks, 'expert', split_axis=0, concat_axis=0, axis_index_...  39.7 us
    all_to_all x2, waiting for transfers between devices, line_sum(): lax.all_to_all(both, 'dp', split_axis=0, concat_axis=0, axis_index_groups...  26.9 us
    all_to_all x2, starting transfers between devices, line_sum(): lax.all_to_all(both, 'dp', split_axis=0, concat_axis=0, axis_index_groups...  23.9 us
    ppermute x4, starting transfers between devices, across(): return lax.ppermute(value, BOTH, pairs)  15.2 us
    ppermute x1, waiting for transfers between devices, on_device(): other_gate_up = lax.ppermute(gate_up_sum, 'expert', swap)  12 us
    convert_element_type x2, other arithmetic, line_sum(): (keep.astype(jnp.float32) + taken.astype(jnp.float32)).astype(jnp.bfloat16)  9.11 us
  transfers between devices with their start and end apart: 15, of which 12 were waited for; matrix products, arithmetic and copies ran while one was open for 19% of the time, Pallas kernels for 0%

profile of v2, /device:TPU:54, one launch (start us, length us, event | category | flops | bytes accessed | tf_op | source)
XLA Modules:
  0.0 354.5 jit_solution(3869537082232265770)
XLA Ops:
  0.7 2.2 copy.29
  2.9 1.9 constant_dynamic-update-slice_fusion.4
  7.9 5.8 %collective-permute-start = (bf16[128,2176]{0,1:T(8,128)(2,1)}, bf16[128,2176]{0,1:T(8,128)(2,1)}, u32[]{:S(2)}, u32[]{:S(2)}) collective-permute-start(bf16[128,2176]{0,1:T(8,128)(2,1)} %constant_dynamic-update-slice_fusion), channel_id=1, source_target_pairs={{0,196},{1,197},{2,198},{3,199},{4,192},{5,193},{6,194},{7,195},{8... | collective-permute-start | bytes 1671176 | tf_op jit(solution)/shard_map/ppermute | solution.py:28
  14.0 12.8 %collective-permute-done = bf16[128,2176]{0,1:T(8,128)(2,1)} collective-permute-done((bf16[128,2176]{0,1:T(8,128)(2,1)}, bf16[128,2176]{0,1:T(8,128)(2,1)}, u32[]{:S(2)}, u32[]{:S(2)}) %collective-permute-start) | collective-permute-done | bytes 557088 | tf_op jit(solution)/shard_map/ppermute | solution.py:28
  27.8 2.5 convolution_convert_fusion.2
  30.4 7.2 %all-to-all-start.1 = ((bf16[16,16,2176]{2,1,0:T(8,128)(2,1)}), bf16[16,16,2176]{2,1,0:T(8,128)(2,1)}, u32[]{:S(2)}, u32[]{:S(2)}) async-start(bf16[16,16,2176]{2,1,0:T(8,128)(2,1)} %bitcast.99), calls=%async_computation.1 | async-start | bytes 2228224 | tf_op jit(solution)/shard_map/all_to_all | solution.py:32
  38.0 3.1 concatenate.36
  41.1 3.3 convolution_convert_fusion.1
  44.4 6.9 %all-to-all-done.1 = bf16[16,16,2176]{2,1,0:T(8,128)(2,1)} async-done(((bf16[16,16,2176]{2,1,0:T(8,128)(2,1)}), bf16[16,16,2176]{2,1,0:T(8,128)(2,1)}, u32[]{:S(2)}, u32[]{:S(2)}) %all-to-all-start.1) | async-done | bytes 1114144 | tf_op jit(solution)/shard_map/all_to_all | solution.py:32
  51.3 8.4 %all-to-all-start = ((bf16[16,16,4224]{2,1,0:T(8,128)(2,1)}), bf16[16,16,4224]{2,1,0:T(8,128)(2,1)}, u32[]{:S(2)}, u32[]{:S(2)}) async-start(bf16[16,16,4224]{2,1,0:T(8,128)(2,1)} %bitcast.94), calls=%async_computation | async-start | bytes 4325376 | tf_op jit(solution)/shard_map/all_to_all | solution.py:32
  59.6 4.3 %collective-permute-start.1 = (bf16[128,2048]{1,0:T(8,128)(2,1)}, bf16[128,2048]{1,0:T(8,128)(2,1)}, u32[]{:S(2)}, u32[]{:S(2)}) collective-permute-start(bf16[128,2048]{1,0:T(8,128)(2,1)} %param.9), channel_id=1, source_target_pairs={{0,196},{1,197},{2,198},{3,199},{4,192},{5,193},{6,194},{7,195},{8... | collective-permute-start | bytes 1572872 | tf_op jit(solution)/shard_map/ppermute | solution.py:28
  63.9 9.8 %collective-permute-done.1 = bf16[128,2048]{1,0:T(8,128)(2,1)} collective-permute-done((bf16[128,2048]{1,0:T(8,128)(2,1)}, bf16[128,2048]{1,0:T(8,128)(2,1)}, u32[]{:S(2)}, u32[]{:S(2)}) %collective-permute-start.1) | collective-permute-done | bytes 524320 | tf_op jit(solution)/shard_map/ppermute | solution.py:28
  73.8 2.5 convolution_convert_fusion.4
  77.2 2.3 slice.137
  79.5 5.3 %all-to-all-done = bf16[16,16,4224]{2,1,0:T(8,128)(2,1)} async-done(((bf16[16,16,4224]{2,1,0:T(8,128)(2,1)}), bf16[16,16,4224]{2,1,0:T(8,128)(2,1)}, u32[]{:S(2)}, u32[]{:S(2)}) %all-to-all-start) | async-done | bytes 2162720 | tf_op jit(solution)/shard_map/all_to_all | solution.py:32
  84.8 7.8 %all-to-all-start.2 = ((bf16[16,16,2048]{2,1,0:T(8,128)(2,1)}), bf16[16,16,2048]{2,1,0:T(8,128)(2,1)}, u32[]{:S(2)}, u32[]{:S(2)}) async-start(bf16[16,16,2048]{2,1,0:T(8,128)(2,1)} %bitcast.100), calls=%async_computation.2 | async-start | bytes 2097152 | tf_op jit(solution)/shard_map/all_to_all | solution.py:32
  92.6 1.0 slice.130
  93.7 2.9 fusion.66
  96.5 1.0 copy-done.9
  97.6 3.0 fusion.11
  100.5 2.7 all-to-all-done.2
  103.3 4.5 %fusion.5 = f32[512,768]{1,0:T(8,128)S(1)} fusion(bf16[1,768,2048]{2,1,0:T(8,128)(2,1)} %param.15, f32[512]{0:T(512)S(1)} %select_reduce_fusion, bf16[256,2048]{1,0:T(8,128)(2,1)} %bitcast.15, bf16[256,2048]{1,0:T(8,128)(2,1)} %get-tuple-element.15), kind=kOutput, calls=%fused_computation.17 | convolution fusion | flops 1616904192 | bytes 6817792 | tf_op jit(solution)/shard_map/dot_general | solution.py:147
  107.8 2.3 multiply_convert_fusion.2
  110.2 5.3 %fusion.1 = (f32[512]{0:T(512)S(1)}, bf16[512,2048]{1,0:T(8,128)(2,1)}) fusion(bf16[256,2048]{1,0:T(8,128)(2,1)} %bitcast.15, bf16[256,2048]{1,0:T(8,128)(2,1)S(1)} %copy-done.11, f32[512]{0:T(512)S(1)} %select_reduce_fusion, bf16[512,768]{1,0:T(8,128)(2,1)S(1)} %get-tuple-element.11, bf16[1,768,2048]{2,1,0:T(8,128)(2,1)S(1)} %copy-done.21), kind=kOutput, calls=%fused_computation.6 | convolution fusion | flops 1619000832 | bytes 8130560 | tf_op jit(solution)/shard_map/dot_general | solution.py:135
  115.5 1.8 fusion.9
  117.4 1.8 add_convert_fusion
  119.5 1.6 pad_maximum_fusion.3
  121.1 8.5 %all-to-all-start.4 = ((bf16[16,32,2048]{2,1,0:T(8,128)(2,1)}), bf16[16,32,2048]{2,1,0:T(8,128)(2,1)}, u32[]{:S(2)}, u32[]{:S(2)}) async-start(bf16[16,32,2048]{2,1,0:T(8,128)(2,1)} %pad_maximum_fusion.3), calls=%async_computation.4 | async-start | bytes 4194304 | tf_op jit(solution)/shard_map/all_to_all | solution.py:32
  130.1 3.7 %convolution_convert_fusion.3 = bf16[768,2048]{1,0:T(8,128)(2,1)S(1)} fusion(bf16[512,768]{1,0:T(8,128)(2,1)} %copy-done.29, f32[512]{0:T(512)} %copy-done.20, bf16[256,2048]{1,0:T(8,128)(2,1)} %bitcast.15, bf16[256,2048]{1,0:T(8,128)(2,1)} %get-tuple-element.15), kind=kOutput, calls=%fused_computation.14 | convolution fusion | flops 1618477056 | bytes 6031360 | tf_op jit(solution)/shard_map/dot_general | solution.py:143
  133.8 1.5 dynamic-slice_bitcast_fusion.1
  136.7 3.7 %concatenate.41 = bf16[512,2176]{1,0:T(8,128)(2,1)S(1)} concatenate(bf16[512,2048]{1,0:T(8,128)(2,1)} %get-tuple-element.9, bf16[512,16]{1,0:T(8,128)(2,1)S(1)} %copy.30, bf16[512,16]{1,0:T(8,128)(2,1)S(1)} %copy.31, bf16[512,16]{1,0:T(8,128)(2,1)S(1)} %copy.32, bf16[512,80]{1,0:T(8,128)(2,1)} %broadcast_in_dim.98), dimensions={1} | concatenate | bytes 4456448 | tf_op jit(solution)/shard_map/concatenate | solution.py:166
  140.5 1.6 pad_maximum_fusion
  142.0 11.8 %all-to-all-done.4 = bf16[16,32,2048]{2,1,0:T(8,128)(2,1)} async-done(((bf16[16,32,2048]{2,1,0:T(8,128)(2,1)}), bf16[16,32,2048]{2,1,0:T(8,128)(2,1)}, u32[]{:S(2)}, u32[]{:S(2)}) %all-to-all-start.4) | async-done | bytes 2097184 | tf_op jit(solution)/shard_map/all_to_all | solution.py:32
  153.9 7.8 %all-to-all-start.3 = ((bf16[16,32,2176]{2,1,0:T(8,128)(2,1)}), bf16[16,32,2176]{2,1,0:T(8,128)(2,1)S(1)}, u32[]{:S(2)}, u32[]{:S(2)}) async-start(bf16[16,32,2176]{2,1,0:T(8,128)(2,1)} %pad_maximum_fusion), calls=%async_computation.3 | async-start | bytes 4456448 | tf_op jit(solution)/shard_map/all_to_all | solution.py:32
  161.7 5.2 %convolution_convert_fusion = bf16[2048,1536]{1,0:T(8,128)(2,1)S(1)} fusion(bf16[512,768]{1,0:T(8,128)(2,1)} %copy-done.27, bf16[512,768]{1,0:T(8,128)(2,1)S(1)} %copy-done.26, bf16[256,2048]{1,0:T(8,128)(2,1)} %slice.137, bf16[256,2048]{1,0:T(8,128)(2,1)} %copy-done.9), kind=kOutput, calls=%fused_computation | convolution fusion | flops 3231711232 | bytes 9961472 | tf_op jit(solution)/shard_map/dot_general | solution.py:155
  167.0 2.0 dynamic-slice_bitcast_fusion
  169.0 1.6 copy-done.4
  170.6 3.7 %fusion.4 = bf16[4,96,2048]{2,1,0:T(8,128)(2,1)} fusion(bf16[4,96,2048]{2,1,0:T(8,128)(2,1)} %collective-permute-done.6, bf16[4,2,96,2048]{3,2,1,0:T(8,128)(2,1)} %bitcast.104, s32[]{:T(128)S(6)} %select_n.134), kind=kLoop, calls=%fused_computation.16 | loop fusion | flops 3145728 | bytes 4718596 | tf_op jit(solution)/shard_map/convert_element_type | solution.py:84
  174.3 13.3 %all-to-all-done.3 = bf16[16,32,2176]{2,1,0:T(8,128)(2,1)S(1)} async-done(((bf16[16,32,2176]{2,1,0:T(8,128)(2,1)}), bf16[16,32,2176]{2,1,0:T(8,128)(2,1)S(1)}, u32[]{:S(2)}, u32[]{:S(2)}) %all-to-all-start.3) | async-done | bytes 2228256 | tf_op jit(solution)/shard_map/all_to_all | solution.py:32
  187.6 16.8 %all-to-all-start.6 = ((bf16[4,96,2048]{2,1,0:T(8,128)(2,1)}), bf16[4,96,2048]{2,1,0:T(8,128)(2,1)}, u32[]{:S(2)}, u32[]{:S(2)}) async-start(bf16[4,96,2048]{2,1,0:T(8,128)(2,1)} %fusion.4), calls=%async_computation.6 | async-start | bytes 3145728 | tf_op jit(solution)/shard_map/all_to_all | solution.py:85
  204.5 5.4 %fusion = bf16[4,256,1536]{2,1,0:T(8,128)(2,1)} fusion(bf16[4,256,1536]{2,1,0:T(8,128)(2,1)} %collective-permute-done.4, bf16[4,2,256,1536]{3,2,1,0:T(8,128)(2,1)} %bitcast.96, s32[]{:T(128)S(6)} %select_n.134), kind=kLoop, calls=%fused_computation.3 | loop fusion | flops 6291456 | bytes 9437188 | tf_op jit(solution)/shard_map/convert_element_type | solution.py:84
  209.9 26.9 %all-to-all-done.6 = bf16[4,96,2048]{2,1,0:T(8,128)(2,1)} async-done(((bf16[4,96,2048]{2,1,0:T(8,128)(2,1)}), bf16[4,96,2048]{2,1,0:T(8,128)(2,1)}, u32[]{:S(2)}, u32[]{:S(2)}) %all-to-all-start.6) | async-done | bytes 1572896 | tf_op jit(solution)/shard_map/all_to_all | solution.py:85
  236.8 7.0 %all-to-all-start.5 = ((bf16[4,256,1536]{2,1,0:T(8,128)(2,1)}), bf16[4,256,1536]{2,1,0:T(8,128)(2,1)S(1)}, u32[]{:S(2)}, u32[]{:S(2)}) async-start(bf16[4,256,1536]{2,1,0:T(8,128)(2,1)} %fusion), calls=%async_computation.5 | async-start | bytes 6291456 | tf_op jit(solution)/shard_map/all_to_all | solution.py:85
  245.2 2.4 fusion.19
  247.7 3.3 collective-permute-start.3
  251.0 2.5 fusion.3
  253.5 1.7 collective-permute-start.2
  255.7 1.0 copy-done.5
  256.8 52.7 %collective-permute-done.3 = bf16[128,2048]{1,0:T(8,128)(2,1)} collective-permute-done((bf16[128,2048]{1,0:T(8,128)(2,1)}, bf16[128,2048]{1,0:T(8,128)(2,1)}, u32[]{:S(2)}, u32[]{:S(2)}) %collective-permute-start.3) | collective-permute-done | bytes 524320 | tf_op jit(solution)/shard_map/ppermute | solution.py:28
  309.5 2.6 add_convert_fusion.1
  312.1 8.8 %collective-permute-done.2 = bf16[128,2176]{1,0:T(8,128)(2,1)} collective-permute-done((bf16[128,2176]{1,0:T(8,128)(2,1)}, bf16[128,2176]{1,0:T(8,128)(2,1)}, u32[]{:S(2)}, u32[]{:S(2)}) %collective-permute-start.2) | collective-permute-done | bytes 557088 | tf_op jit(solution)/shard_map/ppermute | solution.py:28
  320.8 2.2 convert_element_type.122
  323.0 1.7 reduce_sum.75
  324.7 0.9 collective-permute-start.7
  325.6 2.5 fusion.27
  328.0 1.6 reduce_sum.74
  329.6 2.7 collective-permute-start.5
  332.3 1.1 slice_add_fusion.1
  333.4 1.4 fusion.36
  334.8 3.6 %collective-permute-done.7 = bf16[96,2048]{1,0:T(8,128)(2,1)} collective-permute-done((bf16[96,2048]{1,0:T(8,128)(2,1)S(1)}, bf16[96,2048]{1,0:T(8,128)(2,1)}, u32[]{:S(2)}, u32[]{:S(2)}) %collective-permute-start.7) | collective-permute-done | bytes 393248 | tf_op jit(solution)/shard_map/ppermute | solution.py:190
  338.5 1.9 select_bitcast_fusion
  340.4 12.0 %collective-permute-done.5 = bf16[256,1536]{1,0:T(8,128)(2,1)} collective-permute-done((bf16[256,1536]{1,0:T(8,128)(2,1)}, bf16[256,1536]{1,0:T(8,128)(2,1)}, u32[]{:S(2)}, u32[]{:S(2)}) %collective-permute-start.5) | collective-permute-done | bytes 786464 | tf_op jit(solution)/shard_map/ppermute | solution.py:191
  352.4 1.2 broadcast_select_fusion
  353.6 0.9 slice_bitcast_fusion
  (99 shorter events, 9.3 us)
Async XLA Ops:
  0.6 107.1 %copy-start = (bf16[1,2048,768]{2,1,0:T(8,128)(2,1)S(1)}, bf16[1,2048,768]{2,1,0:T(8,128)(2,1)}, u32[]{:S(2)}) copy-start(bf16[1,2048,768]{2,1,0:T(8,128)(2,1)} %param.13) | copy-start | bytes 9437188
  4.7 9.0 %copy-start.18 = (s32[16]{0:T(128)}, s32[16]{0:T(128)S(1)}, u32[]{:S(2)}) copy-start(s32[16]{0:T(128)S(1)} %get-tuple-element.29) | copy-start | bytes 196
  4.7 9.1 %copy-start.19 = (s32[16]{0:T(128)}, s32[16]{0:T(128)S(1)}, u32[]{:S(2)}) copy-start(s32[16]{0:T(128)S(1)} %get-tuple-element.30) | copy-start | bytes 196
  7.9 18.9 %collective-permute-start = (bf16[128,2176]{0,1:T(8,128)(2,1)}, bf16[128,2176]{0,1:T(8,128)(2,1)}, u32[]{:S(2)}, u32[]{:S(2)}) collective-permute-start(bf16[128,2176]{0,1:T(8,128)(2,1)} %constant_dynamic-update-slice_fusion), channel_id=1, source_target_pairs={{0,196},{1,197},{2,198},{3,199},{4,192},{5,193},{6,194},{7,195},{8... | collective-permute-start | bytes 1671176 | tf_op jit(solution)/shard_map/ppermute | solution.py:28
  13.8 13.8 %copy-start.16 = (f32[16]{0:T(128)}, f32[16]{0:T(128)S(1)}, u32[]{:S(2)}) copy-start(f32[16]{0:T(128)S(1)} %iota_convert_fusion) | copy-start | bytes 196
  13.9 23.7 %copy-start.14 = (pred[16,128]{1,0:T(8,128)(4,1)}, pred[16,128]{1,0:T(8,128)(4,1)S(1)}, u32[]{:S(2)}) copy-start(pred[16,128]{1,0:T(8,128)(4,1)S(1)} %fusion.81) | copy-start | bytes 6148
  27.6 10.0 %copy-start.12 = (pred[16,128]{1,0:T(8,128)(4,1)}, pred[16,128]{1,0:T(8,128)(4,1)S(1)}, u32[]{:S(2)}) copy-start(pred[16,128]{1,0:T(8,128)(4,1)S(1)} %fusion.80) | copy-start | bytes 6148
  30.4 20.9 %all-to-all-start.1 = ((bf16[16,16,2176]{2,1,0:T(8,128)(2,1)}), bf16[16,16,2176]{2,1,0:T(8,128)(2,1)}, u32[]{:S(2)}, u32[]{:S(2)}) async-start(bf16[16,16,2176]{2,1,0:T(8,128)(2,1)} %bitcast.99), calls=%async_computation.1 | async-start | bytes 2228224 | tf_op jit(solution)/shard_map/all_to_all | solution.py:32
  51.3 33.5 %all-to-all-start = ((bf16[16,16,4224]{2,1,0:T(8,128)(2,1)}), bf16[16,16,4224]{2,1,0:T(8,128)(2,1)}, u32[]{:S(2)}, u32[]{:S(2)}) async-start(bf16[16,16,4224]{2,1,0:T(8,128)(2,1)} %bitcast.94), calls=%async_computation | async-start | bytes 4325376 | tf_op jit(solution)/shard_map/all_to_all | solution.py:32
  59.6 14.2 %collective-permute-start.1 = (bf16[128,2048]{1,0:T(8,128)(2,1)}, bf16[128,2048]{1,0:T(8,128)(2,1)}, u32[]{:S(2)}, u32[]{:S(2)}) collective-permute-start(bf16[128,2048]{1,0:T(8,128)(2,1)} %param.9), channel_id=1, source_target_pairs={{0,196},{1,197},{2,198},{3,199},{4,192},{5,193},{6,194},{7,195},{8... | collective-permute-start | bytes 1572872 | tf_op jit(solution)/shard_map/ppermute | solution.py:28
  84.8 18.5 %all-to-all-start.2 = ((bf16[16,16,2048]{2,1,0:T(8,128)(2,1)}), bf16[16,16,2048]{2,1,0:T(8,128)(2,1)}, u32[]{:S(2)}, u32[]{:S(2)}) async-start(bf16[16,16,2048]{2,1,0:T(8,128)(2,1)} %bitcast.100), calls=%async_computation.2 | async-start | bytes 2097152 | tf_op jit(solution)/shard_map/all_to_all | solution.py:32
  92.5 5.0 %copy-start.7 = (bf16[256,2048]{1,0:T(8,128)(2,1)S(1)}, bf16[256,2048]{1,0:T(8,128)(2,1)}, u32[]{:S(2)}) copy-start(bf16[256,2048]{1,0:T(8,128)(2,1)} %slice.137) | copy-start | bytes 3145732
  92.5 5.0 %copy-start.22 = (bf16[1,2048,768]{2,1,0:T(8,128)(2,1)S(1)}, bf16[1,2048,768]{2,1,0:T(8,128)(2,1)}, u32[]{:S(2)}) copy-start(bf16[1,2048,768]{2,1,0:T(8,128)(2,1)} %param.14) | copy-start | bytes 9437188
  93.7 16.5 %copy-start.20 = (f32[512]{0:T(512)}, f32[512]{0:T(512)S(1)}, u32[]{:S(2)}) copy-start(f32[512]{0:T(512)S(1)} %select_reduce_fusion) | copy-start | bytes 6148
  96.5 1.0 copy-start.9
  103.2 4.5 %copy-start.8 = (bf16[256,2048]{1,0:T(8,128)(2,1)S(1)}, bf16[256,2048]{1,0:T(8,128)(2,1)}, u32[]{:S(2)}) copy-start(bf16[256,2048]{1,0:T(8,128)(2,1)} %slice.137) | copy-start | bytes 3145732
  103.2 4.5 %copy-start.10 = (bf16[256,2048]{1,0:T(8,128)(2,1)S(1)}, bf16[256,2048]{1,0:T(8,128)(2,1)}, u32[]{:S(2)}) copy-start(bf16[256,2048]{1,0:T(8,128)(2,1)} %copy-done.9) | copy-start | bytes 3145732
  103.2 4.5 %copy-start.28 = (f32[512,768]{1,0:T(8,128)S(1)}, f32[512,768]{1,0:T(8,128)}, u32[]{:S(2)}) copy-start(f32[512,768]{1,0:T(8,128)} %fusion.11) | copy-start | bytes 4718596
  107.8 2.4 copy-start.11
  107.8 2.4 copy-start.21
  110.2 5.4 %copy-start.29 = (bf16[512,768]{1,0:T(8,128)(2,1)}, bf16[512,768]{1,0:T(8,128)(2,1)S(1)}, u32[]{:S(2)}) copy-start(bf16[512,768]{1,0:T(8,128)(2,1)S(1)} %get-tuple-element.11) | copy-start | bytes 2359300
  110.2 5.4 %copy-start.27 = (bf16[512,768]{1,0:T(8,128)(2,1)}, bf16[512,768]{1,0:T(8,128)(2,1)S(1)}, u32[]{:S(2)}) copy-start(bf16[512,768]{1,0:T(8,128)(2,1)S(1)} %get-tuple-element.12) | copy-start | bytes 2359300
  110.2 7.2 %copy-start.25 = (bf16[512,768]{1,0:T(8,128)(2,1)}, bf16[512,768]{1,0:T(8,128)(2,1)S(1)}, u32[]{:S(2)}) copy-start(bf16[512,768]{1,0:T(8,128)(2,1)S(1)} %get-tuple-element.10) | copy-start | bytes 2359300
  110.2 5.3 %copy-start.23 = (bf16[1,2048,768]{2,1,0:T(8,128)(2,1)S(1)}, bf16[1,2048,768]{2,1,0:T(8,128)(2,1)}, u32[]{:S(2)}) copy-start(bf16[1,2048,768]{2,1,0:T(8,128)(2,1)} %param.14) | copy-start | bytes 9437188
  121.1 32.8 %all-to-all-start.4 = ((bf16[16,32,2048]{2,1,0:T(8,128)(2,1)}), bf16[16,32,2048]{2,1,0:T(8,128)(2,1)}, u32[]{:S(2)}, u32[]{:S(2)}) async-start(bf16[16,32,2048]{2,1,0:T(8,128)(2,1)} %pad_maximum_fusion.3), calls=%async_computation.4 | async-start | bytes 4194304 | tf_op jit(solution)/shard_map/all_to_all | solution.py:32
  133.8 2.2 copy-start.6
  135.3 35.3 %collective-permute-start.6 = (bf16[4,96,2048]{2,1,0:T(8,128)(2,1)}, bf16[4,96,2048]{2,1,0:T(8,128)(2,1)}, u32[]{:S(2)}, u32[]{:S(2)}) collective-permute-start(bf16[4,96,2048]{2,1,0:T(8,128)(2,1)} %dynamic-slice_bitcast_fusion.1), channel_id=1, source_target_pairs={{0,32},{32,0},{64,96},{96,64},{128,160},{160,128},{192,224},{224,1... | collective-permute-start | bytes 4718600 | tf_op jit(solution)/shard_map/ppermute | solution.py:83
  142.0 19.7 %copy-start.26 = (bf16[512,768]{1,0:T(8,128)(2,1)S(1)}, bf16[512,768]{1,0:T(8,128)(2,1)}, u32[]{:S(2)}) copy-start(bf16[512,768]{1,0:T(8,128)(2,1)} %copy-done.25) | copy-start | bytes 2359300
  153.9 33.7 %all-to-all-start.3 = ((bf16[16,32,2176]{2,1,0:T(8,128)(2,1)}), bf16[16,32,2176]{2,1,0:T(8,128)(2,1)S(1)}, u32[]{:S(2)}, u32[]{:S(2)}) async-start(bf16[16,32,2176]{2,1,0:T(8,128)(2,1)} %pad_maximum_fusion), calls=%async_computation.3 | async-start | bytes 4456448 | tf_op jit(solution)/shard_map/all_to_all | solution.py:32
  167.0 3.6 %copy-start.4 = (bf16[2048,1536]{1,0:T(8,128)(2,1)}, bf16[2048,1536]{1,0:T(8,128)(2,1)S(1)}, u32[]{:S(2)}) copy-start(bf16[2048,1536]{1,0:T(8,128)(2,1)S(1)} %convolution_convert_fusion) | copy-start | bytes 18874372
  170.6 33.9 %collective-permute-start.4 = (bf16[4,256,1536]{2,1,0:T(8,128)(2,1)}, bf16[4,256,1536]{2,1,0:T(8,128)(2,1)}, u32[]{:S(2)}, u32[]{:S(2)}) collective-permute-start(bf16[4,256,1536]{2,1,0:T(8,128)(2,1)} %dynamic-slice_bitcast_fusion), channel_id=1, source_target_pairs={{0,32},{32,0},{64,96},{96,64},{128,160},{160,128},{192,224},{224,1... | collective-permute-start | bytes 9437192 | tf_op jit(solution)/shard_map/ppermute | solution.py:83
  187.6 22.2 %copy-start.2 = (bf16[16,32,2176]{2,1,0:T(8,128)(2,1)}, bf16[16,32,2176]{2,1,0:T(8,128)(2,1)S(1)}, u32[]{:S(2)}) copy-start(bf16[16,32,2176]{2,1,0:T(8,128)(2,1)S(1)} %all-to-all-done.3) | copy-start | bytes 6684676
  187.6 49.2 %all-to-all-start.6 = ((bf16[4,96,2048]{2,1,0:T(8,128)(2,1)}), bf16[4,96,2048]{2,1,0:T(8,128)(2,1)}, u32[]{:S(2)}, u32[]{:S(2)}) async-start(bf16[4,96,2048]{2,1,0:T(8,128)(2,1)} %fusion.4), calls=%async_computation.6 | async-start | bytes 3145728 | tf_op jit(solution)/shard_map/all_to_all | solution.py:85
  209.9 34.0 %copy-start.24 = (s32[32]{0:T(128)S(1)}, s32[32]{0:T(128)}, u32[]{:S(2)}) copy-start(s32[32]{0:T(128)} %param.12) | copy-start | bytes 388
  209.9 35.3 %copy-start.13 = (pred[16,128]{1,0:T(8,128)(4,1)S(1)}, pred[16,128]{1,0:T(8,128)(4,1)}, u32[]{:S(2)}) copy-start(pred[16,128]{1,0:T(8,128)(4,1)} %copy-done.12) | copy-start | bytes 6148
  209.9 35.3 %copy-start.17 = (f32[16]{0:T(128)S(1)}, f32[16]{0:T(128)}, u32[]{:S(2)}) copy-start(f32[16]{0:T(128)} %copy-done.16) | copy-start | bytes 196
  236.8 91.2 %all-to-all-start.5 = ((bf16[4,256,1536]{2,1,0:T(8,128)(2,1)}), bf16[4,256,1536]{2,1,0:T(8,128)(2,1)S(1)}, u32[]{:S(2)}, u32[]{:S(2)}) async-start(bf16[4,256,1536]{2,1,0:T(8,128)(2,1)} %fusion), calls=%async_computation.5 | async-start | bytes 6291456 | tf_op jit(solution)/shard_map/all_to_all | solution.py:85
  243.9 11.3 %copy-start.15 = (pred[16,128]{1,0:T(8,128)(4,1)S(1)}, pred[16,128]{1,0:T(8,128)(4,1)}, u32[]{:S(2)}) copy-start(pred[16,128]{1,0:T(8,128)(4,1)} %copy-done.14) | copy-start | bytes 6148
  243.9 11.3 %copy-start.3 = (bf16[16,32,2176]{2,1,0:T(8,128)(2,1)S(1)}, bf16[16,32,2176]{2,1,0:T(8,128)(2,1)}, u32[]{:S(2)}) copy-start(bf16[16,32,2176]{2,1,0:T(8,128)(2,1)} %copy-done.2) | copy-start | bytes 6684676
  247.7 61.8 %collective-permute-start.3 = (bf16[128,2048]{1,0:T(8,128)(2,1)}, bf16[128,2048]{1,0:T(8,128)(2,1)}, u32[]{:S(2)}, u32[]{:S(2)}) collective-permute-start(bf16[128,2048]{1,0:T(8,128)(2,1)} %fusion.19), channel_id=1, source_target_pairs={{0,196},{1,197},{2,198},{3,199},{4,192},{5,193},{6,194},{7,195},{8... | collective-permute-start | bytes 1572872 | tf_op jit(solution)/shard_map/ppermute | solution.py:28
  253.5 67.3 %collective-permute-start.2 = (bf16[128,2176]{1,0:T(8,128)(2,1)}, bf16[128,2176]{1,0:T(8,128)(2,1)}, u32[]{:S(2)}, u32[]{:S(2)}) collective-permute-start(bf16[128,2176]{1,0:T(8,128)(2,1)} %fusion.3), channel_id=1, source_target_pairs={{0,196},{1,197},{2,198},{3,199},{4,192},{5,193},{6,194},{7,195},{8... | collective-permute-start | bytes 1671176 | tf_op jit(solution)/shard_map/ppermute | solution.py:28
  255.7 1.0 copy-start.5
  324.7 13.7 %collective-permute-start.7 = (bf16[96,2048]{1,0:T(8,128)(2,1)S(1)}, bf16[96,2048]{1,0:T(8,128)(2,1)}, u32[]{:S(2)}, u32[]{:S(2)}) collective-permute-start(bf16[96,2048]{1,0:T(8,128)(2,1)S(1)} %reduce_sum.75), channel_id=1, source_target_pairs={{0,16},{1,17},{2,18},{3,19},{4,20},{5,21},{6,22},{7,23},{8,24},{9,... | collective-permute-start | bytes 1179656 | tf_op jit(solution)/shard_map/ppermute | solution.py:190
  329.6 22.8 %collective-permute-start.5 = (bf16[256,1536]{1,0:T(8,128)(2,1)}, bf16[256,1536]{1,0:T(8,128)(2,1)}, u32[]{:S(2)}, u32[]{:S(2)}) collective-permute-start(bf16[256,1536]{1,0:T(8,128)(2,1)} %reduce_sum.74), channel_id=1, source_target_pairs={{0,16},{1,17},{2,18},{3,19},{4,20},{5,21},{6,22},{7,23},{8,24},{9,... | collective-permute-start | bytes 2359304 | tf_op jit(solution)/shard_map/ppermute | solution.py:191
  338.4 16.1 %copy-start.1 = (bf16[1,2048,768]{2,1,0:T(8,128)(2,1)S(1)}, bf16[1,2048,768]{2,1,0:T(8,128)(2,1)}, u32[]{:S(2)}) copy-start(bf16[1,2048,768]{2,1,0:T(8,128)(2,1)} %param.13) | copy-start | bytes 9437188

commit v3 on v2

v3 whole, which is shorter than its diff:
```python
import jax
import jax.numpy as jnp
from jax import lax
from jax.sharding import PartitionSpec as P

MOST = 16
X_SIZE, HI_SIZE, Y_SIZE = 4, 2, 4
LO_SIZE, CORES = 4, 2
PLANE = X_SIZE * Y_SIZE
SIDE = 128

BOTH = ("dp", "expert")
PLANE_GROUPS = [
    [x * HI_SIZE * Y_SIZE + hi * Y_SIZE + y for x in range(X_SIZE) for y in range(Y_SIZE)]
    for hi in range(HI_SIZE)
]


def across(value):
    experts = lax.axis_size("expert")
    pairs = []
    for dp in range(lax.axis_size("dp")):
        lo, core = divmod(dp, CORES)
        other_dp = (LO_SIZE - 1 - lo) * CORES + core
        for expert in range(experts):
            pairs.append((dp * experts + expert, other_dp * experts + (expert ^ Y_SIZE)))
    return lax.ppermute(value, BOTH, pairs)


def to_plane(blocks):
    return lax.all_to_all(
        blocks, "expert", split_axis=0, concat_axis=0, axis_index_groups=PLANE_GROUPS, tiled=True
    )


def half_experts(half):
    place = lax.broadcasted_iota(jnp.int32, (1, 1, PLANE), 2)
    return (place // Y_SIZE) * (HI_SIZE * Y_SIZE) + half * Y_SIZE + place % Y_SIZE


def split_columns(values):
    high = lax.reduce_precision(values, 8, 7)
    middle = lax.reduce_precision(values - high, 8, 7)
    low = lax.reduce_precision(values - high - middle, 8, 7)
    rest = jnp.zeros((values.shape[0], SIDE - 3 * PLANE), jnp.float32)
    return jnp.concatenate([high, middle, low, rest], axis=1).astype(jnp.bfloat16)


def join_columns(columns):
    parts = columns[:, : 3 * PLANE].astype(jnp.float32)
    return parts[:, :PLANE] + parts[:, PLANE : 2 * PLANE] + parts[:, 2 * PLANE :]


def selection(gate_table):
    rows = gate_table.shape[0]
    chosen = jnp.transpose(gate_table) > 0
    before = (
        lax.broadcasted_iota(jnp.int32, (rows, rows), 0)
        < lax.broadcasted_iota(jnp.int32, (rows, rows), 1)
    ).astype(jnp.bfloat16)
    rank = jnp.dot(chosen.astype(jnp.bfloat16), before, preferred_element_type=jnp.float32)
    slot = lax.broadcasted_iota(jnp.int32, (1, MOST, 1), 1).astype(jnp.float32)
    hit = jnp.logical_and(rank[:, None, :] == slot, chosen[:, None, :])
    return hit.astype(jnp.bfloat16).reshape(PLANE * MOST, rows)


def fill(picked, values):
    return jnp.dot(picked, values, preferred_element_type=jnp.float32).astype(jnp.bfloat16)


def collect(picked, values):
    return lax.dot_general(
        picked, values, (((0,), (0,)), ((), ())), preferred_element_type=jnp.float32
    )


def neighbours(steps):
    return [(a * CORES + core, b * CORES + core) for a, b in steps for core in range(CORES)]


def shard_of(parts, index):
    index = jnp.clip(index, 0, LO_SIZE - 1)
    return lax.dynamic_index_in_dim(parts, index, axis=0, keepdims=False).astype(jnp.float32)


def core_swap(partial, core):
    rows = partial.shape[0] // (LO_SIZE * CORES)
    parts = partial.reshape(LO_SIZE, CORES, rows, partial.shape[1])
    give = lax.dynamic_index_in_dim(parts, 1 - core, axis=1, keepdims=False)
    keep = lax.dynamic_index_in_dim(parts, core, axis=1, keepdims=False)
    taken = lax.ppermute(give, "dp", [(i, i ^ 1) for i in range(LO_SIZE * CORES)])
    return (keep.astype(jnp.float32) + taken.astype(jnp.float32)).astype(jnp.bfloat16)


def line_sum(parts, lo):
    first = jnp.where(lo == 0, parts[LO_SIZE - 1], parts[0])
    arrived = lax.ppermute(first, "dp", neighbours([(0, 1), (3, 2)])).astype(jnp.float32)
    up = (shard_of(parts, lo + 2) + arrived).astype(jnp.bfloat16)
    down = (shard_of(parts, lo - 2) + arrived).astype(jnp.bfloat16)
    up = lax.ppermute(up, "dp", neighbours([(0, 1), (1, 2)])).astype(jnp.float32)
    down = lax.ppermute(down, "dp", neighbours([(3, 2), (2, 1)])).astype(jnp.float32)
    up = (shard_of(parts, lo + 1) + up).astype(jnp.bfloat16)
    down = (shard_of(parts, lo - 1) + down).astype(jnp.bfloat16)
    up = lax.ppermute(up, "dp", neighbours([(0, 1), (1, 2), (2, 3)])).astype(jnp.float32)
    down = lax.ppermute(down, "dp", neighbours([(3, 2), (2, 1), (1, 0)])).astype(jnp.float32)
    return (shard_of(parts, lo) + up + down).astype(jnp.bfloat16)


CONTRACT_LAST = (((1,), (1,)), ((), ()))
CONTRACT_FIRST = (((0,), (0,)), ((), ()))


def expert(rows, place, gate_w, up_w, down_w):
    width = gate_w.shape[0]
    row_block = rows[:, :width]
    grad_rows = rows[:, width + SIDE :].astype(jnp.float32)
    lane = lax.broadcasted_iota(jnp.int32, (1, SIDE), 1)
    mine = jnp.logical_and(lane % PLANE == place, lane < 3 * PLANE)
    side_block = rows[:, width : width + SIDE].astype(jnp.float32)
    slot_gate = jnp.sum(jnp.where(mine, side_block, 0.0), axis=1, keepdims=True)
    gate_pre = jnp.dot(row_block, gate_w, preferred_element_type=jnp.float32)
    up_pre = jnp.dot(row_block, up_w, preferred_element_type=jnp.float32)
    sigmoid = jax.nn.sigmoid(gate_pre)
    hidden = (gate_pre * sigmoid * up_pre).astype(jnp.bfloat16)
    pick_grad = (slot_gate * grad_rows).astype(jnp.bfloat16)
    hidden_grad = lax.dot_general(
        pick_grad, down_w, CONTRACT_LAST, preferred_element_type=jnp.float32
    )
    gate_grad = (hidden_grad * up_pre * sigmoid * (1.0 + gate_pre * (1.0 - sigmoid))).astype(
        jnp.bfloat16
    )
    up_grad = (hidden_grad * gate_pre * sigmoid).astype(jnp.bfloat16)
    expert_out = jnp.dot(hidden, down_w, preferred_element_type=jnp.float32)
    gate_dots = jnp.sum(grad_rows * expert_out, axis=1, keepdims=True)
    weighted_out = (slot_gate * expert_out).astype(jnp.bfloat16)
    row_grads = lax.dot_general(gate_grad, gate_w, CONTRACT_LAST, preferred_element_type=jnp.float32)
    row_grads = row_grads + lax.dot_general(
        up_grad, up_w, CONTRACT_LAST, preferred_element_type=jnp.float32
    )
    dot_table = jnp.where(lane[:, :PLANE] == place, gate_dots, 0.0)
    back = jnp.concatenate(
        [weighted_out, split_columns(dot_table), row_grads.astype(jnp.bfloat16)], axis=1
    )
    both_grads = jnp.concatenate([gate_grad, up_grad], axis=1)
    return back, row_block, hidden, pick_grad, both_grads


def on_device(tokens, out_grad, expert_ids, route_gates, swap_flags, gate_proj, up_proj, down_proj):
    devices = lax.axis_size("expert")
    my_expert = lax.axis_index("expert")
    lo = lax.axis_index("dp") // CORES
    core = lax.axis_index("dp") % CORES
    half = (my_expert // Y_SIZE) % HI_SIZE
    place = (my_expert // (HI_SIZE * Y_SIZE)) * Y_SIZE + my_expert % Y_SIZE
    width = tokens.shape[1]
    hidden_width = gate_proj.shape[2]
    weights = (gate_proj[0], up_proj[0], down_proj[0])

    own_names = half_experts(half)
    far_names = half_experts(1 - half)
    own_hits = expert_ids[:, :, None] == own_names
    far_hits = expert_ids[:, :, None] == far_names
    own_gates = jnp.sum(jnp.where(own_hits, route_gates[:, :, None], 0.0), axis=1)
    far_gates = jnp.sum(jnp.where(far_hits, route_gates[:, :, None], 0.0), axis=1)

    far_source = across(jnp.concatenate([tokens, split_columns(far_gates), out_grad], axis=1))
    near_picked = selection(own_gates)
    near_source = jnp.concatenate([tokens, split_columns(own_gates), out_grad], axis=1)
    near_blocks = fill(near_picked, near_source).reshape(PLANE, MOST, -1)
    near_rows = to_plane(near_blocks).reshape(PLANE * MOST, -1)

    far_source, near_blocks = lax.optimization_barrier((far_source, near_blocks))
    far_picked = selection(join_columns(far_source[:, width : width + SIDE]))
    far_rows = to_plane(fill(far_picked, far_source).reshape(PLANE, MOST, -1))
    far_rows = far_rows.reshape(PLANE * MOST, -1)

    near_back, near_x, near_hidden, near_pick, near_grads = expert(near_rows, place, *weights)
    far_rows, near_back = lax.optimization_barrier((far_rows, near_back))
    near_returned = to_plane(near_back.reshape(PLANE, MOST, -1)).reshape(PLANE * MOST, -1)
    far_back, far_x, far_hidden, far_pick, far_grads = expert(far_rows, place, *weights)

    down_part = lax.dot_general(
        jnp.concatenate([near_hidden, far_hidden], axis=0),
        jnp.concatenate([near_pick, far_pick], axis=0),
        CONTRACT_FIRST,
        preferred_element_type=jnp.float32,
    ).astype(jnp.bfloat16)
    gate_up_part = lax.dot_general(
        jnp.concatenate([near_x, far_x], axis=0),
        jnp.concatenate([near_grads, far_grads], axis=0),
        CONTRACT_FIRST,
        preferred_element_type=jnp.float32,
    ).astype(jnp.bfloat16)
    down_parts = core_swap(down_part, core)
    gate_up_parts = core_swap(gate_up_part, core)
    down_sum = line_sum(down_parts, lo)
    gate_up_sum = line_sum(gate_up_parts, lo)

    far_returned = to_plane(far_back.reshape(PLANE, MOST, -1)).reshape(PLANE * MOST, -1)
    near_total = collect(near_picked, near_returned)
    far_total = across(collect(far_picked, far_returned).astype(jnp.bfloat16)).astype(jnp.float32)
    layer_out = (near_total[:, :width] + far_total[:, :width]).astype(jnp.bfloat16)
    grad_tokens = (near_total[:, width + SIDE :] + far_total[:, width + SIDE :]).astype(jnp.bfloat16)
    near_dots = join_columns(near_total[:, width : width + SIDE])
    far_dots = join_columns(far_total[:, width : width + SIDE])
    gate_grads = jnp.sum(
        jnp.where(own_hits, near_dots[:, None, :], 0.0)
        + jnp.where(far_hits, far_dots[:, None, :], 0.0),
        axis=2,
    )

    is_moved = swap_flags[my_expert] == 1
    swap = [(i, i ^ (devices // 2)) for i in range(devices)]
    other_down = lax.ppermute(down_sum, "expert", swap)
    other_gate_up = lax.ppermute(gate_up_sum, "expert", swap)
    down_sum = jnp.where(is_moved, other_down, down_sum)
    gate_up_sum = jnp.where(is_moved, other_gate_up, gate_up_sum)
    grad_gate = gate_up_sum[:, :hidden_width]
    grad_up = gate_up_sum[:, hidden_width:]
    return (layer_out, grad_tokens, gate_grads, grad_gate[None], grad_up[None], down_sum[None])


def solution(mesh):
    return jax.shard_map(
        on_device,
        mesh=mesh,
        in_specs=(
            P(("dp", "expert"), None),
            P(("dp", "expert"), None),
            P(("dp", "expert"), None),
            P(("dp", "expert"), None),
            P(),
            P("expert", None, None),
            P("expert", None, None),
            P("expert", None, None),
        ),
        out_specs=(
            P(("dp", "expert"), None),
            P(("dp", "expert"), None),
            P(("dp", "expert"), None),
            P("expert", "dp", None),
            P("expert", "dp", None),
            P("expert", "dp", None),
        ),
        check_vma=False,
    )
```

time: 356 us -> 301 us (0.85)
  the two profiles are of different devices: /device:TPU:54 before, /device:TPU:16 now
where the time goes in v3:
time: 301 us; the launch traced here: 298 us
  waiting for transfers between devices  110 us (37%)
  starting transfers between devices  69 us (23%)
  matrix products  53.5 us (18%)
  local copies, waits for them, and re-layouts  37.2 us (12%)
  other arithmetic  26.8 us (9%)
    ppermute x2, waiting for transfers between devices, across(): return lax.ppermute(value, BOTH, pairs)  32.5 us
    all_to_all x4, starting transfers between devices, to_plane(): lax.all_to_all(blocks, 'expert', split_axis=0, concat_axis=0, axis_index_...  28.6 us
    ppermute x2, waiting for transfers between devices, line_sum(): lax.ppermute(up, 'dp', neighbours([(0, 1), (1, 2)])).astype(jnp.float32)  27.6 us
    all_to_all x4, waiting for transfers between devices, to_plane(): lax.all_to_all(blocks, 'expert', split_axis=0, concat_axis=0, axis_index_...  16.7 us
    ppermute x1, waiting for transfers between devices, on_device(): other_gate_up = lax.ppermute(gate_up_sum, 'expert', swap)  13.7 us
    unnamed x80, local copies, waits for them, and re-layouts  12.1 us
    ppermute x2, waiting for transfers between devices, line_sum(): lax.ppermute(up, 'dp', neighbours([(0, 1), (1, 2), (2, 3)]))  11.4 us
    concatenate x2, local copies, waits for them, and re-layouts, expert(): jnp.concatenate([weighted_out, split_columns(dot_table), row_grads.astype...  9.33 us
  transfers between devices with their start and end apart: 20, of which 9 were waited for; matrix products, arithmetic and copies ran while one was open for 26% of the time, Pallas kernels for 0%

profile of v3, /device:TPU:16, one launch (start us, length us, event | category | flops | bytes accessed | tf_op | source)
XLA Modules:
  0.0 298.1 jit_solution(9452063558899501483)
XLA Ops:
  0.7 2.2 copy.30
  2.9 2.0 copy.31
  4.9 1.9 constant_dynamic-update-slice_fusion.5
  9.3 1.9 constant_dynamic-update-slice_fusion
  11.2 5.9 %collective-permute-start = (bf16[128,4224]{0,1:T(8,128)(2,1)}, bf16[128,4224]{0,1:T(8,128)(2,1)}, u32[]{:S(2)}, u32[]{:S(2)}) collective-permute-start(bf16[128,4224]{0,1:T(8,128)(2,1)} %constant_dynamic-update-slice_fusion), channel_id=1, source_target_pairs={{0,196},{1,197},{2,198},{3,199},{4,192},{5,193},{6,194},{7,195},{8... | collective-permute-start | bytes 3244040 | tf_op jit(solution)/shard_map/ppermute | solution.py:27
  18.1 3.1 %concatenate.43 = bf16[128,4224]{1,0:T(8,128)(2,1)} concatenate(bf16[128,2048]{1,0:T(8,128)(2,1)} %param.8, bf16[128,16]{1,0:T(8,128)(2,1)S(1)} %copy.32, bf16[128,16]{1,0:T(8,128)(2,1)S(1)} %copy.33, bf16[128,16]{1,0:T(8,128)(2,1)S(1)} %copy.34, bf16[128,80]{1,0:T(8,128)(2,1)S(1)} %broadcast.217.clone, bf16[128,2048]{1,0:T(8,128)(2,1)} %param.9), dimensions={1} | concatenate | bytes 2162688 | tf_op jit(solution)/shard_map/concatenate | solution.py:168
  21.3 3.3 %convolution_convert_fusion.2 = bf16[256,4224]{1,0:T(8,128)(2,1)} fusion(pred[256,128]{1,0:T(32,128)(4,1)S(1)} %fusion.75, bf16[128,4224]{1,0:T(8,128)(2,1)} %concatenate.43), kind=kOutput, calls=%fused_computation.2 | convolution fusion | flops 277905408 | bytes 3276800 | tf_op jit(solution)/shard_map/dot_general | solution.py:68
  24.6 7.3 %all-to-all-start.1 = ((bf16[16,16,4224]{2,1,0:T(8,128)(2,1)}), bf16[16,16,4224]{2,1,0:T(8,128)(2,1)}, u32[]{:S(2)}, u32[]{:S(2)}) async-start(bf16[16,16,4224]{2,1,0:T(8,128)(2,1)} %bitcast.150), calls=%async_computation.1 | async-start | bytes 4325376 | tf_op jit(solution)/shard_map/all_to_all | solution.py:31
  31.9 32.5 %collective-permute-done = bf16[128,4224]{0,1:T(8,128)(2,1)} collective-permute-done((bf16[128,4224]{0,1:T(8,128)(2,1)}, bf16[128,4224]{0,1:T(8,128)(2,1)}, u32[]{:S(2)}, u32[]{:S(2)}) %collective-permute-start) | collective-permute-done | bytes 1081376 | tf_op jit(solution)/shard_map/ppermute | solution.py:27
  65.8 3.3 %convolution_convert_fusion.1 = bf16[256,4224]{1,0:T(8,128)(2,1)} fusion(pred[256,128]{1,0:T(32,128)(4,1)S(1)} %fusion.76, bf16[128,4224]{0,1:T(8,128)(2,1)} %collective-permute-done), kind=kOutput, calls=%fused_computation.1 | convolution fusion | flops 277905408 | bytes 3276800 | tf_op jit(solution)/shard_map/dot_general | solution.py:68
  69.2 7.3 %all-to-all-start = ((bf16[16,16,4224]{2,1,0:T(8,128)(2,1)}), bf16[16,16,4224]{2,1,0:T(8,128)(2,1)}, u32[]{:S(2)}, u32[]{:S(2)}) async-start(bf16[16,16,4224]{2,1,0:T(8,128)(2,1)} %bitcast.151), calls=%async_computation | async-start | bytes 4325376 | tf_op jit(solution)/shard_map/all_to_all | solution.py:31
  76.5 2.3 slice.127
  78.8 3.3 %fusion.25 = f32[256,768]{1,0:T(8,128)S(1)} fusion(bf16[1,2048,768]{2,1,0:T(8,128)(2,1)} %param.13, bf16[256,4224]{1,0:T(8,128)(2,1)} %bitcast.9), kind=kOutput, calls=%fused_computation.33 | convolution fusion | flops 805306368 | bytes 4980736 | tf_op jit(solution)/shard_map/dot_general | solution.py:121
  82.1 3.4 %multiply_convert_fusion.7 = (bf16[256,768]{1,0:T(8,128)(2,1)S(1)}, f32[256,768]{1,0:T(8,128)}) fusion(f32[256,768]{1,0:T(8,128)S(1)} %fusion.25, bf16[1,2048,768]{2,1,0:T(8,128)(2,1)S(1)} %copy-done.4, bf16[256,4224]{1,0:T(8,128)(2,1)} %bitcast.9), kind=kOutput, calls=%fused_computation.101 | convolution fusion | flops 806486016 | bytes 6160384 | tf_op jit(solution)/shard_map/dot_general | solution.py:122
  86.5 3.8 %fusion.40 = (bf16[256,2048]{1,0:T(8,128)(2,1)}, f32[256]{0:T(256)S(1)}, bf16[256,2048]{1,0:T(8,128)(2,1)}) fusion(f32[256]{0:T(256)S(1)} %select_reduce_fusion.1, bf16[256,4224]{1,0:T(8,128)(2,1)} %bitcast.9, bf16[256,768]{1,0:T(8,128)(2,1)S(1)} %get-tuple-element.45, bf16[1,768,2048]{2,1,0:T(8,128)(2,1)S(1)} %copy-done), kind=kOutput, calls=%fused_computation.45 | convolution fusion | flops 808976128 | bytes 6686720 | tf_op jit(solution)/shard_map/dot_general | solution.py:133
  90.8 3.0 %multiply_convert_fusion.6 = (bf16[256,768]{1,0:T(8,128)(2,1)S(1)}, bf16[256,768]{1,0:T(8,128)(2,1)S(1)}) fusion(f32[256,768]{1,0:T(8,128)} %copy-done.34, f32[256,768]{1,0:T(8,128)} %get-tuple-element.46, bf16[256,2048]{1,0:T(8,128)(2,1)} %get-tuple-element.22, bf16[1,768,2048]{2,1,0:T(8,128)(2,1)S(1)} %copy-done), kind=kOutput, calls=%fused_computation.100 | convolution fusion | flops 807862272 | bytes 6553600 | tf_op jit(solution)/shard_map/dot_general | solution.py:126
  96.0 2.0 fusion.36
  98.0 4.7 %concatenate.44 = bf16[256,4224]{1,0:T(8,128)(2,1)} concatenate(bf16[256,2048]{1,0:T(8,128)(2,1)} %get-tuple-element.24, bf16[256,16]{1,0:T(8,128)(2,1)S(1)} %copy.36, bf16[256,16]{1,0:T(8,128)(2,1)S(1)} %copy.37, bf16[256,16]{1,0:T(8,128)(2,1)S(1)} %copy.38, bf16[256,80]{1,0:T(8,128)(2,1)S(1)} %broadcast.220, bf16[256,2048]{1,0:T(8,128)(2,1)} %fusion.36), dimensions={1} | concatenate | bytes 4325376 | tf_op jit(solution)/shard_map/concatenate | solution.py:141
  102.7 1.7 all-to-all-done
  105.3 3.3 %fusion.21 = f32[256,768]{1,0:T(8,128)S(1)} fusion(bf16[1,2048,768]{2,1,0:T(8,128)(2,1)} %param.13, bf16[256,4224]{1,0:T(8,128)(2,1)} %bitcast.8), kind=kOutput, calls=%fused_computation.29 | convolution fusion | flops 805306368 | bytes 4980736 | tf_op jit(solution)/shard_map/dot_general | solution.py:121
  108.7 1.3 slice.106
  110.0 2.3 multiply_convert_fusion.4
  112.3 3.4 %fusion.42 = (bf16[256,2048]{1,0:T(8,128)(2,1)S(1)}, f32[256]{0:T(256)S(1)}, bf16[256,2048]{1,0:T(8,128)(2,1)}) fusion(f32[256]{0:T(256)S(1)} %select_reduce_fusion, bf16[256,4224]{1,0:T(8,128)(2,1)} %bitcast.8, bf16[256,768]{1,0:T(8,128)(2,1)S(1)} %get-tuple-element.47, bf16[1,768,2048]{2,1,0:T(8,128)(2,1)S(1)} %copy-done), kind=kOutput, calls=%fused_computation.47 | convolution fusion | flops 808976128 | bytes 6686720 | tf_op jit(solution)/shard_map/dot_general | solution.py:133
  115.6 1.2 multiply_convert_fusion.3
  117.1 8.4 %convolution_convert_fusion = bf16[2048,1536]{1,0:T(8,128)(2,1)S(1)} fusion(bf16[256,2048]{1,0:T(8,128)(2,1)S(1)} %slice.106, bf16[256,2048]{1,0:T(8,128)(2,1)S(1)} %copy-done.14, bf16[256,768]{1,0:T(8,128)(2,1)S(1)} %get-tuple-element.31, bf16[256,768]{1,0:T(8,128)(2,1)S(1)} %get-tuple-element.30, bf16[256,768]{1,0:T(8,128)(2,1)S(1)} %copy-done.21, ...), kind=kOutput, calls=%fused_computation | convolution fusion | flops 3234856960 | bytes 9961472 | tf_op jit(solution)/shard_map/dot_general | solution.py:188
  125.5 1.9 dynamic-slice_bitcast_fusion
  127.5 1.6 copy-done.12
  129.1 1.8 convolution_convert_fusion.3
  131.0 1.5 dynamic-slice_bitcast_fusion.1
  133.2 7.2 %all-to-all-start.2 = ((bf16[16,16,4224]{2,1,0:T(8,128)(2,1)}), bf16[16,16,4224]{2,1,0:T(8,128)(2,1)}, u32[]{:S(2)}, u32[]{:S(2)}) async-start(bf16[16,16,4224]{2,1,0:T(8,128)(2,1)} %bitcast.14), calls=%async_computation.2 | async-start | bytes 4325376 | tf_op jit(solution)/shard_map/all_to_all | solution.py:31
  142.1 3.2 %fusion.11 = f32[256,2048]{1,0:T(8,128)S(1)} fusion(bf16[256,768]{1,0:T(8,128)(2,1)} %copy-done.19, bf16[1,2048,768]{2,1,0:T(8,128)(2,1)} %param.14), kind=kOutput, calls=%fused_computation.19 | convolution fusion | flops 805306368 | bytes 5636096 | tf_op jit(solution)/shard_map/dot_general | solution.py:137
  145.3 2.0 fusion.33
  147.3 4.7 %concatenate.45 = bf16[256,4224]{1,0:T(8,128)(2,1)} concatenate(bf16[256,2048]{1,0:T(8,128)(2,1)} %get-tuple-element.25, bf16[256,16]{1,0:T(8,128)(2,1)S(1)} %copy.39, bf16[256,16]{1,0:T(8,128)(2,1)S(1)} %copy.40, bf16[256,16]{1,0:T(8,128)(2,1)S(1)} %copy.41, bf16[256,80]{1,0:T(8,128)(2,1)S(1)} %broadcast.220, bf16[256,2048]{1,0:T(8,128)(2,1)} %fusion.33), dimensions={1} | concatenate | bytes 4325376 | tf_op jit(solution)/shard_map/concatenate | solution.py:141
  152.0 2.5 fusion.2
  154.6 2.0 collective-permute-start.10
  156.6 15.0 %all-to-all-done.2 = bf16[16,16,4224]{2,1,0:T(8,128)(2,1)} async-done(((bf16[16,16,4224]{2,1,0:T(8,128)(2,1)}), bf16[16,16,4224]{2,1,0:T(8,128)(2,1)}, u32[]{:S(2)}, u32[]{:S(2)}) %all-to-all-start.2) | async-done | bytes 2162720 | tf_op jit(solution)/shard_map/all_to_all | solution.py:31
  171.7 6.9 %all-to-all-start.3 = ((bf16[16,16,4224]{2,1,0:T(8,128)(2,1)}), bf16[16,16,4224]{2,1,0:T(8,128)(2,1)}, u32[]{:S(2)}, u32[]{:S(2)}) async-start(bf16[16,16,4224]{2,1,0:T(8,128)(2,1)} %bitcast.152), calls=%async_computation.3 | async-start | bytes 4325376 | tf_op jit(solution)/shard_map/all_to_all | solution.py:31
  178.6 3.7 %fusion = bf16[4,256,1536]{2,1,0:T(8,128)(2,1)S(1)} fusion(bf16[4,256,1536]{2,1,0:T(8,128)(2,1)} %collective-permute-done.2, bf16[4,2,256,1536]{3,2,1,0:T(8,128)(2,1)} %bitcast.154, s32[]{:T(128)S(6)} %select_n.177), kind=kLoop, calls=%fused_computation.4 | loop fusion | flops 6291456 | bytes 9437188 | tf_op jit(solution)/shard_map/convert_element_type | solution.py:92
  183.3 2.2 collective-permute-start.3
  185.5 1.9 fusion.64
  187.4 2.1 collective-permute-start.11
  189.5 1.4 collective-permute-start.13
  190.9 2.2 convolution_bitcast_fusion.1
  193.1 1.4 copy-done.10
  196.1 6.8 %collective-permute-done.3 = bf16[256,1536]{1,0:T(8,128)(2,1)} collective-permute-done((bf16[256,1536]{1,0:T(8,128)(2,1)}, bf16[256,1536]{1,0:T(8,128)(2,1)}, u32[]{:S(2)}, u32[]{:S(2)}) %collective-permute-start.3) | collective-permute-done | bytes 786464 | tf_op jit(solution)/shard_map/ppermute | solution.py:97
  202.9 2.6 fusion.49
  205.5 5.3 %collective-permute-start.4 = (bf16[256,1536]{1,0:T(8,128)(2,1)}, bf16[256,1536]{1,0:T(8,128)(2,1)}, u32[]{:S(2)}, u32[]{:S(2)}) collective-permute-start(bf16[256,1536]{1,0:T(8,128)(2,1)} %get-tuple-element.16), channel_id=1, source_target_pairs={{0,64},{32,96},{64,128},{96,160},{1,65},{33,97},{65,129},{97,161},... | collective-permute-start | bytes 2359304 | tf_op jit(solution)/shard_map/ppermute | solution.py:100
  210.8 1.5 collective-permute-start.6
  212.3 2.3 fusion.1
  214.6 1.7 collective-permute-start.1
  216.4 1.4 fusion.71
  217.8 4.6 %collective-permute-start.12 = (bf16[96,2048]{1,0:T(8,128)(2,1)S(1)}, bf16[96,2048]{1,0:T(8,128)(2,1)S(1)}, u32[]{:S(2)}, u32[]{:S(2)}) collective-permute-start(bf16[96,2048]{1,0:T(8,128)(2,1)S(1)} %get-tuple-element.28), channel_id=1, source_target_pairs={{0,64},{32,96},{64,128},{96,160},{128,192},{160,224},{1,65},{33,97... | collective-permute-start | bytes 1179656 | tf_op jit(solution)/shard_map/ppermute | solution.py:104
  222.4 1.3 collective-permute-start.14
  223.7 27.6 %collective-permute-done.4 = bf16[256,1536]{1,0:T(8,128)(2,1)} collective-permute-done((bf16[256,1536]{1,0:T(8,128)(2,1)}, bf16[256,1536]{1,0:T(8,128)(2,1)}, u32[]{:S(2)}, u32[]{:S(2)}) %collective-permute-start.4) | collective-permute-done | bytes 786464 | tf_op jit(solution)/shard_map/ppermute | solution.py:100
  251.3 1.8 fusion.59
  253.1 4.4 %collective-permute-start.5 = (bf16[256,1536]{1,0:T(8,128)(2,1)S(1)}, bf16[256,1536]{1,0:T(8,128)(2,1)S(1)}, u32[]{:S(2)}, u32[]{:S(2)}) collective-permute-start(bf16[256,1536]{1,0:T(8,128)(2,1)S(1)} %get-tuple-element.18), channel_id=1, source_target_pairs={{0,64},{32,96},{64,128},{96,160},{128,192},{160,224},{1,65},{33,97... | collective-permute-start | bytes 2359304 | tf_op jit(solution)/shard_map/ppermute | solution.py:104
  257.5 1.4 collective-permute-start.7
  259.8 3.1 %collective-permute-start.15 = (bf16[96,2048]{1,0:T(8,128)(2,1)S(1)}, bf16[96,2048]{1,0:T(8,128)(2,1)}, u32[]{:S(2)}, u32[]{:S(2)}) collective-permute-start(bf16[96,2048]{1,0:T(8,128)(2,1)S(1)} %fusion.73), channel_id=1, source_target_pairs={{0,16},{1,17},{2,18},{3,19},{4,20},{5,21},{6,22},{7,23},{8,24},{9,... | collective-permute-start | bytes 1179656 | tf_op jit(solution)/shard_map/ppermute | solution.py:214
  264.2 10.7 %collective-permute-done.5 = bf16[256,1536]{1,0:T(8,128)(2,1)S(1)} collective-permute-done((bf16[256,1536]{1,0:T(8,128)(2,1)S(1)}, bf16[256,1536]{1,0:T(8,128)(2,1)S(1)}, u32[]{:S(2)}, u32[]{:S(2)}) %collective-permute-start.5) | collective-permute-done | bytes 786464 | tf_op jit(solution)/shard_map/ppermute | solution.py:104
  275.7 1.2 fusion.61
  276.9 3.0 collective-permute-start.8
  280.0 1.4 fusion.83
  282.2 13.7 %collective-permute-done.8 = bf16[256,1536]{1,0:T(8,128)(2,1)} collective-permute-done((bf16[256,1536]{1,0:T(8,128)(2,1)}, bf16[256,1536]{1,0:T(8,128)(2,1)}, u32[]{:S(2)}, u32[]{:S(2)}) %collective-permute-start.8) | collective-permute-done | bytes 786464 | tf_op jit(solution)/shard_map/ppermute | solution.py:215
  295.9 1.2 broadcast_select_fusion
  (137 shorter events, 18.9 us)
Async XLA Ops:
  0.6 85.9 %copy-start = (bf16[1,768,2048]{2,1,0:T(8,128)(2,1)S(1)}, bf16[1,768,2048]{2,1,0:T(8,128)(2,1)}, u32[]{:S(2)}) copy-start(bf16[1,768,2048]{2,1,0:T(8,128)(2,1)} %param.15) | copy-start | bytes 9437188
  0.6 6.2 %copy-start.25 = (s32[128,8]{0,1:T(8,128)S(1)}, s32[128,8]{0,1:T(8,128)}, u32[]{:S(2)}) copy-start(s32[128,8]{0,1:T(8,128)} %param.10) | copy-start | bytes 12292
  0.7 6.2 %copy-start.32 = (f32[128,8]{0,1:T(8,128)S(1)}, f32[128,8]{0,1:T(8,128)}, u32[]{:S(2)}) copy-start(f32[128,8]{0,1:T(8,128)} %param.11) | copy-start | bytes 12292
  6.8 1.9 copy-start.29
  6.8 1.9 copy-start.31
  11.2 53.2 %collective-permute-start = (bf16[128,4224]{0,1:T(8,128)(2,1)}, bf16[128,4224]{0,1:T(8,128)(2,1)}, u32[]{:S(2)}, u32[]{:S(2)}) collective-permute-start(bf16[128,4224]{0,1:T(8,128)(2,1)} %constant_dynamic-update-slice_fusion), channel_id=1, source_target_pairs={{0,196},{1,197},{2,198},{3,199},{4,192},{5,193},{6,194},{7,195},{8... | collective-permute-start | bytes 3244040 | tf_op jit(solution)/shard_map/ppermute | solution.py:27
  17.1 0.6 copy-start.27
  17.1 0.9 copy-start.22
  24.6 44.6 %all-to-all-start.1 = ((bf16[16,16,4224]{2,1,0:T(8,128)(2,1)}), bf16[16,16,4224]{2,1,0:T(8,128)(2,1)}, u32[]{:S(2)}, u32[]{:S(2)}) async-start(bf16[16,16,4224]{2,1,0:T(8,128)(2,1)} %bitcast.150), calls=%async_computation.1 | async-start | bytes 4325376 | tf_op jit(solution)/shard_map/all_to_all | solution.py:31
  65.1 0.6 copy-start.24
  69.2 35.2 %all-to-all-start = ((bf16[16,16,4224]{2,1,0:T(8,128)(2,1)}), bf16[16,16,4224]{2,1,0:T(8,128)(2,1)}, u32[]{:S(2)}, u32[]{:S(2)}) async-start(bf16[16,16,4224]{2,1,0:T(8,128)(2,1)} %bitcast.151), calls=%async_computation | async-start | bytes 4325376 | tf_op jit(solution)/shard_map/all_to_all | solution.py:31
  78.8 3.3 %copy-start.4 = (bf16[1,2048,768]{2,1,0:T(8,128)(2,1)S(1)}, bf16[1,2048,768]{2,1,0:T(8,128)(2,1)}, u32[]{:S(2)}) copy-start(bf16[1,2048,768]{2,1,0:T(8,128)(2,1)} %param.14) | copy-start | bytes 9437188
  82.1 3.4 %copy-start.34 = (f32[256,768]{1,0:T(8,128)}, f32[256,768]{1,0:T(8,128)S(1)}, u32[]{:S(2)}) copy-start(f32[256,768]{1,0:T(8,128)S(1)} %fusion.25) | copy-start | bytes 2359300
  85.5 4.8 %copy-start.36 = (bf16[256,768]{1,0:T(8,128)(2,1)}, bf16[256,768]{1,0:T(8,128)(2,1)S(1)}, u32[]{:S(2)}) copy-start(bf16[256,768]{1,0:T(8,128)(2,1)S(1)} %get-tuple-element.45) | copy-start | bytes 1179652
  90.8 3.1 %copy-start.5 = (bf16[1,2048,768]{2,1,0:T(8,128)(2,1)S(1)}, bf16[1,2048,768]{2,1,0:T(8,128)(2,1)}, u32[]{:S(2)}) copy-start(bf16[1,2048,768]{2,1,0:T(8,128)(2,1)} %param.14) | copy-start | bytes 9437188
  93.8 1.1 copy-start.20
  93.8 1.1 copy-start.17
  93.9 2.2 copy-start.2
  105.3 4.7 %copy-start.6 = (bf16[1,2048,768]{2,1,0:T(8,128)(2,1)S(1)}, bf16[1,2048,768]{2,1,0:T(8,128)(2,1)}, u32[]{:S(2)}) copy-start(bf16[1,2048,768]{2,1,0:T(8,128)(2,1)} %param.14) | copy-start | bytes 9437188
  115.6 1.2 copy-start.14
  115.6 1.3 copy-start.18
  115.6 1.4 copy-start.21
  116.8 8.6 %copy-start.15 = (bf16[256,768]{1,0:T(8,128)(2,1)}, bf16[256,768]{1,0:T(8,128)(2,1)S(1)}, u32[]{:S(2)}) copy-start(bf16[256,768]{1,0:T(8,128)(2,1)S(1)} %get-tuple-element.30) | copy-start | bytes 1179652
  116.9 8.6 %copy-start.19 = (bf16[256,768]{1,0:T(8,128)(2,1)}, bf16[256,768]{1,0:T(8,128)(2,1)S(1)}, u32[]{:S(2)}) copy-start(bf16[256,768]{1,0:T(8,128)(2,1)S(1)} %get-tuple-element.31) | copy-start | bytes 1179652
  125.5 3.6 %copy-start.12 = (bf16[2048,1536]{1,0:T(8,128)(2,1)}, bf16[2048,1536]{1,0:T(8,128)(2,1)S(1)}, u32[]{:S(2)}) copy-start(bf16[2048,1536]{1,0:T(8,128)(2,1)S(1)} %convolution_convert_fusion) | copy-start | bytes 18874372
  125.5 3.6 %copy-start.35 = (bf16[256,2048]{1,0:T(8,128)(2,1)S(1)}, bf16[256,2048]{1,0:T(8,128)(2,1)}, u32[]{:S(2)}) copy-start(bf16[256,2048]{1,0:T(8,128)(2,1)} %get-tuple-element.22) | copy-start | bytes 3145732
  125.5 3.6 %copy-start.37 = (bf16[256,768]{1,0:T(8,128)(2,1)S(1)}, bf16[256,768]{1,0:T(8,128)(2,1)}, u32[]{:S(2)}) copy-start(bf16[256,768]{1,0:T(8,128)(2,1)} %copy-done.36) | copy-start | bytes 1179652
  129.1 49.5 %collective-permute-start.2 = (bf16[4,256,1536]{2,1,0:T(8,128)(2,1)}, bf16[4,256,1536]{2,1,0:T(8,128)(2,1)}, u32[]{:S(2)}, u32[]{:S(2)}) collective-permute-start(bf16[4,256,1536]{2,1,0:T(8,128)(2,1)} %dynamic-slice_bitcast_fusion), channel_id=1, source_target_pairs={{0,32},{32,0},{64,96},{96,64},{128,160},{160,128},{192,224},{224,1... | collective-permute-start | bytes 9437192 | tf_op jit(solution)/shard_map/ppermute | solution.py:91
  131.0 2.3 copy-start.13
  132.5 19.4 %collective-permute-start.9 = (bf16[4,96,2048]{2,1,0:T(8,128)(2,1)}, bf16[4,96,2048]{2,1,0:T(8,128)(2,1)}, u32[]{:S(2)}, u32[]{:S(2)}) collective-permute-start(bf16[4,96,2048]{2,1,0:T(8,128)(2,1)} %dynamic-slice_bitcast_fusion.1), channel_id=1, source_target_pairs={{0,32},{32,0},{64,96},{96,64},{128,160},{160,128},{192,224},{224,1... | collective-permute-start | bytes 4718600 | tf_op jit(solution)/shard_map/ppermute | solution.py:91
  133.0 7.3 %copy-start.33 = (s32[32]{0:T(128)S(1)}, s32[32]{0:T(128)}, u32[]{:S(2)}) copy-start(s32[32]{0:T(128)} %param.12) | copy-start | bytes 388
  133.2 38.4 %all-to-all-start.2 = ((bf16[16,16,4224]{2,1,0:T(8,128)(2,1)}), bf16[16,16,4224]{2,1,0:T(8,128)(2,1)}, u32[]{:S(2)}, u32[]{:S(2)}) async-start(bf16[16,16,4224]{2,1,0:T(8,128)(2,1)} %bitcast.14), calls=%async_computation.2 | async-start | bytes 4325376 | tf_op jit(solution)/shard_map/all_to_all | solution.py:31
  142.1 3.2 %copy-start.3 = (bf16[1,2048,768]{2,1,0:T(8,128)(2,1)S(1)}, bf16[1,2048,768]{2,1,0:T(8,128)(2,1)}, u32[]{:S(2)}) copy-start(bf16[1,2048,768]{2,1,0:T(8,128)(2,1)} %param.13) | copy-start | bytes 9437188
  142.1 3.2 %copy-start.16 = (bf16[256,768]{1,0:T(8,128)(2,1)S(1)}, bf16[256,768]{1,0:T(8,128)(2,1)}, u32[]{:S(2)}) copy-start(bf16[256,768]{1,0:T(8,128)(2,1)} %copy-done.15) | copy-start | bytes 1179652
  154.5 17.1 %copy-start.7 = (bf16[4,96,2048]{2,1,0:T(8,128)(2,1)}, bf16[4,96,2048]{2,1,0:T(8,128)(2,1)S(1)}, u32[]{:S(2)}) copy-start(bf16[4,96,2048]{2,1,0:T(8,128)(2,1)S(1)} %fusion.2) | copy-start | bytes 4718596
  154.6 30.9 %collective-permute-start.10 = (bf16[96,2048]{1,0:T(8,128)(2,1)S(1)}, bf16[96,2048]{1,0:T(8,128)(2,1)}, u32[]{:S(2)}, u32[]{:S(2)}) collective-permute-start(bf16[96,2048]{1,0:T(8,128)(2,1)S(1)} %fusion.74), channel_id=1, source_target_pairs={{0,64},{32,96},{192,128},{224,160},{1,65},{33,97},{193,129},{225,1... | collective-permute-start | bytes 1179656 | tf_op jit(solution)/shard_map/ppermute | solution.py:97
  171.7 40.7 %all-to-all-start.3 = ((bf16[16,16,4224]{2,1,0:T(8,128)(2,1)}), bf16[16,16,4224]{2,1,0:T(8,128)(2,1)}, u32[]{:S(2)}, u32[]{:S(2)}) async-start(bf16[16,16,4224]{2,1,0:T(8,128)(2,1)} %bitcast.152), calls=%async_computation.3 | async-start | bytes 4325376 | tf_op jit(solution)/shard_map/all_to_all | solution.py:31
  182.3 3.2 %copy-start.8 = (bf16[4,96,2048]{2,1,0:T(8,128)(2,1)S(1)}, bf16[4,96,2048]{2,1,0:T(8,128)(2,1)}, u32[]{:S(2)}) copy-start(bf16[4,96,2048]{2,1,0:T(8,128)(2,1)} %copy-done.7) | copy-start | bytes 4718596
  182.3 8.6 %copy-start.23 = (pred[16,128]{1,0:T(8,128)(4,1)S(1)}, pred[16,128]{1,0:T(8,128)(4,1)}, u32[]{:S(2)}) copy-start(pred[16,128]{1,0:T(8,128)(4,1)} %copy-done.22) | copy-start | bytes 6148
  182.3 8.6 %copy-start.28 = (f32[16]{0:T(128)S(1)}, f32[16]{0:T(128)}, u32[]{:S(2)}) copy-start(f32[16]{0:T(128)} %copy-done.27) | copy-start | bytes 196
  183.3 19.6 %collective-permute-start.3 = (bf16[256,1536]{1,0:T(8,128)(2,1)}, bf16[256,1536]{1,0:T(8,128)(2,1)}, u32[]{:S(2)}, u32[]{:S(2)}) collective-permute-start(bf16[256,1536]{1,0:T(8,128)(2,1)} %fusion.66), channel_id=1, source_target_pairs={{0,64},{32,96},{192,128},{224,160},{1,65},{33,97},{193,129},{225,1... | collective-permute-start | bytes 2359304 | tf_op jit(solution)/shard_map/ppermute | solution.py:97
  187.4 29.0 %collective-permute-start.11 = (bf16[96,2048]{1,0:T(8,128)(2,1)}, bf16[96,2048]{1,0:T(8,128)(2,1)}, u32[]{:S(2)}, u32[]{:S(2)}) collective-permute-start(bf16[96,2048]{1,0:T(8,128)(2,1)} %get-tuple-element.26), channel_id=1, source_target_pairs={{0,64},{32,96},{64,128},{96,160},{1,65},{33,97},{65,129},{97,161},... | collective-permute-start | bytes 1179656 | tf_op jit(solution)/shard_map/ppermute | solution.py:100
  189.5 26.9 %collective-permute-start.13 = (bf16[96,2048]{1,0:T(8,128)(2,1)S(1)}, bf16[96,2048]{1,0:T(8,128)(2,1)}, u32[]{:S(2)}, u32[]{:S(2)}) collective-permute-start(bf16[96,2048]{1,0:T(8,128)(2,1)S(1)} %get-tuple-element.27), channel_id=1, source_target_pairs={{192,128},{224,160},{128,64},{160,96},{193,129},{225,161},{129,65}... | collective-permute-start | bytes 1179656 | tf_op jit(solution)/shard_map/ppermute | solution.py:101
  193.1 1.4 copy-start.10
  205.5 45.8 %collective-permute-start.4 = (bf16[256,1536]{1,0:T(8,128)(2,1)}, bf16[256,1536]{1,0:T(8,128)(2,1)}, u32[]{:S(2)}, u32[]{:S(2)}) collective-permute-start(bf16[256,1536]{1,0:T(8,128)(2,1)} %get-tuple-element.16), channel_id=1, source_target_pairs={{0,64},{32,96},{64,128},{96,160},{1,65},{33,97},{65,129},{97,161},... | collective-permute-start | bytes 2359304 | tf_op jit(solution)/shard_map/ppermute | solution.py:100
  210.8 40.6 %collective-permute-start.6 = (bf16[256,1536]{1,0:T(8,128)(2,1)}, bf16[256,1536]{1,0:T(8,128)(2,1)}, u32[]{:S(2)}, u32[]{:S(2)}) collective-permute-start(bf16[256,1536]{1,0:T(8,128)(2,1)} %get-tuple-element.17), channel_id=1, source_target_pairs={{192,128},{224,160},{128,64},{160,96},{193,129},{225,161},{129,65}... | collective-permute-start | bytes 2359304 | tf_op jit(solution)/shard_map/ppermute | solution.py:101
  212.3 4.1 %copy-start.9 = (bf16[4,96,2048]{2,1,0:T(8,128)(2,1)S(1)}, bf16[4,96,2048]{2,1,0:T(8,128)(2,1)}, u32[]{:S(2)}) copy-start(bf16[4,96,2048]{2,1,0:T(8,128)(2,1)} %copy-done.7) | copy-start | bytes 4718596
  214.6 48.2 %collective-permute-start.1 = (bf16[128,4224]{1,0:T(8,128)(2,1)S(1)}, bf16[128,4224]{1,0:T(8,128)(2,1)S(1)}, u32[]{:S(2)}, u32[]{:S(2)}) collective-permute-start(bf16[128,4224]{1,0:T(8,128)(2,1)S(1)} %fusion.1), channel_id=1, source_target_pairs={{0,196},{1,197},{2,198},{3,199},{4,192},{5,193},{6,194},{7,195},{8... | collective-permute-start | bytes 3244040 | tf_op jit(solution)/shard_map/ppermute | solution.py:27
  217.8 41.9 %collective-permute-start.12 = (bf16[96,2048]{1,0:T(8,128)(2,1)S(1)}, bf16[96,2048]{1,0:T(8,128)(2,1)S(1)}, u32[]{:S(2)}, u32[]{:S(2)}) collective-permute-start(bf16[96,2048]{1,0:T(8,128)(2,1)S(1)} %get-tuple-element.28), channel_id=1, source_target_pairs={{0,64},{32,96},{64,128},{96,160},{128,192},{160,224},{1,65},{33,97... | collective-permute-start | bytes 1179656 | tf_op jit(solution)/shard_map/ppermute | solution.py:104
  222.4 37.3 %collective-permute-start.14 = (bf16[96,2048]{1,0:T(8,128)(2,1)S(1)}, bf16[96,2048]{1,0:T(8,128)(2,1)S(1)}, u32[]{:S(2)}, u32[]{:S(2)}) collective-permute-start(bf16[96,2048]{1,0:T(8,128)(2,1)S(1)} %get-tuple-element.29), channel_id=1, source_target_pairs={{192,128},{224,160},{128,64},{160,96},{64,0},{96,32},{193,129},{22... | collective-permute-start | bytes 1179656 | tf_op jit(solution)/shard_map/ppermute | solution.py:105
  253.1 21.8 %collective-permute-start.5 = (bf16[256,1536]{1,0:T(8,128)(2,1)S(1)}, bf16[256,1536]{1,0:T(8,128)(2,1)S(1)}, u32[]{:S(2)}, u32[]{:S(2)}) collective-permute-start(bf16[256,1536]{1,0:T(8,128)(2,1)S(1)} %get-tuple-element.18), channel_id=1, source_target_pairs={{0,64},{32,96},{64,128},{96,160},{128,192},{160,224},{1,65},{33,97... | collective-permute-start | bytes 2359304 | tf_op jit(solution)/shard_map/ppermute | solution.py:104
  257.5 5.5 %copy-start.11 = (f32[128,4224]{1,0:T(8,128)S(1)}, f32[128,4224]{1,0:T(8,128)}, u32[]{:S(2)}) copy-start(f32[128,4224]{1,0:T(8,128)} %copy-done.10) | copy-start | bytes 6488068
  257.5 18.1 %collective-permute-start.7 = (bf16[256,1536]{1,0:T(8,128)(2,1)S(1)}, bf16[256,1536]{1,0:T(8,128)(2,1)S(1)}, u32[]{:S(2)}, u32[]{:S(2)}) collective-permute-start(bf16[256,1536]{1,0:T(8,128)(2,1)S(1)} %get-tuple-element.19), channel_id=1, source_target_pairs={{192,128},{224,160},{128,64},{160,96},{64,0},{96,32},{193,129},{22... | collective-permute-start | bytes 2359304 | tf_op jit(solution)/shard_map/ppermute | solution.py:105
  259.8 21.6 %collective-permute-start.15 = (bf16[96,2048]{1,0:T(8,128)(2,1)S(1)}, bf16[96,2048]{1,0:T(8,128)(2,1)}, u32[]{:S(2)}, u32[]{:S(2)}) collective-permute-start(bf16[96,2048]{1,0:T(8,128)(2,1)S(1)} %fusion.73), channel_id=1, source_target_pairs={{0,16},{1,17},{2,18},{3,19},{4,20},{5,21},{6,22},{7,23},{8,24},{9,... | collective-permute-start | bytes 1179656 | tf_op jit(solution)/shard_map/ppermute | solution.py:214
  264.2 15.8 %copy-start.26 = (s32[128,8]{0,1:T(8,128)S(1)}, s32[128,8]{0,1:T(8,128)}, u32[]{:S(2)}) copy-start(s32[128,8]{0,1:T(8,128)} %param.10) | copy-start | bytes 12292
  264.2 15.8 %copy-start.30 = (s32[16]{0:T(128)S(1)}, s32[16]{0:T(128)}, u32[]{:S(2)}) copy-start(s32[16]{0:T(128)} %copy-done.29) | copy-start | bytes 196
  276.9 19.0 %collective-permute-start.8 = (bf16[256,1536]{1,0:T(8,128)(2,1)}, bf16[256,1536]{1,0:T(8,128)(2,1)}, u32[]{:S(2)}, u32[]{:S(2)}) collective-permute-start(bf16[256,1536]{1,0:T(8,128)(2,1)} %fusion.61), channel_id=1, source_target_pairs={{0,16},{1,17},{2,18},{3,19},{4,20},{5,21},{6,22},{7,23},{8,24},{9,... | collective-permute-start | bytes 2359304 | tf_op jit(solution)/shard_map/ppermute | solution.py:215
  281.4 16.7 %copy-start.1 = (bf16[1,768,2048]{2,1,0:T(8,128)(2,1)S(1)}, bf16[1,768,2048]{2,1,0:T(8,128)(2,1)}, u32[]{:S(2)}) copy-start(bf16[1,768,2048]{2,1,0:T(8,128)(2,1)} %param.15) | copy-start | bytes 9437188

commit v4 on v2

v4 whole, which is shorter than its diff:
```python
import functools

import jax
import jax.numpy as jnp
from jax import lax
from jax.experimental import pallas as pl
from jax.experimental.pallas import tpu as pltpu
from jax.sharding import PartitionSpec as P

MOST = 16
HI_SIZE, Y_SIZE = 2, 4
LO_SIZE, CORES = 4, 2
PLANE = 16
SIDE = 128
PARTS = 3

BOTH = ("dp", "expert")
PLANE_GROUPS = [
    [x * HI_SIZE * Y_SIZE + hi * Y_SIZE + y for x in range(PLANE // Y_SIZE) for y in range(Y_SIZE)]
    for hi in range(HI_SIZE)
]
CONTRACT_LAST = (((1,), (1,)), ((), ()))
CONTRACT_FIRST = (((0,), (0,)), ((), ()))
BF16, F32 = jnp.bfloat16, jnp.float32
WHOLE = pl.BlockSpec(memory_space=pltpu.VMEM)
SCALAR = pl.BlockSpec(memory_space=pltpu.SMEM)
ANYWHERE = pl.BlockSpec(memory_space=pl.ANY)


def limits():
    return pltpu.CompilerParams(vmem_limit_bytes=48 << 20)


def cost(flops, moved):
    return pl.CostEstimate(flops=flops, bytes_accessed=moved, transcendentals=0)


def across(value):
    experts = lax.axis_size("expert")
    pairs = []
    for dp in range(lax.axis_size("dp")):
        lo, core = divmod(dp, CORES)
        other_dp = (LO_SIZE - 1 - lo) * CORES + core
        for expert in range(experts):
            pairs.append((dp * experts + expert, other_dp * experts + (expert ^ Y_SIZE)))
    return lax.ppermute(value, BOTH, pairs)


def to_plane(blocks):
    return lax.all_to_all(
        blocks, "expert", split_axis=0, concat_axis=0, axis_index_groups=PLANE_GROUPS, tiled=True
    )


def lane_names(shape, half):
    place = lax.broadcasted_iota(jnp.int32, shape, 1) & (PLANE - 1)
    return (place >> 2) * (HI_SIZE * Y_SIZE) + half * Y_SIZE + (place & (Y_SIZE - 1))


def split_parts(values, shape):
    part = lax.broadcasted_iota(jnp.int32, shape, 1) >> 4
    high = values.astype(BF16).astype(F32)
    middle = (values - high).astype(BF16).astype(F32)
    low = values - high - middle
    chosen = jnp.where(part == 0, high, jnp.where(part == 1, middle, low))
    return jnp.where(part < PARTS, chosen, 0.0).astype(BF16)


def route_kernel(half_ref, ids_ref, gates_ref, own_ref, far_ref):
    half = half_ref[0]
    shape = own_ref.shape
    for which, ref in ((half, own_ref), (1 - half, far_ref)):
        names = lane_names(shape, which)
        total = jnp.zeros(shape, F32)
        for k in range(ids_ref.shape[1]):
            total += jnp.where(ids_ref[:, k : k + 1] == names, gates_ref[:, k : k + 1], 0.0)
        ref[...] = split_parts(total, shape)


def route(half, ids, gates):
    table = jax.ShapeDtypeStruct((ids.shape[0], SIDE), BF16)
    return pl.pallas_call(
        route_kernel,
        out_shape=(table, table),
        in_specs=[SCALAR, WHOLE, WHOLE],
        out_specs=(WHOLE, WHOLE),
        cost_estimate=cost(1000000, 200000),
        name="route",
    )(half, ids, gates)


def fill_kernel(sides_ref, tokens_ref, grads_ref, blocks_ref, picked_ref):
    rows = sides_ref.shape[0]
    width = tokens_ref.shape[1]
    turned = jnp.transpose(sides_ref[...].astype(F32))
    chosen = jnp.where(turned[:PLANE] > 0, 1.0, 0.0)
    before = jnp.where(
        lax.broadcasted_iota(jnp.int32, (rows, rows), 0)
        < lax.broadcasted_iota(jnp.int32, (rows, rows), 1),
        1.0,
        0.0,
    ).astype(BF16)
    rank = jnp.dot(chosen.astype(BF16), before, preferred_element_type=F32)
    rank = jnp.where(chosen > 0, rank, -1.0)
    slot = lax.broadcasted_iota(jnp.int32, (MOST, rows), 0).astype(F32)
    for j in range(PLANE):
        hit = jnp.where(rank[j : j + 1] == slot, 1.0, 0.0)
        picked_ref[j * MOST : (j + 1) * MOST, :] = hit.astype(BF16)
    picked = picked_ref[...]
    blocks_ref[:, width : width + SIDE] = jnp.dot(
        picked, sides_ref[...], preferred_element_type=F32
    ).astype(BF16)
    step = min(512, width)
    for n in range(0, width, step):
        blocks_ref[:, n : n + step] = jnp.dot(
            picked, tokens_ref[:, n : n + step], preferred_element_type=F32
        ).astype(BF16)
        blocks_ref[:, width + SIDE + n : width + SIDE + n + step] = jnp.dot(
            picked, grads_ref[:, n : n + step], preferred_element_type=F32
        ).astype(BF16)


def fill(sides, tokens, grads):
    rows, width = tokens.shape
    slots = PLANE * MOST
    return pl.pallas_call(
        fill_kernel,
        out_shape=(
            jax.ShapeDtypeStruct((slots, 2 * width + SIDE), BF16),
            jax.ShapeDtypeStruct((slots, rows), BF16),
        ),
        in_specs=[WHOLE] * 3,
        out_specs=(WHOLE, WHOLE),
        compiler_params=limits(),
        cost_estimate=cost(4 * slots * rows * width, 8 * slots * width),
        name="fill",
    )(sides, tokens, grads)


def expert_kernel(
    which, place_ref, rows_ref, gate_hbm, up_hbm, down_hbm, *refs
):
    if which:
        refs = refs[1:]
    back_ref, hidden_ref, pick_ref, grads_ref, gate_w, up_w, down_w, sems = refs
    copies = [
        pltpu.make_async_copy(source, target, sems.at[i])
        for i, (source, target) in enumerate(
            ((gate_hbm, gate_w), (up_hbm, up_w), (down_hbm, down_w))
        )
    ]
    for copy in copies:
        copy.start()
    place = place_ref[0]
    slots = rows_ref.shape[0]
    width, hidden_width = gate_w.shape
    lane = lax.broadcasted_iota(jnp.int32, (slots, SIDE), 1)
    mine = jnp.where((lane & (PLANE - 1)) == place, 1.0, 0.0)
    side = rows_ref[:, width : width + SIDE].astype(F32)
    slot_gate = jnp.sum(side * mine, axis=1, keepdims=True)
    pick_ref[...] = (slot_gate * rows_ref[:, width + SIDE :].astype(F32)).astype(BF16)
    for copy in copies:
        copy.wait()

    step = min(256, hidden_width)

    def forward(j, carry):
        span = pl.ds(pl.multiple_of(j * step, step), step)
        gate_pre = jnp.dot(rows_ref[:, :width], gate_w[:, span], preferred_element_type=F32)
        up_pre = jnp.dot(rows_ref[:, :width], up_w[:, span], preferred_element_type=F32)
        hidden_grad = lax.dot_general(
            pick_ref[...], down_w[span, :], CONTRACT_LAST, preferred_element_type=F32
        )
        sigmoid = jax.nn.sigmoid(gate_pre)
        silu = gate_pre * sigmoid
        hidden_ref[:, span] = (silu * up_pre).astype(BF16)
        gate_grad = hidden_grad * up_pre * sigmoid * (1.0 + gate_pre * (1.0 - sigmoid))
        grads_ref[:, span] = gate_grad.astype(BF16)
        second = pl.ds(pl.multiple_of(hidden_width + j * step, step), step)
        grads_ref[:, second] = (hidden_grad * silu).astype(BF16)
        return carry

    lax.fori_loop(0, hidden_width // step, forward, 0)

    wide = min(256, width)
    lead = back_ref.shape[:2]

    def outward(n, dots):
        start = pl.multiple_of(n * wide, wide)
        out = jnp.dot(hidden_ref[...], down_w[:, pl.ds(start, wide)], preferred_element_type=F32)
        ahead = pl.ds(pl.multiple_of(width + SIDE + n * wide, SIDE), wide)
        dots += jnp.sum(rows_ref[:, ahead].astype(F32) * out, axis=1, keepdims=True)
        back_ref[:, :, pl.ds(start, wide)] = (slot_gate * out).astype(BF16).reshape(*lead, wide)
        row_grad = lax.dot_general(
            grads_ref[:, :hidden_width],
            gate_w[pl.ds(start, wide), :],
            CONTRACT_LAST,
            preferred_element_type=F32,
        )
        row_grad += lax.dot_general(
            grads_ref[:, hidden_width:],
            up_w[pl.ds(start, wide), :],
            CONTRACT_LAST,
            preferred_element_type=F32,
        )
        back_ref[:, :, ahead] = row_grad.astype(BF16).reshape(*lead, wide)
        return dots

    dots = lax.fori_loop(0, width // wide, outward, jnp.zeros((slots, 1), F32))
    table = split_parts(dots * mine, (slots, SIDE))
    back_ref[:, :, width : width + SIDE] = table.reshape(*lead, SIDE)


def run_expert(which, place, rows, weights, back):
    slots = rows.shape[0]
    width, hidden_width = weights[0].shape
    full = 2 * width + SIDE
    out_shape = (
        jax.ShapeDtypeStruct((PLANE, 2 * MOST, full), BF16),
        jax.ShapeDtypeStruct((slots, hidden_width), BF16),
        jax.ShapeDtypeStruct((slots, width), BF16),
        jax.ShapeDtypeStruct((slots, 2 * hidden_width), BF16),
    )
    operands = [place, rows, *weights] + ([back] if which else [])
    return pl.pallas_call(
        functools.partial(expert_kernel, which),
        grid=(1,),
        out_shape=out_shape,
        in_specs=[SCALAR, pl.BlockSpec((slots, full), lambda i: (0, 0))]
        + [ANYWHERE] * (len(operands) - 2),
        out_specs=(
            pl.BlockSpec((PLANE, MOST, full), lambda i: (0, which, 0)),
            pl.BlockSpec((slots, hidden_width), lambda i: (0, 0)),
            pl.BlockSpec((slots, width), lambda i: (0, 0)),
            pl.BlockSpec((slots, 2 * hidden_width), lambda i: (0, 0)),
        ),
        scratch_shapes=[
            pltpu.VMEM((width, hidden_width), BF16),
            pltpu.VMEM((width, hidden_width), BF16),
            pltpu.VMEM((hidden_width, width), BF16),
            pltpu.SemaphoreType.DMA((3,)),
        ],
        input_output_aliases={5: 0} if which else {},
        compiler_params=limits(),
        cost_estimate=cost(12 * slots * width * hidden_width, 6 * width * hidden_width),
        name="expert",
    )(*operands)


def wide_kernel(has_sum, select_ref, near_x, far_x, near_grads, far_grads, *refs):
    out_ref = refs[-1]
    columns = out_ref.shape[2]
    step = min(512, columns)
    for n in range(0, columns, step):
        total = lax.dot_general(
            near_x[...], near_grads[:, n : n + step], CONTRACT_FIRST, preferred_element_type=F32
        )
        total += lax.dot_general(
            far_x[...], far_grads[:, n : n + step], CONTRACT_FIRST, preferred_element_type=F32
        )
        if has_sum:
            total += refs[0][0, :, n : n + step].astype(F32)
        out_ref[0, :, n : n + step] = total.astype(BF16)


def wide_grads(select, rows, grads, width, taken=None):
    shard = width // (LO_SIZE * CORES)
    slots, columns = grads[0].shape
    block = pl.BlockSpec((1, shard, columns), lambda z, s: (z, 0, 0))
    pick = pl.BlockSpec((slots, shard), lambda z, s: (0, z * CORES + s[0]))
    same = pl.BlockSpec((slots, columns), lambda z, s: (0, 0))
    extra = [] if taken is None else [taken]
    return pl.pallas_call(
        functools.partial(wide_kernel, taken is not None),
        grid_spec=pltpu.PrefetchScalarGridSpec(
            num_scalar_prefetch=1,
            grid=(LO_SIZE,),
            in_specs=[pick, pick, same, same] + [block] * len(extra),
            out_specs=block,
        ),
        out_shape=jax.ShapeDtypeStruct((LO_SIZE, shard, columns), BF16),
        compiler_params=limits(),
        cost_estimate=cost(2 * slots * width * columns, 2 * width * columns),
        name="wide",
    )(select, *rows, *grads, *extra)


def down_kernel(core_ref, near_hidden, far_hidden, near_pick, far_pick, give_ref, keep_ref, acc):
    core = core_ref[0]
    shard = give_ref.shape[1]
    acc[...] = lax.dot_general(
        near_hidden[...], near_pick[...], CONTRACT_FIRST, preferred_element_type=F32
    )
    acc[...] += lax.dot_general(
        far_hidden[...], far_pick[...], CONTRACT_FIRST, preferred_element_type=F32
    )
    for z in range(LO_SIZE):
        for which, ref in ((1 - core, give_ref), (core, keep_ref)):
            start = pl.multiple_of((z * CORES + which) * shard, shard)
            ref[z] = acc[pl.ds(start, shard), :].astype(BF16)


def down_grads(core, hidden, pick):
    slots, hidden_width = hidden[0].shape
    width = pick[0].shape[1]
    shard = hidden_width // (LO_SIZE * CORES)
    step = min(512, width)
    same = pl.BlockSpec((slots, hidden_width), lambda n, s: (0, 0))
    part = pl.BlockSpec((slots, step), lambda n, s: (0, n))
    block = pl.BlockSpec((LO_SIZE, shard, step), lambda n, s: (0, 0, n))
    shape = jax.ShapeDtypeStruct((LO_SIZE, shard, width), BF16)
    return pl.pallas_call(
        down_kernel,
        grid_spec=pltpu.PrefetchScalarGridSpec(
            num_scalar_prefetch=1,
            grid=(width // step,),
            in_specs=[same, same, part, part],
            out_specs=(block, block),
            scratch_shapes=[pltpu.VMEM((hidden_width, step), F32)],
        ),
        out_shape=(shape, shape),
        compiler_params=limits(),
        cost_estimate=cost(4 * slots * width * hidden_width, 4 * width * hidden_width),
        name="down",
    )(core, *hidden, *pick)


def turned_picks(picked_ref):
    return jnp.transpose(picked_ref[...].astype(F32)).astype(BF16)


def gather_rows(turned, returned_ref, start, size):
    block = returned_ref[:, :, start : start + size].reshape(PLANE * MOST, size)
    return jnp.dot(turned, block, preferred_element_type=F32)


def spans(width):
    step = min(512, width)
    return [(n, step) for n in range(0, width, step)]


def collect_kernel(picked_ref, returned_ref, out_ref):
    turned = turned_picks(picked_ref)
    full = out_ref.shape[1]
    width = (full - SIDE) // 2
    for start, size in spans(width) + [(width, SIDE)] + [
        (width + SIDE + n, step) for n, step in spans(width)
    ]:
        out_ref[:, start : start + size] = gather_rows(turned, returned_ref, start, size).astype(
            BF16
        )


def collect(picked, returned, which):
    slots, rows = picked.shape
    full = returned.shape[2]
    return pl.pallas_call(
        collect_kernel,
        grid=(1,),
        in_specs=[
            pl.BlockSpec((slots, rows), lambda i: (0, 0)),
            pl.BlockSpec((PLANE, MOST, full), lambda i: (0, which, 0)),
        ],
        out_specs=pl.BlockSpec((rows, full), lambda i: (0, 0)),
        out_shape=jax.ShapeDtypeStruct((rows, full), BF16),
        compiler_params=limits(),
        cost_estimate=cost(2 * slots * rows * full, 2 * slots * full),
        name="collect",
    )(picked, returned)


def finish_kernel(half_ref, ids_ref, picked_ref, returned_ref, far_ref, out_ref, token_ref, gate_ref):
    turned = turned_picks(picked_ref)
    rows, width = out_ref.shape
    for n, step in spans(width):
        near = gather_rows(turned, returned_ref, n, step)
        out_ref[:, n : n + step] = (near + far_ref[:, n : n + step].astype(F32)).astype(BF16)
        start = width + SIDE + n
        near = gather_rows(turned, returned_ref, start, step)
        far = far_ref[:, start : start + step].astype(F32)
        token_ref[:, n : n + step] = (near + far).astype(BF16)
    near_dots = gather_rows(turned, returned_ref, width, SIDE)
    far_dots = far_ref[:, width : width + SIDE].astype(F32)
    half = half_ref[0]
    near_names = lane_names((rows, SIDE), half)
    far_names = lane_names((rows, SIDE), 1 - half)
    for k in range(ids_ref.shape[1]):
        ids = ids_ref[:, k : k + 1]
        found = jnp.where(ids == near_names, near_dots, 0.0)
        found += jnp.where(ids == far_names, far_dots, 0.0)
        gate_ref[:, k : k + 1] = jnp.sum(found, axis=1, keepdims=True)


def finish(half, ids, picked, returned, far_total):
    slots, rows = picked.shape
    full = returned.shape[2]
    width = (full - SIDE) // 2
    whole = lambda shape: pl.BlockSpec(shape, lambda i: (0,) * len(shape))
    wide = jax.ShapeDtypeStruct((rows, width), BF16)
    return pl.pallas_call(
        finish_kernel,
        grid=(1,),
        in_specs=[
            SCALAR,
            whole(ids.shape),
            whole(picked.shape),
            pl.BlockSpec((PLANE, MOST, full), lambda i: (0, 0, 0)),
            whole(far_total.shape),
        ],
        out_specs=(whole((rows, width)), whole((rows, width)), whole(ids.shape)),
        out_shape=(wide, wide, jax.ShapeDtypeStruct(ids.shape, F32)),
        compiler_params=limits(),
        cost_estimate=cost(2 * slots * rows * full, 2 * slots * full),
        name="finish",
    )(half, ids, picked, returned, far_total)


def neighbours(steps):
    return [(a * CORES + core, b * CORES + core) for a, b in steps for core in range(CORES)]


def core_swap(give):
    return lax.ppermute(give, "dp", [(i, i ^ 1) for i in range(LO_SIZE * CORES)])


def shard_of(parts, index):
    index = jnp.clip(index, 0, LO_SIZE - 1)
    return lax.dynamic_index_in_dim(parts, index, axis=0, keepdims=False).astype(F32)


def line_sum(parts, lo):
    first = jnp.where(lo == 0, parts[LO_SIZE - 1], parts[0])
    arrived = lax.ppermute(first, "dp", neighbours([(0, 1), (3, 2)])).astype(F32)
    up = (shard_of(parts, lo + 2) + arrived).astype(BF16)
    down = (shard_of(parts, lo - 2) + arrived).astype(BF16)
    up = lax.ppermute(up, "dp", neighbours([(0, 1), (1, 2)]))
    down = lax.ppermute(down, "dp", neighbours([(3, 2), (2, 1)]))
    middle = up
    up = (shard_of(parts, lo + 1) + up.astype(F32)).astype(BF16)
    down = (shard_of(parts, lo - 1) + down.astype(F32)).astype(BF16)
    up = lax.ppermute(up, "dp", neighbours([(0, 1), (1, 2), (2, 3)])).astype(F32)
    down = lax.ppermute(down, "dp", neighbours([(3, 2), (2, 1), (1, 0)])).astype(F32)
    return (shard_of(parts, lo) + up + down).astype(BF16), middle


def on_device(tokens, out_grad, expert_ids, route_gates, swap_flags, gate_proj, up_proj, down_proj):
    devices = lax.axis_size("expert")
    my_expert = lax.axis_index("expert")
    lo = lax.axis_index("dp") // CORES
    core = lax.axis_index("dp") % CORES
    half = ((my_expert // Y_SIZE) % HI_SIZE).astype(jnp.int32)[None]
    place = (my_expert // (HI_SIZE * Y_SIZE)) * Y_SIZE + my_expert % Y_SIZE
    place = place.astype(jnp.int32)[None]
    here = core.astype(jnp.int32)[None]
    width = tokens.shape[1]
    hidden_width = gate_proj.shape[2]
    weights = (gate_proj[0], up_proj[0], down_proj[0])

    far_tokens = across(tokens)
    far_out_grad = across(out_grad)
    own_sides, far_sides = route(half, expert_ids, route_gates)
    far_sides = across(far_sides)
    near_blocks, near_picked = fill(own_sides, tokens, out_grad)
    near_rows = to_plane(near_blocks.reshape(PLANE, MOST, -1)).reshape(PLANE * MOST, -1)

    far_tokens, near_blocks = lax.optimization_barrier((far_tokens, near_blocks))
    far_blocks, far_picked = fill(far_sides, far_tokens, far_out_grad)
    far_rows = to_plane(far_blocks.reshape(PLANE, MOST, -1)).reshape(PLANE * MOST, -1)

    back, near_hidden, near_pick, near_grads = run_expert(0, place, near_rows, weights, None)
    back, far_hidden, far_pick, far_grads = run_expert(1, place, far_rows, weights, back)

    rows, grads = (near_rows, far_rows), (near_grads, far_grads)
    taken = core_swap(wide_grads(1 - here, rows, grads, width))
    give_down, keep_down = down_grads(here, (near_hidden, far_hidden), (near_pick, far_pick))
    taken_down = core_swap(give_down)
    gate_up_parts = wide_grads(here, rows, grads, width, taken)
    down_parts = (keep_down.astype(F32) + taken_down.astype(F32)).astype(BF16)
    gate_up_sum, middle = line_sum(gate_up_parts, lo)
    down_sum, unused = line_sum(down_parts, lo)

    returned = to_plane(back)
    returned, middle = lax.optimization_barrier((returned, middle))
    far_total = across(collect(far_picked, returned, 1))
    layer_out, grad_tokens, gate_grads = finish(half, expert_ids, near_picked, returned, far_total)

    is_moved = swap_flags[my_expert] == 1
    swap = [(i, i ^ (devices // 2)) for i in range(devices)]
    other_gate_up = lax.ppermute(gate_up_sum, "expert", swap)
    other_down = lax.ppermute(down_sum, "expert", swap)
    gate_up_sum = jnp.where(is_moved, other_gate_up, gate_up_sum)
    down_sum = jnp.where(is_moved, other_down, down_sum)
    grad_gate = gate_up_sum[:, :hidden_width]
    grad_up = gate_up_sum[:, hidden_width:]
    return (layer_out, grad_tokens, gate_grads, grad_gate[None], grad_up[None], down_sum[None])


def solution(mesh):
    return jax.shard_map(
        on_device,
        mesh=mesh,
        in_specs=(
            P(("dp", "expert"), None),
            P(("dp", "expert"), None),
            P(("dp", "expert"), None),
            P(("dp", "expert"), None),
            P(),
            P("expert", None, None),
            P("expert", None, None),
            P("expert", None, None),
        ),
        out_specs=(
            P(("dp", "expert"), None),
            P(("dp", "expert"), None),
            P(("dp", "expert"), None),
            P("expert", "dp", None),
            P("expert", "dp", None),
            P("expert", "dp", None),
        ),
        check_vma=False,
    )
```

time: 356 us -> 270 us (0.76)
  the two profiles are of different devices: /device:TPU:54 before, /device:TPU:16 now
where the time goes in v4:
time: 270 us; the launch traced here: 267 us
  waiting for transfers between devices  111 us (41%)
  starting transfers between devices  68.9 us (26%)
  Pallas kernels  49.9 us (18%)
  other arithmetic  20.4 us (8%)
  local copies, waits for them, and re-layouts  15.6 us (6%)
    ppermute x4, waiting for transfers between devices, across(): return lax.ppermute(value, BOTH, pairs)  51 us
    ppermute x2, waiting for transfers between devices, line_sum(): lax.ppermute(up, 'dp', neighbours([(0, 1), (1, 2), (2, 3)])).astype(F32)  27.5 us
    pallas_call x2, Pallas kernels, run_expert(): pl.pallas_call(functools.partial(expert_kernel, which), grid=(1,), out_sh...  26.1 us
    all_to_all x3, starting transfers between devices, to_plane(): lax.all_to_all(blocks, 'expert', split_axis=0, concat_axis=0, axis_index_...  21.9 us
    unnamed x43, local copies, waits for them, and re-layouts  14.1 us
    all_to_all x3, waiting for transfers between devices, to_plane(): lax.all_to_all(blocks, 'expert', split_axis=0, concat_axis=0, axis_index_...  13.8 us
    ppermute x2, starting transfers between devices, line_sum(): lax.ppermute(up, 'dp', neighbours([(0, 1), (1, 2), (2, 3)])).astype(F32)  11.4 us
    ppermute x4, starting transfers between devices, across(): return lax.ppermute(value, BOTH, pairs)  10.9 us
  transfers between devices with their start and end apart: 21, of which 7 were waited for; matrix products, arithmetic and copies ran while one was open for 8% of the time, Pallas kernels for 10%

profile of v4, /device:TPU:16, one launch (start us, length us, event | category | flops | bytes accessed | tf_op | source)
XLA Modules:
  0.0 267.4 jit_solution(15544086496832375497)
XLA Ops:
  0.7 1.4 copy.17.ids_ref
  2.1 1.4 copy.16.gates_ref
  3.5 2.1 route.1
  5.6 1.0 copy-done.6
  6.7 1.0 copy-done.8
  7.7 0.8 copy-done.10
  8.5 0.9 fill.2
  9.4 1.4 copy-done.3
  10.8 7.4 %all-to-all-start.1 = ((bf16[16,16,4224]{2,1,0:T(8,128)(2,1)}), bf16[16,16,4224]{2,1,0:T(8,128)(2,1)S(1)}, u32[]{:S(2)}, u32[]{:S(2)}) async-start(bf16[16,16,4224]{2,1,0:T(8,128)(2,1)} %bitcast.55), calls=%async_computation.1 | async-start | bytes 4325376 | tf_op jit(solution)/shard_map/all_to_all | solution.py:50
  18.2 5.9 %collective-permute-start.1 = (bf16[128,2048]{1,0:T(8,128)(2,1)S(1)}, bf16[128,2048]{1,0:T(8,128)(2,1)S(1)}, u32[]{:S(2)}, u32[]{:S(2)}) collective-permute-start(bf16[128,2048]{1,0:T(8,128)(2,1)S(1)} %copy-done.7), channel_id=1, source_target_pairs={{0,196},{1,197},{2,198},{3,199},{4,192},{5,193},{6,194},{7,195},{8... | collective-permute-start | bytes 1572872 | tf_op jit(solution)/shard_map/ppermute | solution.py:46
  24.1 0.1 collective-permute-start.2
  24.2 3.1 %collective-permute-start = (bf16[128,128]{1,0:T(8,128)(2,1)S(1)}, bf16[128,128]{1,0:T(8,128)(2,1)S(1)}, u32[]{:S(2)}, u32[]{:S(2)}) collective-permute-start(bf16[128,128]{1,0:T(8,128)(2,1)S(1)} %copy-done.18), channel_id=1, source_target_pairs={{0,196},{1,197},{2,198},{3,199},{4,192},{5,193},{6,194},{7,195},{8... | collective-permute-start | bytes 98312 | tf_op jit(solution)/shard_map/ppermute | solution.py:46
  27.4 32.1 %collective-permute-done.1.tokens_ref = bf16[128,2048]{1,0:T(8,128)(2,1)S(1)} collective-permute-done((bf16[128,2048]{1,0:T(8,128)(2,1)S(1)}, bf16[128,2048]{1,0:T(8,128)(2,1)S(1)}, u32[]{:S(2)}, u32[]{:S(2)}) %collective-permute-start.1) | collective-permute-done | bytes 524320 | tf_op jit(solution)/shard_map/ppermute | solution.py:46
  59.4 11.2 %collective-permute-done.sides_ref = bf16[128,128]{1,0:T(8,128)(2,1)S(1)} collective-permute-done((bf16[128,128]{1,0:T(8,128)(2,1)S(1)}, bf16[128,128]{1,0:T(8,128)(2,1)S(1)}, u32[]{:S(2)}, u32[]{:S(2)}) %collective-permute-start) | collective-permute-done | bytes 32800 | tf_op jit(solution)/shard_map/ppermute | solution.py:46
  70.6 0.9 fill.3
  71.5 1.4 copy-done.2
  72.9 7.2 %all-to-all-start = ((bf16[16,16,4224]{2,1,0:T(8,128)(2,1)}), bf16[16,16,4224]{2,1,0:T(8,128)(2,1)}, u32[]{:S(2)}, u32[]{:S(2)}) async-start(bf16[16,16,4224]{2,1,0:T(8,128)(2,1)} %bitcast.54), calls=%async_computation | async-start | bytes 4325376 | tf_op jit(solution)/shard_map/all_to_all | solution.py:50
  80.1 12.3 %expert.2 = (bf16[16,32,4224]{2,1,0:T(8,128)(2,1)}, bf16[256,768]{1,0:T(8,128)(2,1)S(1)}, bf16[256,2048]{1,0:T(8,128)(2,1)S(1)}, bf16[256,1536]{1,0:T(8,128)(2,1)S(1)}) custom-call(s32[1]{0:T(128)} %bitcast.1.place_ref, bf16[256,4224]{1,0:T(8,128)(2,1)S(1)} %bitcast.51, bf16[2048,768]{1,0:T(8,128)(2,1)} %bitcast.56, bf16[2048,768]{1,0:T(8,128)(2,1)} %bitcast.58, ...), custom_call_target="tpu_custom_call" | custom-call | flops 4831838208 | bytes 9437184 | tf_op jit(solution)/shard_map/expert/pallas_call | solution.py:225
  92.4 1.0 copy-done.11
  93.4 0.7 copy-done.13
  94.1 13.8 %all-to-all-done = bf16[16,16,4224]{2,1,0:T(8,128)(2,1)} async-done(((bf16[16,16,4224]{2,1,0:T(8,128)(2,1)}), bf16[16,16,4224]{2,1,0:T(8,128)(2,1)}, u32[]{:S(2)}, u32[]{:S(2)}) %all-to-all-start) | async-done | bytes 2162720 | tf_op jit(solution)/shard_map/all_to_all | solution.py:50
  107.9 13.8 %expert.3 = (bf16[16,32,4224]{2,1,0:T(8,128)(2,1)}, bf16[256,768]{1,0:T(8,128)(2,1)S(1)}, bf16[256,2048]{1,0:T(8,128)(2,1)S(1)}, bf16[256,1536]{1,0:T(8,128)(2,1)S(1)}) custom-call(s32[1]{0:T(128)} %bitcast.1.place_ref, bf16[256,4224]{1,0:T(8,128)(2,1)} %bitcast.3.rows_ref.far_x, bf16[2048,768]{1,0:T(8,128)(2,1)} %bitcast.57, ...), custom_call_target="tpu_custom_call", output_to_operand_aliasing={{0}: (5, {})} | custom-call | flops 4831838208 | bytes 9437184 | tf_op jit(solution)/shard_map/expert/pallas_call | solution.py:225
  121.7 5.3 %wide.2 = bf16[4,256,1536]{2,1,0:T(8,128)(2,1)} custom-call(s32[1]{0:T(128)S(6)} %sub.23.select_ref, bf16[256,4224]{1,0:T(8,128)(2,1)S(1)} %bitcast.52, bf16[256,4224]{1,0:T(8,128)(2,1)} %bitcast.3.rows_ref.far_x, bf16[256,1536]{1,0:T(8,128)(2,1)S(1)} %get-tuple-element.35.near_grads, bf16[256,1536]{1,0:T(8,128)(2,1)S(1)} %get-tuple-element.36.far_grads), custom_call_target="tpu_custom_call" | custom-call | flops 1610612736 | bytes 6291456 | tf_op jit(solution)/shard_map/wide/pallas_call | solution.py:273
  127.1 3.8 %down.1 = (bf16[4,96,2048]{2,1,0:T(8,128)(2,1)}, bf16[4,96,2048]{2,1,0:T(8,128)(2,1)S(1)}) custom-call(s32[1]{0:T(128)} %bitcast.9.select_ref.core_ref, bf16[256,768]{1,0:T(8,128)(2,1)S(1)} %copy-done.14, bf16[256,768]{1,0:T(8,128)(2,1)S(1)} %get-tuple-element.43.far_hidden, bf16[256,2048]{1,0:T(8,128)(2,1)S(1)} %copy-done.12, ...), custom_call_target="tpu_custom_call" | custom-call | flops 1610612736 | bytes 6291456 | tf_op jit(solution)/shard_map/down/pallas_call | solution.py:312
  130.9 1.2 copy-done.4
  132.1 0.5 collective-permute-start.11
  132.6 7.3 %all-to-all-start.2 = ((bf16[16,32,4224]{2,1,0:T(8,128)(2,1)}), bf16[16,32,4224]{2,1,0:T(8,128)(2,1)}, u32[]{:S(2)}, u32[]{:S(2)}) async-start(bf16[16,32,4224]{2,1,0:T(8,128)(2,1)} %get-tuple-element.34), calls=%async_computation.2 | async-start | bytes 8650752 | tf_op jit(solution)/shard_map/all_to_all | solution.py:50
  139.9 2.5 add_convert_fusion
  142.4 1.2 copy-done.16
  143.6 0.8 fusion.13
  144.4 2.1 collective-permute-start.12
  146.5 5.6 %wide.3 = bf16[4,256,1536]{2,1,0:T(8,128)(2,1)} custom-call(s32[1]{0:T(128)} %bitcast.9.select_ref.core_ref, bf16[256,4224]{1,0:T(8,128)(2,1)S(1)} %bitcast.53, bf16[256,4224]{1,0:T(8,128)(2,1)} %bitcast.3.rows_ref.far_x, bf16[256,1536]{1,0:T(8,128)(2,1)S(1)} %get-tuple-element.35.near_grads, bf16[256,1536]{1,0:T(8,128)(2,1)S(1)} %copy-done.1, ...), custom_call_target="tpu_custom_call" | custom-call | flops 1610612736 | bytes 6291456 | tf_op jit(solution)/shard_map/wide/pallas_call | solution.py:273
  152.1 2.5 fusion.8
  154.6 2.2 collective-permute-start.4
  156.8 2.3 fusion.6
  159.1 2.9 %collective-permute-start.13 = (bf16[96,2048]{1,0:T(8,128)(2,1)}, bf16[96,2048]{1,0:T(8,128)(2,1)}, u32[]{:S(2)}, u32[]{:S(2)}) collective-permute-start(bf16[96,2048]{1,0:T(8,128)(2,1)} %get-tuple-element.58), channel_id=1, source_target_pairs={{0,64},{32,96},{64,128},{96,160},{1,65},{33,97},{65,129},{97,161},... | collective-permute-start | bytes 1179656 | tf_op jit(solution)/shard_map/ppermute | solution.py:436
  162.0 1.4 collective-permute-start.15
  163.4 10.7 %collective-permute-done.4 = bf16[256,1536]{1,0:T(8,128)(2,1)} collective-permute-done((bf16[256,1536]{1,0:T(8,128)(2,1)}, bf16[256,1536]{1,0:T(8,128)(2,1)}, u32[]{:S(2)}, u32[]{:S(2)}) %collective-permute-start.4) | collective-permute-done | bytes 786464 | tf_op jit(solution)/shard_map/ppermute | solution.py:433
  174.1 2.6 fusion.1
  176.7 5.3 %collective-permute-start.5 = (bf16[256,1536]{1,0:T(8,128)(2,1)}, bf16[256,1536]{1,0:T(8,128)(2,1)}, u32[]{:S(2)}, u32[]{:S(2)}) collective-permute-start(bf16[256,1536]{1,0:T(8,128)(2,1)} %get-tuple-element.55), channel_id=1, source_target_pairs={{0,64},{32,96},{64,128},{96,160},{1,65},{33,97},{65,129},{97,161},... | collective-permute-start | bytes 2359304 | tf_op jit(solution)/shard_map/ppermute | solution.py:436
  182.0 1.6 collective-permute-start.8
  183.6 2.5 fusion.10
  186.1 4.1 %collective-permute-start.14 = (bf16[96,2048]{1,0:T(8,128)(2,1)}, bf16[96,2048]{1,0:T(8,128)(2,1)}, u32[]{:S(2)}, u32[]{:S(2)}) collective-permute-start(bf16[96,2048]{1,0:T(8,128)(2,1)} %get-tuple-element.60), channel_id=1, source_target_pairs={{0,64},{32,96},{64,128},{96,160},{128,192},{160,224},{1,65},{33,97... | collective-permute-start | bytes 1179656 | tf_op jit(solution)/shard_map/ppermute | solution.py:441
  190.2 1.3 collective-permute-start.16
  191.5 7.9 %collective-permute-done.5 = bf16[256,1536]{1,0:T(8,128)(2,1)} collective-permute-done((bf16[256,1536]{1,0:T(8,128)(2,1)}, bf16[256,1536]{1,0:T(8,128)(2,1)}, u32[]{:S(2)}, u32[]{:S(2)}) %collective-permute-start.5) | collective-permute-done | bytes 786464 | tf_op jit(solution)/shard_map/ppermute | solution.py:436
  199.4 2.9 %fusion.3 = (bf16[256,1536]{1,0:T(8,128)(2,1)}, bf16[256,1536]{1,0:T(8,128)(2,1)}) fusion(bf16[256,1536]{1,0:T(8,128)(2,1)} %collective-permute-done.5, bf16[4,256,1536]{2,1,0:T(8,128)(2,1)S(1)} %copy-done.15, s32[]{:T(128)S(6)} %min.23, bf16[256,1536]{1,0:T(8,128)(2,1)} %collective-permute-done.8, s32[]{:T(128)S(6)} %min.24), kind=kLoop, calls=%fused_computation.8 | loop fusion | flops 3145728 | bytes 4718600 | tf_op jit(solution)/shard_map/convert_element_type | solution.py:439
  202.3 7.3 %collective-permute-start.7 = (bf16[256,1536]{1,0:T(8,128)(2,1)}, bf16[256,1536]{1,0:T(8,128)(2,1)S(1)}, u32[]{:S(2)}, u32[]{:S(2)}) collective-permute-start(bf16[256,1536]{1,0:T(8,128)(2,1)} %get-tuple-element.56), channel_id=1, source_target_pairs={{0,64},{32,96},{64,128},{96,160},{128,192},{160,224},{1,65},{33,97... | collective-permute-start | bytes 2359304 | tf_op jit(solution)/shard_map/ppermute | solution.py:441
  209.6 1.3 collective-permute-start.9
  211.0 1.4 fusion.12
  212.4 3.1 %collective-permute-start.17 = (bf16[96,2048]{1,0:T(8,128)(2,1)S(1)}, bf16[96,2048]{1,0:T(8,128)(2,1)}, u32[]{:S(2)}, u32[]{:S(2)}) collective-permute-start(bf16[96,2048]{1,0:T(8,128)(2,1)S(1)} %fusion.12), channel_id=1, source_target_pairs={{0,16},{1,17},{2,18},{3,19},{4,20},{5,21},{6,22},{7,23},{8,24},{9,... | collective-permute-start | bytes 1179656 | tf_op jit(solution)/shard_map/ppermute | solution.py:490
  215.5 2.1 collect.1
  217.6 0.0 copy-start.19
  217.6 1.8 collective-permute-start.6
  219.4 27.5 %collective-permute-done.7 = bf16[256,1536]{1,0:T(8,128)(2,1)S(1)} collective-permute-done((bf16[256,1536]{1,0:T(8,128)(2,1)}, bf16[256,1536]{1,0:T(8,128)(2,1)S(1)}, u32[]{:S(2)}, u32[]{:S(2)}) %collective-permute-start.7) | collective-permute-done | bytes 786464 | tf_op jit(solution)/shard_map/ppermute | solution.py:441
  246.9 0.9 copy-done.17
  247.8 1.9 fusion.5
  249.7 3.1 %collective-permute-start.10 = (bf16[256,1536]{1,0:T(8,128)(2,1)S(1)}, bf16[256,1536]{1,0:T(8,128)(2,1)}, u32[]{:S(2)}, u32[]{:S(2)}) collective-permute-start(bf16[256,1536]{1,0:T(8,128)(2,1)S(1)} %fusion.5), channel_id=1, source_target_pairs={{0,16},{1,17},{2,18},{3,19},{4,20},{5,21},{6,22},{7,23},{8,24},{9,... | collective-permute-start | bytes 2359304 | tf_op jit(solution)/shard_map/ppermute | solution.py:489
  252.8 0.6 dynamic_slice.36
  254.1 0.8 select_bitcast_fusion
  254.9 7.8 %collective-permute-done.6.far_ref = bf16[128,4224]{1,0:T(8,128)(2,1)S(1)} collective-permute-done((bf16[128,4224]{1,0:T(8,128)(2,1)S(1)}, bf16[128,4224]{1,0:T(8,128)(2,1)S(1)}, u32[]{:S(2)}, u32[]{:S(2)}) %collective-permute-start.6) | collective-permute-done | bytes 1081376 | tf_op jit(solution)/shard_map/ppermute | solution.py:46
  262.7 3.0 %finish.1 = (bf16[128,2048]{1,0:T(8,128)(2,1)}, bf16[128,2048]{1,0:T(8,128)(2,1)}, f32[128,8]{1,0:T(8,128)S(1)}) custom-call(s32[1]{0:T(128)} %bitcast.half_ref, s32[128,8]{1,0:T(8,128)S(1)} %copy-done.5, bf16[256,128]{1,0:T(8,128)(2,1)S(1)} %get-tuple-element.28.picked_ref, bf16[16,32,4224]{2,1,0:T(8,128)(2,1)} %all-to-all-done.2.returned_ref, ...), custom_call_target="tpu_custom_call" | custom-call | flops 276824064 | bytes 2162688 | tf_op jit(solution)/shard_map/finish/pallas_call | solution.py:400
  265.7 0.7 copy.18
  266.4 0.1 broadcast_select_fusion
  266.5 0.9 slice_bitcast_fusion
  (44 shorter events, 0.1 us)
Async XLA Ops:
  5.6 1.0 copy-start.6
  6.7 1.0 copy-start.8
  7.7 0.8 copy-start.10
  9.4 1.4 copy-start.3
  10.8 7.4 %copy-start.7 = (bf16[128,2048]{1,0:T(8,128)(2,1)S(1)}, bf16[128,2048]{1,0:T(8,128)(2,1)}, u32[]{:S(2)}) copy-start(bf16[128,2048]{1,0:T(8,128)(2,1)} %tokens_ref.1) | copy-start | bytes 1572868
  10.8 13.4 %copy-start.9 = (bf16[128,2048]{1,0:T(8,128)(2,1)S(1)}, bf16[128,2048]{1,0:T(8,128)(2,1)}, u32[]{:S(2)}) copy-start(bf16[128,2048]{1,0:T(8,128)(2,1)} %grads_ref.1) | copy-start | bytes 1572868
  10.8 13.5 %copy-start.18 = (bf16[128,128]{1,0:T(8,128)(2,1)S(1)}, bf16[128,128]{1,0:T(8,128)(2,1)}, u32[]{:S(2)}) copy-start(bf16[128,128]{1,0:T(8,128)(2,1)} %get-tuple-element.29) | copy-start | bytes 98308
  10.8 62.1 %all-to-all-start.1 = ((bf16[16,16,4224]{2,1,0:T(8,128)(2,1)}), bf16[16,16,4224]{2,1,0:T(8,128)(2,1)S(1)}, u32[]{:S(2)}, u32[]{:S(2)}) async-start(bf16[16,16,4224]{2,1,0:T(8,128)(2,1)} %bitcast.55), calls=%async_computation.1 | async-start | bytes 4325376 | tf_op jit(solution)/shard_map/all_to_all | solution.py:50
  18.2 41.2 %collective-permute-start.1 = (bf16[128,2048]{1,0:T(8,128)(2,1)S(1)}, bf16[128,2048]{1,0:T(8,128)(2,1)S(1)}, u32[]{:S(2)}, u32[]{:S(2)}) collective-permute-start(bf16[128,2048]{1,0:T(8,128)(2,1)S(1)} %copy-done.7), channel_id=1, source_target_pairs={{0,196},{1,197},{2,198},{3,199},{4,192},{5,193},{6,194},{7,195},{8... | collective-permute-start | bytes 1572872 | tf_op jit(solution)/shard_map/ppermute | solution.py:46
  24.1 46.5 %collective-permute-start.2 = (bf16[128,2048]{1,0:T(8,128)(2,1)S(1)}, bf16[128,2048]{1,0:T(8,128)(2,1)S(1)}, u32[]{:S(2)}, u32[]{:S(2)}) collective-permute-start(bf16[128,2048]{1,0:T(8,128)(2,1)S(1)} %copy-done.9), channel_id=1, source_target_pairs={{0,196},{1,197},{2,198},{3,199},{4,192},{5,193},{6,194},{7,195},{8... | collective-permute-start | bytes 1572872 | tf_op jit(solution)/shard_map/ppermute | solution.py:46
  24.2 46.4 %collective-permute-start = (bf16[128,128]{1,0:T(8,128)(2,1)S(1)}, bf16[128,128]{1,0:T(8,128)(2,1)S(1)}, u32[]{:S(2)}, u32[]{:S(2)}) collective-permute-start(bf16[128,128]{1,0:T(8,128)(2,1)S(1)} %copy-done.18), channel_id=1, source_target_pairs={{0,196},{1,197},{2,198},{3,199},{4,192},{5,193},{6,194},{7,195},{8... | collective-permute-start | bytes 98312 | tf_op jit(solution)/shard_map/ppermute | solution.py:46
  71.5 1.4 copy-start.2
  72.9 35.0 %all-to-all-start = ((bf16[16,16,4224]{2,1,0:T(8,128)(2,1)}), bf16[16,16,4224]{2,1,0:T(8,128)(2,1)}, u32[]{:S(2)}, u32[]{:S(2)}) async-start(bf16[16,16,4224]{2,1,0:T(8,128)(2,1)} %bitcast.54), calls=%async_computation | async-start | bytes 4325376 | tf_op jit(solution)/shard_map/all_to_all | solution.py:50
  92.4 1.0 copy-start.11
  93.4 0.7 copy-start.13
  121.7 5.3 %copy-start = (bf16[256,1536]{1,0:T(8,128)(2,1)}, bf16[256,1536]{1,0:T(8,128)(2,1)S(1)}, u32[]{:S(2)}) copy-start(bf16[256,1536]{1,0:T(8,128)(2,1)S(1)} %get-tuple-element.36.far_grads) | copy-start | bytes 2359300
  121.7 5.3 %copy-start.12 = (bf16[256,2048]{1,0:T(8,128)(2,1)S(1)}, bf16[256,2048]{1,0:T(8,128)(2,1)}, u32[]{:S(2)}) copy-start(bf16[256,2048]{1,0:T(8,128)(2,1)} %copy-done.11) | copy-start | bytes 3145732
  121.7 5.3 %copy-start.14 = (bf16[256,768]{1,0:T(8,128)(2,1)S(1)}, bf16[256,768]{1,0:T(8,128)(2,1)}, u32[]{:S(2)}) copy-start(bf16[256,768]{1,0:T(8,128)(2,1)} %copy-done.13) | copy-start | bytes 1179652
  127.0 19.4 %collective-permute-start.3 = (bf16[4,256,1536]{2,1,0:T(8,128)(2,1)}, bf16[4,256,1536]{2,1,0:T(8,128)(2,1)}, u32[]{:S(2)}, u32[]{:S(2)}) collective-permute-start(bf16[4,256,1536]{2,1,0:T(8,128)(2,1)} %wide.2), channel_id=1, source_target_pairs={{0,32},{32,0},{64,96},{96,64},{128,160},{160,128},{192,224},{224,1... | collective-permute-start | bytes 9437192 | tf_op jit(solution)/shard_map/ppermute | solution.py:423
  130.9 1.2 copy-start.4
  132.1 7.8 %collective-permute-start.11 = (bf16[4,96,2048]{2,1,0:T(8,128)(2,1)}, bf16[4,96,2048]{2,1,0:T(8,128)(2,1)}, u32[]{:S(2)}, u32[]{:S(2)}) collective-permute-start(bf16[4,96,2048]{2,1,0:T(8,128)(2,1)} %get-tuple-element.47), channel_id=1, source_target_pairs={{0,32},{32,0},{64,96},{96,64},{128,160},{160,128},{192,224},{224,1... | collective-permute-start | bytes 4718600 | tf_op jit(solution)/shard_map/ppermute | solution.py:423
  132.6 82.9 %all-to-all-start.2 = ((bf16[16,32,4224]{2,1,0:T(8,128)(2,1)}), bf16[16,32,4224]{2,1,0:T(8,128)(2,1)}, u32[]{:S(2)}, u32[]{:S(2)}) async-start(bf16[16,32,4224]{2,1,0:T(8,128)(2,1)} %get-tuple-element.34), calls=%async_computation.2 | async-start | bytes 8650752 | tf_op jit(solution)/shard_map/all_to_all | solution.py:50
  142.4 1.2 copy-start.16
  143.6 2.9 %copy-start.1 = (bf16[256,1536]{1,0:T(8,128)(2,1)S(1)}, bf16[256,1536]{1,0:T(8,128)(2,1)}, u32[]{:S(2)}) copy-start(bf16[256,1536]{1,0:T(8,128)(2,1)} %copy-done) | copy-start | bytes 2359300
  144.4 12.4 %collective-permute-start.12 = (bf16[96,2048]{1,0:T(8,128)(2,1)}, bf16[96,2048]{1,0:T(8,128)(2,1)}, u32[]{:S(2)}, u32[]{:S(2)}) collective-permute-start(bf16[96,2048]{1,0:T(8,128)(2,1)} %fusion.13), channel_id=1, source_target_pairs={{0,64},{32,96},{192,128},{224,160},{1,65},{33,97},{193,129},{225,1... | collective-permute-start | bytes 1179656 | tf_op jit(solution)/shard_map/ppermute | solution.py:433
  152.1 22.1 %copy-start.15 = (bf16[4,256,1536]{2,1,0:T(8,128)(2,1)S(1)}, bf16[4,256,1536]{2,1,0:T(8,128)(2,1)}, u32[]{:S(2)}) copy-start(bf16[4,256,1536]{2,1,0:T(8,128)(2,1)} %wide.3) | copy-start | bytes 9437188
  154.6 19.5 %collective-permute-start.4 = (bf16[256,1536]{1,0:T(8,128)(2,1)}, bf16[256,1536]{1,0:T(8,128)(2,1)}, u32[]{:S(2)}, u32[]{:S(2)}) collective-permute-start(bf16[256,1536]{1,0:T(8,128)(2,1)} %fusion.8), channel_id=1, source_target_pairs={{0,64},{32,96},{192,128},{224,160},{1,65},{33,97},{193,129},{225,1... | collective-permute-start | bytes 2359304 | tf_op jit(solution)/shard_map/ppermute | solution.py:433
  159.1 24.5 %collective-permute-start.13 = (bf16[96,2048]{1,0:T(8,128)(2,1)}, bf16[96,2048]{1,0:T(8,128)(2,1)}, u32[]{:S(2)}, u32[]{:S(2)}) collective-permute-start(bf16[96,2048]{1,0:T(8,128)(2,1)} %get-tuple-element.58), channel_id=1, source_target_pairs={{0,64},{32,96},{64,128},{96,160},{1,65},{33,97},{65,129},{97,161},... | collective-permute-start | bytes 1179656 | tf_op jit(solution)/shard_map/ppermute | solution.py:436
  162.0 21.6 %collective-permute-start.15 = (bf16[96,2048]{1,0:T(8,128)(2,1)}, bf16[96,2048]{1,0:T(8,128)(2,1)}, u32[]{:S(2)}, u32[]{:S(2)}) collective-permute-start(bf16[96,2048]{1,0:T(8,128)(2,1)} %get-tuple-element.59), channel_id=1, source_target_pairs={{192,128},{224,160},{128,64},{160,96},{193,129},{225,161},{129,65}... | collective-permute-start | bytes 1179656 | tf_op jit(solution)/shard_map/ppermute | solution.py:437
  176.7 22.7 %collective-permute-start.5 = (bf16[256,1536]{1,0:T(8,128)(2,1)}, bf16[256,1536]{1,0:T(8,128)(2,1)}, u32[]{:S(2)}, u32[]{:S(2)}) collective-permute-start(bf16[256,1536]{1,0:T(8,128)(2,1)} %get-tuple-element.55), channel_id=1, source_target_pairs={{0,64},{32,96},{64,128},{96,160},{1,65},{33,97},{65,129},{97,161},... | collective-permute-start | bytes 2359304 | tf_op jit(solution)/shard_map/ppermute | solution.py:436
  182.0 17.4 %collective-permute-start.8 = (bf16[256,1536]{1,0:T(8,128)(2,1)}, bf16[256,1536]{1,0:T(8,128)(2,1)}, u32[]{:S(2)}, u32[]{:S(2)}) collective-permute-start(bf16[256,1536]{1,0:T(8,128)(2,1)} %get-tuple-element.54), channel_id=1, source_target_pairs={{192,128},{224,160},{128,64},{160,96},{193,129},{225,161},{129,65}... | collective-permute-start | bytes 2359304 | tf_op jit(solution)/shard_map/ppermute | solution.py:437
  186.1 24.9 %collective-permute-start.14 = (bf16[96,2048]{1,0:T(8,128)(2,1)}, bf16[96,2048]{1,0:T(8,128)(2,1)}, u32[]{:S(2)}, u32[]{:S(2)}) collective-permute-start(bf16[96,2048]{1,0:T(8,128)(2,1)} %get-tuple-element.60), channel_id=1, source_target_pairs={{0,64},{32,96},{64,128},{96,160},{128,192},{160,224},{1,65},{33,97... | collective-permute-start | bytes 1179656 | tf_op jit(solution)/shard_map/ppermute | solution.py:441
  190.2 20.8 %collective-permute-start.16 = (bf16[96,2048]{1,0:T(8,128)(2,1)}, bf16[96,2048]{1,0:T(8,128)(2,1)}, u32[]{:S(2)}, u32[]{:S(2)}) collective-permute-start(bf16[96,2048]{1,0:T(8,128)(2,1)} %get-tuple-element.61), channel_id=1, source_target_pairs={{192,128},{224,160},{128,64},{160,96},{64,0},{96,32},{193,129},{22... | collective-permute-start | bytes 1179656 | tf_op jit(solution)/shard_map/ppermute | solution.py:442
  202.3 44.6 %collective-permute-start.7 = (bf16[256,1536]{1,0:T(8,128)(2,1)}, bf16[256,1536]{1,0:T(8,128)(2,1)S(1)}, u32[]{:S(2)}, u32[]{:S(2)}) collective-permute-start(bf16[256,1536]{1,0:T(8,128)(2,1)} %get-tuple-element.56), channel_id=1, source_target_pairs={{0,64},{32,96},{64,128},{96,160},{128,192},{160,224},{1,65},{33,97... | collective-permute-start | bytes 2359304 | tf_op jit(solution)/shard_map/ppermute | solution.py:441
  209.6 38.2 %collective-permute-start.9 = (bf16[256,1536]{1,0:T(8,128)(2,1)}, bf16[256,1536]{1,0:T(8,128)(2,1)}, u32[]{:S(2)}, u32[]{:S(2)}) collective-permute-start(bf16[256,1536]{1,0:T(8,128)(2,1)} %get-tuple-element.57), channel_id=1, source_target_pairs={{192,128},{224,160},{128,64},{160,96},{64,0},{96,32},{193,129},{22... | collective-permute-start | bytes 2359304 | tf_op jit(solution)/shard_map/ppermute | solution.py:442
  212.4 41.7 %collective-permute-start.17 = (bf16[96,2048]{1,0:T(8,128)(2,1)S(1)}, bf16[96,2048]{1,0:T(8,128)(2,1)}, u32[]{:S(2)}, u32[]{:S(2)}) collective-permute-start(bf16[96,2048]{1,0:T(8,128)(2,1)S(1)} %fusion.12), channel_id=1, source_target_pairs={{0,16},{1,17},{2,18},{3,19},{4,20},{5,21},{6,22},{7,23},{8,24},{9,... | collective-permute-start | bytes 1179656 | tf_op jit(solution)/shard_map/ppermute | solution.py:490
  217.6 35.2 %copy-start.19 = (s32[32]{0:T(128)S(1)}, s32[32]{0:T(128)}, u32[]{:S(2)}) copy-start(s32[32]{0:T(128)} %param.12) | copy-start | bytes 388
  217.6 45.1 %copy-start.5 = (s32[128,8]{1,0:T(8,128)S(1)}, s32[128,8]{1,0:T(8,128)}, u32[]{:S(2)}) copy-start(s32[128,8]{1,0:T(8,128)} %copy.17.ids_ref) | copy-start | bytes 12292
  217.6 45.1 %collective-permute-start.6 = (bf16[128,4224]{1,0:T(8,128)(2,1)S(1)}, bf16[128,4224]{1,0:T(8,128)(2,1)S(1)}, u32[]{:S(2)}, u32[]{:S(2)}) collective-permute-start(bf16[128,4224]{1,0:T(8,128)(2,1)S(1)} %collect.1), channel_id=1, source_target_pairs={{0,196},{1,197},{2,198},{3,199},{4,192},{5,193},{6,194},{7,195},{8... | collective-permute-start | bytes 3244040 | tf_op jit(solution)/shard_map/ppermute | solution.py:46
  246.9 0.9 copy-start.17
  249.7 16.6 %collective-permute-start.10 = (bf16[256,1536]{1,0:T(8,128)(2,1)S(1)}, bf16[256,1536]{1,0:T(8,128)(2,1)}, u32[]{:S(2)}, u32[]{:S(2)}) collective-permute-start(bf16[256,1536]{1,0:T(8,128)(2,1)S(1)} %fusion.5), channel_id=1, source_target_pairs={{0,16},{1,17},{2,18},{3,19},{4,20},{5,21},{6,22},{7,23},{8,24},{9,... | collective-permute-start | bytes 2359304 | tf_op jit(solution)/shard_map/ppermute | solution.py:489

commit v5 on v4

--- a/solution.py
+++ b/solution.py
@@ -8,7 +8,7 @@
 from jax.sharding import PartitionSpec as P
 
 MOST = 16
-HI_SIZE, Y_SIZE = 2, 4
+X_SIZE, HI_SIZE, Y_SIZE = 4, 2, 4
 LO_SIZE, CORES = 4, 2
 PLANE = 16
 SIDE = 128
@@ -16,7 +16,7 @@
 
 BOTH = ("dp", "expert")
 PLANE_GROUPS = [
-    [x * HI_SIZE * Y_SIZE + hi * Y_SIZE + y for x in range(PLANE // Y_SIZE) for y in range(Y_SIZE)]
+    [x * HI_SIZE * Y_SIZE + hi * Y_SIZE + y for y in range(Y_SIZE) for x in range(X_SIZE)]
     for hi in range(HI_SIZE)
 ]
 CONTRACT_LAST = (((1,), (1,)), ((), ()))
@@ -54,7 +54,7 @@
 
 def lane_names(shape, half):
     place = lax.broadcasted_iota(jnp.int32, shape, 1) & (PLANE - 1)
-    return (place >> 2) * (HI_SIZE * Y_SIZE) + half * Y_SIZE + (place & (Y_SIZE - 1))
+    return (place & (X_SIZE - 1)) * (HI_SIZE * Y_SIZE) + half * Y_SIZE + (place >> 2)
 
 
 def split_parts(values, shape):
@@ -138,34 +138,48 @@
 
 
 def expert_kernel(
-    which, place_ref, rows_ref, gate_hbm, up_hbm, down_hbm, *refs
+    place_ref,
+    rows_ref,
+    gate_hbm,
+    up_hbm,
+    down_hbm,
+    back_ref,
+    hidden_ref,
+    pick_ref,
+    grads_ref,
+    gate_w,
+    up_w,
+    down_w,
+    sems,
 ):
-    if which:
-        refs = refs[1:]
-    back_ref, hidden_ref, pick_ref, grads_ref, gate_w, up_w, down_w, sems = refs
-    copies = [
-        pltpu.make_async_copy(source, target, sems.at[i])
-        for i, (source, target) in enumerate(
-            ((gate_hbm, gate_w), (up_hbm, up_w), (down_hbm, down_w))
+    width, hidden_width = gate_w.shape
+    step = min(256, hidden_width)
+    chunks = []
+    for j in range(hidden_width // step):
+        span = pl.ds(j * step, step)
+        pairs = (
+            (gate_hbm.at[:, span], gate_w.at[:, span]),
+            (up_hbm.at[:, span], up_w.at[:, span]),
+            (down_hbm.at[span, :], down_w.at[span, :]),
         )
-    ]
-    for copy in copies:
-        copy.start()
+        chunks.append(
+            [pltpu.make_async_copy(*pair, sems.at[j, i]) for i, pair in enumerate(pairs)]
+        )
+    for chunk in chunks:
+        for copy in chunk:
+            copy.start()
     place = place_ref[0]
     slots = rows_ref.shape[0]
-    width, hidden_width = gate_w.shape
     lane = lax.broadcasted_iota(jnp.int32, (slots, SIDE), 1)
     mine = jnp.where((lane & (PLANE - 1)) == place, 1.0, 0.0)
     side = rows_ref[:, width : width + SIDE].astype(F32)
     slot_gate = jnp.sum(side * mine, axis=1, keepdims=True)
     pick_ref[...] = (slot_gate * rows_ref[:, width + SIDE :].astype(F32)).astype(BF16)
-    for copy in copies:
-        copy.wait()
-
-    step = min(256, hidden_width)
-
-    def forward(j, carry):
-        span = pl.ds(pl.multiple_of(j * step, step), step)
+
+    for j, chunk in enumerate(chunks):
+        for copy in chunk:
+            copy.wait()
+        span = slice(j * step, (j + 1) * step)
         gate_pre = jnp.dot(rows_ref[:, :width], gate_w[:, span], preferred_element_type=F32)
         up_pre = jnp.dot(rows_ref[:, :width], up_w[:, span], preferred_element_type=F32)
         hidden_grad = lax.dot_general(
@@ -176,11 +190,8 @@
         hidden_ref[:, span] = (silu * up_pre).astype(BF16)
         gate_grad = hidden_grad * up_pre * sigmoid * (1.0 + gate_pre * (1.0 - sigmoid))
         grads_ref[:, span] = gate_grad.astype(BF16)
-        second = pl.ds(pl.multiple_of(hidden_width + j * step, step), step)
+        second = slice(hidden_width + j * step, hidden_width + (j + 1) * step)
         grads_ref[:, second] = (hidden_grad * silu).astype(BF16)
-        return carry
-
-    lax.fori_loop(0, hidden_width // step, forward, 0)
 
     wide = min(256, width)
     lead = back_ref.shape[:2]
@@ -211,89 +222,109 @@
     back_ref[:, :, width : width + SIDE] = table.reshape(*lead, SIDE)
 
 
-def run_expert(which, place, rows, weights, back):
+def run_expert(place, rows, weights):
     slots = rows.shape[0]
     width, hidden_width = weights[0].shape
     full = 2 * width + SIDE
-    out_shape = (
-        jax.ShapeDtypeStruct((PLANE, 2 * MOST, full), BF16),
-        jax.ShapeDtypeStruct((slots, hidden_width), BF16),
-        jax.ShapeDtypeStruct((slots, width), BF16),
-        jax.ShapeDtypeStruct((slots, 2 * hidden_width), BF16),
-    )
-    operands = [place, rows, *weights] + ([back] if which else [])
-    return pl.pallas_call(
-        functools.partial(expert_kernel, which),
-        grid=(1,),
-        out_shape=out_shape,
-        in_specs=[SCALAR, pl.BlockSpec((slots, full), lambda i: (0, 0))]
-        + [ANYWHERE] * (len(operands) - 2),
-        out_specs=(
-            pl.BlockSpec((PLANE, MOST, full), lambda i: (0, which, 0)),
-            pl.BlockSpec((slots, hidden_width), lambda i: (0, 0)),
-            pl.BlockSpec((slots, width), lambda i: (0, 0)),
-            pl.BlockSpec((slots, 2 * hidden_width), lambda i: (0, 0)),
+    pieces = hidden_width // min(256, hidden_width)
+    return pl.pallas_call(
+        expert_kernel,
+        out_shape=(
+            jax.ShapeDtypeStruct((PLANE, MOST, full), BF16),
+            jax.ShapeDtypeStruct((slots, hidden_width), BF16),
+            jax.ShapeDtypeStruct((slots, width), BF16),
+            jax.ShapeDtypeStruct((slots, 2 * hidden_width), BF16),
         ),
+        in_specs=[SCALAR, WHOLE] + [ANYWHERE] * 3,
+        out_specs=(WHOLE,) * 4,
         scratch_shapes=[
             pltpu.VMEM((width, hidden_width), BF16),
             pltpu.VMEM((width, hidden_width), BF16),
             pltpu.VMEM((hidden_width, width), BF16),
-            pltpu.SemaphoreType.DMA((3,)),
+            pltpu.SemaphoreType.DMA((pieces, 3)),
         ],
-        input_output_aliases={5: 0} if which else {},
         compiler_params=limits(),
         cost_estimate=cost(12 * slots * width * hidden_width, 6 * width * hidden_width),
         name="expert",
-    )(*operands)
-
-
-def wide_kernel(has_sum, select_ref, near_x, far_x, near_grads, far_grads, *refs):
-    out_ref = refs[-1]
-    columns = out_ref.shape[2]
-    step = min(512, columns)
-    for n in range(0, columns, step):
-        total = lax.dot_general(
-            near_x[...], near_grads[:, n : n + step], CONTRACT_FIRST, preferred_element_type=F32
-        )
-        total += lax.dot_general(
-            far_x[...], far_grads[:, n : n + step], CONTRACT_FIRST, preferred_element_type=F32
-        )
-        if has_sum:
-            total += refs[0][0, :, n : n + step].astype(F32)
-        out_ref[0, :, n : n + step] = total.astype(BF16)
-
-
-def wide_grads(select, rows, grads, width, taken=None):
+    )(place, rows, *weights)
+
+
+def wide_kernel(keep, shard, where_ref, near_x, far_x, near_grads, far_grads, *refs):
+    turned, columns = refs[-2:]
+    slots = near_x.shape[0]
+
+    @pl.when(pl.program_id(0) == 0)
+    def _():
+        for z in range(LO_SIZE):
+            span = pl.ds(pl.multiple_of((z * CORES + where_ref[0]) * shard, shard), shard)
+            here = slice(z * shard, (z + 1) * shard)
+            turned[here, :slots] = jnp.transpose(near_x[:, span])
+            turned[here, slots:] = jnp.transpose(far_x[:, span])
+
+    columns[:slots] = near_grads[...]
+    columns[slots:] = far_grads[...]
+    total = jnp.dot(turned[...], columns[...], preferred_element_type=F32)
+    if keep:
+        taken_ref, out_ref, first_ref = refs[:3]
+        for z in range(LO_SIZE):
+            part = total[z * shard : (z + 1) * shard] + taken_ref[z].astype(F32)
+            part = part.astype(BF16)
+            out_ref[z] = part
+            if z in (0, LO_SIZE - 1):
+
+                @pl.when((where_ref[1] == 0) == (z != 0))
+                def _():
+                    first_ref[...] = part
+    else:
+        for z in range(LO_SIZE):
+            refs[0][z] = total[z * shard : (z + 1) * shard].astype(BF16)
+
+
+def wide_grads(where, rows, grads, width, taken=None):
     shard = width // (LO_SIZE * CORES)
     slots, columns = grads[0].shape
-    block = pl.BlockSpec((1, shard, columns), lambda z, s: (z, 0, 0))
-    pick = pl.BlockSpec((slots, shard), lambda z, s: (0, z * CORES + s[0]))
-    same = pl.BlockSpec((slots, columns), lambda z, s: (0, 0))
+    step = min(512, columns)
+    block = pl.BlockSpec((LO_SIZE, shard, step), lambda n, s: (0, 0, n))
+    tokens = pl.BlockSpec((slots, width), lambda n, s: (0, 0))
+    part = pl.BlockSpec((slots, step), lambda n, s: (0, n))
+    shape = jax.ShapeDtypeStruct((LO_SIZE, shard, columns), BF16)
     extra = [] if taken is None else [taken]
-    return pl.pallas_call(
-        functools.partial(wide_kernel, taken is not None),
+    first = jax.ShapeDtypeStruct((shard, columns), BF16)
+    first_block = pl.BlockSpec((shard, step), lambda n, s: (0, n))
+    return pl.pallas_call(
+        functools.partial(wide_kernel, taken is not None, shard),
         grid_spec=pltpu.PrefetchScalarGridSpec(
             num_scalar_prefetch=1,
-            grid=(LO_SIZE,),
-            in_specs=[pick, pick, same, same] + [block] * len(extra),
-            out_specs=block,
+            grid=(columns // step,),
+            in_specs=[tokens, tokens, part, part] + [block] * len(extra),
+            out_specs=(block, first_block) if extra else block,
+            scratch_shapes=[
+                pltpu.VMEM((LO_SIZE * shard, 2 * slots), BF16),
+                pltpu.VMEM((2 * slots, step), BF16),
+            ],
         ),
-        out_shape=jax.ShapeDtypeStruct((LO_SIZE, shard, columns), BF16),
+        out_shape=(shape, first) if extra else shape,
         compiler_params=limits(),
         cost_estimate=cost(2 * slots * width * columns, 2 * width * columns),
         name="wide",
-    )(select, *rows, *grads, *extra)
-
-
-def down_kernel(core_ref, near_hidden, far_hidden, near_pick, far_pick, give_ref, keep_ref, acc):
+    )(where, *rows, *grads, *extra)
+
+
+def down_kernel(
+    core_ref, near_hidden, far_hidden, near_pick, far_pick, give_ref, keep_ref, turned, columns, acc
+):
     core = core_ref[0]
     shard = give_ref.shape[1]
-    acc[...] = lax.dot_general(
-        near_hidden[...], near_pick[...], CONTRACT_FIRST, preferred_element_type=F32
-    )
-    acc[...] += lax.dot_general(
-        far_hidden[...], far_pick[...], CONTRACT_FIRST, preferred_element_type=F32
-    )
+    slots = near_hidden.shape[0]
+
+    @pl.when(pl.program_id(0) == 0)
+    def _():
+        turned[:, :slots] = jnp.transpose(near_hidden[...])
+        turned[:, slots:] = jnp.transpose(far_hidden[...])
+
+    columns[:slots] = near_pick[...]
+    columns[slots:] = far_pick[...]
+    acc[...] = jnp.dot(turned[...], columns[...], preferred_element_type=F32)
     for z in range(LO_SIZE):
         for which, ref in ((1 - core, give_ref), (core, keep_ref)):
             start = pl.multiple_of((z * CORES + which) * shard, shard)
@@ -316,7 +347,11 @@
             grid=(width // step,),
             in_specs=[same, same, part, part],
             out_specs=(block, block),
-            scratch_shapes=[pltpu.VMEM((hidden_width, step), F32)],
+            scratch_shapes=[
+                pltpu.VMEM((hidden_width, 2 * slots), BF16),
+                pltpu.VMEM((2 * slots, step), BF16),
+                pltpu.VMEM((hidden_width, step), F32),
+            ],
         ),
         out_shape=(shape, shape),
         compiler_params=limits(),
@@ -351,17 +386,13 @@
         )
 
 
-def collect(picked, returned, which):
+def collect(picked, returned):
     slots, rows = picked.shape
     full = returned.shape[2]
     return pl.pallas_call(
         collect_kernel,
-        grid=(1,),
-        in_specs=[
-            pl.BlockSpec((slots, rows), lambda i: (0, 0)),
-            pl.BlockSpec((PLANE, MOST, full), lambda i: (0, which, 0)),
-        ],
-        out_specs=pl.BlockSpec((rows, full), lambda i: (0, 0)),
+        in_specs=[WHOLE, WHOLE],
+        out_specs=WHOLE,
         out_shape=jax.ShapeDtypeStruct((rows, full), BF16),
         compiler_params=limits(),
         cost_estimate=cost(2 * slots * rows * full, 2 * slots * full),
@@ -395,19 +426,11 @@
     slots, rows = picked.shape
     full = returned.shape[2]
     width = (full - SIDE) // 2
-    whole = lambda shape: pl.BlockSpec(shape, lambda i: (0,) * len(shape))
     wide = jax.ShapeDtypeStruct((rows, width), BF16)
     return pl.pallas_call(
         finish_kernel,
-        grid=(1,),
-        in_specs=[
-            SCALAR,
-            whole(ids.shape),
-            whole(picked.shape),
-            pl.BlockSpec((PLANE, MOST, full), lambda i: (0, 0, 0)),
-            whole(far_total.shape),
-        ],
-        out_specs=(whole((rows, width)), whole((rows, width)), whole(ids.shape)),
+        in_specs=[SCALAR] + [WHOLE] * 4,
+        out_specs=(WHOLE,) * 3,
         out_shape=(wide, wide, jax.ShapeDtypeStruct(ids.shape, F32)),
         compiler_params=limits(),
         cost_estimate=cost(2 * slots * rows * full, 2 * slots * full),
@@ -428,14 +451,13 @@
     return lax.dynamic_index_in_dim(parts, index, axis=0, keepdims=False).astype(F32)
 
 
-def line_sum(parts, lo):
-    first = jnp.where(lo == 0, parts[LO_SIZE - 1], parts[0])
+def line_sum(parts, first, lo):
     arrived = lax.ppermute(first, "dp", neighbours([(0, 1), (3, 2)])).astype(F32)
     up = (shard_of(parts, lo + 2) + arrived).astype(BF16)
     down = (shard_of(parts, lo - 2) + arrived).astype(BF16)
+    middle = up
     up = lax.ppermute(up, "dp", neighbours([(0, 1), (1, 2)]))
     down = lax.ppermute(down, "dp", neighbours([(3, 2), (2, 1)]))
-    middle = up
     up = (shard_of(parts, lo + 1) + up.astype(F32)).astype(BF16)
     down = (shard_of(parts, lo - 1) + down.astype(F32)).astype(BF16)
     up = lax.ppermute(up, "dp", neighbours([(0, 1), (1, 2), (2, 3)])).astype(F32)
@@ -449,9 +471,10 @@
     lo = lax.axis_index("dp") // CORES
     core = lax.axis_index("dp") % CORES
     half = ((my_expert // Y_SIZE) % HI_SIZE).astype(jnp.int32)[None]
-    place = (my_expert // (HI_SIZE * Y_SIZE)) * Y_SIZE + my_expert % Y_SIZE
+    place = (my_expert % Y_SIZE) * X_SIZE + my_expert // (HI_SIZE * Y_SIZE)
     place = place.astype(jnp.int32)[None]
     here = core.astype(jnp.int32)[None]
+    line = lo.astype(jnp.int32)[None]
     width = tokens.shape[1]
     hidden_width = gate_proj.shape[2]
     weights = (gate_proj[0], up_proj[0], down_proj[0])
@@ -460,29 +483,38 @@
     far_out_grad = across(out_grad)
     own_sides, far_sides = route(half, expert_ids, route_gates)
     far_sides = across(far_sides)
+    far_tokens, far_sides, own_sides = lax.optimization_barrier((far_tokens, far_sides, own_sides))
     near_blocks, near_picked = fill(own_sides, tokens, out_grad)
     near_rows = to_plane(near_blocks.reshape(PLANE, MOST, -1)).reshape(PLANE * MOST, -1)
-
-    far_tokens, near_blocks = lax.optimization_barrier((far_tokens, near_blocks))
     far_blocks, far_picked = fill(far_sides, far_tokens, far_out_grad)
+    far_blocks, near_blocks = lax.optimization_barrier((far_blocks, near_blocks))
     far_rows = to_plane(far_blocks.reshape(PLANE, MOST, -1)).reshape(PLANE * MOST, -1)
 
-    back, near_hidden, near_pick, near_grads = run_expert(0, place, near_rows, weights, None)
-    back, far_hidden, far_pick, far_grads = run_expert(1, place, far_rows, weights, back)
+    near_back, near_hidden, near_pick, near_grads = run_expert(place, near_rows, weights)
+    far_back, far_hidden, far_pick, far_grads = run_expert(place, far_rows, weights)
 
     rows, grads = (near_rows, far_rows), (near_grads, far_grads)
-    taken = core_swap(wide_grads(1 - here, rows, grads, width))
+    give = wide_grads(jnp.concatenate([1 - here, line]), rows, grads, width)
+    taken = core_swap(give)
+    far_back, give = lax.optimization_barrier((far_back, give))
+    far_returned = to_plane(far_back)
     give_down, keep_down = down_grads(here, (near_hidden, far_hidden), (near_pick, far_pick))
+    taken, keep_down = lax.optimization_barrier((taken, keep_down))
+    gate_up_parts, first = wide_grads(jnp.concatenate([here, line]), rows, grads, width, taken)
+    give_down, first = lax.optimization_barrier((give_down, first))
     taken_down = core_swap(give_down)
-    gate_up_parts = wide_grads(here, rows, grads, width, taken)
+    gate_up_sum, middle = line_sum(gate_up_parts, first, lo)
     down_parts = (keep_down.astype(F32) + taken_down.astype(F32)).astype(BF16)
-    gate_up_sum, middle = line_sum(gate_up_parts, lo)
-    down_sum, unused = line_sum(down_parts, lo)
-
-    returned = to_plane(back)
-    returned, middle = lax.optimization_barrier((returned, middle))
-    far_total = across(collect(far_picked, returned, 1))
-    layer_out, grad_tokens, gate_grads = finish(half, expert_ids, near_picked, returned, far_total)
+    first_down = jnp.where(lo == 0, down_parts[LO_SIZE - 1], down_parts[0])
+    down_sum, unused = line_sum(down_parts, first_down, lo)
+
+    near_back, far_returned = lax.optimization_barrier((near_back, far_returned))
+    near_returned = to_plane(near_back)
+    far_returned, middle = lax.optimization_barrier((far_returned, middle))
+    far_total = across(collect(far_picked, far_returned))
+    layer_out, grad_tokens, gate_grads = finish(
+        half, expert_ids, near_picked, near_returned, far_total
+    )
 
     is_moved = swap_flags[my_expert] == 1
     swap = [(i, i ^ (devices // 2)) for i in range(devices)]

time: 270 us -> 270 us (level)
  waiting for transfers between devices: 111 us -> 115 us
  other arithmetic: 20.4 us -> 16.9 us
  Pallas kernels: 49.9 us -> 46.6 us
    all_to_all x3 -> x4, waiting for transfers between devices: 13.8 us -> 32.3 us  [to_plane(): lax.all_to_all(blocks, 'expert', split_axis=0, concat_axis=0, axis_index_...]
    ppermute x4, waiting for transfers between devices: 51 us -> 36.1 us  [across(): return lax.ppermute(value, BOTH, pairs)]
    ppermute x2, waiting for transfers between devices: 7.94 us -> 0.01 us  [line_sum(): up = lax.ppermute(up, 'dp', neighbours([(0, 1), (1, 2)]))]
    all_to_all x3 -> x4, starting transfers between devices: 21.9 us -> 27.3 us  [to_plane(): lax.all_to_all(blocks, 'expert', split_axis=0, concat_axis=0, axis_index_...]
    ppermute x2, waiting for transfers between devices: 27.5 us -> 22.2 us  [line_sum(): lax.ppermute(up, 'dp', neighbours([(0, 1), (1, 2), (2, 3)])).astype(F32)]
    ppermute x2, waiting for transfers between devices: 0.01 us -> 5.29 us  [line_sum(): lax.ppermute(down, 'dp', neighbours([(3, 2), (2, 1), (1, 0)])).astype(F32)]
    ppermute x1, waiting for transfers between devices: 0.01 us -> 5.28 us  [on_device(): other_down = lax.ppermute(down_sum, 'expert', swap)]
    pallas_call x6, Pallas kernels: 42.1 us -> 38.7 us  [the longest x2 22.6 us: run_expert(): pl.pallas_call(expert_kernel, out_shape=(jax.ShapeDtypeStruct((PLANE, MOS...]
  transfers between devices with their start and end apart: 21 -> 22, of which waited for: 7 -> 11; matrix products, arithmetic and copies ran while one was open for 8% -> 8% of each run, Pallas kernels for 10% -> 8%
where the time goes in v5:
time: 270 us; the launch traced here: 269 us
  waiting for transfers between devices  115 us (43%)
  starting transfers between devices  70.4 us (26%)
  Pallas kernels  46.6 us (17%)
  local copies, waits for them, and re-layouts  17.9 us (7%)
  other arithmetic  16.9 us (6%)
    ppermute x4, waiting for transfers between devices, across(): return lax.ppermute(value, BOTH, pairs)  36.1 us
    all_to_all x4, waiting for transfers between devices, to_plane(): lax.all_to_all(blocks, 'expert', split_axis=0, concat_axis=0, axis_index_...  32.3 us
    all_to_all x4, starting transfers between devices, to_plane(): lax.all_to_all(blocks, 'expert', split_axis=0, concat_axis=0, axis_index_...  27.3 us
    pallas_call x2, Pallas kernels, run_expert(): pl.pallas_call(expert_kernel, out_shape=(jax.ShapeDtypeStruct((PLANE, MOS...  22.6 us
    ppermute x2, waiting for transfers between devices, line_sum(): lax.ppermute(up, 'dp', neighbours([(0, 1), (1, 2), (2, 3)])).astype(F32)  22.2 us
    unnamed x41, local copies, waits for them, and re-layouts  16.4 us
    pallas_call x2, Pallas kernels, wide_grads(): pl.pallas_call(functools.partial(wide_kernel, taken is not None, shard),...  12.6 us
    ppermute x2, starting transfers between devices, line_sum(): lax.ppermute(up, 'dp', neighbours([(0, 1), (1, 2), (2, 3)])).astype(F32)  12.3 us
  transfers between devices with their start and end apart: 22, of which 11 were waited for; matrix products, arithmetic and copies ran while one was open for 8% of the time, Pallas kernels for 8%

profile of v5, /device:TPU:16, one launch (start us, length us, event | category | flops | bytes accessed | tf_op | source)
XLA Modules:
  0.0 268.6 jit_solution(7421029168738586790)
XLA Ops:
  0.6 5.9 %collective-permute-start = (bf16[128,2048]{1,0:T(8,128)(2,1)}, bf16[128,2048]{1,0:T(8,128)(2,1)S(1)}, u32[]{:S(2)}, u32[]{:S(2)}) collective-permute-start(bf16[128,2048]{1,0:T(8,128)(2,1)} %tokens_ref.1), channel_id=1, source_target_pairs={{0,196},{1,197},{2,198},{3,199},{4,192},{5,193},{6,194},{7,195},{8... | collective-permute-start | bytes 1572872 | tf_op jit(solution)/shard_map/ppermute | solution.py:46
  6.6 1.4 copy.16.ids_ref
  8.0 1.4 copy.15.gates_ref
  9.4 2.1 route.1
  11.6 19.8 %collective-permute-done.1.sides_ref = bf16[128,128]{1,0:T(8,128)(2,1)S(1)} collective-permute-done((bf16[128,128]{1,0:T(8,128)(2,1)}, bf16[128,128]{1,0:T(8,128)(2,1)S(1)}, u32[]{:S(2)}, u32[]{:S(2)}) %collective-permute-start.1) | collective-permute-done | bytes 32800 | tf_op jit(solution)/shard_map/ppermute | solution.py:46
  31.4 1.0 copy-done.8
  32.4 1.0 copy-done.9
  33.4 0.8 copy-done.11
  34.2 0.9 fill.2
  35.1 1.4 copy-done.5
  36.5 7.4 %all-to-all-start = ((bf16[16,16,4224]{2,1,0:T(8,128)(2,1)}), bf16[16,16,4224]{2,1,0:T(8,128)(2,1)S(1)}, u32[]{:S(2)}, u32[]{:S(2)}) async-start(bf16[16,16,4224]{2,1,0:T(8,128)(2,1)} %bitcast.54), calls=%async_computation | async-start | bytes 4325376 | tf_op jit(solution)/shard_map/all_to_all | solution.py:50
  43.9 3.0 %collective-permute-start.2 = (bf16[128,2048]{1,0:T(8,128)(2,1)S(1)}, bf16[128,2048]{1,0:T(8,128)(2,1)S(1)}, u32[]{:S(2)}, u32[]{:S(2)}) collective-permute-start(bf16[128,2048]{1,0:T(8,128)(2,1)S(1)} %copy-done.10), channel_id=1, source_target_pairs={{0,196},{1,197},{2,198},{3,199},{4,192},{5,193},{6,194},{7,195},{8... | collective-permute-start | bytes 1572872 | tf_op jit(solution)/shard_map/ppermute | solution.py:46
  46.9 12.4 %collective-permute-done.2.grads_ref = bf16[128,2048]{1,0:T(8,128)(2,1)S(1)} collective-permute-done((bf16[128,2048]{1,0:T(8,128)(2,1)S(1)}, bf16[128,2048]{1,0:T(8,128)(2,1)S(1)}, u32[]{:S(2)}, u32[]{:S(2)}) %collective-permute-start.2) | collective-permute-done | bytes 524320 | tf_op jit(solution)/shard_map/ppermute | solution.py:46
  59.3 0.9 fill.3
  60.2 1.3 copy-done.3
  61.6 11.8 %all-to-all-done = bf16[16,16,4224]{2,1,0:T(8,128)(2,1)S(1)} async-done(((bf16[16,16,4224]{2,1,0:T(8,128)(2,1)}), bf16[16,16,4224]{2,1,0:T(8,128)(2,1)S(1)}, u32[]{:S(2)}, u32[]{:S(2)}) %all-to-all-start) | async-done | bytes 2162720 | tf_op jit(solution)/shard_map/all_to_all | solution.py:50
  73.3 1.4 copy-done
  74.7 6.7 %all-to-all-start.1 = ((bf16[16,16,4224]{2,1,0:T(8,128)(2,1)}), bf16[16,16,4224]{2,1,0:T(8,128)(2,1)}, u32[]{:S(2)}, u32[]{:S(2)}) async-start(bf16[16,16,4224]{2,1,0:T(8,128)(2,1)} %bitcast.53), calls=%async_computation.1 | async-start | bytes 4325376 | tf_op jit(solution)/shard_map/all_to_all | solution.py:50
  81.5 11.2 %expert.2 = (bf16[16,16,4224]{2,1,0:T(8,128)(2,1)S(1)}, bf16[256,768]{1,0:T(8,128)(2,1)S(1)}, bf16[256,2048]{1,0:T(8,128)(2,1)S(1)}, bf16[256,1536]{1,0:T(8,128)(2,1)S(1)}) custom-call(s32[1]{0:T(128)} %bitcast.1.place_ref, bf16[256,4224]{1,0:T(8,128)(2,1)} %bitcast.50, bf16[2048,768]{1,0:T(8,128)(2,1)} %bitcast.55, bf16[2048,768]{1,0:T(8,128)(2,1)} %bitcast.57, ...), custom_call_target="tpu_custom_call" | custom-call | flops 4831838208 | bytes 9437184 | tf_op jit(solution)/shard_map/expert/pallas_call | solution.py:230
  92.8 1.4 copy-done.2
  94.2 0.7 copy-done.12
  94.9 14.4 %all-to-all-done.1 = bf16[16,16,4224]{2,1,0:T(8,128)(2,1)} async-done(((bf16[16,16,4224]{2,1,0:T(8,128)(2,1)}), bf16[16,16,4224]{2,1,0:T(8,128)(2,1)}, u32[]{:S(2)}, u32[]{:S(2)}) %all-to-all-start.1) | async-done | bytes 2162720 | tf_op jit(solution)/shard_map/all_to_all | solution.py:50
  109.3 11.3 %expert.3 = (bf16[16,16,4224]{2,1,0:T(8,128)(2,1)S(1)}, bf16[256,768]{1,0:T(8,128)(2,1)S(1)}, bf16[256,2048]{1,0:T(8,128)(2,1)S(1)}, bf16[256,1536]{1,0:T(8,128)(2,1)S(1)}) custom-call(s32[1]{0:T(128)} %bitcast.1.place_ref, bf16[256,4224]{1,0:T(8,128)(2,1)} %bitcast.8.rows_ref.far_x, bf16[2048,768]{1,0:T(8,128)(2,1)} %bitcast.56, ...), custom_call_target="tpu_custom_call" | custom-call | flops 4831838208 | bytes 9437184 | tf_op jit(solution)/shard_map/expert/pallas_call | solution.py:230
  120.7 1.3 copy-done.4
  122.0 5.7 %wide.2 = bf16[4,256,1536]{2,1,0:T(8,128)(2,1)} custom-call(s32[2]{0:T(128)S(1)} %get-tuple-element.88.where_ref, bf16[256,4224]{1,0:T(8,128)(2,1)S(1)} %bitcast.51, bf16[256,4224]{1,0:T(8,128)(2,1)} %bitcast.8.rows_ref.far_x, bf16[256,1536]{1,0:T(8,128)(2,1)S(1)} %get-tuple-element.50.near_grads, bf16[256,1536]{1,0:T(8,128)(2,1)S(1)} %get-tuple-element.51.far_grads), custom_call_target="tpu_custom_call" | custom-call | flops 1610612736 | bytes 6291456 | tf_op jit(solution)/shard_map/wide/pallas_call | solution.py:294
  127.8 4.0 %down.1 = (bf16[4,96,2048]{2,1,0:T(8,128)(2,1)}, bf16[4,96,2048]{2,1,0:T(8,128)(2,1)S(1)}) custom-call(s32[1]{0:T(128)} %bitcast.9.core_ref, bf16[256,768]{1,0:T(8,128)(2,1)S(1)} %copy-done.13, bf16[256,768]{1,0:T(8,128)(2,1)S(1)} %get-tuple-element.57.far_hidden, bf16[256,2048]{1,0:T(8,128)(2,1)S(1)} %get-tuple-element.58.near_pick, ...), custom_call_target="tpu_custom_call" | custom-call | flops 1610612736 | bytes 6291456 | tf_op jit(solution)/shard_map/down/pallas_call | solution.py:343
  131.7 1.9 collective-permute-done.3.refs_0_
  133.6 1.7 copy-done.17
  135.3 6.9 %wide.3 = (bf16[4,256,1536]{2,1,0:T(8,128)(2,1)}, bf16[256,1536]{1,0:T(8,128)(2,1)S(1)}) custom-call(s32[2]{0:T(128)S(1)} %get-tuple-element.89.where_ref, bf16[256,4224]{1,0:T(8,128)(2,1)S(1)} %bitcast.52, bf16[256,4224]{1,0:T(8,128)(2,1)} %bitcast.8.rows_ref.far_x, bf16[256,1536]{1,0:T(8,128)(2,1)S(1)} %get-tuple-element.50.near_grads, ...), custom_call_target="tpu_custom_call" | custom-call | flops 1610612736 | bytes 6291456 | tf_op jit(solution)/shard_map/wide/pallas_call | solution.py:294
  142.3 6.2 %all-to-all-start.2 = ((bf16[16,16,4224]{2,1,0:T(8,128)(2,1)}), bf16[16,16,4224]{2,1,0:T(8,128)(2,1)S(1)}, u32[]{:S(2)}, u32[]{:S(2)}) async-start(bf16[16,16,4224]{2,1,0:T(8,128)(2,1)} %copy-done.4), calls=%async_computation.2 | async-start | bytes 4325376 | tf_op jit(solution)/shard_map/all_to_all | solution.py:50
  148.5 1.3 collective-permute-start.4
  149.9 2.6 add_convert_fusion
  152.5 0.8 fusion.12
  153.4 2.1 collective-permute-start.12
  155.4 12.2 %collective-permute-done.4 = bf16[256,1536]{1,0:T(8,128)(2,1)S(1)} collective-permute-done((bf16[256,1536]{1,0:T(8,128)(2,1)S(1)}, bf16[256,1536]{1,0:T(8,128)(2,1)S(1)}, u32[]{:S(2)}, u32[]{:S(2)}) %collective-permute-start.4) | collective-permute-done | bytes 786464 | tf_op jit(solution)/shard_map/ppermute | solution.py:455
  167.7 1.5 fusion.1
  169.1 4.4 %collective-permute-start.6 = (bf16[256,1536]{1,0:T(8,128)(2,1)}, bf16[256,1536]{1,0:T(8,128)(2,1)S(1)}, u32[]{:S(2)}, u32[]{:S(2)}) collective-permute-start(bf16[256,1536]{1,0:T(8,128)(2,1)} %get-tuple-element.79), channel_id=1, source_target_pairs={{0,64},{32,96},{64,128},{96,160},{1,65},{33,97},{65,129},{97,161},... | collective-permute-start | bytes 2359304 | tf_op jit(solution)/shard_map/ppermute | solution.py:459
  173.6 1.5 collective-permute-start.8
  175.1 6.1 %all-to-all-done.2.returned_ref = bf16[16,16,4224]{2,1,0:T(8,128)(2,1)S(1)} async-done(((bf16[16,16,4224]{2,1,0:T(8,128)(2,1)}), bf16[16,16,4224]{2,1,0:T(8,128)(2,1)S(1)}, u32[]{:S(2)}, u32[]{:S(2)}) %all-to-all-start.2) | async-done | bytes 2162720 | tf_op jit(solution)/shard_map/all_to_all | solution.py:50
  181.2 7.0 %all-to-all-start.3 = ((bf16[16,16,4224]{2,1,0:T(8,128)(2,1)}), bf16[16,16,4224]{2,1,0:T(8,128)(2,1)}, u32[]{:S(2)}, u32[]{:S(2)}) async-start(bf16[16,16,4224]{2,1,0:T(8,128)(2,1)} %copy-done.2), calls=%async_computation.3 | async-start | bytes 4325376 | tf_op jit(solution)/shard_map/all_to_all | solution.py:50
  188.2 2.3 fusion.6
  190.5 2.0 collective-permute-start.13
  192.5 1.4 collective-permute-start.15
  193.9 3.2 %fusion.3 = (bf16[256,1536]{1,0:T(8,128)(2,1)}, bf16[256,1536]{1,0:T(8,128)(2,1)}) fusion(bf16[256,1536]{1,0:T(8,128)(2,1)S(1)} %collective-permute-done.6, bf16[4,256,1536]{2,1,0:T(8,128)(2,1)} %get-tuple-element.62, s32[]{:T(128)S(6)} %min.23, bf16[256,1536]{1,0:T(8,128)(2,1)} %collective-permute-done.8, s32[]{:T(128)S(6)} %min.24), kind=kLoop, calls=%fused_computation.8 | loop fusion | flops 3145728 | bytes 4718600 | tf_op jit(solution)/shard_map/convert_element_type | solution.py:461
  197.1 1.3 collective-permute-start.9
  198.4 6.7 %collective-permute-start.7 = (bf16[256,1536]{1,0:T(8,128)(2,1)}, bf16[256,1536]{1,0:T(8,128)(2,1)}, u32[]{:S(2)}, u32[]{:S(2)}) collective-permute-start(bf16[256,1536]{1,0:T(8,128)(2,1)} %get-tuple-element.80), channel_id=1, source_target_pairs={{0,64},{32,96},{64,128},{96,160},{128,192},{160,224},{1,65},{33,97... | collective-permute-start | bytes 2359304 | tf_op jit(solution)/shard_map/ppermute | solution.py:463
  205.1 0.5 collect.1
  205.7 0.8 copy-done.15
  206.5 2.3 fusion.9
  208.8 1.3 collective-permute-start.16
  210.1 5.6 %collective-permute-start.14 = (bf16[96,2048]{1,0:T(8,128)(2,1)}, bf16[96,2048]{1,0:T(8,128)(2,1)}, u32[]{:S(2)}, u32[]{:S(2)}) collective-permute-start(bf16[96,2048]{1,0:T(8,128)(2,1)} %get-tuple-element.84), channel_id=1, source_target_pairs={{0,64},{32,96},{64,128},{96,160},{128,192},{160,224},{1,65},{33,97... | collective-permute-start | bytes 1179656 | tf_op jit(solution)/shard_map/ppermute | solution.py:463
  215.7 5.3 %collective-permute-done.9 = bf16[256,1536]{1,0:T(8,128)(2,1)} collective-permute-done((bf16[256,1536]{1,0:T(8,128)(2,1)}, bf16[256,1536]{1,0:T(8,128)(2,1)}, u32[]{:S(2)}, u32[]{:S(2)}) %collective-permute-start.9) | collective-permute-done | bytes 786464 | tf_op jit(solution)/shard_map/ppermute | solution.py:464
  221.0 22.2 %collective-permute-done.7 = bf16[256,1536]{1,0:T(8,128)(2,1)} collective-permute-done((bf16[256,1536]{1,0:T(8,128)(2,1)}, bf16[256,1536]{1,0:T(8,128)(2,1)}, u32[]{:S(2)}, u32[]{:S(2)}) %collective-permute-start.7) | collective-permute-done | bytes 786464 | tf_op jit(solution)/shard_map/ppermute | solution.py:463
  243.2 1.9 fusion.5
  245.1 3.1 %collective-permute-start.10 = (bf16[256,1536]{1,0:T(8,128)(2,1)S(1)}, bf16[256,1536]{1,0:T(8,128)(2,1)}, u32[]{:S(2)}, u32[]{:S(2)}) collective-permute-start(bf16[256,1536]{1,0:T(8,128)(2,1)S(1)} %fusion.5), channel_id=1, source_target_pairs={{0,16},{1,17},{2,18},{3,19},{4,20},{5,21},{6,22},{7,23},{8,24},{9,... | collective-permute-start | bytes 2359304 | tf_op jit(solution)/shard_map/ppermute | solution.py:521
  248.2 0.6 dynamic_slice.36
  249.4 3.9 %collective-permute-done.5.far_ref = bf16[128,4224]{1,0:T(8,128)(2,1)S(1)} collective-permute-done((bf16[128,4224]{1,0:T(8,128)(2,1)S(1)}, bf16[128,4224]{1,0:T(8,128)(2,1)S(1)}, u32[]{:S(2)}, u32[]{:S(2)}) %collective-permute-start.5) | collective-permute-done | bytes 1081376 | tf_op jit(solution)/shard_map/ppermute | solution.py:46
  253.3 3.0 %finish.1 = (bf16[128,2048]{1,0:T(8,128)(2,1)}, bf16[128,2048]{1,0:T(8,128)(2,1)}, f32[128,8]{1,0:T(8,128)S(1)}) custom-call(s32[1]{0:T(128)} %bitcast.half_ref, s32[128,8]{1,0:T(8,128)S(1)} %copy-done.7, bf16[256,128]{1,0:T(8,128)(2,1)S(1)} %get-tuple-element.42.picked_ref, bf16[16,16,4224]{2,1,0:T(8,128)(2,1)} %all-to-all-done.3.returned_ref, ...), custom_call_target="tpu_custom_call" | custom-call | flops 276824064 | bytes 2162688 | tf_op jit(solution)/shard_map/finish/pallas_call | solution.py:430
  256.4 0.7 copy.17
  257.0 1.4 fusion.11
  258.4 3.1 %collective-permute-start.17 = (bf16[96,2048]{1,0:T(8,128)(2,1)S(1)}, bf16[96,2048]{1,0:T(8,128)(2,1)S(1)}, u32[]{:S(2)}, u32[]{:S(2)}) collective-permute-start(bf16[96,2048]{1,0:T(8,128)(2,1)S(1)} %fusion.11), channel_id=1, source_target_pairs={{0,16},{1,17},{2,18},{3,19},{4,20},{5,21},{6,22},{7,23},{8,24},{9,... | collective-permute-start | bytes 1179656 | tf_op jit(solution)/shard_map/ppermute | solution.py:522
  261.6 0.9 slice_bitcast_fusion
  262.5 5.3 %collective-permute-done.17 = bf16[96,2048]{1,0:T(8,128)(2,1)S(1)} collective-permute-done((bf16[96,2048]{1,0:T(8,128)(2,1)S(1)}, bf16[96,2048]{1,0:T(8,128)(2,1)S(1)}, u32[]{:S(2)}, u32[]{:S(2)}) %collective-permute-start.17) | collective-permute-done | bytes 393248 | tf_op jit(solution)/shard_map/ppermute | solution.py:522
  267.8 0.8 select_bitcast_fusion
  (44 shorter events, 0.5 us)
Async XLA Ops:
  0.6 30.7 %collective-permute-start = (bf16[128,2048]{1,0:T(8,128)(2,1)}, bf16[128,2048]{1,0:T(8,128)(2,1)S(1)}, u32[]{:S(2)}, u32[]{:S(2)}) collective-permute-start(bf16[128,2048]{1,0:T(8,128)(2,1)} %tokens_ref.1), channel_id=1, source_target_pairs={{0,196},{1,197},{2,198},{3,199},{4,192},{5,193},{6,194},{7,195},{8... | collective-permute-start | bytes 1572872 | tf_op jit(solution)/shard_map/ppermute | solution.py:46
  11.5 19.8 %collective-permute-start.1 = (bf16[128,128]{1,0:T(8,128)(2,1)}, bf16[128,128]{1,0:T(8,128)(2,1)S(1)}, u32[]{:S(2)}, u32[]{:S(2)}) collective-permute-start(bf16[128,128]{1,0:T(8,128)(2,1)} %get-tuple-element.39), channel_id=1, source_target_pairs={{0,196},{1,197},{2,198},{3,199},{4,192},{5,193},{6,194},{7,195},{8... | collective-permute-start | bytes 98312 | tf_op jit(solution)/shard_map/ppermute | solution.py:46
  31.4 1.0 copy-start.8
  32.4 1.0 copy-start.9
  33.4 0.8 copy-start.11
  35.1 1.4 copy-start.5
  36.5 7.4 %copy-start.10 = (bf16[128,2048]{1,0:T(8,128)(2,1)S(1)}, bf16[128,2048]{1,0:T(8,128)(2,1)}, u32[]{:S(2)}) copy-start(bf16[128,2048]{1,0:T(8,128)(2,1)} %grads_ref.1) | copy-start | bytes 1572868
  36.5 36.9 %all-to-all-start = ((bf16[16,16,4224]{2,1,0:T(8,128)(2,1)}), bf16[16,16,4224]{2,1,0:T(8,128)(2,1)S(1)}, u32[]{:S(2)}, u32[]{:S(2)}) async-start(bf16[16,16,4224]{2,1,0:T(8,128)(2,1)} %bitcast.54), calls=%async_computation | async-start | bytes 4325376 | tf_op jit(solution)/shard_map/all_to_all | solution.py:50
  43.9 15.4 %collective-permute-start.2 = (bf16[128,2048]{1,0:T(8,128)(2,1)S(1)}, bf16[128,2048]{1,0:T(8,128)(2,1)S(1)}, u32[]{:S(2)}, u32[]{:S(2)}) collective-permute-start(bf16[128,2048]{1,0:T(8,128)(2,1)S(1)} %copy-done.10), channel_id=1, source_target_pairs={{0,196},{1,197},{2,198},{3,199},{4,192},{5,193},{6,194},{7,195},{8... | collective-permute-start | bytes 1572872 | tf_op jit(solution)/shard_map/ppermute | solution.py:46
  60.2 1.3 copy-start.3
  73.3 1.4 copy-start
  74.7 34.6 %all-to-all-start.1 = ((bf16[16,16,4224]{2,1,0:T(8,128)(2,1)}), bf16[16,16,4224]{2,1,0:T(8,128)(2,1)}, u32[]{:S(2)}, u32[]{:S(2)}) async-start(bf16[16,16,4224]{2,1,0:T(8,128)(2,1)} %bitcast.53), calls=%async_computation.1 | async-start | bytes 4325376 | tf_op jit(solution)/shard_map/all_to_all | solution.py:50
  92.8 1.4 copy-start.2
  94.2 0.7 copy-start.12
  109.3 12.7 %copy-start.1 = (bf16[16,16,4224]{2,1,0:T(8,128)(2,1)S(1)}, bf16[16,16,4224]{2,1,0:T(8,128)(2,1)}, u32[]{:S(2)}) copy-start(bf16[16,16,4224]{2,1,0:T(8,128)(2,1)} %copy-done) | copy-start | bytes 6488068
  120.7 1.3 copy-start.4
  122.0 5.7 %copy-start.13 = (bf16[256,768]{1,0:T(8,128)(2,1)S(1)}, bf16[256,768]{1,0:T(8,128)(2,1)}, u32[]{:S(2)}) copy-start(bf16[256,768]{1,0:T(8,128)(2,1)} %copy-done.12) | copy-start | bytes 1179652
  127.8 5.9 %collective-permute-start.3 = (bf16[4,256,1536]{2,1,0:T(8,128)(2,1)}, bf16[4,256,1536]{2,1,0:T(8,128)(2,1)S(1)}, u32[]{:S(2)}, u32[]{:S(2)}) collective-permute-start(bf16[4,256,1536]{2,1,0:T(8,128)(2,1)} %wide.2), channel_id=1, source_target_pairs={{0,32},{32,0},{64,96},{96,64},{128,160},{160,128},{192,224},{224,1... | collective-permute-start | bytes 9437192 | tf_op jit(solution)/shard_map/ppermute | solution.py:446
  131.7 10.4 %copy-start.6 = (bf16[4,96,2048]{2,1,0:T(8,128)(2,1)}, bf16[4,96,2048]{2,1,0:T(8,128)(2,1)S(1)}, u32[]{:S(2)}) copy-start(bf16[4,96,2048]{2,1,0:T(8,128)(2,1)S(1)} %get-tuple-element.70) | copy-start | bytes 4718596
  133.6 1.7 copy-start.17
  142.2 7.7 %collective-permute-start.11 = (bf16[4,96,2048]{2,1,0:T(8,128)(2,1)}, bf16[4,96,2048]{2,1,0:T(8,128)(2,1)}, u32[]{:S(2)}, u32[]{:S(2)}) collective-permute-start(bf16[4,96,2048]{2,1,0:T(8,128)(2,1)} %get-tuple-element.71), channel_id=1, source_target_pairs={{0,32},{32,0},{64,96},{96,64},{128,160},{160,128},{192,224},{224,1... | collective-permute-start | bytes 4718600 | tf_op jit(solution)/shard_map/ppermute | solution.py:446
  142.3 38.9 %all-to-all-start.2 = ((bf16[16,16,4224]{2,1,0:T(8,128)(2,1)}), bf16[16,16,4224]{2,1,0:T(8,128)(2,1)S(1)}, u32[]{:S(2)}, u32[]{:S(2)}) async-start(bf16[16,16,4224]{2,1,0:T(8,128)(2,1)} %copy-done.4), calls=%async_computation.2 | async-start | bytes 4325376 | tf_op jit(solution)/shard_map/all_to_all | solution.py:50
  148.5 19.1 %collective-permute-start.4 = (bf16[256,1536]{1,0:T(8,128)(2,1)S(1)}, bf16[256,1536]{1,0:T(8,128)(2,1)S(1)}, u32[]{:S(2)}, u32[]{:S(2)}) collective-permute-start(bf16[256,1536]{1,0:T(8,128)(2,1)S(1)} %get-tuple-element.65), channel_id=1, source_target_pairs={{0,64},{32,96},{192,128},{224,160},{1,65},{33,97},{193,129},{225,1... | collective-permute-start | bytes 2359304 | tf_op jit(solution)/shard_map/ppermute | solution.py:455
  149.9 17.8 %copy-start.16 = (bf16[4,256,1536]{2,1,0:T(8,128)(2,1)S(1)}, bf16[4,256,1536]{2,1,0:T(8,128)(2,1)}, u32[]{:S(2)}) copy-start(bf16[4,256,1536]{2,1,0:T(8,128)(2,1)} %get-tuple-element.62) | copy-start | bytes 9437188
  152.5 16.6 %copy-start.14 = (bf16[4,96,2048]{2,1,0:T(8,128)(2,1)}, bf16[4,96,2048]{2,1,0:T(8,128)(2,1)S(1)}, u32[]{:S(2)}) copy-start(bf16[4,96,2048]{2,1,0:T(8,128)(2,1)S(1)} %add_convert_fusion) | copy-start | bytes 4718596
  153.4 34.8 %collective-permute-start.12 = (bf16[96,2048]{1,0:T(8,128)(2,1)}, bf16[96,2048]{1,0:T(8,128)(2,1)}, u32[]{:S(2)}, u32[]{:S(2)}) collective-permute-start(bf16[96,2048]{1,0:T(8,128)(2,1)} %fusion.12), channel_id=1, source_target_pairs={{0,64},{32,96},{192,128},{224,160},{1,65},{33,97},{193,129},{225,1... | collective-permute-start | bytes 1179656 | tf_op jit(solution)/shard_map/ppermute | solution.py:455
  169.1 24.8 %collective-permute-start.6 = (bf16[256,1536]{1,0:T(8,128)(2,1)}, bf16[256,1536]{1,0:T(8,128)(2,1)S(1)}, u32[]{:S(2)}, u32[]{:S(2)}) collective-permute-start(bf16[256,1536]{1,0:T(8,128)(2,1)} %get-tuple-element.79), channel_id=1, source_target_pairs={{0,64},{32,96},{64,128},{96,160},{1,65},{33,97},{65,129},{97,161},... | collective-permute-start | bytes 2359304 | tf_op jit(solution)/shard_map/ppermute | solution.py:459
  173.6 20.4 %collective-permute-start.8 = (bf16[256,1536]{1,0:T(8,128)(2,1)}, bf16[256,1536]{1,0:T(8,128)(2,1)}, u32[]{:S(2)}, u32[]{:S(2)}) collective-permute-start(bf16[256,1536]{1,0:T(8,128)(2,1)} %get-tuple-element.78), channel_id=1, source_target_pairs={{192,128},{224,160},{128,64},{160,96},{193,129},{225,161},{129,65}... | collective-permute-start | bytes 2359304 | tf_op jit(solution)/shard_map/ppermute | solution.py:460
  181.2 68.2 %all-to-all-start.3 = ((bf16[16,16,4224]{2,1,0:T(8,128)(2,1)}), bf16[16,16,4224]{2,1,0:T(8,128)(2,1)}, u32[]{:S(2)}, u32[]{:S(2)}) async-start(bf16[16,16,4224]{2,1,0:T(8,128)(2,1)} %copy-done.2), calls=%async_computation.3 | async-start | bytes 4325376 | tf_op jit(solution)/shard_map/all_to_all | solution.py:50
  190.5 15.2 %collective-permute-start.13 = (bf16[96,2048]{1,0:T(8,128)(2,1)}, bf16[96,2048]{1,0:T(8,128)(2,1)}, u32[]{:S(2)}, u32[]{:S(2)}) collective-permute-start(bf16[96,2048]{1,0:T(8,128)(2,1)} %get-tuple-element.82), channel_id=1, source_target_pairs={{0,64},{32,96},{64,128},{96,160},{1,65},{33,97},{65,129},{97,161},... | collective-permute-start | bytes 1179656 | tf_op jit(solution)/shard_map/ppermute | solution.py:459
  192.5 13.2 %collective-permute-start.15 = (bf16[96,2048]{1,0:T(8,128)(2,1)}, bf16[96,2048]{1,0:T(8,128)(2,1)}, u32[]{:S(2)}, u32[]{:S(2)}) collective-permute-start(bf16[96,2048]{1,0:T(8,128)(2,1)} %get-tuple-element.83), channel_id=1, source_target_pairs={{192,128},{224,160},{128,64},{160,96},{193,129},{225,161},{129,65}... | collective-permute-start | bytes 1179656 | tf_op jit(solution)/shard_map/ppermute | solution.py:460
  197.1 23.9 %collective-permute-start.9 = (bf16[256,1536]{1,0:T(8,128)(2,1)}, bf16[256,1536]{1,0:T(8,128)(2,1)}, u32[]{:S(2)}, u32[]{:S(2)}) collective-permute-start(bf16[256,1536]{1,0:T(8,128)(2,1)} %get-tuple-element.81), channel_id=1, source_target_pairs={{192,128},{224,160},{128,64},{160,96},{64,0},{96,32},{193,129},{22... | collective-permute-start | bytes 2359304 | tf_op jit(solution)/shard_map/ppermute | solution.py:464
  198.4 44.8 %collective-permute-start.7 = (bf16[256,1536]{1,0:T(8,128)(2,1)}, bf16[256,1536]{1,0:T(8,128)(2,1)}, u32[]{:S(2)}, u32[]{:S(2)}) collective-permute-start(bf16[256,1536]{1,0:T(8,128)(2,1)} %get-tuple-element.80), channel_id=1, source_target_pairs={{0,64},{32,96},{64,128},{96,160},{128,192},{160,224},{1,65},{33,97... | collective-permute-start | bytes 2359304 | tf_op jit(solution)/shard_map/ppermute | solution.py:463
  205.1 1.4 copy-start.15
  205.6 47.7 %collective-permute-start.5 = (bf16[128,4224]{1,0:T(8,128)(2,1)S(1)}, bf16[128,4224]{1,0:T(8,128)(2,1)S(1)}, u32[]{:S(2)}, u32[]{:S(2)}) collective-permute-start(bf16[128,4224]{1,0:T(8,128)(2,1)S(1)} %collect.1), channel_id=1, source_target_pairs={{0,196},{1,197},{2,198},{3,199},{4,192},{5,193},{6,194},{7,195},{8... | collective-permute-start | bytes 3244040 | tf_op jit(solution)/shard_map/ppermute | solution.py:46
  208.8 48.3 %collective-permute-start.16 = (bf16[96,2048]{1,0:T(8,128)(2,1)}, bf16[96,2048]{1,0:T(8,128)(2,1)}, u32[]{:S(2)}, u32[]{:S(2)}) collective-permute-start(bf16[96,2048]{1,0:T(8,128)(2,1)} %get-tuple-element.85), channel_id=1, source_target_pairs={{192,128},{224,160},{128,64},{160,96},{64,0},{96,32},{193,129},{22... | collective-permute-start | bytes 1179656 | tf_op jit(solution)/shard_map/ppermute | solution.py:464
  210.1 38.1 %copy-start.18 = (s32[32]{0:T(128)S(1)}, s32[32]{0:T(128)}, u32[]{:S(2)}) copy-start(s32[32]{0:T(128)} %param.12) | copy-start | bytes 388
  210.1 43.3 %copy-start.7 = (s32[128,8]{1,0:T(8,128)S(1)}, s32[128,8]{1,0:T(8,128)}, u32[]{:S(2)}) copy-start(s32[128,8]{1,0:T(8,128)} %copy.16.ids_ref) | copy-start | bytes 12292
  210.1 47.0 %collective-permute-start.14 = (bf16[96,2048]{1,0:T(8,128)(2,1)}, bf16[96,2048]{1,0:T(8,128)(2,1)}, u32[]{:S(2)}, u32[]{:S(2)}) collective-permute-start(bf16[96,2048]{1,0:T(8,128)(2,1)} %get-tuple-element.84), channel_id=1, source_target_pairs={{0,64},{32,96},{64,128},{96,160},{128,192},{160,224},{1,65},{33,97... | collective-permute-start | bytes 1179656 | tf_op jit(solution)/shard_map/ppermute | solution.py:463
  245.1 16.4 %collective-permute-start.10 = (bf16[256,1536]{1,0:T(8,128)(2,1)S(1)}, bf16[256,1536]{1,0:T(8,128)(2,1)}, u32[]{:S(2)}, u32[]{:S(2)}) collective-permute-start(bf16[256,1536]{1,0:T(8,128)(2,1)S(1)} %fusion.5), channel_id=1, source_target_pairs={{0,16},{1,17},{2,18},{3,19},{4,20},{5,21},{6,22},{7,23},{8,24},{9,... | collective-permute-start | bytes 2359304 | tf_op jit(solution)/shard_map/ppermute | solution.py:521
  258.4 9.4 %collective-permute-start.17 = (bf16[96,2048]{1,0:T(8,128)(2,1)S(1)}, bf16[96,2048]{1,0:T(8,128)(2,1)S(1)}, u32[]{:S(2)}, u32[]{:S(2)}) collective-permute-start(bf16[96,2048]{1,0:T(8,128)(2,1)S(1)} %fusion.11), channel_id=1, source_target_pairs={{0,16},{1,17},{2,18},{3,19},{4,20},{5,21},{6,22},{7,23},{8,24},{9,... | collective-permute-start | bytes 1179656 | tf_op jit(solution)/shard_map/ppermute | solution.py:522

commit v6 on v5

--- a/solution.py
+++ b/solution.py
@@ -120,7 +120,7 @@
         ).astype(BF16)
 
 
-def fill(sides, tokens, grads):
+def fill(sides, tokens, grads, weight):
     rows, width = tokens.shape
     slots = PLANE * MOST
     return pl.pallas_call(
@@ -132,7 +132,7 @@
         in_specs=[WHOLE] * 3,
         out_specs=(WHOLE, WHOLE),
         compiler_params=limits(),
-        cost_estimate=cost(4 * slots * rows * width, 8 * slots * width),
+        cost_estimate=cost(weight, 8 * slots * width),
         name="fill",
     )(sides, tokens, grads)
 
@@ -249,35 +249,33 @@
     )(place, rows, *weights)
 
 
+def shard_start(where_ref, core, r, shard):
+    lo = (where_ref[1] + r) & (LO_SIZE - 1)
+    return pl.multiple_of((lo * CORES + core) * shard, shard)
+
+
 def wide_kernel(keep, shard, where_ref, near_x, far_x, near_grads, far_grads, *refs):
     turned, columns = refs[-2:]
     slots = near_x.shape[0]
+    core = where_ref[0] if keep else 1 - where_ref[0]
 
     @pl.when(pl.program_id(0) == 0)
     def _():
-        for z in range(LO_SIZE):
-            span = pl.ds(pl.multiple_of((z * CORES + where_ref[0]) * shard, shard), shard)
-            here = slice(z * shard, (z + 1) * shard)
+        for r in range(LO_SIZE):
+            span = pl.ds(shard_start(where_ref, core, r, shard), shard)
+            here = slice(r * shard, (r + 1) * shard)
             turned[here, :slots] = jnp.transpose(near_x[:, span])
             turned[here, slots:] = jnp.transpose(far_x[:, span])
 
     columns[:slots] = near_grads[...]
     columns[slots:] = far_grads[...]
     total = jnp.dot(turned[...], columns[...], preferred_element_type=F32)
-    if keep:
-        taken_ref, out_ref, first_ref = refs[:3]
-        for z in range(LO_SIZE):
-            part = total[z * shard : (z + 1) * shard] + taken_ref[z].astype(F32)
-            part = part.astype(BF16)
-            out_ref[z] = part
-            if z in (0, LO_SIZE - 1):
-
-                @pl.when((where_ref[1] == 0) == (z != 0))
-                def _():
-                    first_ref[...] = part
-    else:
-        for z in range(LO_SIZE):
-            refs[0][z] = total[z * shard : (z + 1) * shard].astype(BF16)
+    for r in range(LO_SIZE):
+        part = total[r * shard : (r + 1) * shard]
+        if keep:
+            refs[1 + r][...] = (part + refs[0][r].astype(F32)).astype(BF16)
+        else:
+            refs[0][r] = part.astype(BF16)
 
 
 def wide_grads(where, rows, grads, width, taken=None):
@@ -287,33 +285,35 @@
     block = pl.BlockSpec((LO_SIZE, shard, step), lambda n, s: (0, 0, n))
     tokens = pl.BlockSpec((slots, width), lambda n, s: (0, 0))
     part = pl.BlockSpec((slots, step), lambda n, s: (0, n))
-    shape = jax.ShapeDtypeStruct((LO_SIZE, shard, columns), BF16)
-    extra = [] if taken is None else [taken]
-    first = jax.ShapeDtypeStruct((shard, columns), BF16)
-    first_block = pl.BlockSpec((shard, step), lambda n, s: (0, n))
-    return pl.pallas_call(
-        functools.partial(wide_kernel, taken is not None, shard),
+    one = pl.BlockSpec((shard, step), lambda n, s: (0, n))
+    keep = taken is not None
+    if keep:
+        out_shape = (jax.ShapeDtypeStruct((shard, columns), BF16),) * LO_SIZE
+    else:
+        out_shape = jax.ShapeDtypeStruct((LO_SIZE, shard, columns), BF16)
+    return pl.pallas_call(
+        functools.partial(wide_kernel, keep, shard),
         grid_spec=pltpu.PrefetchScalarGridSpec(
             num_scalar_prefetch=1,
             grid=(columns // step,),
-            in_specs=[tokens, tokens, part, part] + [block] * len(extra),
-            out_specs=(block, first_block) if extra else block,
+            in_specs=[tokens, tokens, part, part] + ([block] if keep else []),
+            out_specs=(one,) * LO_SIZE if keep else block,
             scratch_shapes=[
                 pltpu.VMEM((LO_SIZE * shard, 2 * slots), BF16),
                 pltpu.VMEM((2 * slots, step), BF16),
             ],
         ),
-        out_shape=(shape, first) if extra else shape,
+        out_shape=out_shape,
         compiler_params=limits(),
         cost_estimate=cost(2 * slots * width * columns, 2 * width * columns),
         name="wide",
-    )(where, *rows, *grads, *extra)
+    )(where, *rows, *grads, *([taken] if keep else []))
 
 
 def down_kernel(
-    core_ref, near_hidden, far_hidden, near_pick, far_pick, give_ref, keep_ref, turned, columns, acc
+    where_ref, near_hidden, far_hidden, near_pick, far_pick, give_ref, keep_ref, turned, columns, acc
 ):
-    core = core_ref[0]
+    core = where_ref[0]
     shard = give_ref.shape[1]
     slots = near_hidden.shape[0]
 
@@ -325,13 +325,13 @@
     columns[:slots] = near_pick[...]
     columns[slots:] = far_pick[...]
     acc[...] = jnp.dot(turned[...], columns[...], preferred_element_type=F32)
-    for z in range(LO_SIZE):
+    for r in range(LO_SIZE):
         for which, ref in ((1 - core, give_ref), (core, keep_ref)):
-            start = pl.multiple_of((z * CORES + which) * shard, shard)
-            ref[z] = acc[pl.ds(start, shard), :].astype(BF16)
-
-
-def down_grads(core, hidden, pick):
+            start = shard_start(where_ref, which, r, shard)
+            ref[r] = acc[pl.ds(start, shard), :].astype(BF16)
+
+
+def down_grads(where, hidden, pick):
     slots, hidden_width = hidden[0].shape
     width = pick[0].shape[1]
     shard = hidden_width // (LO_SIZE * CORES)
@@ -357,7 +357,7 @@
         compiler_params=limits(),
         cost_estimate=cost(4 * slots * width * hidden_width, 4 * width * hidden_width),
         name="down",
-    )(core, *hidden, *pick)
+    )(where, *hidden, *pick)
 
 
 def turned_picks(picked_ref):
@@ -438,31 +438,47 @@
     )(half, ids, picked, returned, far_total)
 
 
-def neighbours(steps):
-    return [(a * CORES + core, b * CORES + core) for a, b in steps for core in range(CORES)]
-
-
 def core_swap(give):
     return lax.ppermute(give, "dp", [(i, i ^ 1) for i in range(LO_SIZE * CORES)])
 
 
-def shard_of(parts, index):
-    index = jnp.clip(index, 0, LO_SIZE - 1)
-    return lax.dynamic_index_in_dim(parts, index, axis=0, keepdims=False).astype(F32)
-
-
-def line_sum(parts, first, lo):
-    arrived = lax.ppermute(first, "dp", neighbours([(0, 1), (3, 2)])).astype(F32)
-    up = (shard_of(parts, lo + 2) + arrived).astype(BF16)
-    down = (shard_of(parts, lo - 2) + arrived).astype(BF16)
-    middle = up
-    up = lax.ppermute(up, "dp", neighbours([(0, 1), (1, 2)]))
-    down = lax.ppermute(down, "dp", neighbours([(3, 2), (2, 1)]))
-    up = (shard_of(parts, lo + 1) + up.astype(F32)).astype(BF16)
-    down = (shard_of(parts, lo - 1) + down.astype(F32)).astype(BF16)
-    up = lax.ppermute(up, "dp", neighbours([(0, 1), (1, 2), (2, 3)])).astype(F32)
-    down = lax.ppermute(down, "dp", neighbours([(3, 2), (2, 1), (1, 0)])).astype(F32)
-    return (shard_of(parts, lo) + up + down).astype(BF16), middle
+def shift(value, distance, leave=()):
+    pairs = [(lo, (lo + distance) % LO_SIZE) for lo in range(LO_SIZE) if lo not in leave]
+    pairs = [(a * CORES + c, b * CORES + c) for a, b in pairs for c in range(CORES)]
+    return lax.ppermute(value, "dp", pairs)
+
+
+def between_halves(value, steps):
+    experts = lax.axis_size("expert")
+    pairs = [
+        ((a * CORES + c) * experts + e, (b * CORES + c) * experts + (e ^ Y_SIZE))
+        for a, b in steps
+        for c in range(CORES)
+        for e in range(experts)
+    ]
+    return lax.ppermute(value, BOTH, pairs)
+
+
+def total(terms):
+    result = terms[0].astype(F32)
+    for term in terms[1:]:
+        result = result + term.astype(F32)
+    return result.astype(BF16)
+
+
+def line_sums(wide, down):
+    last = LO_SIZE - 1
+    half_way = between_halves(wide[2], [(0, last), (last, 0)])
+    wide_one = shift(wide[1], 1)
+    half_way, wide_one, down_send = lax.optimization_barrier((half_way, wide_one, down[1]))
+    down_one = shift(down_send, 1)
+    relayed = between_halves(half_way, [(last, 2), (0, 1)])
+    direct = shift(wide[2], 2, leave=(0, last))
+    wide_three = shift(wide[3], 3)
+    wide_three, down_one = lax.optimization_barrier((wide_three, down_one))
+    wide_sum = total([wide[0], wide_one, direct, wide_three, relayed])
+    down_sum = total([down[0], down_one, shift(down[2], 2), shift(down[3], 3)])
+    return wide_sum, down_sum
 
 
 def on_device(tokens, out_grad, expert_ids, route_gates, swap_flags, gate_proj, up_proj, down_proj):
@@ -473,8 +489,7 @@
     half = ((my_expert // Y_SIZE) % HI_SIZE).astype(jnp.int32)[None]
     place = (my_expert % Y_SIZE) * X_SIZE + my_expert // (HI_SIZE * Y_SIZE)
     place = place.astype(jnp.int32)[None]
-    here = core.astype(jnp.int32)[None]
-    line = lo.astype(jnp.int32)[None]
+    where = jnp.stack([core, lo]).astype(jnp.int32)
     width = tokens.shape[1]
     hidden_width = gate_proj.shape[2]
     weights = (gate_proj[0], up_proj[0], down_proj[0])
@@ -483,10 +498,9 @@
     far_out_grad = across(out_grad)
     own_sides, far_sides = route(half, expert_ids, route_gates)
     far_sides = across(far_sides)
-    far_tokens, far_sides, own_sides = lax.optimization_barrier((far_tokens, far_sides, own_sides))
-    near_blocks, near_picked = fill(own_sides, tokens, out_grad)
+    near_blocks, near_picked = fill(own_sides, tokens, out_grad, 10**9)
     near_rows = to_plane(near_blocks.reshape(PLANE, MOST, -1)).reshape(PLANE * MOST, -1)
-    far_blocks, far_picked = fill(far_sides, far_tokens, far_out_grad)
+    far_blocks, far_picked = fill(far_sides, far_tokens, far_out_grad, 10**12)
     far_blocks, near_blocks = lax.optimization_barrier((far_blocks, near_blocks))
     far_rows = to_plane(far_blocks.reshape(PLANE, MOST, -1)).reshape(PLANE * MOST, -1)
 
@@ -494,23 +508,20 @@
     far_back, far_hidden, far_pick, far_grads = run_expert(place, far_rows, weights)
 
     rows, grads = (near_rows, far_rows), (near_grads, far_grads)
-    give = wide_grads(jnp.concatenate([1 - here, line]), rows, grads, width)
+    give = wide_grads(where, rows, grads, width)
     taken = core_swap(give)
     far_back, give = lax.optimization_barrier((far_back, give))
     far_returned = to_plane(far_back)
-    give_down, keep_down = down_grads(here, (near_hidden, far_hidden), (near_pick, far_pick))
+    give_down, keep_down = down_grads(where, (near_hidden, far_hidden), (near_pick, far_pick))
     taken, keep_down = lax.optimization_barrier((taken, keep_down))
-    gate_up_parts, first = wide_grads(jnp.concatenate([here, line]), rows, grads, width, taken)
-    give_down, first = lax.optimization_barrier((give_down, first))
+    gate_up_parts = wide_grads(where, rows, grads, width, taken)
+    give_down, unused = lax.optimization_barrier((give_down, gate_up_parts[0]))
     taken_down = core_swap(give_down)
-    gate_up_sum, middle = line_sum(gate_up_parts, first, lo)
-    down_parts = (keep_down.astype(F32) + taken_down.astype(F32)).astype(BF16)
-    first_down = jnp.where(lo == 0, down_parts[LO_SIZE - 1], down_parts[0])
-    down_sum, unused = line_sum(down_parts, first_down, lo)
+    down_parts = [total([keep_down[r], taken_down[r]]) for r in range(LO_SIZE)]
+    gate_up_sum, down_sum = line_sums(gate_up_parts, down_parts)
 
     near_back, far_returned = lax.optimization_barrier((near_back, far_returned))
     near_returned = to_plane(near_back)
-    far_returned, middle = lax.optimization_barrier((far_returned, middle))
     far_total = across(collect(far_picked, far_returned))
     layer_out, grad_tokens, gate_grads = finish(
         half, expert_ids, near_picked, near_returned, far_total

time: 270 us -> 275 us (1.019)
  waiting for transfers between devices: 115 us -> 128 us
  starting transfers between devices: 70.4 us -> 60.5 us
  local copies, waits for them, and re-layouts: 17.9 us -> 25.2 us
  other arithmetic: 16.9 us -> 9.79 us
    ppermute x10 -> x8, waiting for transfers between devices: 39.8 us -> 68.4 us  [the longest x6 68.4 us: shift(): return lax.ppermute(value, 'dp', pairs)]
    ppermute x1, waiting for transfers between devices: 0.01 us -> 10.7 us  [on_device(): other_gate_up = lax.ppermute(gate_up_sum, 'expert', swap)]
    ppermute x10 -> x8, starting transfers between devices: 27.7 us -> 17.3 us  [the longest x6 9 us: shift(): return lax.ppermute(value, 'dp', pairs)]
    all_to_all x4, waiting for transfers between devices: 32.3 us -> 22.5 us  [to_plane(): lax.all_to_all(blocks, 'expert', split_axis=0, concat_axis=0, axis_index_...]
    ppermute x4, waiting for transfers between devices: 36.1 us -> 26.7 us  [across(): return lax.ppermute(value, BOTH, pairs)]
    convert_element_type x7 -> x3, other arithmetic: 15.1 us -> 6.71 us  [total(): return result.astype(BF16)]
    unnamed x41 -> x53, local copies, waits for them, and re-layouts: 16.4 us -> 23.7 us
    ppermute x1, waiting for transfers between devices: 5.28 us -> 0.01 us  [on_device(): other_down = lax.ppermute(down_sum, 'expert', swap)]
  transfers between devices with their start and end apart: 22 -> 20, of which waited for: 11 -> 10; matrix products, arithmetic and copies ran while one was open for 8% -> 5% of each run, Pallas kernels for 8% -> 11%
where the time goes in v6:
time: 275 us; the launch traced here: 273 us
  waiting for transfers between devices  128 us (47%)
  starting transfers between devices  60.5 us (22%)
  Pallas kernels  48 us (17%)
  local copies, waits for them, and re-layouts  25.2 us (9%)
  other arithmetic  9.79 us (4%)
    ppermute x6, waiting for transfers between devices, shift(): return lax.ppermute(value, 'dp', pairs)  68.4 us
    all_to_all x4, starting transfers between devices, to_plane(): lax.all_to_all(blocks, 'expert', split_axis=0, concat_axis=0, axis_index_...  27.8 us
    ppermute x4, waiting for transfers between devices, across(): return lax.ppermute(value, BOTH, pairs)  26.7 us
    unnamed x53, local copies, waits for them, and re-layouts  23.7 us
    all_to_all x4, waiting for transfers between devices, to_plane(): lax.all_to_all(blocks, 'expert', split_axis=0, concat_axis=0, axis_index_...  22.5 us
    pallas_call x2, Pallas kernels, run_expert(): pl.pallas_call(expert_kernel, out_shape=(jax.ShapeDtypeStruct((PLANE, MOS...  22.3 us
    pallas_call x2, Pallas kernels, wide_grads(): pl.pallas_call(functools.partial(wide_kernel, keep, shard), grid_spec=plt...  12.4 us
    ppermute x1, waiting for transfers between devices, on_device(): other_gate_up = lax.ppermute(gate_up_sum, 'expert', swap)  10.7 us
  transfers between devices with their start and end apart: 20, of which 10 were waited for; matrix products, arithmetic and copies ran while one was open for 5% of the time, Pallas kernels for 11%

profile of v6, /device:TPU:16, one launch (start us, length us, event | category | flops | bytes accessed | tf_op | source)
XLA Modules:
  0.0 273.3 jit_solution(2525624603390087853)
XLA Ops:
  0.6 5.9 %collective-permute-start.1 = (bf16[128,2048]{1,0:T(8,128)(2,1)}, bf16[128,2048]{1,0:T(8,128)(2,1)S(1)}, u32[]{:S(2)}, u32[]{:S(2)}) collective-permute-start(bf16[128,2048]{1,0:T(8,128)(2,1)} %tokens_ref.1), channel_id=1, source_target_pairs={{0,196},{1,197},{2,198},{3,199},{4,192},{5,193},{6,194},{7,195},{8... | collective-permute-start | bytes 1572872 | tf_op jit(solution)/shard_map/ppermute | solution.py:46
  6.6 0.1 collective-permute-start.2
  6.7 1.4 copy.16.ids_ref
  8.1 1.4 copy.15.gates_ref
  9.5 2.1 route.1
  11.6 3.1 %collective-permute-start = (bf16[128,128]{1,0:T(8,128)(2,1)}, bf16[128,128]{1,0:T(8,128)(2,1)S(1)}, u32[]{:S(2)}, u32[]{:S(2)}) collective-permute-start(bf16[128,128]{1,0:T(8,128)(2,1)} %get-tuple-element.45), channel_id=1, source_target_pairs={{0,196},{1,197},{2,198},{3,199},{4,192},{5,193},{6,194},{7,195},{8... | collective-permute-start | bytes 98312 | tf_op jit(solution)/shard_map/ppermute | solution.py:46
  14.8 1.0 copy-done.11
  15.8 1.0 copy-done.12
  16.9 0.8 copy-done.13
  17.6 2.3 fill.2
  19.9 7.3 %all-to-all-start = ((bf16[16,16,4224]{2,1,0:T(8,128)(2,1)}), bf16[16,16,4224]{2,1,0:T(8,128)(2,1)}, u32[]{:S(2)}, u32[]{:S(2)}) async-start(bf16[16,16,4224]{2,1,0:T(8,128)(2,1)} %bitcast.2), calls=%async_computation | async-start | bytes 4325376 | tf_op jit(solution)/shard_map/all_to_all | solution.py:50
  27.2 26.6 %collective-permute-done.sides_ref = bf16[128,128]{1,0:T(8,128)(2,1)S(1)} collective-permute-done((bf16[128,128]{1,0:T(8,128)(2,1)}, bf16[128,128]{1,0:T(8,128)(2,1)S(1)}, u32[]{:S(2)}, u32[]{:S(2)}) %collective-permute-start) | collective-permute-done | bytes 32800 | tf_op jit(solution)/shard_map/ppermute | solution.py:46
  53.8 0.9 fill.3
  54.7 1.4 copy-done.5
  56.1 7.3 %all-to-all-start.1 = ((bf16[16,16,4224]{2,1,0:T(8,128)(2,1)}), bf16[16,16,4224]{2,1,0:T(8,128)(2,1)S(1)}, u32[]{:S(2)}, u32[]{:S(2)}) async-start(bf16[16,16,4224]{2,1,0:T(8,128)(2,1)} %bitcast.32), calls=%async_computation.1 | async-start | bytes 4325376 | tf_op jit(solution)/shard_map/all_to_all | solution.py:50
  63.5 11.2 %expert.2 = (bf16[16,16,4224]{2,1,0:T(8,128)(2,1)S(1)}, bf16[256,768]{1,0:T(8,128)(2,1)S(1)}, bf16[256,2048]{1,0:T(8,128)(2,1)S(1)}, bf16[256,1536]{1,0:T(8,128)(2,1)S(1)}) custom-call(s32[1]{0:T(128)} %bitcast.1.place_ref, bf16[256,4224]{1,0:T(8,128)(2,1)} %bitcast.3.rows_ref.near_x, bf16[2048,768]{1,0:T(8,128)(2,1)} %bitcast.33, ...), custom_call_target="tpu_custom_call" | custom-call | flops 4831838208 | bytes 9437184 | tf_op jit(solution)/shard_map/expert/pallas_call | solution.py:230
  74.6 1.4 copy-done.4
  76.1 1.0 copy-done.14
  77.0 0.7 copy-done.18
  77.8 15.1 %all-to-all-done.1 = bf16[16,16,4224]{2,1,0:T(8,128)(2,1)S(1)} async-done(((bf16[16,16,4224]{2,1,0:T(8,128)(2,1)}), bf16[16,16,4224]{2,1,0:T(8,128)(2,1)S(1)}, u32[]{:S(2)}, u32[]{:S(2)}) %all-to-all-start.1) | async-done | bytes 2162720 | tf_op jit(solution)/shard_map/all_to_all | solution.py:50
  92.8 1.3 copy-done
  94.1 11.1 %expert.3 = (bf16[16,16,4224]{2,1,0:T(8,128)(2,1)S(1)}, bf16[256,768]{1,0:T(8,128)(2,1)S(1)}, bf16[256,2048]{1,0:T(8,128)(2,1)S(1)}, bf16[256,1536]{1,0:T(8,128)(2,1)S(1)}) custom-call(s32[1]{0:T(128)} %bitcast.1.place_ref, bf16[256,4224]{1,0:T(8,128)(2,1)} %bitcast.29, bf16[2048,768]{1,0:T(8,128)(2,1)} %bitcast.34, bf16[2048,768]{1,0:T(8,128)(2,1)} %bitcast.36, ...), custom_call_target="tpu_custom_call" | custom-call | flops 4831838208 | bytes 9437184 | tf_op jit(solution)/shard_map/expert/pallas_call | solution.py:230
  105.3 1.4 copy-done.6
  106.7 1.0 copy-done.16
  107.7 0.7 copy-done.20
  108.5 1.9 copy-done.1
  110.3 5.7 %wide.2 = bf16[4,256,1536]{2,1,0:T(8,128)(2,1)} custom-call(s32[2]{0:T(128)S(1)} %pad_add_fusion.where_ref, bf16[256,4224]{1,0:T(8,128)(2,1)} %bitcast.3.rows_ref.near_x, bf16[256,4224]{1,0:T(8,128)(2,1)S(1)} %bitcast.31, bf16[256,1536]{1,0:T(8,128)(2,1)S(1)} %get-tuple-element.49.near_grads, bf16[256,1536]{1,0:T(8,128)(2,1)S(1)} %get-tuple-element.50.far_grads), custom_call_target="tpu_custom_call" | custom-call | flops 1610612736 | bytes 6291456 | tf_op jit(solution)/shard_map/wide/pallas_call | solution.py:294
  116.0 6.1 %all-to-all-start.2 = ((bf16[16,16,4224]{2,1,0:T(8,128)(2,1)}), bf16[16,16,4224]{2,1,0:T(8,128)(2,1)S(1)}, u32[]{:S(2)}, u32[]{:S(2)}) async-start(bf16[16,16,4224]{2,1,0:T(8,128)(2,1)} %copy-done.6), calls=%async_computation.2 | async-start | bytes 4325376 | tf_op jit(solution)/shard_map/all_to_all | solution.py:50
  122.1 1.2 copy-done.15
  123.4 1.2 copy-done.17
  124.6 1.0 copy-done.19
  125.6 1.0 copy-done.21
  126.6 4.5 %down.1 = (bf16[4,96,2048]{2,1,0:T(8,128)(2,1)}, bf16[4,96,2048]{2,1,0:T(8,128)(2,1)S(1)}) custom-call(s32[2]{0:T(128)S(1)} %pad_add_fusion.where_ref, bf16[256,768]{1,0:T(8,128)(2,1)S(1)} %copy-done.19, bf16[256,768]{1,0:T(8,128)(2,1)S(1)} %copy-done.21, bf16[256,2048]{1,0:T(8,128)(2,1)S(1)} %copy-done.15, bf16[256,2048]{1,0:T(8,128)(2,1)S(1)} %copy-done.17), custom_call_target="tpu_custom_call" | custom-call | flops 1610612736 | bytes 6291456 | tf_op jit(solution)/shard_map/down/pallas_call | solution.py:343
  131.1 1.1 copy-done.7
  132.3 6.7 %wide.3 = (bf16[256,1536]{1,0:T(8,128)(2,1)S(1)}, bf16[256,1536]{1,0:T(8,128)(2,1)}, bf16[256,1536]{1,0:T(8,128)(2,1)}, bf16[256,1536]{1,0:T(8,128)(2,1)}) custom-call(s32[2]{0:T(128)S(1)} %pad_add_fusion.where_ref, bf16[256,4224]{1,0:T(8,128)(2,1)} %bitcast.3.rows_ref.near_x, bf16[256,4224]{1,0:T(8,128)(2,1)} %bitcast.30, ...), custom_call_target="tpu_custom_call" | custom-call | flops 1610612736 | bytes 6291456 | tf_op jit(solution)/shard_map/wide/pallas_call | solution.py:294
  139.0 0.9 copy-done.8
  139.9 0.2 collective-permute-start.7
  140.1 3.6 %collective-permute-start.5 = (bf16[256,1536]{1,0:T(8,128)(2,1)}, bf16[256,1536]{1,0:T(8,128)(2,1)}, u32[]{:S(2)}, u32[]{:S(2)}) collective-permute-start(bf16[256,1536]{1,0:T(8,128)(2,1)} %get-tuple-element.65), channel_id=1, source_target_pairs={{0,196},{1,197},{2,198},{3,199},{4,192},{5,193},{6,194},{7,195},{8... | collective-permute-start | bytes 2359304 | tf_op jit(solution)/shard_map/ppermute | solution.py:459
  143.7 0.1 collective-permute-start.6
  143.8 3.8 %collective-permute-start.9 = (bf16[256,1536]{1,0:T(8,128)(2,1)}, bf16[256,1536]{1,0:T(8,128)(2,1)}, u32[]{:S(2)}, u32[]{:S(2)}) collective-permute-start(bf16[256,1536]{1,0:T(8,128)(2,1)} %get-tuple-element.71), channel_id=1, source_target_pairs={{0,192},{32,224},{64,0},{96,32},{128,64},{160,96},{192,128},{224,1... | collective-permute-start | bytes 2359304 | tf_op jit(solution)/shard_map/ppermute | solution.py:448
  147.6 7.5 %all-to-all-done.2.returned_ref = bf16[16,16,4224]{2,1,0:T(8,128)(2,1)S(1)} async-done(((bf16[16,16,4224]{2,1,0:T(8,128)(2,1)}), bf16[16,16,4224]{2,1,0:T(8,128)(2,1)S(1)}, u32[]{:S(2)}, u32[]{:S(2)}) %all-to-all-start.2) | async-done | bytes 2162720 | tf_op jit(solution)/shard_map/all_to_all | solution.py:50
  155.1 7.1 %all-to-all-start.3 = ((bf16[16,16,4224]{2,1,0:T(8,128)(2,1)}), bf16[16,16,4224]{2,1,0:T(8,128)(2,1)}, u32[]{:S(2)}, u32[]{:S(2)}) async-start(bf16[16,16,4224]{2,1,0:T(8,128)(2,1)} %copy-done.4), calls=%async_computation.3 | async-start | bytes 4325376 | tf_op jit(solution)/shard_map/all_to_all | solution.py:50
  162.2 2.0 fusion.5
  164.3 2.0 collective-permute-done.6
  166.2 3.8 %collective-permute-start.14 = (bf16[96,2048]{1,0:T(8,128)(2,1)S(1)}, bf16[96,2048]{1,0:T(8,128)(2,1)S(1)}, u32[]{:S(2)}, u32[]{:S(2)}) collective-permute-start(bf16[96,2048]{1,0:T(8,128)(2,1)S(1)} %get-tuple-element.83), channel_id=1, source_target_pairs={{0,192},{32,224},{64,0},{96,32},{128,64},{160,96},{192,128},{224,1... | collective-permute-start | bytes 1179656 | tf_op jit(solution)/shard_map/ppermute | solution.py:448
  170.1 1.3 collective-permute-start.8
  171.4 10.2 %collective-permute-done.9 = bf16[256,1536]{1,0:T(8,128)(2,1)} collective-permute-done((bf16[256,1536]{1,0:T(8,128)(2,1)}, bf16[256,1536]{1,0:T(8,128)(2,1)}, u32[]{:S(2)}, u32[]{:S(2)}) %collective-permute-start.9) | collective-permute-done | bytes 786464 | tf_op jit(solution)/shard_map/ppermute | solution.py:448
  181.6 4.7 %collective-permute-start.11 = (bf16[256,1536]{1,0:T(8,128)(2,1)}, bf16[256,1536]{1,0:T(8,128)(2,1)S(1)}, u32[]{:S(2)}, u32[]{:S(2)}) collective-permute-start(bf16[256,1536]{1,0:T(8,128)(2,1)} %collective-permute-done.5), channel_id=1, source_target_pairs={{192,132},{193,133},{194,134},{195,135},{196,128},{197,129},{198,1... | collective-permute-start | bytes 2359304 | tf_op jit(solution)/shard_map/ppermute | solution.py:459
  186.3 0.5 collect.1
  186.8 21.6 %collective-permute-done.10 = bf16[96,2048]{1,0:T(8,128)(2,1)S(1)} collective-permute-done((bf16[96,2048]{1,0:T(8,128)(2,1)S(1)}, bf16[96,2048]{1,0:T(8,128)(2,1)S(1)}, u32[]{:S(2)}, u32[]{:S(2)}) %collective-permute-start.10) | collective-permute-done | bytes 393248 | tf_op jit(solution)/shard_map/ppermute | solution.py:448
  208.4 4.2 %collective-permute-done.14 = bf16[96,2048]{1,0:T(8,128)(2,1)S(1)} collective-permute-done((bf16[96,2048]{1,0:T(8,128)(2,1)S(1)}, bf16[96,2048]{1,0:T(8,128)(2,1)S(1)}, u32[]{:S(2)}, u32[]{:S(2)}) %collective-permute-start.14) | collective-permute-done | bytes 393248 | tf_op jit(solution)/shard_map/ppermute | solution.py:448
  212.6 16.5 %collective-permute-done.13 = bf16[96,2048]{1,0:T(8,128)(2,1)S(1)} collective-permute-done((bf16[96,2048]{1,0:T(8,128)(2,1)S(1)}, bf16[96,2048]{1,0:T(8,128)(2,1)S(1)}, u32[]{:S(2)}, u32[]{:S(2)}) %collective-permute-start.13) | collective-permute-done | bytes 393248 | tf_op jit(solution)/shard_map/ppermute | solution.py:448
  229.1 2.2 fusion.2
  231.2 3.0 %collective-permute-start.15 = (bf16[96,2048]{1,0:T(8,128)(2,1)}, bf16[96,2048]{1,0:T(8,128)(2,1)}, u32[]{:S(2)}, u32[]{:S(2)}) collective-permute-start(bf16[96,2048]{1,0:T(8,128)(2,1)} %fusion.2), channel_id=1, source_target_pairs={{0,16},{1,17},{2,18},{3,19},{4,20},{5,21},{6,22},{7,23},{8,24},{9,... | collective-permute-start | bytes 1179656 | tf_op jit(solution)/shard_map/ppermute | solution.py:533
  234.2 14.0 %collective-permute-done.8 = bf16[256,1536]{1,0:T(8,128)(2,1)S(1)} collective-permute-done((bf16[256,1536]{1,0:T(8,128)(2,1)}, bf16[256,1536]{1,0:T(8,128)(2,1)S(1)}, u32[]{:S(2)}, u32[]{:S(2)}) %collective-permute-start.8) | collective-permute-done | bytes 786464 | tf_op jit(solution)/shard_map/ppermute | solution.py:448
  248.2 2.5 add_convert_fusion
  250.7 3.0 %collective-permute-start.12 = (bf16[256,1536]{1,0:T(8,128)(2,1)}, bf16[256,1536]{1,0:T(8,128)(2,1)}, u32[]{:S(2)}, u32[]{:S(2)}) collective-permute-start(bf16[256,1536]{1,0:T(8,128)(2,1)} %add_convert_fusion), channel_id=1, source_target_pairs={{0,16},{1,17},{2,18},{3,19},{4,20},{5,21},{6,22},{7,23},{8,24},{9,... | collective-permute-start | bytes 2359304 | tf_op jit(solution)/shard_map/ppermute | solution.py:532
  253.7 0.6 dynamic_slice.3
  255.0 3.0 %finish.1 = (bf16[128,2048]{1,0:T(8,128)(2,1)}, bf16[128,2048]{1,0:T(8,128)(2,1)}, f32[128,8]{1,0:T(8,128)S(1)}) custom-call(s32[1]{0:T(128)} %bitcast.half_ref, s32[128,8]{1,0:T(8,128)S(1)} %copy-done.10, bf16[256,128]{1,0:T(8,128)(2,1)S(1)} %get-tuple-element.42.picked_ref, bf16[16,16,4224]{2,1,0:T(8,128)(2,1)} %all-to-all-done.3.returned_ref, ...), custom_call_target="tpu_custom_call" | custom-call | flops 276824064 | bytes 2162688 | tf_op jit(solution)/shard_map/finish/pallas_call | solution.py:430
  258.0 0.7 copy.17
  258.7 1.8 select_bitcast_fusion
  260.4 10.7 %collective-permute-done.12 = bf16[256,1536]{1,0:T(8,128)(2,1)} collective-permute-done((bf16[256,1536]{1,0:T(8,128)(2,1)}, bf16[256,1536]{1,0:T(8,128)(2,1)}, u32[]{:S(2)}, u32[]{:S(2)}) %collective-permute-start.12) | collective-permute-done | bytes 786464 | tf_op jit(solution)/shard_map/ppermute | solution.py:532
  271.1 1.2 broadcast_select_fusion
  272.4 0.9 slice_bitcast_fusion
  (47 shorter events, 0.2 us)
Async XLA Ops:
  0.6 53.2 %collective-permute-start.1 = (bf16[128,2048]{1,0:T(8,128)(2,1)}, bf16[128,2048]{1,0:T(8,128)(2,1)S(1)}, u32[]{:S(2)}, u32[]{:S(2)}) collective-permute-start(bf16[128,2048]{1,0:T(8,128)(2,1)} %tokens_ref.1), channel_id=1, source_target_pairs={{0,196},{1,197},{2,198},{3,199},{4,192},{5,193},{6,194},{7,195},{8... | collective-permute-start | bytes 1572872 | tf_op jit(solution)/shard_map/ppermute | solution.py:46
  6.6 47.3 %collective-permute-start.2 = (bf16[128,2048]{1,0:T(8,128)(2,1)}, bf16[128,2048]{1,0:T(8,128)(2,1)S(1)}, u32[]{:S(2)}, u32[]{:S(2)}) collective-permute-start(bf16[128,2048]{1,0:T(8,128)(2,1)} %grads_ref.1), channel_id=1, source_target_pairs={{0,196},{1,197},{2,198},{3,199},{4,192},{5,193},{6,194},{7,195},{8... | collective-permute-start | bytes 1572872 | tf_op jit(solution)/shard_map/ppermute | solution.py:46
  11.6 42.2 %collective-permute-start = (bf16[128,128]{1,0:T(8,128)(2,1)}, bf16[128,128]{1,0:T(8,128)(2,1)S(1)}, u32[]{:S(2)}, u32[]{:S(2)}) collective-permute-start(bf16[128,128]{1,0:T(8,128)(2,1)} %get-tuple-element.45), channel_id=1, source_target_pairs={{0,196},{1,197},{2,198},{3,199},{4,192},{5,193},{6,194},{7,195},{8... | collective-permute-start | bytes 98312 | tf_op jit(solution)/shard_map/ppermute | solution.py:46
  14.8 1.0 copy-start.11
  15.8 1.0 copy-start.12
  16.9 0.8 copy-start.13
  19.9 36.2 %all-to-all-start = ((bf16[16,16,4224]{2,1,0:T(8,128)(2,1)}), bf16[16,16,4224]{2,1,0:T(8,128)(2,1)}, u32[]{:S(2)}, u32[]{:S(2)}) async-start(bf16[16,16,4224]{2,1,0:T(8,128)(2,1)} %bitcast.2), calls=%async_computation | async-start | bytes 4325376 | tf_op jit(solution)/shard_map/all_to_all | solution.py:50
  54.7 1.4 copy-start.5
  56.1 36.7 %all-to-all-start.1 = ((bf16[16,16,4224]{2,1,0:T(8,128)(2,1)}), bf16[16,16,4224]{2,1,0:T(8,128)(2,1)S(1)}, u32[]{:S(2)}, u32[]{:S(2)}) async-start(bf16[16,16,4224]{2,1,0:T(8,128)(2,1)} %bitcast.32), calls=%async_computation.1 | async-start | bytes 4325376 | tf_op jit(solution)/shard_map/all_to_all | solution.py:50
  74.6 1.4 copy-start.4
  76.0 1.0 copy-start.14
  77.0 0.7 copy-start.18
  92.8 1.3 copy-start
  105.3 1.4 copy-start.6
  106.7 1.0 copy-start.16
  107.7 0.7 copy-start.20
  108.4 7.6 %copy-start.2 = (bf16[256,1536]{1,0:T(8,128)(2,1)}, bf16[256,1536]{1,0:T(8,128)(2,1)S(1)}, u32[]{:S(2)}) copy-start(bf16[256,1536]{1,0:T(8,128)(2,1)S(1)} %get-tuple-element.50.far_grads) | copy-start | bytes 2359300
  108.5 1.9 copy-start.1
  116.0 16.2 %collective-permute-start.4 = (bf16[4,256,1536]{2,1,0:T(8,128)(2,1)}, bf16[4,256,1536]{2,1,0:T(8,128)(2,1)}, u32[]{:S(2)}, u32[]{:S(2)}) collective-permute-start(bf16[4,256,1536]{2,1,0:T(8,128)(2,1)} %wide.2), channel_id=1, source_target_pairs={{0,32},{32,0},{64,96},{96,64},{128,160},{160,128},{192,224},{224,1... | collective-permute-start | bytes 9437192 | tf_op jit(solution)/shard_map/ppermute | solution.py:442
  116.0 39.0 %all-to-all-start.2 = ((bf16[16,16,4224]{2,1,0:T(8,128)(2,1)}), bf16[16,16,4224]{2,1,0:T(8,128)(2,1)S(1)}, u32[]{:S(2)}, u32[]{:S(2)}) async-start(bf16[16,16,4224]{2,1,0:T(8,128)(2,1)} %copy-done.6), calls=%async_computation.2 | async-start | bytes 4325376 | tf_op jit(solution)/shard_map/all_to_all | solution.py:50
  122.1 1.2 copy-start.15
  123.4 1.2 copy-start.17
  124.6 1.0 copy-start.19
  125.6 1.0 copy-start.21
  126.6 5.7 %copy-start.3 = (bf16[256,1536]{1,0:T(8,128)(2,1)S(1)}, bf16[256,1536]{1,0:T(8,128)(2,1)}, u32[]{:S(2)}) copy-start(bf16[256,1536]{1,0:T(8,128)(2,1)} %copy-done.2) | copy-start | bytes 2359300
  131.1 1.1 copy-start.7
  139.0 0.9 copy-start.8
  139.9 22.4 %collective-permute-start.7 = (bf16[4,96,2048]{2,1,0:T(8,128)(2,1)}, bf16[4,96,2048]{2,1,0:T(8,128)(2,1)}, u32[]{:S(2)}, u32[]{:S(2)}) collective-permute-start(bf16[4,96,2048]{2,1,0:T(8,128)(2,1)} %get-tuple-element.69), channel_id=1, source_target_pairs={{0,32},{32,0},{64,96},{96,64},{128,160},{160,128},{192,224},{224,1... | collective-permute-start | bytes 4718600 | tf_op jit(solution)/shard_map/ppermute | solution.py:442
  140.1 24.2 %collective-permute-start.5 = (bf16[256,1536]{1,0:T(8,128)(2,1)}, bf16[256,1536]{1,0:T(8,128)(2,1)}, u32[]{:S(2)}, u32[]{:S(2)}) collective-permute-start(bf16[256,1536]{1,0:T(8,128)(2,1)} %get-tuple-element.65), channel_id=1, source_target_pairs={{0,196},{1,197},{2,198},{3,199},{4,192},{5,193},{6,194},{7,195},{8... | collective-permute-start | bytes 2359304 | tf_op jit(solution)/shard_map/ppermute | solution.py:459
  143.7 22.5 %collective-permute-start.6 = (bf16[256,1536]{1,0:T(8,128)(2,1)}, bf16[256,1536]{1,0:T(8,128)(2,1)S(1)}, u32[]{:S(2)}, u32[]{:S(2)}) collective-permute-start(bf16[256,1536]{1,0:T(8,128)(2,1)} %get-tuple-element.66), channel_id=1, source_target_pairs={{0,64},{32,96},{64,128},{96,160},{128,192},{160,224},{192,0},{224,... | collective-permute-start | bytes 2359304 | tf_op jit(solution)/shard_map/ppermute | solution.py:448
  143.8 37.8 %collective-permute-start.9 = (bf16[256,1536]{1,0:T(8,128)(2,1)}, bf16[256,1536]{1,0:T(8,128)(2,1)}, u32[]{:S(2)}, u32[]{:S(2)}) collective-permute-start(bf16[256,1536]{1,0:T(8,128)(2,1)} %get-tuple-element.71), channel_id=1, source_target_pairs={{0,192},{32,224},{64,0},{96,32},{128,64},{160,96},{192,128},{224,1... | collective-permute-start | bytes 2359304 | tf_op jit(solution)/shard_map/ppermute | solution.py:448
  155.1 99.9 %all-to-all-start.3 = ((bf16[16,16,4224]{2,1,0:T(8,128)(2,1)}), bf16[16,16,4224]{2,1,0:T(8,128)(2,1)}, u32[]{:S(2)}, u32[]{:S(2)}) async-start(bf16[16,16,4224]{2,1,0:T(8,128)(2,1)} %copy-done.4), calls=%async_computation.3 | async-start | bytes 4325376 | tf_op jit(solution)/shard_map/all_to_all | solution.py:50
  166.2 20.0 %copy-start.22 = (bf16[256,1536]{1,0:T(8,128)(2,1)}, bf16[256,1536]{1,0:T(8,128)(2,1)S(1)}, u32[]{:S(2)}) copy-start(bf16[256,1536]{1,0:T(8,128)(2,1)S(1)} %collective-permute-done.6) | copy-start | bytes 2359300
  166.2 42.2 %collective-permute-start.10 = (bf16[96,2048]{1,0:T(8,128)(2,1)S(1)}, bf16[96,2048]{1,0:T(8,128)(2,1)S(1)}, u32[]{:S(2)}, u32[]{:S(2)}) collective-permute-start(bf16[96,2048]{1,0:T(8,128)(2,1)S(1)} %get-tuple-element.72), channel_id=1, source_target_pairs={{0,64},{32,96},{64,128},{96,160},{128,192},{160,224},{192,0},{224,... | collective-permute-start | bytes 1179656 | tf_op jit(solution)/shard_map/ppermute | solution.py:448
  166.2 46.3 %collective-permute-start.14 = (bf16[96,2048]{1,0:T(8,128)(2,1)S(1)}, bf16[96,2048]{1,0:T(8,128)(2,1)S(1)}, u32[]{:S(2)}, u32[]{:S(2)}) collective-permute-start(bf16[96,2048]{1,0:T(8,128)(2,1)S(1)} %get-tuple-element.83), channel_id=1, source_target_pairs={{0,192},{32,224},{64,0},{96,32},{128,64},{160,96},{192,128},{224,1... | collective-permute-start | bytes 1179656 | tf_op jit(solution)/shard_map/ppermute | solution.py:448
  170.1 59.0 %collective-permute-start.13 = (bf16[96,2048]{1,0:T(8,128)(2,1)S(1)}, bf16[96,2048]{1,0:T(8,128)(2,1)S(1)}, u32[]{:S(2)}, u32[]{:S(2)}) collective-permute-start(bf16[96,2048]{1,0:T(8,128)(2,1)S(1)} %get-tuple-element.82), channel_id=1, source_target_pairs={{0,128},{32,160},{64,192},{96,224},{128,0},{160,32},{192,64},{224,... | collective-permute-start | bytes 1179656 | tf_op jit(solution)/shard_map/ppermute | solution.py:448
  170.1 78.1 %collective-permute-start.8 = (bf16[256,1536]{1,0:T(8,128)(2,1)}, bf16[256,1536]{1,0:T(8,128)(2,1)S(1)}, u32[]{:S(2)}, u32[]{:S(2)}) collective-permute-start(bf16[256,1536]{1,0:T(8,128)(2,1)} %get-tuple-element.65), channel_id=1, source_target_pairs={{64,192},{96,224},{128,0},{160,32},{65,193},{97,225},{129,1},{161,... | collective-permute-start | bytes 2359304 | tf_op jit(solution)/shard_map/ppermute | solution.py:448
  181.6 66.6 %collective-permute-start.11 = (bf16[256,1536]{1,0:T(8,128)(2,1)}, bf16[256,1536]{1,0:T(8,128)(2,1)S(1)}, u32[]{:S(2)}, u32[]{:S(2)}) collective-permute-start(bf16[256,1536]{1,0:T(8,128)(2,1)} %collective-permute-done.5), channel_id=1, source_target_pairs={{192,132},{193,133},{194,134},{195,135},{196,128},{197,129},{198,1... | collective-permute-start | bytes 2359304 | tf_op jit(solution)/shard_map/ppermute | solution.py:459
  186.8 61.4 %copy-start.9 = (bf16[256,1536]{1,0:T(8,128)(2,1)S(1)}, bf16[256,1536]{1,0:T(8,128)(2,1)}, u32[]{:S(2)}) copy-start(bf16[256,1536]{1,0:T(8,128)(2,1)} %copy-done.8) | copy-start | bytes 2359300
  186.8 61.4 %copy-start.23 = (bf16[256,1536]{1,0:T(8,128)(2,1)S(1)}, bf16[256,1536]{1,0:T(8,128)(2,1)}, u32[]{:S(2)}) copy-start(bf16[256,1536]{1,0:T(8,128)(2,1)} %copy-done.22) | copy-start | bytes 2359300
  208.4 46.5 %collective-permute-start.3 = (bf16[128,4224]{1,0:T(8,128)(2,1)S(1)}, bf16[128,4224]{1,0:T(8,128)(2,1)S(1)}, u32[]{:S(2)}, u32[]{:S(2)}) collective-permute-start(bf16[128,4224]{1,0:T(8,128)(2,1)S(1)} %collect.1), channel_id=1, source_target_pairs={{0,196},{1,197},{2,198},{3,199},{4,192},{5,193},{6,194},{7,195},{8... | collective-permute-start | bytes 3244040 | tf_op jit(solution)/shard_map/ppermute | solution.py:46
  231.2 22.5 %copy-start.24 = (s32[32]{0:T(128)S(1)}, s32[32]{0:T(128)}, u32[]{:S(2)}) copy-start(s32[32]{0:T(128)} %param.12) | copy-start | bytes 388
  231.2 23.7 %copy-start.10 = (s32[128,8]{1,0:T(8,128)S(1)}, s32[128,8]{1,0:T(8,128)}, u32[]{:S(2)}) copy-start(s32[128,8]{1,0:T(8,128)} %copy.16.ids_ref) | copy-start | bytes 12292
  231.2 27.4 %collective-permute-start.15 = (bf16[96,2048]{1,0:T(8,128)(2,1)}, bf16[96,2048]{1,0:T(8,128)(2,1)}, u32[]{:S(2)}, u32[]{:S(2)}) collective-permute-start(bf16[96,2048]{1,0:T(8,128)(2,1)} %fusion.2), channel_id=1, source_target_pairs={{0,16},{1,17},{2,18},{3,19},{4,20},{5,21},{6,22},{7,23},{8,24},{9,... | collective-permute-start | bytes 1179656 | tf_op jit(solution)/shard_map/ppermute | solution.py:533
  250.7 20.4 %collective-permute-start.12 = (bf16[256,1536]{1,0:T(8,128)(2,1)}, bf16[256,1536]{1,0:T(8,128)(2,1)}, u32[]{:S(2)}, u32[]{:S(2)}) collective-permute-start(bf16[256,1536]{1,0:T(8,128)(2,1)} %add_convert_fusion), channel_id=1, source_target_pairs={{0,16},{1,17},{2,18},{3,19},{4,20},{5,21},{6,22},{7,23},{8,24},{9,... | collective-permute-start | bytes 2359304 | tf_op jit(solution)/shard_map/ppermute | solution.py:532

commit v7 on v6

--- a/solution.py
+++ b/solution.py
@@ -27,8 +27,12 @@
 ANYWHERE = pl.BlockSpec(memory_space=pl.ANY)
 
 
+def block_of(shape):
+    return pl.BlockSpec(shape, lambda i: (0,) * len(shape))
+
+
 def limits():
-    return pltpu.CompilerParams(vmem_limit_bytes=48 << 20)
+    return pltpu.CompilerParams(vmem_limit_bytes=60 << 20)
 
 
 def cost(flops, moved):
@@ -129,8 +133,9 @@
             jax.ShapeDtypeStruct((slots, 2 * width + SIDE), BF16),
             jax.ShapeDtypeStruct((slots, rows), BF16),
         ),
-        in_specs=[WHOLE] * 3,
-        out_specs=(WHOLE, WHOLE),
+        grid=(1,),
+        in_specs=[block_of(sides.shape), block_of(tokens.shape), block_of(grads.shape)],
+        out_specs=(block_of((slots, 2 * width + SIDE)), block_of((slots, rows))),
         compiler_params=limits(),
         cost_estimate=cost(weight, 8 * slots * width),
         name="fill",
@@ -235,8 +240,14 @@
             jax.ShapeDtypeStruct((slots, width), BF16),
             jax.ShapeDtypeStruct((slots, 2 * hidden_width), BF16),
         ),
-        in_specs=[SCALAR, WHOLE] + [ANYWHERE] * 3,
-        out_specs=(WHOLE,) * 4,
+        grid=(1,),
+        in_specs=[SCALAR, block_of(rows.shape)] + [ANYWHERE] * 3,
+        out_specs=(
+            block_of((PLANE, MOST, full)),
+            block_of((slots, hidden_width)),
+            block_of((slots, width)),
+            block_of((slots, 2 * hidden_width)),
+        ),
         scratch_shapes=[
             pltpu.VMEM((width, hidden_width), BF16),
             pltpu.VMEM((width, hidden_width), BF16),
@@ -273,7 +284,12 @@
     for r in range(LO_SIZE):
         part = total[r * shard : (r + 1) * shard]
         if keep:
-            refs[1 + r][...] = (part + refs[0][r].astype(F32)).astype(BF16)
+            part = (part + refs[0][r].astype(F32)).astype(BF16)
+            refs[1 + r][...] = part
+            if r & 1:
+                @pl.when((where_ref[1] == 0) == (r != 1))
+                def _():
+                    refs[1 + LO_SIZE][...] = part
         else:
             refs[0][r] = part.astype(BF16)
 
@@ -288,7 +304,7 @@
     one = pl.BlockSpec((shard, step), lambda n, s: (0, n))
     keep = taken is not None
     if keep:
-        out_shape = (jax.ShapeDtypeStruct((shard, columns), BF16),) * LO_SIZE
+        out_shape = (jax.ShapeDtypeStruct((shard, columns), BF16),) * (LO_SIZE + 1)
     else:
         out_shape = jax.ShapeDtypeStruct((LO_SIZE, shard, columns), BF16)
     return pl.pallas_call(
@@ -297,7 +313,7 @@
             num_scalar_prefetch=1,
             grid=(columns // step,),
             in_specs=[tokens, tokens, part, part] + ([block] if keep else []),
-            out_specs=(one,) * LO_SIZE if keep else block,
+            out_specs=(one,) * (LO_SIZE + 1) if keep else block,
             scratch_shapes=[
                 pltpu.VMEM((LO_SIZE * shard, 2 * slots), BF16),
                 pltpu.VMEM((2 * slots, step), BF16),
@@ -391,8 +407,9 @@
     full = returned.shape[2]
     return pl.pallas_call(
         collect_kernel,
-        in_specs=[WHOLE, WHOLE],
-        out_specs=WHOLE,
+        grid=(1,),
+        in_specs=[block_of(picked.shape), block_of(returned.shape)],
+        out_specs=block_of((rows, full)),
         out_shape=jax.ShapeDtypeStruct((rows, full), BF16),
         compiler_params=limits(),
         cost_estimate=cost(2 * slots * rows * full, 2 * slots * full),
@@ -429,8 +446,10 @@
     wide = jax.ShapeDtypeStruct((rows, width), BF16)
     return pl.pallas_call(
         finish_kernel,
-        in_specs=[SCALAR] + [WHOLE] * 4,
-        out_specs=(WHOLE,) * 3,
+        grid=(1,),
+        in_specs=[SCALAR]
+        + [block_of(value.shape) for value in (ids, picked, returned, far_total)],
+        out_specs=(block_of((rows, width)), block_of((rows, width)), block_of(ids.shape)),
         out_shape=(wide, wide, jax.ShapeDtypeStruct(ids.shape, F32)),
         compiler_params=limits(),
         cost_estimate=cost(2 * slots * rows * full, 2 * slots * full),
@@ -442,21 +461,17 @@
     return lax.ppermute(give, "dp", [(i, i ^ 1) for i in range(LO_SIZE * CORES)])
 
 
-def shift(value, distance, leave=()):
-    pairs = [(lo, (lo + distance) % LO_SIZE) for lo in range(LO_SIZE) if lo not in leave]
-    pairs = [(a * CORES + c, b * CORES + c) for a, b in pairs for c in range(CORES)]
+def move(value, steps):
+    pairs = [(a * CORES + c, b * CORES + c) for a, b in steps for c in range(CORES)]
     return lax.ppermute(value, "dp", pairs)
 
 
-def between_halves(value, steps):
-    experts = lax.axis_size("expert")
-    pairs = [
-        ((a * CORES + c) * experts + e, (b * CORES + c) * experts + (e ^ Y_SIZE))
-        for a, b in steps
-        for c in range(CORES)
-        for e in range(experts)
-    ]
-    return lax.ppermute(value, BOTH, pairs)
+def to_next(value):
+    return move(value, [(0, 1), (1, 2)]), move(value, [(3, 2), (2, 1)])
+
+
+def to_owner(up, down):
+    return move(up, [(0, 1), (1, 2), (2, 3)]), move(down, [(3, 2), (2, 1), (1, 0)])
 
 
 def total(terms):
@@ -464,21 +479,6 @@
     for term in terms[1:]:
         result = result + term.astype(F32)
     return result.astype(BF16)
-
-
-def line_sums(wide, down):
-    last = LO_SIZE - 1
-    half_way = between_halves(wide[2], [(0, last), (last, 0)])
-    wide_one = shift(wide[1], 1)
-    half_way, wide_one, down_send = lax.optimization_barrier((half_way, wide_one, down[1]))
-    down_one = shift(down_send, 1)
-    relayed = between_halves(half_way, [(last, 2), (0, 1)])
-    direct = shift(wide[2], 2, leave=(0, last))
-    wide_three = shift(wide[3], 3)
-    wide_three, down_one = lax.optimization_barrier((wide_three, down_one))
-    wide_sum = total([wide[0], wide_one, direct, wide_three, relayed])
-    down_sum = total([down[0], down_one, shift(down[2], 2), shift(down[3], 3)])
-    return wide_sum, down_sum
 
 
 def on_device(tokens, out_grad, expert_ids, route_gates, swap_flags, gate_proj, up_proj, down_proj):
@@ -514,15 +514,32 @@
     far_returned = to_plane(far_back)
     give_down, keep_down = down_grads(where, (near_hidden, far_hidden), (near_pick, far_pick))
     taken, keep_down = lax.optimization_barrier((taken, keep_down))
-    gate_up_parts = wide_grads(where, rows, grads, width, taken)
-    give_down, unused = lax.optimization_barrier((give_down, gate_up_parts[0]))
+    *wide, wide_first = wide_grads(where, rows, grads, width, taken)
+    give_down, unused = lax.optimization_barrier((give_down, wide_first))
+
+    arrived = move(wide_first, [(0, 1), (3, 2)])
     taken_down = core_swap(give_down)
-    down_parts = [total([keep_down[r], taken_down[r]]) for r in range(LO_SIZE)]
-    gate_up_sum, down_sum = line_sums(gate_up_parts, down_parts)
+    narrow = [total([keep_down[r], taken_down[r]]) for r in range(LO_SIZE)]
+    narrow_arrived = move(jnp.where(lo == 0, narrow[3], narrow[1]), [(0, 1), (3, 2)])
 
     near_back, far_returned = lax.optimization_barrier((near_back, far_returned))
     near_returned = to_plane(near_back)
-    far_total = across(collect(far_picked, far_returned))
+    collected = collect(far_picked, far_returned)
+    far_total = across(collected)
+    arrived, unused = lax.optimization_barrier((arrived, collected))
+
+    up, down = to_next(total([wide[2], arrived]))
+    narrow_up, narrow_down = to_next(total([narrow[2], narrow_arrived]))
+    up, down, far_total = lax.optimization_barrier((up, down, far_total))
+    up, down = total([wide[1], up]), total([wide[3], down])
+    sent = lax.optimization_barrier((up, down))
+    narrow_up, narrow_down, unused = lax.optimization_barrier((narrow_up, narrow_down, sent))
+    narrow_up, narrow_down = total([narrow[1], narrow_up]), total([narrow[3], narrow_down])
+    up, down = to_owner(*sent)
+    narrow_up, narrow_down = to_owner(narrow_up, narrow_down)
+    gate_up_sum = total([wide[0], up, down])
+    down_sum = total([narrow[0], narrow_up, narrow_down])
+
     layer_out, grad_tokens, gate_grads = finish(
         half, expert_ids, near_picked, near_returned, far_total
     )

time: 275 us -> 275 us (level)
  Pallas kernels: 48 us -> 62.2 us
  waiting for transfers between devices: 128 us -> 114 us
  local copies, waits for them, and re-layouts: 25.2 us -> 11.5 us
  starting transfers between devices: 60.5 us -> 68.8 us
  other arithmetic: 9.79 us -> 13.4 us
    ppermute x8 -> x10, waiting for transfers between devices: 68.4 us -> 13.5 us  [move(): return lax.ppermute(value, 'dp', pairs)]
    ppermute x4, waiting for transfers between devices: 26.7 us -> 56.4 us  [across(): return lax.ppermute(value, BOTH, pairs)]
    unnamed x53 -> x29, local copies, waits for them, and re-layouts: 23.7 us -> 9.96 us
    all_to_all x4, waiting for transfers between devices: 22.5 us -> 32.2 us  [to_plane(): lax.all_to_all(blocks, 'expert', split_axis=0, concat_axis=0, axis_index_...]
    ppermute x8 -> x10, starting transfers between devices: 17.3 us -> 26.3 us  [move(): return lax.ppermute(value, 'dp', pairs)]
    pallas_call x2, Pallas kernels: 3.17 us -> 6.97 us  [fill(): pl.pallas_call(fill_kernel, out_shape=(jax.ShapeDtypeStruct((slots, 2 * w...]
    pallas_call x2, Pallas kernels: 22.3 us -> 25.6 us  [run_expert(): pl.pallas_call(expert_kernel, out_shape=(jax.ShapeDtypeStruct((PLANE, MOS...]
    convert_element_type x3 -> x6, other arithmetic: 6.71 us -> 9.83 us  [total(): return result.astype(BF16)]
  transfers between devices with their start and end apart: 20 -> 22, of which waited for: 10 -> 10; matrix products, arithmetic and copies ran while one was open for 5% -> 7% of each run, Pallas kernels for 11% -> 16%
where the time goes in v7:
time: 275 us; the launch traced here: 271 us
  waiting for transfers between devices  114 us (41%)
  starting transfers between devices  68.8 us (25%)
  Pallas kernels  62.2 us (23%)
  other arithmetic  13.4 us (5%)
  local copies, waits for them, and re-layouts  11.5 us (4%)
    ppermute x4, waiting for transfers between devices, across(): return lax.ppermute(value, BOTH, pairs)  56.4 us
    all_to_all x4, waiting for transfers between devices, to_plane(): lax.all_to_all(blocks, 'expert', split_axis=0, concat_axis=0, axis_index_...  32.2 us
    all_to_all x4, starting transfers between devices, to_plane(): lax.all_to_all(blocks, 'expert', split_axis=0, concat_axis=0, axis_index_...  27.7 us
    ppermute x10, starting transfers between devices, move(): return lax.ppermute(value, 'dp', pairs)  26.3 us
    pallas_call x2, Pallas kernels, run_expert(): pl.pallas_call(expert_kernel, out_shape=(jax.ShapeDtypeStruct((PLANE, MOS...  25.6 us
    pallas_call x2, Pallas kernels, wide_grads(): pl.pallas_call(functools.partial(wide_kernel, keep, shard), grid_spec=plt...  14.5 us
    ppermute x10, waiting for transfers between devices, move(): return lax.ppermute(value, 'dp', pairs)  13.5 us
    ppermute x4, starting transfers between devices, across(): return lax.ppermute(value, BOTH, pairs)  10.9 us
  transfers between devices with their start and end apart: 22, of which 10 were waited for; matrix products, arithmetic and copies ran while one was open for 7% of the time, Pallas kernels for 16%

profile of v7, /device:TPU:16, one launch (start us, length us, event | category | flops | bytes accessed | tf_op | source)
XLA Modules:
  0.0 271.4 jit_solution(14353609894514963409)
XLA Ops:
  0.6 5.9 %collective-permute-start.1 = (bf16[128,2048]{1,0:T(8,128)(2,1)}, bf16[128,2048]{1,0:T(8,128)(2,1)S(1)}, u32[]{:S(2)}, u32[]{:S(2)}) collective-permute-start(bf16[128,2048]{1,0:T(8,128)(2,1)} %tokens_ref.1), channel_id=1, source_target_pairs={{0,196},{1,197},{2,198},{3,199},{4,192},{5,193},{6,194},{7,195},{8... | collective-permute-start | bytes 1572872 | tf_op jit(solution)/shard_map/ppermute | solution.py:50
  6.6 0.1 collective-permute-start.2
  6.7 1.4 copy.16.ids_ref
  8.1 1.4 copy.15.gates_ref
  9.5 2.1 route.1
  11.6 3.1 %collective-permute-start = (bf16[128,128]{1,0:T(8,128)(2,1)}, bf16[128,128]{1,0:T(8,128)(2,1)S(1)}, u32[]{:S(2)}, u32[]{:S(2)}) collective-permute-start(bf16[128,128]{1,0:T(8,128)(2,1)} %get-tuple-element.49), channel_id=1, source_target_pairs={{0,196},{1,197},{2,198},{3,199},{4,192},{5,193},{6,194},{7,195},{8... | collective-permute-start | bytes 98312 | tf_op jit(solution)/shard_map/ppermute | solution.py:50
  14.8 3.5 %fill.2 = (bf16[256,4224]{1,0:T(8,128)(2,1)}, bf16[256,128]{1,0:T(8,128)(2,1)}) custom-call(bf16[128,128]{1,0:T(8,128)(2,1)} %get-tuple-element.45.sides_ref, bf16[128,2048]{1,0:T(8,128)(2,1)} %tokens_ref.1, bf16[128,2048]{1,0:T(8,128)(2,1)} %grads_ref.1), custom_call_target="tpu_custom_call" | custom-call | flops 1000000000 | bytes 4194304 | tf_op jit(solution)/shard_map/fill/pallas_call | solution.py:130
  18.3 7.3 %all-to-all-start = ((bf16[16,16,4224]{2,1,0:T(8,128)(2,1)}), bf16[16,16,4224]{2,1,0:T(8,128)(2,1)}, u32[]{:S(2)}, u32[]{:S(2)}) async-start(bf16[16,16,4224]{2,1,0:T(8,128)(2,1)} %bitcast.40), calls=%async_computation | async-start | bytes 4325376 | tf_op jit(solution)/shard_map/all_to_all | solution.py:54
  25.6 28.3 %collective-permute-done.sides_ref = bf16[128,128]{1,0:T(8,128)(2,1)S(1)} collective-permute-done((bf16[128,128]{1,0:T(8,128)(2,1)}, bf16[128,128]{1,0:T(8,128)(2,1)S(1)}, u32[]{:S(2)}, u32[]{:S(2)}) %collective-permute-start) | collective-permute-done | bytes 32800 | tf_op jit(solution)/shard_map/ppermute | solution.py:50
  53.8 0.6 copy-done.11
  54.4 0.2 copy-done.9
  54.6 0.8 copy-done.10
  55.4 3.5 %fill.3 = (bf16[256,4224]{1,0:T(8,128)(2,1)}, bf16[256,128]{1,0:T(8,128)(2,1)}) custom-call(bf16[128,128]{1,0:T(8,128)(2,1)} %copy-done.11, bf16[128,2048]{1,0:T(8,128)(2,1)} %copy-done.9, bf16[128,2048]{1,0:T(8,128)(2,1)} %copy-done.10), custom_call_target="tpu_custom_call" | custom-call | flops 999999995904 | bytes 4194304 | tf_op jit(solution)/shard_map/fill/pallas_call | solution.py:130
  58.9 7.3 %all-to-all-start.1 = ((bf16[16,16,4224]{2,1,0:T(8,128)(2,1)}), bf16[16,16,4224]{2,1,0:T(8,128)(2,1)S(1)}, u32[]{:S(2)}, u32[]{:S(2)}) async-start(bf16[16,16,4224]{2,1,0:T(8,128)(2,1)} %bitcast.39), calls=%async_computation.1 | async-start | bytes 4325376 | tf_op jit(solution)/shard_map/all_to_all | solution.py:54
  66.2 0.6 pad_add_fusion.where_ref
  66.8 12.8 %expert.2 = (bf16[16,16,4224]{2,1,0:T(8,128)(2,1)}, bf16[256,768]{1,0:T(8,128)(2,1)}, bf16[256,2048]{1,0:T(8,128)(2,1)}, bf16[256,1536]{1,0:T(8,128)(2,1)}) custom-call(s32[1]{0:T(128)} %bitcast.1.place_ref, bf16[256,4224]{1,0:T(8,128)(2,1)} %bitcast.3.rows_ref.near_x, bf16[2048,768]{1,0:T(8,128)(2,1)} %bitcast.41, bf16[2048,768]{1,0:T(8,128)(2,1)} %bitcast.43, ...), custom_call_target="tpu_custom_call" | custom-call | flops 4831838208 | bytes 9437184 | tf_op jit(solution)/shard_map/expert/pallas_call | solution.py:235
  79.6 16.0 %all-to-all-done.1 = bf16[16,16,4224]{2,1,0:T(8,128)(2,1)S(1)} async-done(((bf16[16,16,4224]{2,1,0:T(8,128)(2,1)}), bf16[16,16,4224]{2,1,0:T(8,128)(2,1)S(1)}, u32[]{:S(2)}, u32[]{:S(2)}) %all-to-all-start.1) | async-done | bytes 2162720 | tf_op jit(solution)/shard_map/all_to_all | solution.py:54
  95.6 1.3 copy-done
  96.9 12.8 %expert.3 = (bf16[16,16,4224]{2,1,0:T(8,128)(2,1)}, bf16[256,768]{1,0:T(8,128)(2,1)}, bf16[256,2048]{1,0:T(8,128)(2,1)}, bf16[256,1536]{1,0:T(8,128)(2,1)}) custom-call(s32[1]{0:T(128)} %bitcast.1.place_ref, bf16[256,4224]{1,0:T(8,128)(2,1)} %bitcast.36, bf16[2048,768]{1,0:T(8,128)(2,1)} %bitcast.42, bf16[2048,768]{1,0:T(8,128)(2,1)} %bitcast.44, ...), custom_call_target="tpu_custom_call" | custom-call | flops 4831838208 | bytes 9437184 | tf_op jit(solution)/shard_map/expert/pallas_call | solution.py:235
  109.8 6.6 %wide.2 = bf16[4,256,1536]{2,1,0:T(8,128)(2,1)} custom-call(s32[2]{0:T(128)} %pad_add_fusion.where_ref, bf16[256,4224]{1,0:T(8,128)(2,1)} %bitcast.3.rows_ref.near_x, bf16[256,4224]{1,0:T(8,128)(2,1)} %bitcast.37, bf16[256,1536]{1,0:T(8,128)(2,1)} %get-tuple-element.53.near_grads, bf16[256,1536]{1,0:T(8,128)(2,1)} %get-tuple-element.54.far_grads), custom_call_target="tpu_custom_call" | custom-call | flops 1610612736 | bytes 6291456 | tf_op jit(solution)/shard_map/wide/pallas_call | solution.py:310
  116.3 0.0 collective-permute-start.3
  116.3 6.1 %all-to-all-start.2 = ((bf16[16,16,4224]{2,1,0:T(8,128)(2,1)}), bf16[16,16,4224]{2,1,0:T(8,128)(2,1)S(1)}, u32[]{:S(2)}, u32[]{:S(2)}) async-start(bf16[16,16,4224]{2,1,0:T(8,128)(2,1)} %get-tuple-element.55), calls=%async_computation.2 | async-start | bytes 4325376 | tf_op jit(solution)/shard_map/all_to_all | solution.py:54
  122.4 6.4 %down.1 = (bf16[4,96,2048]{2,1,0:T(8,128)(2,1)}, bf16[4,96,2048]{2,1,0:T(8,128)(2,1)}) custom-call(s32[2]{0:T(128)} %pad_add_fusion.where_ref, bf16[256,768]{1,0:T(8,128)(2,1)} %get-tuple-element.57.near_hidden, bf16[256,768]{1,0:T(8,128)(2,1)} %get-tuple-element.58.far_hidden, bf16[256,2048]{1,0:T(8,128)(2,1)} %get-tuple-element.59.near_pick, ...), custom_call_target="tpu_custom_call" | custom-call | flops 1610612736 | bytes 6291456 | tf_op jit(solution)/shard_map/down/pallas_call | solution.py:359
  128.8 8.0 %wide.3 = (bf16[256,1536]{1,0:T(8,128)(2,1)}, bf16[256,1536]{1,0:T(8,128)(2,1)}, bf16[256,1536]{1,0:T(8,128)(2,1)}, bf16[256,1536]{1,0:T(8,128)(2,1)}, bf16[256,1536]{1,0:T(8,128)(2,1)}) custom-call(s32[2]{0:T(128)} %pad_add_fusion.where_ref, bf16[256,4224]{1,0:T(8,128)(2,1)} %bitcast.3.rows_ref.near_x, bf16[256,4224]{1,0:T(8,128)(2,1)} %bitcast.38, ...), custom_call_target="tpu_custom_call" | custom-call | flops 1610612736 | bytes 6291456 | tf_op jit(solution)/shard_map/wide/pallas_call | solution.py:310
  136.8 0.2 collective-permute-start.11
  137.1 2.2 collective-permute-start.4
  139.3 16.1 %all-to-all-done.2.returned_ref = bf16[16,16,4224]{2,1,0:T(8,128)(2,1)S(1)} async-done(((bf16[16,16,4224]{2,1,0:T(8,128)(2,1)}), bf16[16,16,4224]{2,1,0:T(8,128)(2,1)S(1)}, u32[]{:S(2)}, u32[]{:S(2)}) %all-to-all-start.2) | async-done | bytes 2162720 | tf_op jit(solution)/shard_map/all_to_all | solution.py:54
  155.4 1.3 copy-done.1
  156.7 3.1 %collect.1 = bf16[128,4224]{1,0:T(8,128)(2,1)} custom-call(bf16[256,128]{1,0:T(8,128)(2,1)} %get-tuple-element.65.picked_ref, bf16[16,16,4224]{2,1,0:T(8,128)(2,1)} %copy-done.1), custom_call_target="tpu_custom_call" | custom-call | flops 276824064 | bytes 2162688 | tf_op jit(solution)/shard_map/collect/pallas_call | solution.py:408
  159.9 1.7 collective-permute-start.7
  161.6 0.0 collective-permute-done.4
  161.6 2.4 add_convert_fusion.3
  164.0 1.6 collective-permute-start.6
  165.6 2.2 collective-permute-start.5
  167.8 2.1 select_bitcast_fusion.1
  169.9 2.0 collective-permute-start.12
  171.9 7.0 %all-to-all-start.3 = ((bf16[16,16,4224]{2,1,0:T(8,128)(2,1)}), bf16[16,16,4224]{2,1,0:T(8,128)(2,1)S(1)}, u32[]{:S(2)}, u32[]{:S(2)}) async-start(bf16[16,16,4224]{2,1,0:T(8,128)(2,1)} %get-tuple-element.56), calls=%async_computation.3 | async-start | bytes 4325376 | tf_op jit(solution)/shard_map/all_to_all | solution.py:54
  179.0 28.1 %collective-permute-done.7.far_ref = bf16[128,4224]{1,0:T(8,128)(2,1)S(1)} collective-permute-done((bf16[128,4224]{1,0:T(8,128)(2,1)}, bf16[128,4224]{1,0:T(8,128)(2,1)S(1)}, u32[]{:S(2)}, u32[]{:S(2)}) %collective-permute-start.7) | collective-permute-done | bytes 1081376 | tf_op jit(solution)/shard_map/ppermute | solution.py:50
  207.1 1.3 collective-permute-done.12
  208.4 1.4 fusion.1
  209.8 0.7 collective-permute-start.14
  210.4 5.0 %collective-permute-start.13 = (bf16[96,2048]{1,0:T(8,128)(2,1)S(1)}, bf16[96,2048]{1,0:T(8,128)(2,1)S(1)}, u32[]{:S(2)}, u32[]{:S(2)}) collective-permute-start(bf16[96,2048]{1,0:T(8,128)(2,1)S(1)} %fusion.1), channel_id=1, source_target_pairs={{0,64},{32,96},{64,128},{96,160},{1,65},{33,97},{65,129},{97,161},... | collective-permute-start | bytes 1179656 | tf_op jit(solution)/shard_map/ppermute | solution.py:466
  215.5 1.9 add_convert_fusion.1
  217.4 4.7 %collective-permute-start.8 = (bf16[256,1536]{1,0:T(8,128)(2,1)S(1)}, bf16[256,1536]{1,0:T(8,128)(2,1)S(1)}, u32[]{:S(2)}, u32[]{:S(2)}) collective-permute-start(bf16[256,1536]{1,0:T(8,128)(2,1)S(1)} %get-tuple-element.77), channel_id=1, source_target_pairs={{0,64},{32,96},{64,128},{96,160},{128,192},{160,224},{1,65},{33,97... | collective-permute-start | bytes 2359304 | tf_op jit(solution)/shard_map/ppermute | solution.py:466
  222.1 1.3 collective-permute-start.9
  223.4 1.5 collective-permute-done.13
  224.9 2.3 fusion.2
  227.2 5.3 %collective-permute-start.15 = (bf16[96,2048]{1,0:T(8,128)(2,1)}, bf16[96,2048]{1,0:T(8,128)(2,1)}, u32[]{:S(2)}, u32[]{:S(2)}) collective-permute-start(bf16[96,2048]{1,0:T(8,128)(2,1)} %get-tuple-element.90), channel_id=1, source_target_pairs={{0,64},{32,96},{64,128},{96,160},{128,192},{160,224},{1,65},{33,97... | collective-permute-start | bytes 1179656 | tf_op jit(solution)/shard_map/ppermute | solution.py:466
  232.5 1.3 collective-permute-start.16
  233.8 8.0 %collective-permute-done.8 = bf16[256,1536]{1,0:T(8,128)(2,1)S(1)} collective-permute-done((bf16[256,1536]{1,0:T(8,128)(2,1)S(1)}, bf16[256,1536]{1,0:T(8,128)(2,1)S(1)}, u32[]{:S(2)}, u32[]{:S(2)}) %collective-permute-start.8) | collective-permute-done | bytes 786464 | tf_op jit(solution)/shard_map/ppermute | solution.py:466
  241.8 2.7 %collective-permute-done.9 = bf16[256,1536]{1,0:T(8,128)(2,1)S(1)} collective-permute-done((bf16[256,1536]{1,0:T(8,128)(2,1)S(1)}, bf16[256,1536]{1,0:T(8,128)(2,1)S(1)}, u32[]{:S(2)}, u32[]{:S(2)}) %collective-permute-start.9) | collective-permute-done | bytes 786464 | tf_op jit(solution)/shard_map/ppermute | solution.py:466
  244.5 0.3 add_convert_fusion
  244.8 0.8 collective-permute-start.10
  245.6 0.6 dynamic_slice.3
  246.9 1.3 copy-done.2
  248.2 3.4 %finish.1 = (bf16[128,2048]{1,0:T(8,128)(2,1)}, bf16[128,2048]{1,0:T(8,128)(2,1)}, f32[128,8]{1,0:T(8,128)}) custom-call(s32[1]{0:T(128)} %bitcast.half_ref, s32[128,8]{1,0:T(8,128)} %copy.16.ids_ref, bf16[256,128]{1,0:T(8,128)(2,1)} %get-tuple-element.46.picked_ref, bf16[16,16,4224]{2,1,0:T(8,128)(2,1)} %copy-done.2, bf16[128,4224]{1,0:T(8,128)(2,1)} %copy-done.5), custom_call_target="tpu_custom_call" | custom-call | flops 276824064 | bytes 2162688 | tf_op jit(solution)/shard_map/finish/pallas_call | solution.py:447
  251.6 1.5 copy.17
  253.1 1.6 fusion.4
  254.7 2.9 %collective-permute-start.17 = (bf16[96,2048]{1,0:T(8,128)(2,1)S(1)}, bf16[96,2048]{1,0:T(8,128)(2,1)S(1)}, u32[]{:S(2)}, u32[]{:S(2)}) collective-permute-start(bf16[96,2048]{1,0:T(8,128)(2,1)S(1)} %fusion.4), channel_id=1, source_target_pairs={{0,16},{1,17},{2,18},{3,19},{4,20},{5,21},{6,22},{7,23},{8,24},{9,... | collective-permute-start | bytes 1179656 | tf_op jit(solution)/shard_map/ppermute | solution.py:550
  257.6 8.9 %collective-permute-done.10 = bf16[256,1536]{1,0:T(8,128)(2,1)} collective-permute-done((bf16[256,1536]{1,0:T(8,128)(2,1)S(1)}, bf16[256,1536]{1,0:T(8,128)(2,1)}, u32[]{:S(2)}, u32[]{:S(2)}) %collective-permute-start.10) | collective-permute-done | bytes 786464 | tf_op jit(solution)/shard_map/ppermute | solution.py:549
  266.5 0.1 broadcast_select_fusion
  266.6 0.9 slice_bitcast_fusion
  267.6 3.1 %collective-permute-done.17 = bf16[96,2048]{1,0:T(8,128)(2,1)S(1)} collective-permute-done((bf16[96,2048]{1,0:T(8,128)(2,1)S(1)}, bf16[96,2048]{1,0:T(8,128)(2,1)S(1)}, u32[]{:S(2)}, u32[]{:S(2)}) %collective-permute-start.17) | collective-permute-done | bytes 393248 | tf_op jit(solution)/shard_map/ppermute | solution.py:550
  270.6 0.8 select_bitcast_fusion
  (31 shorter events, 0.1 us)
Async XLA Ops:
  0.6 53.2 %collective-permute-start.1 = (bf16[128,2048]{1,0:T(8,128)(2,1)}, bf16[128,2048]{1,0:T(8,128)(2,1)S(1)}, u32[]{:S(2)}, u32[]{:S(2)}) collective-permute-start(bf16[128,2048]{1,0:T(8,128)(2,1)} %tokens_ref.1), channel_id=1, source_target_pairs={{0,196},{1,197},{2,198},{3,199},{4,192},{5,193},{6,194},{7,195},{8... | collective-permute-start | bytes 1572872 | tf_op jit(solution)/shard_map/ppermute | solution.py:50
  6.6 47.3 %collective-permute-start.2 = (bf16[128,2048]{1,0:T(8,128)(2,1)}, bf16[128,2048]{1,0:T(8,128)(2,1)S(1)}, u32[]{:S(2)}, u32[]{:S(2)}) collective-permute-start(bf16[128,2048]{1,0:T(8,128)(2,1)} %grads_ref.1), channel_id=1, source_target_pairs={{0,196},{1,197},{2,198},{3,199},{4,192},{5,193},{6,194},{7,195},{8... | collective-permute-start | bytes 1572872 | tf_op jit(solution)/shard_map/ppermute | solution.py:50
  11.6 42.2 %collective-permute-start = (bf16[128,128]{1,0:T(8,128)(2,1)}, bf16[128,128]{1,0:T(8,128)(2,1)S(1)}, u32[]{:S(2)}, u32[]{:S(2)}) collective-permute-start(bf16[128,128]{1,0:T(8,128)(2,1)} %get-tuple-element.49), channel_id=1, source_target_pairs={{0,196},{1,197},{2,198},{3,199},{4,192},{5,193},{6,194},{7,195},{8... | collective-permute-start | bytes 98312 | tf_op jit(solution)/shard_map/ppermute | solution.py:50
  18.3 40.6 %all-to-all-start = ((bf16[16,16,4224]{2,1,0:T(8,128)(2,1)}), bf16[16,16,4224]{2,1,0:T(8,128)(2,1)}, u32[]{:S(2)}, u32[]{:S(2)}) async-start(bf16[16,16,4224]{2,1,0:T(8,128)(2,1)} %bitcast.40), calls=%async_computation | async-start | bytes 4325376 | tf_op jit(solution)/shard_map/all_to_all | solution.py:54
  53.8 0.6 copy-start.11
  53.8 0.8 copy-start.9
  54.6 0.8 copy-start.10
  58.9 36.7 %all-to-all-start.1 = ((bf16[16,16,4224]{2,1,0:T(8,128)(2,1)}), bf16[16,16,4224]{2,1,0:T(8,128)(2,1)S(1)}, u32[]{:S(2)}, u32[]{:S(2)}) async-start(bf16[16,16,4224]{2,1,0:T(8,128)(2,1)} %bitcast.39), calls=%async_computation.1 | async-start | bytes 4325376 | tf_op jit(solution)/shard_map/all_to_all | solution.py:54
  95.6 1.3 copy-start
  116.3 12.5 %collective-permute-start.3 = (bf16[4,256,1536]{2,1,0:T(8,128)(2,1)}, bf16[4,256,1536]{2,1,0:T(8,128)(2,1)}, u32[]{:S(2)}, u32[]{:S(2)}) collective-permute-start(bf16[4,256,1536]{2,1,0:T(8,128)(2,1)} %wide.2), channel_id=1, source_target_pairs={{0,32},{32,0},{64,96},{96,64},{128,160},{160,128},{192,224},{224,1... | collective-permute-start | bytes 9437192 | tf_op jit(solution)/shard_map/ppermute | solution.py:461
  116.3 39.0 %all-to-all-start.2 = ((bf16[16,16,4224]{2,1,0:T(8,128)(2,1)}), bf16[16,16,4224]{2,1,0:T(8,128)(2,1)S(1)}, u32[]{:S(2)}, u32[]{:S(2)}) async-start(bf16[16,16,4224]{2,1,0:T(8,128)(2,1)} %get-tuple-element.55), calls=%async_computation.2 | async-start | bytes 4325376 | tf_op jit(solution)/shard_map/all_to_all | solution.py:54
  136.8 30.9 %collective-permute-start.11 = (bf16[4,96,2048]{2,1,0:T(8,128)(2,1)}, bf16[4,96,2048]{2,1,0:T(8,128)(2,1)}, u32[]{:S(2)}, u32[]{:S(2)}) collective-permute-start(bf16[4,96,2048]{2,1,0:T(8,128)(2,1)} %get-tuple-element.81), channel_id=1, source_target_pairs={{0,32},{32,0},{64,96},{96,64},{128,160},{160,128},{192,224},{224,1... | collective-permute-start | bytes 4718600 | tf_op jit(solution)/shard_map/ppermute | solution.py:461
  137.1 24.5 %collective-permute-start.4 = (bf16[256,1536]{1,0:T(8,128)(2,1)}, bf16[256,1536]{1,0:T(8,128)(2,1)}, u32[]{:S(2)}, u32[]{:S(2)}) collective-permute-start(bf16[256,1536]{1,0:T(8,128)(2,1)} %get-tuple-element.64), channel_id=1, source_target_pairs={{0,64},{32,96},{192,128},{224,160},{1,65},{33,97},{193,129},{225,1... | collective-permute-start | bytes 2359304 | tf_op jit(solution)/shard_map/ppermute | solution.py:466
  155.4 1.4 copy-start.1
  159.9 7.9 %copy-start.3 = (bf16[4,96,2048]{2,1,0:T(8,128)(2,1)S(1)}, bf16[4,96,2048]{2,1,0:T(8,128)(2,1)}, u32[]{:S(2)}) copy-start(bf16[4,96,2048]{2,1,0:T(8,128)(2,1)} %get-tuple-element.79) | copy-start | bytes 4718596
  159.9 47.2 %collective-permute-start.7 = (bf16[128,4224]{1,0:T(8,128)(2,1)}, bf16[128,4224]{1,0:T(8,128)(2,1)S(1)}, u32[]{:S(2)}, u32[]{:S(2)}) collective-permute-start(bf16[128,4224]{1,0:T(8,128)(2,1)} %collect.1), channel_id=1, source_target_pairs={{0,196},{1,197},{2,198},{3,199},{4,192},{5,193},{6,194},{7,195},{8... | collective-permute-start | bytes 3244040 | tf_op jit(solution)/shard_map/ppermute | solution.py:50
  164.0 43.0 %collective-permute-start.6 = (bf16[256,1536]{1,0:T(8,128)(2,1)}, bf16[256,1536]{1,0:T(8,128)(2,1)}, u32[]{:S(2)}, u32[]{:S(2)}) collective-permute-start(bf16[256,1536]{1,0:T(8,128)(2,1)} %add_convert_fusion.3), channel_id=1, source_target_pairs={{192,128},{224,160},{128,64},{160,96},{193,129},{225,161},{129,65}... | collective-permute-start | bytes 2359304 | tf_op jit(solution)/shard_map/ppermute | solution.py:466
  165.6 41.5 %collective-permute-start.5 = (bf16[256,1536]{1,0:T(8,128)(2,1)}, bf16[256,1536]{1,0:T(8,128)(2,1)}, u32[]{:S(2)}, u32[]{:S(2)}) collective-permute-start(bf16[256,1536]{1,0:T(8,128)(2,1)} %add_convert_fusion.3), channel_id=1, source_target_pairs={{0,64},{32,96},{64,128},{96,160},{1,65},{33,97},{65,129},{97,161},... | collective-permute-start | bytes 2359304 | tf_op jit(solution)/shard_map/ppermute | solution.py:466
  169.9 38.5 %collective-permute-start.12 = (bf16[96,2048]{1,0:T(8,128)(2,1)}, bf16[96,2048]{1,0:T(8,128)(2,1)}, u32[]{:S(2)}, u32[]{:S(2)}) collective-permute-start(bf16[96,2048]{1,0:T(8,128)(2,1)} %select_bitcast_fusion.1), channel_id=1, source_target_pairs={{0,64},{32,96},{192,128},{224,160},{1,65},{33,97},{193,129},{225,1... | collective-permute-start | bytes 1179656 | tf_op jit(solution)/shard_map/ppermute | solution.py:466
  171.9 75.0 %all-to-all-start.3 = ((bf16[16,16,4224]{2,1,0:T(8,128)(2,1)}), bf16[16,16,4224]{2,1,0:T(8,128)(2,1)S(1)}, u32[]{:S(2)}, u32[]{:S(2)}) async-start(bf16[16,16,4224]{2,1,0:T(8,128)(2,1)} %get-tuple-element.56), calls=%async_computation.3 | async-start | bytes 4325376 | tf_op jit(solution)/shard_map/all_to_all | solution.py:54
  178.9 36.5 %copy-start.6 = (bf16[256,1536]{1,0:T(8,128)(2,1)S(1)}, bf16[256,1536]{1,0:T(8,128)(2,1)}, u32[]{:S(2)}) copy-start(bf16[256,1536]{1,0:T(8,128)(2,1)} %get-tuple-element.73) | copy-start | bytes 2359300
  179.0 36.5 %copy-start.7 = (bf16[256,1536]{1,0:T(8,128)(2,1)S(1)}, bf16[256,1536]{1,0:T(8,128)(2,1)}, u32[]{:S(2)}) copy-start(bf16[256,1536]{1,0:T(8,128)(2,1)} %get-tuple-element.75) | copy-start | bytes 2359300
  207.1 10.3 %copy-start.5 = (bf16[128,4224]{1,0:T(8,128)(2,1)}, bf16[128,4224]{1,0:T(8,128)(2,1)S(1)}, u32[]{:S(2)}) copy-start(bf16[128,4224]{1,0:T(8,128)(2,1)S(1)} %collective-permute-done.7.far_ref) | copy-start | bytes 3244036
  209.8 13.7 %collective-permute-start.14 = (bf16[96,2048]{1,0:T(8,128)(2,1)S(1)}, bf16[96,2048]{1,0:T(8,128)(2,1)S(1)}, u32[]{:S(2)}, u32[]{:S(2)}) collective-permute-start(bf16[96,2048]{1,0:T(8,128)(2,1)S(1)} %fusion.1), channel_id=1, source_target_pairs={{192,128},{224,160},{128,64},{160,96},{193,129},{225,161},{129,65}... | collective-permute-start | bytes 1179656 | tf_op jit(solution)/shard_map/ppermute | solution.py:466
  210.4 14.5 %collective-permute-start.13 = (bf16[96,2048]{1,0:T(8,128)(2,1)S(1)}, bf16[96,2048]{1,0:T(8,128)(2,1)S(1)}, u32[]{:S(2)}, u32[]{:S(2)}) collective-permute-start(bf16[96,2048]{1,0:T(8,128)(2,1)S(1)} %fusion.1), channel_id=1, source_target_pairs={{0,64},{32,96},{64,128},{96,160},{1,65},{33,97},{65,129},{97,161},... | collective-permute-start | bytes 1179656 | tf_op jit(solution)/shard_map/ppermute | solution.py:466
  215.5 9.4 %copy-start.4 = (bf16[4,96,2048]{2,1,0:T(8,128)(2,1)S(1)}, bf16[4,96,2048]{2,1,0:T(8,128)(2,1)}, u32[]{:S(2)}) copy-start(bf16[4,96,2048]{2,1,0:T(8,128)(2,1)} %get-tuple-element.79) | copy-start | bytes 4718596
  217.4 27.1 %copy-start.8 = (bf16[256,1536]{1,0:T(8,128)(2,1)S(1)}, bf16[256,1536]{1,0:T(8,128)(2,1)}, u32[]{:S(2)}) copy-start(bf16[256,1536]{1,0:T(8,128)(2,1)} %get-tuple-element.72) | copy-start | bytes 2359300
  217.4 24.4 %collective-permute-start.8 = (bf16[256,1536]{1,0:T(8,128)(2,1)S(1)}, bf16[256,1536]{1,0:T(8,128)(2,1)S(1)}, u32[]{:S(2)}, u32[]{:S(2)}) collective-permute-start(bf16[256,1536]{1,0:T(8,128)(2,1)S(1)} %get-tuple-element.77), channel_id=1, source_target_pairs={{0,64},{32,96},{64,128},{96,160},{128,192},{160,224},{1,65},{33,97... | collective-permute-start | bytes 2359304 | tf_op jit(solution)/shard_map/ppermute | solution.py:466
  222.1 22.4 %collective-permute-start.9 = (bf16[256,1536]{1,0:T(8,128)(2,1)S(1)}, bf16[256,1536]{1,0:T(8,128)(2,1)S(1)}, u32[]{:S(2)}, u32[]{:S(2)}) collective-permute-start(bf16[256,1536]{1,0:T(8,128)(2,1)S(1)} %get-tuple-element.78), channel_id=1, source_target_pairs={{192,128},{224,160},{128,64},{160,96},{64,0},{96,32},{193,129},{22... | collective-permute-start | bytes 2359304 | tf_op jit(solution)/shard_map/ppermute | solution.py:466
  227.2 25.9 %collective-permute-start.15 = (bf16[96,2048]{1,0:T(8,128)(2,1)}, bf16[96,2048]{1,0:T(8,128)(2,1)}, u32[]{:S(2)}, u32[]{:S(2)}) collective-permute-start(bf16[96,2048]{1,0:T(8,128)(2,1)} %get-tuple-element.90), channel_id=1, source_target_pairs={{0,64},{32,96},{64,128},{96,160},{128,192},{160,224},{1,65},{33,97... | collective-permute-start | bytes 1179656 | tf_op jit(solution)/shard_map/ppermute | solution.py:466
  232.5 20.6 %collective-permute-start.16 = (bf16[96,2048]{1,0:T(8,128)(2,1)S(1)}, bf16[96,2048]{1,0:T(8,128)(2,1)}, u32[]{:S(2)}, u32[]{:S(2)}) collective-permute-start(bf16[96,2048]{1,0:T(8,128)(2,1)S(1)} %get-tuple-element.91), channel_id=1, source_target_pairs={{192,128},{224,160},{128,64},{160,96},{64,0},{96,32},{193,129},{22... | collective-permute-start | bytes 1179656 | tf_op jit(solution)/shard_map/ppermute | solution.py:466
  244.5 1.1 copy-start.12
  244.8 21.7 %collective-permute-start.10 = (bf16[256,1536]{1,0:T(8,128)(2,1)S(1)}, bf16[256,1536]{1,0:T(8,128)(2,1)}, u32[]{:S(2)}, u32[]{:S(2)}) collective-permute-start(bf16[256,1536]{1,0:T(8,128)(2,1)S(1)} %add_convert_fusion), channel_id=1, source_target_pairs={{0,16},{1,17},{2,18},{3,19},{4,20},{5,21},{6,22},{7,23},{8,24},{9,... | collective-permute-start | bytes 2359304 | tf_op jit(solution)/shard_map/ppermute | solution.py:549
  246.9 1.4 copy-start.2
  254.7 15.9 %collective-permute-start.17 = (bf16[96,2048]{1,0:T(8,128)(2,1)S(1)}, bf16[96,2048]{1,0:T(8,128)(2,1)S(1)}, u32[]{:S(2)}, u32[]{:S(2)}) collective-permute-start(bf16[96,2048]{1,0:T(8,128)(2,1)S(1)} %fusion.4), channel_id=1, source_target_pairs={{0,16},{1,17},{2,18},{3,19},{4,20},{5,21},{6,22},{7,23},{8,24},{9,... | collective-permute-start | bytes 1179656 | tf_op jit(solution)/shard_map/ppermute | solution.py:550

commit v8 on v7

--- a/solution.py
+++ b/solution.py
@@ -32,7 +32,7 @@
 
 
 def limits():
-    return pltpu.CompilerParams(vmem_limit_bytes=60 << 20)
+    return pltpu.CompilerParams(vmem_limit_bytes=62 << 20)
 
 
 def cost(flops, moved):
@@ -44,7 +44,7 @@
     pairs = []
     for dp in range(lax.axis_size("dp")):
         lo, core = divmod(dp, CORES)
-        other_dp = (LO_SIZE - 1 - lo) * CORES + core
+        other_dp = (lo ^ 1) * CORES + core
         for expert in range(experts):
             pairs.append((dp * experts + expert, other_dp * experts + (expert ^ Y_SIZE)))
     return lax.ppermute(value, BOTH, pairs)
@@ -529,14 +529,17 @@
     arrived, unused = lax.optimization_barrier((arrived, collected))
 
     up, down = to_next(total([wide[2], arrived]))
+    up, down, far_total, narrow_arrived = lax.optimization_barrier(
+        (up, down, far_total, narrow_arrived)
+    )
+    sent = lax.optimization_barrier((total([wide[1], up]), total([wide[3], down])))
+    up, down = to_owner(*sent)
+    narrow_arrived, unused = lax.optimization_barrier((narrow_arrived, sent))
     narrow_up, narrow_down = to_next(total([narrow[2], narrow_arrived]))
-    up, down, far_total = lax.optimization_barrier((up, down, far_total))
-    up, down = total([wide[1], up]), total([wide[3], down])
-    sent = lax.optimization_barrier((up, down))
-    narrow_up, narrow_down, unused = lax.optimization_barrier((narrow_up, narrow_down, sent))
-    narrow_up, narrow_down = total([narrow[1], narrow_up]), total([narrow[3], narrow_down])
-    up, down = to_owner(*sent)
-    narrow_up, narrow_down = to_owner(narrow_up, narrow_down)
+    narrow_up, narrow_down, up, down = lax.optimization_barrier((narrow_up, narrow_down, up, down))
+    narrow_up, narrow_down = to_owner(
+        total([narrow[1], narrow_up]), total([narrow[3], narrow_down])
+    )
     gate_up_sum = total([wide[0], up, down])
     down_sum = total([narrow[0], narrow_up, narrow_down])
 

time: 275 us -> 298 us (1.084)
  starting transfers between devices: 68.8 us -> 85.8 us
  waiting for transfers between devices: 114 us -> 122 us
  local copies, waits for them, and re-layouts: 11.5 us -> 7.44 us
    ppermute x10, starting transfers between devices: 26.3 us -> 37.6 us  [move(): return lax.ppermute(value, 'dp', pairs)]
    ppermute x10, waiting for transfers between devices: 13.5 us -> 21.8 us  [move(): return lax.ppermute(value, 'dp', pairs)]
    ppermute x4, starting transfers between devices: 10.9 us -> 17.3 us  [across(): return lax.ppermute(value, BOTH, pairs)]
    unnamed x29 -> x17, local copies, waits for them, and re-layouts: 9.96 us -> 5.93 us
    all_to_all x4, waiting for transfers between devices: 32.2 us -> 28.3 us  [to_plane(): lax.all_to_all(blocks, 'expert', split_axis=0, concat_axis=0, axis_index_...]
  transfers between devices with their start and end apart: 22 -> 22, of which waited for: 10 -> 9; matrix products, arithmetic and copies ran while one was open for 7% -> 7% of each run, Pallas kernels for 16% -> 15%
where the time goes in v8:
time: 298 us; the launch traced here: 294 us
  waiting for transfers between devices  122 us (41%)
  starting transfers between devices  85.8 us (29%)
  Pallas kernels  62.2 us (21%)
  other arithmetic  14.7 us (5%)
  local copies, waits for them, and re-layouts  7.44 us (2%)
    ppermute x4, waiting for transfers between devices, across(): return lax.ppermute(value, BOTH, pairs)  58 us
    ppermute x10, starting transfers between devices, move(): return lax.ppermute(value, 'dp', pairs)  37.6 us
    all_to_all x4, starting transfers between devices, to_plane(): lax.all_to_all(blocks, 'expert', split_axis=0, concat_axis=0, axis_index_...  28.5 us
    all_to_all x4, waiting for transfers between devices, to_plane(): lax.all_to_all(blocks, 'expert', split_axis=0, concat_axis=0, axis_index_...  28.3 us
    pallas_call x2, Pallas kernels, run_expert(): pl.pallas_call(expert_kernel, out_shape=(jax.ShapeDtypeStruct((PLANE, MOS...  25.5 us
    ppermute x10, waiting for transfers between devices, move(): return lax.ppermute(value, 'dp', pairs)  21.8 us
    ppermute x4, starting transfers between devices, across(): return lax.ppermute(value, BOTH, pairs)  17.3 us
    pallas_call x2, Pallas kernels, wide_grads(): pl.pallas_call(functools.partial(wide_kernel, keep, shard), grid_spec=plt...  14.6 us
  transfers between devices with their start and end apart: 22, of which 9 were waited for; matrix products, arithmetic and copies ran while one was open for 7% of the time, Pallas kernels for 15%

profile of v8, /device:TPU:16, one launch (start us, length us, event | category | flops | bytes accessed | tf_op | source)
XLA Modules:
  0.0 293.6 jit_solution(5914886659974961398)
XLA Ops:
  0.6 6.8 %collective-permute-start.1 = (bf16[128,2048]{1,0:T(8,128)(2,1)}, bf16[128,2048]{1,0:T(8,128)(2,1)S(1)}, u32[]{:S(2)}, u32[]{:S(2)}) collective-permute-start(bf16[128,2048]{1,0:T(8,128)(2,1)} %tokens_ref.1), channel_id=1, source_target_pairs={{0,68},{1,69},{2,70},{3,71},{4,64},{5,65},{6,66},{7,67},{8,76},{9,... | collective-permute-start | bytes 1572872 | tf_op jit(solution)/shard_map/ppermute | solution.py:50
  7.5 0.1 collective-permute-start.2
  7.6 1.4 copy.16.ids_ref
  9.0 1.4 copy.15.gates_ref
  10.4 2.1 route.1
  12.5 4.9 %collective-permute-start = (bf16[128,128]{1,0:T(8,128)(2,1)}, bf16[128,128]{1,0:T(8,128)(2,1)S(1)}, u32[]{:S(2)}, u32[]{:S(2)}) collective-permute-start(bf16[128,128]{1,0:T(8,128)(2,1)} %get-tuple-element.53), channel_id=1, source_target_pairs={{0,68},{1,69},{2,70},{3,71},{4,64},{5,65},{6,66},{7,67},{8,76},{9,... | collective-permute-start | bytes 98312 | tf_op jit(solution)/shard_map/ppermute | solution.py:50
  17.5 3.5 %fill.2 = (bf16[256,4224]{1,0:T(8,128)(2,1)}, bf16[256,128]{1,0:T(8,128)(2,1)}) custom-call(bf16[128,128]{1,0:T(8,128)(2,1)} %get-tuple-element.49.sides_ref, bf16[128,2048]{1,0:T(8,128)(2,1)} %tokens_ref.1, bf16[128,2048]{1,0:T(8,128)(2,1)} %grads_ref.1), custom_call_target="tpu_custom_call" | custom-call | flops 1000000000 | bytes 4194304 | tf_op jit(solution)/shard_map/fill/pallas_call | solution.py:130
  20.9 7.3 %all-to-all-start = ((bf16[16,16,4224]{2,1,0:T(8,128)(2,1)}), bf16[16,16,4224]{2,1,0:T(8,128)(2,1)}, u32[]{:S(2)}, u32[]{:S(2)}) async-start(bf16[16,16,4224]{2,1,0:T(8,128)(2,1)} %bitcast.37), calls=%async_computation | async-start | bytes 4325376 | tf_op jit(solution)/shard_map/all_to_all | solution.py:54
  28.2 25.9 %collective-permute-done.sides_ref = bf16[128,128]{1,0:T(8,128)(2,1)S(1)} collective-permute-done((bf16[128,128]{1,0:T(8,128)(2,1)}, bf16[128,128]{1,0:T(8,128)(2,1)S(1)}, u32[]{:S(2)}, u32[]{:S(2)}) %collective-permute-start) | collective-permute-done | bytes 32800 | tf_op jit(solution)/shard_map/ppermute | solution.py:50
  54.1 0.0 collective-permute-done.1.tokens_ref
  54.1 0.0 collective-permute-done.2.grads_ref
  54.1 0.6 copy-done.5
  54.7 0.2 copy-done.3
  54.9 0.8 copy-done.4
  55.7 3.5 %fill.3 = (bf16[256,4224]{1,0:T(8,128)(2,1)}, bf16[256,128]{1,0:T(8,128)(2,1)}) custom-call(bf16[128,128]{1,0:T(8,128)(2,1)} %copy-done.5, bf16[128,2048]{1,0:T(8,128)(2,1)} %copy-done.3, bf16[128,2048]{1,0:T(8,128)(2,1)} %copy-done.4), custom_call_target="tpu_custom_call" | custom-call | flops 999999995904 | bytes 4194304 | tf_op jit(solution)/shard_map/fill/pallas_call | solution.py:130
  59.1 7.3 %all-to-all-start.1 = ((bf16[16,16,4224]{2,1,0:T(8,128)(2,1)}), bf16[16,16,4224]{2,1,0:T(8,128)(2,1)}, u32[]{:S(2)}, u32[]{:S(2)}) async-start(bf16[16,16,4224]{2,1,0:T(8,128)(2,1)} %bitcast.36), calls=%async_computation.1 | async-start | bytes 4325376 | tf_op jit(solution)/shard_map/all_to_all | solution.py:54
  66.4 0.6 pad_add_fusion.where_ref
  67.0 12.8 %expert.2 = (bf16[16,16,4224]{2,1,0:T(8,128)(2,1)}, bf16[256,768]{1,0:T(8,128)(2,1)}, bf16[256,2048]{1,0:T(8,128)(2,1)}, bf16[256,1536]{1,0:T(8,128)(2,1)}) custom-call(s32[1]{0:T(128)} %bitcast.1.place_ref, bf16[256,4224]{1,0:T(8,128)(2,1)} %bitcast.3.rows_ref.near_x, bf16[2048,768]{1,0:T(8,128)(2,1)} %bitcast.38, bf16[2048,768]{1,0:T(8,128)(2,1)} %bitcast.40, ...), custom_call_target="tpu_custom_call" | custom-call | flops 4831838208 | bytes 9437184 | tf_op jit(solution)/shard_map/expert/pallas_call | solution.py:235
  79.8 14.8 %all-to-all-done.1 = bf16[16,16,4224]{2,1,0:T(8,128)(2,1)} async-done(((bf16[16,16,4224]{2,1,0:T(8,128)(2,1)}), bf16[16,16,4224]{2,1,0:T(8,128)(2,1)}, u32[]{:S(2)}, u32[]{:S(2)}) %all-to-all-start.1) | async-done | bytes 2162720 | tf_op jit(solution)/shard_map/all_to_all | solution.py:54
  94.6 12.7 %expert.3 = (bf16[16,16,4224]{2,1,0:T(8,128)(2,1)}, bf16[256,768]{1,0:T(8,128)(2,1)}, bf16[256,2048]{1,0:T(8,128)(2,1)}, bf16[256,1536]{1,0:T(8,128)(2,1)}) custom-call(s32[1]{0:T(128)} %bitcast.1.place_ref, bf16[256,4224]{1,0:T(8,128)(2,1)} %bitcast.8.rows_ref.far_x, bf16[2048,768]{1,0:T(8,128)(2,1)} %bitcast.39, bf16[2048,768]{1,0:T(8,128)(2,1)} %bitcast.41, ...), custom_call_target="tpu_custom_call" | custom-call | flops 4831838208 | bytes 9437184 | tf_op jit(solution)/shard_map/expert/pallas_call | solution.py:235
  107.4 6.6 %wide.2 = bf16[4,256,1536]{2,1,0:T(8,128)(2,1)} custom-call(s32[2]{0:T(128)} %pad_add_fusion.where_ref, bf16[256,4224]{1,0:T(8,128)(2,1)} %bitcast.3.rows_ref.near_x, bf16[256,4224]{1,0:T(8,128)(2,1)} %bitcast.8.rows_ref.far_x, bf16[256,1536]{1,0:T(8,128)(2,1)} %get-tuple-element.57.near_grads, bf16[256,1536]{1,0:T(8,128)(2,1)} %get-tuple-element.58.far_grads), custom_call_target="tpu_custom_call" | custom-call | flops 1610612736 | bytes 6291456 | tf_op jit(solution)/shard_map/wide/pallas_call | solution.py:310
  113.9 0.0 collective-permute-start.3
  113.9 6.9 %all-to-all-start.2 = ((bf16[16,16,4224]{2,1,0:T(8,128)(2,1)}), bf16[16,16,4224]{2,1,0:T(8,128)(2,1)}, u32[]{:S(2)}, u32[]{:S(2)}) async-start(bf16[16,16,4224]{2,1,0:T(8,128)(2,1)} %get-tuple-element.59), calls=%async_computation.2 | async-start | bytes 4325376 | tf_op jit(solution)/shard_map/all_to_all | solution.py:54
  120.8 6.4 %down.1 = (bf16[4,96,2048]{2,1,0:T(8,128)(2,1)}, bf16[4,96,2048]{2,1,0:T(8,128)(2,1)}) custom-call(s32[2]{0:T(128)} %pad_add_fusion.where_ref, bf16[256,768]{1,0:T(8,128)(2,1)} %get-tuple-element.61.near_hidden, bf16[256,768]{1,0:T(8,128)(2,1)} %get-tuple-element.62.far_hidden, bf16[256,2048]{1,0:T(8,128)(2,1)} %get-tuple-element.63.near_pick, ...), custom_call_target="tpu_custom_call" | custom-call | flops 1610612736 | bytes 6291456 | tf_op jit(solution)/shard_map/down/pallas_call | solution.py:359
  127.2 0.0 collective-permute-done.3.refs_0_
  127.2 8.1 %wide.3 = (bf16[256,1536]{1,0:T(8,128)(2,1)}, bf16[256,1536]{1,0:T(8,128)(2,1)}, bf16[256,1536]{1,0:T(8,128)(2,1)}, bf16[256,1536]{1,0:T(8,128)(2,1)}, bf16[256,1536]{1,0:T(8,128)(2,1)}) custom-call(s32[2]{0:T(128)} %pad_add_fusion.where_ref, bf16[256,4224]{1,0:T(8,128)(2,1)} %bitcast.3.rows_ref.near_x, bf16[256,4224]{1,0:T(8,128)(2,1)} %bitcast.8.rows_ref.far_x, ...), custom_call_target="tpu_custom_call" | custom-call | flops 1610612736 | bytes 6291456 | tf_op jit(solution)/shard_map/wide/pallas_call | solution.py:310
  135.3 0.2 collective-permute-start.8
  135.5 4.9 %collective-permute-start.4 = (bf16[256,1536]{1,0:T(8,128)(2,1)}, bf16[256,1536]{1,0:T(8,128)(2,1)}, u32[]{:S(2)}, u32[]{:S(2)}) collective-permute-start(bf16[256,1536]{1,0:T(8,128)(2,1)} %get-tuple-element.68), channel_id=1, source_target_pairs={{0,64},{32,96},{192,128},{224,160},{1,65},{33,97},{193,129},{225,1... | collective-permute-start | bytes 2359304 | tf_op jit(solution)/shard_map/ppermute | solution.py:466
  140.4 13.5 %all-to-all-done.2.returned_ref = bf16[16,16,4224]{2,1,0:T(8,128)(2,1)} async-done(((bf16[16,16,4224]{2,1,0:T(8,128)(2,1)}), bf16[16,16,4224]{2,1,0:T(8,128)(2,1)}, u32[]{:S(2)}, u32[]{:S(2)}) %all-to-all-start.2) | async-done | bytes 2162720 | tf_op jit(solution)/shard_map/all_to_all | solution.py:54
  153.9 3.2 %collect.1 = bf16[128,4224]{1,0:T(8,128)(2,1)} custom-call(bf16[256,128]{1,0:T(8,128)(2,1)} %get-tuple-element.69.picked_ref, bf16[16,16,4224]{2,1,0:T(8,128)(2,1)} %all-to-all-done.2.returned_ref), custom_call_target="tpu_custom_call" | custom-call | flops 276824064 | bytes 2162688 | tf_op jit(solution)/shard_map/collect/pallas_call | solution.py:408
  157.1 5.4 %collective-permute-start.7 = (bf16[128,4224]{1,0:T(8,128)(2,1)}, bf16[128,4224]{1,0:T(8,128)(2,1)S(1)}, u32[]{:S(2)}, u32[]{:S(2)}) collective-permute-start(bf16[128,4224]{1,0:T(8,128)(2,1)} %collect.1), channel_id=1, source_target_pairs={{0,68},{1,69},{2,70},{3,71},{4,64},{5,65},{6,66},{7,67},{8,76},{9,... | collective-permute-start | bytes 3244040 | tf_op jit(solution)/shard_map/ppermute | solution.py:50
  162.5 2.5 add_convert_fusion.3
  164.9 1.5 collective-permute-start.6
  166.5 2.2 collective-permute-start.5
  168.7 1.3 select_bitcast_fusion.1
  170.0 1.3 collective-permute-start.9
  171.3 7.1 %all-to-all-start.3 = ((bf16[16,16,4224]{2,1,0:T(8,128)(2,1)}), bf16[16,16,4224]{2,1,0:T(8,128)(2,1)}, u32[]{:S(2)}, u32[]{:S(2)}) async-start(bf16[16,16,4224]{2,1,0:T(8,128)(2,1)} %get-tuple-element.60), calls=%async_computation.3 | async-start | bytes 4325376 | tf_op jit(solution)/shard_map/all_to_all | solution.py:54
  178.4 32.1 %collective-permute-done.7.far_ref = bf16[128,4224]{1,0:T(8,128)(2,1)S(1)} collective-permute-done((bf16[128,4224]{1,0:T(8,128)(2,1)}, bf16[128,4224]{1,0:T(8,128)(2,1)S(1)}, u32[]{:S(2)}, u32[]{:S(2)}) %collective-permute-start.7) | collective-permute-done | bytes 1081376 | tf_op jit(solution)/shard_map/ppermute | solution.py:50
  210.6 0.0 collective-permute-done.6
  210.6 4.4 %collective-permute-done.9 = bf16[96,2048]{1,0:T(8,128)(2,1)S(1)} collective-permute-done((bf16[96,2048]{1,0:T(8,128)(2,1)S(1)}, bf16[96,2048]{1,0:T(8,128)(2,1)S(1)}, u32[]{:S(2)}, u32[]{:S(2)}) %collective-permute-start.9) | collective-permute-done | bytes 393248 | tf_op jit(solution)/shard_map/ppermute | solution.py:466
  215.0 2.2 add_convert_fusion.1
  217.2 11.1 %collective-permute-start.12 = (bf16[256,1536]{1,0:T(8,128)(2,1)S(1)}, bf16[256,1536]{1,0:T(8,128)(2,1)S(1)}, u32[]{:S(2)}, u32[]{:S(2)}) collective-permute-start(bf16[256,1536]{1,0:T(8,128)(2,1)S(1)} %get-tuple-element.85), channel_id=1, source_target_pairs={{0,64},{32,96},{64,128},{96,160},{128,192},{160,224},{1,65},{33,97... | collective-permute-start | bytes 2359304 | tf_op jit(solution)/shard_map/ppermute | solution.py:466
  228.4 1.3 collective-permute-start.13
  229.7 1.1 fusion.4
  230.8 0.8 collective-permute-start.11
  231.7 5.2 %collective-permute-start.10 = (bf16[96,2048]{1,0:T(8,128)(2,1)S(1)}, bf16[96,2048]{1,0:T(8,128)(2,1)S(1)}, u32[]{:S(2)}, u32[]{:S(2)}) collective-permute-start(bf16[96,2048]{1,0:T(8,128)(2,1)S(1)} %fusion.4), channel_id=1, source_target_pairs={{0,64},{32,96},{64,128},{96,160},{1,65},{33,97},{65,129},{97,161},... | collective-permute-start | bytes 1179656 | tf_op jit(solution)/shard_map/ppermute | solution.py:466
  236.9 16.0 %collective-permute-done.10 = bf16[96,2048]{1,0:T(8,128)(2,1)S(1)} collective-permute-done((bf16[96,2048]{1,0:T(8,128)(2,1)S(1)}, bf16[96,2048]{1,0:T(8,128)(2,1)S(1)}, u32[]{:S(2)}, u32[]{:S(2)}) %collective-permute-start.10) | collective-permute-done | bytes 393248 | tf_op jit(solution)/shard_map/ppermute | solution.py:466
  252.9 2.3 fusion.1
  255.1 7.9 %collective-permute-start.15 = (bf16[96,2048]{1,0:T(8,128)(2,1)}, bf16[96,2048]{1,0:T(8,128)(2,1)}, u32[]{:S(2)}, u32[]{:S(2)}) collective-permute-start(bf16[96,2048]{1,0:T(8,128)(2,1)} %get-tuple-element.98), channel_id=1, source_target_pairs={{0,64},{32,96},{64,128},{96,160},{128,192},{160,224},{1,65},{33,97... | collective-permute-start | bytes 1179656 | tf_op jit(solution)/shard_map/ppermute | solution.py:466
  263.0 1.3 collective-permute-start.16
  264.3 0.0 copy-start.6
  264.3 1.2 add_convert_fusion
  265.6 0.6 collective-permute-start.14
  266.2 0.6 dynamic_slice.3
  267.4 3.4 %finish.1 = (bf16[128,2048]{1,0:T(8,128)(2,1)}, bf16[128,2048]{1,0:T(8,128)(2,1)}, f32[128,8]{1,0:T(8,128)}) custom-call(s32[1]{0:T(128)} %bitcast.half_ref, s32[128,8]{1,0:T(8,128)} %copy.16.ids_ref, bf16[256,128]{1,0:T(8,128)(2,1)} %get-tuple-element.50.picked_ref, bf16[16,16,4224]{2,1,0:T(8,128)(2,1)} %all-to-all-done.3.returned_ref, ...), custom_call_target="tpu_custom_call" | custom-call | flops 276824064 | bytes 2162688 | tf_op jit(solution)/shard_map/finish/pallas_call | solution.py:447
  270.8 1.5 copy.17
  272.3 1.4 collective-permute-done.16
  273.7 1.5 fusion.3
  275.2 1.6 collective-permute-start.17
  276.8 11.1 %collective-permute-done.14 = bf16[256,1536]{1,0:T(8,128)(2,1)} collective-permute-done((bf16[256,1536]{1,0:T(8,128)(2,1)}, bf16[256,1536]{1,0:T(8,128)(2,1)}, u32[]{:S(2)}, u32[]{:S(2)}) %collective-permute-start.14) | collective-permute-done | bytes 786464 | tf_op jit(solution)/shard_map/ppermute | solution.py:552
  287.9 1.2 broadcast_select_fusion
  289.1 0.9 slice_bitcast_fusion
  290.0 2.8 collective-permute-done.17
  292.8 0.8 select_bitcast_fusion
  (19 shorter events, 0.0 us)
Async XLA Ops:
  0.6 53.4 %collective-permute-start.1 = (bf16[128,2048]{1,0:T(8,128)(2,1)}, bf16[128,2048]{1,0:T(8,128)(2,1)S(1)}, u32[]{:S(2)}, u32[]{:S(2)}) collective-permute-start(bf16[128,2048]{1,0:T(8,128)(2,1)} %tokens_ref.1), channel_id=1, source_target_pairs={{0,68},{1,69},{2,70},{3,71},{4,64},{5,65},{6,66},{7,67},{8,76},{9,... | collective-permute-start | bytes 1572872 | tf_op jit(solution)/shard_map/ppermute | solution.py:50
  7.5 46.6 %collective-permute-start.2 = (bf16[128,2048]{1,0:T(8,128)(2,1)}, bf16[128,2048]{1,0:T(8,128)(2,1)S(1)}, u32[]{:S(2)}, u32[]{:S(2)}) collective-permute-start(bf16[128,2048]{1,0:T(8,128)(2,1)} %grads_ref.1), channel_id=1, source_target_pairs={{0,68},{1,69},{2,70},{3,71},{4,64},{5,65},{6,66},{7,67},{8,76},{9,... | collective-permute-start | bytes 1572872 | tf_op jit(solution)/shard_map/ppermute | solution.py:50
  12.5 41.5 %collective-permute-start = (bf16[128,128]{1,0:T(8,128)(2,1)}, bf16[128,128]{1,0:T(8,128)(2,1)S(1)}, u32[]{:S(2)}, u32[]{:S(2)}) collective-permute-start(bf16[128,128]{1,0:T(8,128)(2,1)} %get-tuple-element.53), channel_id=1, source_target_pairs={{0,68},{1,69},{2,70},{3,71},{4,64},{5,65},{6,66},{7,67},{8,76},{9,... | collective-permute-start | bytes 98312 | tf_op jit(solution)/shard_map/ppermute | solution.py:50
  20.9 38.2 %all-to-all-start = ((bf16[16,16,4224]{2,1,0:T(8,128)(2,1)}), bf16[16,16,4224]{2,1,0:T(8,128)(2,1)}, u32[]{:S(2)}, u32[]{:S(2)}) async-start(bf16[16,16,4224]{2,1,0:T(8,128)(2,1)} %bitcast.37), calls=%async_computation | async-start | bytes 4325376 | tf_op jit(solution)/shard_map/all_to_all | solution.py:54
  54.1 0.6 copy-start.5
  54.1 0.8 copy-start.3
  54.9 0.8 copy-start.4
  59.1 35.5 %all-to-all-start.1 = ((bf16[16,16,4224]{2,1,0:T(8,128)(2,1)}), bf16[16,16,4224]{2,1,0:T(8,128)(2,1)}, u32[]{:S(2)}, u32[]{:S(2)}) async-start(bf16[16,16,4224]{2,1,0:T(8,128)(2,1)} %bitcast.36), calls=%async_computation.1 | async-start | bytes 4325376 | tf_op jit(solution)/shard_map/all_to_all | solution.py:54
  113.9 13.3 %collective-permute-start.3 = (bf16[4,256,1536]{2,1,0:T(8,128)(2,1)}, bf16[4,256,1536]{2,1,0:T(8,128)(2,1)}, u32[]{:S(2)}, u32[]{:S(2)}) collective-permute-start(bf16[4,256,1536]{2,1,0:T(8,128)(2,1)} %wide.2), channel_id=1, source_target_pairs={{0,32},{32,0},{64,96},{96,64},{128,160},{160,128},{192,224},{224,1... | collective-permute-start | bytes 9437192 | tf_op jit(solution)/shard_map/ppermute | solution.py:461
  113.9 39.9 %all-to-all-start.2 = ((bf16[16,16,4224]{2,1,0:T(8,128)(2,1)}), bf16[16,16,4224]{2,1,0:T(8,128)(2,1)}, u32[]{:S(2)}, u32[]{:S(2)}) async-start(bf16[16,16,4224]{2,1,0:T(8,128)(2,1)} %get-tuple-element.59), calls=%async_computation.2 | async-start | bytes 4325376 | tf_op jit(solution)/shard_map/all_to_all | solution.py:54
  135.3 33.4 %collective-permute-start.8 = (bf16[4,96,2048]{2,1,0:T(8,128)(2,1)}, bf16[4,96,2048]{2,1,0:T(8,128)(2,1)}, u32[]{:S(2)}, u32[]{:S(2)}) collective-permute-start(bf16[4,96,2048]{2,1,0:T(8,128)(2,1)} %get-tuple-element.74), channel_id=1, source_target_pairs={{0,32},{32,0},{64,96},{96,64},{128,160},{160,128},{192,224},{224,1... | collective-permute-start | bytes 4718600 | tf_op jit(solution)/shard_map/ppermute | solution.py:461
  135.5 27.0 %collective-permute-start.4 = (bf16[256,1536]{1,0:T(8,128)(2,1)}, bf16[256,1536]{1,0:T(8,128)(2,1)}, u32[]{:S(2)}, u32[]{:S(2)}) collective-permute-start(bf16[256,1536]{1,0:T(8,128)(2,1)} %get-tuple-element.68), channel_id=1, source_target_pairs={{0,64},{32,96},{192,128},{224,160},{1,65},{33,97},{193,129},{225,1... | collective-permute-start | bytes 2359304 | tf_op jit(solution)/shard_map/ppermute | solution.py:466
  157.1 11.6 %copy-start = (bf16[4,96,2048]{2,1,0:T(8,128)(2,1)S(1)}, bf16[4,96,2048]{2,1,0:T(8,128)(2,1)}, u32[]{:S(2)}) copy-start(bf16[4,96,2048]{2,1,0:T(8,128)(2,1)} %get-tuple-element.72) | copy-start | bytes 4718596
  157.1 53.5 %collective-permute-start.7 = (bf16[128,4224]{1,0:T(8,128)(2,1)}, bf16[128,4224]{1,0:T(8,128)(2,1)S(1)}, u32[]{:S(2)}, u32[]{:S(2)}) collective-permute-start(bf16[128,4224]{1,0:T(8,128)(2,1)} %collect.1), channel_id=1, source_target_pairs={{0,68},{1,69},{2,70},{3,71},{4,64},{5,65},{6,66},{7,67},{8,76},{9,... | collective-permute-start | bytes 3244040 | tf_op jit(solution)/shard_map/ppermute | solution.py:50
  164.9 45.6 %collective-permute-start.6 = (bf16[256,1536]{1,0:T(8,128)(2,1)}, bf16[256,1536]{1,0:T(8,128)(2,1)}, u32[]{:S(2)}, u32[]{:S(2)}) collective-permute-start(bf16[256,1536]{1,0:T(8,128)(2,1)} %add_convert_fusion.3), channel_id=1, source_target_pairs={{192,128},{224,160},{128,64},{160,96},{193,129},{225,161},{129,65}... | collective-permute-start | bytes 2359304 | tf_op jit(solution)/shard_map/ppermute | solution.py:466
  166.5 44.1 %collective-permute-start.5 = (bf16[256,1536]{1,0:T(8,128)(2,1)}, bf16[256,1536]{1,0:T(8,128)(2,1)}, u32[]{:S(2)}, u32[]{:S(2)}) collective-permute-start(bf16[256,1536]{1,0:T(8,128)(2,1)} %add_convert_fusion.3), channel_id=1, source_target_pairs={{0,64},{32,96},{64,128},{96,160},{1,65},{33,97},{65,129},{97,161},... | collective-permute-start | bytes 2359304 | tf_op jit(solution)/shard_map/ppermute | solution.py:466
  170.0 45.0 %collective-permute-start.9 = (bf16[96,2048]{1,0:T(8,128)(2,1)S(1)}, bf16[96,2048]{1,0:T(8,128)(2,1)S(1)}, u32[]{:S(2)}, u32[]{:S(2)}) collective-permute-start(bf16[96,2048]{1,0:T(8,128)(2,1)S(1)} %select_bitcast_fusion.1), channel_id=1, source_target_pairs={{0,64},{32,96},{192,128},{224,160},{1,65},{33,97},{193,129},{225,1... | collective-permute-start | bytes 1179656 | tf_op jit(solution)/shard_map/ppermute | solution.py:466
  171.3 96.1 %all-to-all-start.3 = ((bf16[16,16,4224]{2,1,0:T(8,128)(2,1)}), bf16[16,16,4224]{2,1,0:T(8,128)(2,1)}, u32[]{:S(2)}, u32[]{:S(2)}) async-start(bf16[16,16,4224]{2,1,0:T(8,128)(2,1)} %get-tuple-element.60), calls=%async_computation.3 | async-start | bytes 4325376 | tf_op jit(solution)/shard_map/all_to_all | solution.py:54
  210.6 6.7 %copy-start.1 = (bf16[128,4224]{1,0:T(8,128)(2,1)}, bf16[128,4224]{1,0:T(8,128)(2,1)S(1)}, u32[]{:S(2)}) copy-start(bf16[128,4224]{1,0:T(8,128)(2,1)S(1)} %collective-permute-done.7.far_ref) | copy-start | bytes 3244036
  217.2 35.6 %collective-permute-start.12 = (bf16[256,1536]{1,0:T(8,128)(2,1)S(1)}, bf16[256,1536]{1,0:T(8,128)(2,1)S(1)}, u32[]{:S(2)}, u32[]{:S(2)}) collective-permute-start(bf16[256,1536]{1,0:T(8,128)(2,1)S(1)} %get-tuple-element.85), channel_id=1, source_target_pairs={{0,64},{32,96},{64,128},{96,160},{128,192},{160,224},{1,65},{33,97... | collective-permute-start | bytes 2359304 | tf_op jit(solution)/shard_map/ppermute | solution.py:466
  228.4 24.5 %collective-permute-start.13 = (bf16[256,1536]{1,0:T(8,128)(2,1)S(1)}, bf16[256,1536]{1,0:T(8,128)(2,1)S(1)}, u32[]{:S(2)}, u32[]{:S(2)}) collective-permute-start(bf16[256,1536]{1,0:T(8,128)(2,1)S(1)} %get-tuple-element.86), channel_id=1, source_target_pairs={{192,128},{224,160},{128,64},{160,96},{64,0},{96,32},{193,129},{22... | collective-permute-start | bytes 2359304 | tf_op jit(solution)/shard_map/ppermute | solution.py:466
  230.8 33.5 %copy-start.2 = (bf16[256,1536]{1,0:T(8,128)(2,1)S(1)}, bf16[256,1536]{1,0:T(8,128)(2,1)}, u32[]{:S(2)}) copy-start(bf16[256,1536]{1,0:T(8,128)(2,1)} %get-tuple-element.79) | copy-start | bytes 2359300
  230.8 6.0 %collective-permute-start.11 = (bf16[96,2048]{1,0:T(8,128)(2,1)S(1)}, bf16[96,2048]{1,0:T(8,128)(2,1)S(1)}, u32[]{:S(2)}, u32[]{:S(2)}) collective-permute-start(bf16[96,2048]{1,0:T(8,128)(2,1)S(1)} %fusion.4), channel_id=1, source_target_pairs={{192,128},{224,160},{128,64},{160,96},{193,129},{225,161},{129,65}... | collective-permute-start | bytes 1179656 | tf_op jit(solution)/shard_map/ppermute | solution.py:466
  231.7 21.2 %collective-permute-start.10 = (bf16[96,2048]{1,0:T(8,128)(2,1)S(1)}, bf16[96,2048]{1,0:T(8,128)(2,1)S(1)}, u32[]{:S(2)}, u32[]{:S(2)}) collective-permute-start(bf16[96,2048]{1,0:T(8,128)(2,1)S(1)} %fusion.4), channel_id=1, source_target_pairs={{0,64},{32,96},{64,128},{96,160},{1,65},{33,97},{65,129},{97,161},... | collective-permute-start | bytes 1179656 | tf_op jit(solution)/shard_map/ppermute | solution.py:466
  255.1 17.2 %collective-permute-start.15 = (bf16[96,2048]{1,0:T(8,128)(2,1)}, bf16[96,2048]{1,0:T(8,128)(2,1)}, u32[]{:S(2)}, u32[]{:S(2)}) collective-permute-start(bf16[96,2048]{1,0:T(8,128)(2,1)} %get-tuple-element.98), channel_id=1, source_target_pairs={{0,64},{32,96},{64,128},{96,160},{128,192},{160,224},{1,65},{33,97... | collective-permute-start | bytes 1179656 | tf_op jit(solution)/shard_map/ppermute | solution.py:466
  263.0 10.7 %collective-permute-start.16 = (bf16[96,2048]{1,0:T(8,128)(2,1)S(1)}, bf16[96,2048]{1,0:T(8,128)(2,1)}, u32[]{:S(2)}, u32[]{:S(2)}) collective-permute-start(bf16[96,2048]{1,0:T(8,128)(2,1)S(1)} %get-tuple-element.99), channel_id=1, source_target_pairs={{192,128},{224,160},{128,64},{160,96},{64,0},{96,32},{193,129},{22... | collective-permute-start | bytes 1179656 | tf_op jit(solution)/shard_map/ppermute | solution.py:466
  264.3 1.8 copy-start.6
  265.6 22.3 %collective-permute-start.14 = (bf16[256,1536]{1,0:T(8,128)(2,1)}, bf16[256,1536]{1,0:T(8,128)(2,1)}, u32[]{:S(2)}, u32[]{:S(2)}) collective-permute-start(bf16[256,1536]{1,0:T(8,128)(2,1)} %add_convert_fusion), channel_id=1, source_target_pairs={{0,16},{1,17},{2,18},{3,19},{4,20},{5,21},{6,22},{7,23},{8,24},{9,... | collective-permute-start | bytes 2359304 | tf_op jit(solution)/shard_map/ppermute | solution.py:552
  275.2 17.6 %collective-permute-start.17 = (bf16[96,2048]{1,0:T(8,128)(2,1)S(1)}, bf16[96,2048]{1,0:T(8,128)(2,1)S(1)}, u32[]{:S(2)}, u32[]{:S(2)}) collective-permute-start(bf16[96,2048]{1,0:T(8,128)(2,1)S(1)} %fusion.3), channel_id=1, source_target_pairs={{0,16},{1,17},{2,18},{3,19},{4,20},{5,21},{6,22},{7,23},{8,24},{9,... | collective-permute-start | bytes 1179656 | tf_op jit(solution)/shard_map/ppermute | solution.py:553

commit v9 on v8

--- a/solution.py
+++ b/solution.py
@@ -44,7 +44,7 @@
     pairs = []
     for dp in range(lax.axis_size("dp")):
         lo, core = divmod(dp, CORES)
-        other_dp = (lo ^ 1) * CORES + core
+        other_dp = (LO_SIZE - 1 - lo) * CORES + core
         for expert in range(experts):
             pairs.append((dp * experts + expert, other_dp * experts + (expert ^ Y_SIZE)))
     return lax.ppermute(value, BOTH, pairs)
@@ -524,23 +524,27 @@
 
     near_back, far_returned = lax.optimization_barrier((near_back, far_returned))
     near_returned = to_plane(near_back)
-    collected = collect(far_picked, far_returned)
-    far_total = across(collected)
-    arrived, unused = lax.optimization_barrier((arrived, collected))
 
     up, down = to_next(total([wide[2], arrived]))
-    up, down, far_total, narrow_arrived = lax.optimization_barrier(
-        (up, down, far_total, narrow_arrived)
-    )
+    up, down, narrow_arrived = lax.optimization_barrier((up, down, narrow_arrived))
     sent = lax.optimization_barrier((total([wide[1], up]), total([wide[3], down])))
     up, down = to_owner(*sent)
-    narrow_arrived, unused = lax.optimization_barrier((narrow_arrived, sent))
+    narrow_arrived, far_returned, unused = lax.optimization_barrier(
+        (narrow_arrived, far_returned, sent)
+    )
     narrow_up, narrow_down = to_next(total([narrow[2], narrow_arrived]))
-    narrow_up, narrow_down, up, down = lax.optimization_barrier((narrow_up, narrow_down, up, down))
+    collected = collect(far_picked, far_returned)
+    collected, near_returned, up, down = lax.optimization_barrier(
+        (collected, near_returned, up, down)
+    )
+    far_total = across(collected)
+    gate_up_sum = total([wide[0], up, down])
+    narrow_up, narrow_down, unused = lax.optimization_barrier(
+        (narrow_up, narrow_down, gate_up_sum)
+    )
     narrow_up, narrow_down = to_owner(
         total([narrow[1], narrow_up]), total([narrow[3], narrow_down])
     )
-    gate_up_sum = total([wide[0], up, down])
     down_sum = total([narrow[0], narrow_up, narrow_down])
 
     layer_out, grad_tokens, gate_grads = finish(
@@ -551,6 +555,7 @@
     swap = [(i, i ^ (devices // 2)) for i in range(devices)]
     other_gate_up = lax.ppermute(gate_up_sum, "expert", swap)
     other_down = lax.ppermute(down_sum, "expert", swap)
+    other_down, unused = lax.optimization_barrier((other_down, far_total))
     gate_up_sum = jnp.where(is_moved, other_gate_up, gate_up_sum)
     down_sum = jnp.where(is_moved, other_down, down_sum)
     grad_gate = gate_up_sum[:, :hidden_width]

time: 298 us -> 291 us (0.977)
  starting transfers between devices: 85.8 us -> 74.9 us
  waiting for transfers between devices: 122 us -> 128 us
    ppermute x10, waiting for transfers between devices: 21.8 us -> 35.1 us  [move(): return lax.ppermute(value, 'dp', pairs)]
    ppermute x10, starting transfers between devices: 37.6 us -> 27.2 us  [move(): return lax.ppermute(value, 'dp', pairs)]
    ppermute x1, waiting for transfers between devices: 11.1 us -> 5 us  [on_device(): other_gate_up = lax.ppermute(gate_up_sum, 'expert', swap)]
    ppermute x4, starting transfers between devices: 17.3 us -> 11.5 us  [across(): return lax.ppermute(value, BOTH, pairs)]
    ppermute x4, waiting for transfers between devices: 58 us -> 53.3 us  [across(): return lax.ppermute(value, BOTH, pairs)]
    all_to_all x4, waiting for transfers between devices: 28.3 us -> 32.3 us  [to_plane(): lax.all_to_all(blocks, 'expert', split_axis=0, concat_axis=0, axis_index_...]
    unnamed x17 -> x21, local copies, waits for them, and re-layouts: 5.93 us -> 6.19 us
  transfers between devices with their start and end apart: 22 -> 22, of which waited for: 9 -> 12; matrix products, arithmetic and copies ran while one was open for 7% -> 5% of each run, Pallas kernels for 15% -> 14%
where the time goes in v9:
time: 291 us; the launch traced here: 289 us
  waiting for transfers between devices  128 us (44%)
  starting transfers between devices  74.9 us (26%)
  Pallas kernels  62.2 us (21%)
  other arithmetic  14.6 us (5%)
  local copies, waits for them, and re-layouts  7.7 us (3%)
    ppermute x4, waiting for transfers between devices, across(): return lax.ppermute(value, BOTH, pairs)  53.3 us
    ppermute x10, waiting for transfers between devices, move(): return lax.ppermute(value, 'dp', pairs)  35.1 us
    all_to_all x4, waiting for transfers between devices, to_plane(): lax.all_to_all(blocks, 'expert', split_axis=0, concat_axis=0, axis_index_...  32.3 us
    all_to_all x4, starting transfers between devices, to_plane(): lax.all_to_all(blocks, 'expert', split_axis=0, concat_axis=0, axis_index_...  28.6 us
    ppermute x10, starting transfers between devices, move(): return lax.ppermute(value, 'dp', pairs)  27.2 us
    pallas_call x2, Pallas kernels, run_expert(): pl.pallas_call(expert_kernel, out_shape=(jax.ShapeDtypeStruct((PLANE, MOS...  25.5 us
    pallas_call x2, Pallas kernels, wide_grads(): pl.pallas_call(functools.partial(wide_kernel, keep, shard), grid_spec=plt...  14.7 us
    ppermute x4, starting transfers between devices, across(): return lax.ppermute(value, BOTH, pairs)  11.5 us
  transfers between devices with their start and end apart: 22, of which 12 were waited for; matrix products, arithmetic and copies ran while one was open for 5% of the time, Pallas kernels for 14%

profile of v9, /device:TPU:16, one launch (start us, length us, event | category | flops | bytes accessed | tf_op | source)
XLA Modules:
  0.0 289.3 jit_solution(18177658748048501455)
XLA Ops:
  0.6 5.9 %collective-permute-start.1 = (bf16[128,2048]{1,0:T(8,128)(2,1)}, bf16[128,2048]{1,0:T(8,128)(2,1)S(1)}, u32[]{:S(2)}, u32[]{:S(2)}) collective-permute-start(bf16[128,2048]{1,0:T(8,128)(2,1)} %tokens_ref.1), channel_id=1, source_target_pairs={{0,196},{1,197},{2,198},{3,199},{4,192},{5,193},{6,194},{7,195},{8... | collective-permute-start | bytes 1572872 | tf_op jit(solution)/shard_map/ppermute | solution.py:50
  6.6 0.1 collective-permute-start.2
  6.7 1.4 copy.16.ids_ref
  8.1 1.4 copy.15.gates_ref
  9.5 2.1 route.1
  11.6 3.1 %collective-permute-start = (bf16[128,128]{1,0:T(8,128)(2,1)}, bf16[128,128]{1,0:T(8,128)(2,1)S(1)}, u32[]{:S(2)}, u32[]{:S(2)}) collective-permute-start(bf16[128,128]{1,0:T(8,128)(2,1)} %get-tuple-element.53), channel_id=1, source_target_pairs={{0,196},{1,197},{2,198},{3,199},{4,192},{5,193},{6,194},{7,195},{8... | collective-permute-start | bytes 98312 | tf_op jit(solution)/shard_map/ppermute | solution.py:50
  14.8 3.5 %fill.2 = (bf16[256,4224]{1,0:T(8,128)(2,1)}, bf16[256,128]{1,0:T(8,128)(2,1)}) custom-call(bf16[128,128]{1,0:T(8,128)(2,1)} %get-tuple-element.51.sides_ref, bf16[128,2048]{1,0:T(8,128)(2,1)} %tokens_ref.1, bf16[128,2048]{1,0:T(8,128)(2,1)} %grads_ref.1), custom_call_target="tpu_custom_call" | custom-call | flops 1000000000 | bytes 4194304 | tf_op jit(solution)/shard_map/fill/pallas_call | solution.py:130
  18.2 7.3 %all-to-all-start = ((bf16[16,16,4224]{2,1,0:T(8,128)(2,1)}), bf16[16,16,4224]{2,1,0:T(8,128)(2,1)}, u32[]{:S(2)}, u32[]{:S(2)}) async-start(bf16[16,16,4224]{2,1,0:T(8,128)(2,1)} %bitcast.37), calls=%async_computation | async-start | bytes 4325376 | tf_op jit(solution)/shard_map/all_to_all | solution.py:54
  25.5 28.3 %collective-permute-done.sides_ref = bf16[128,128]{1,0:T(8,128)(2,1)S(1)} collective-permute-done((bf16[128,128]{1,0:T(8,128)(2,1)}, bf16[128,128]{1,0:T(8,128)(2,1)S(1)}, u32[]{:S(2)}, u32[]{:S(2)}) %collective-permute-start) | collective-permute-done | bytes 32800 | tf_op jit(solution)/shard_map/ppermute | solution.py:50
  53.8 0.6 copy-done.7
  54.4 0.2 copy-done.5
  54.6 0.8 copy-done.6
  55.4 3.5 %fill.3 = (bf16[256,4224]{1,0:T(8,128)(2,1)}, bf16[256,128]{1,0:T(8,128)(2,1)}) custom-call(bf16[128,128]{1,0:T(8,128)(2,1)} %copy-done.7, bf16[128,2048]{1,0:T(8,128)(2,1)} %copy-done.5, bf16[128,2048]{1,0:T(8,128)(2,1)} %copy-done.6), custom_call_target="tpu_custom_call" | custom-call | flops 999999995904 | bytes 4194304 | tf_op jit(solution)/shard_map/fill/pallas_call | solution.py:130
  58.9 7.3 %all-to-all-start.1 = ((bf16[16,16,4224]{2,1,0:T(8,128)(2,1)}), bf16[16,16,4224]{2,1,0:T(8,128)(2,1)}, u32[]{:S(2)}, u32[]{:S(2)}) async-start(bf16[16,16,4224]{2,1,0:T(8,128)(2,1)} %bitcast.36), calls=%async_computation.1 | async-start | bytes 4325376 | tf_op jit(solution)/shard_map/all_to_all | solution.py:54
  66.2 0.7 pad_add_fusion.where_ref
  66.8 12.8 %expert.2 = (bf16[16,16,4224]{2,1,0:T(8,128)(2,1)}, bf16[256,768]{1,0:T(8,128)(2,1)}, bf16[256,2048]{1,0:T(8,128)(2,1)}, bf16[256,1536]{1,0:T(8,128)(2,1)}) custom-call(s32[1]{0:T(128)} %bitcast.7.place_ref, bf16[256,4224]{1,0:T(8,128)(2,1)} %bitcast.4.rows_ref.near_x, bf16[2048,768]{1,0:T(8,128)(2,1)} %bitcast.38, bf16[2048,768]{1,0:T(8,128)(2,1)} %bitcast.40, ...), custom_call_target="tpu_custom_call" | custom-call | flops 4831838208 | bytes 9437184 | tf_op jit(solution)/shard_map/expert/pallas_call | solution.py:235
  79.7 16.1 %all-to-all-done.1 = bf16[16,16,4224]{2,1,0:T(8,128)(2,1)} async-done(((bf16[16,16,4224]{2,1,0:T(8,128)(2,1)}), bf16[16,16,4224]{2,1,0:T(8,128)(2,1)}, u32[]{:S(2)}, u32[]{:S(2)}) %all-to-all-start.1) | async-done | bytes 2162720 | tf_op jit(solution)/shard_map/all_to_all | solution.py:54
  95.7 12.7 %expert.3 = (bf16[16,16,4224]{2,1,0:T(8,128)(2,1)}, bf16[256,768]{1,0:T(8,128)(2,1)}, bf16[256,2048]{1,0:T(8,128)(2,1)}, bf16[256,1536]{1,0:T(8,128)(2,1)}) custom-call(s32[1]{0:T(128)} %bitcast.7.place_ref, bf16[256,4224]{1,0:T(8,128)(2,1)} %bitcast.6.rows_ref.far_x, bf16[2048,768]{1,0:T(8,128)(2,1)} %bitcast.39, bf16[2048,768]{1,0:T(8,128)(2,1)} %bitcast.41, ...), custom_call_target="tpu_custom_call" | custom-call | flops 4831838208 | bytes 9437184 | tf_op jit(solution)/shard_map/expert/pallas_call | solution.py:235
  108.4 6.7 %wide.2 = bf16[4,256,1536]{2,1,0:T(8,128)(2,1)} custom-call(s32[2]{0:T(128)} %pad_add_fusion.where_ref, bf16[256,4224]{1,0:T(8,128)(2,1)} %bitcast.4.rows_ref.near_x, bf16[256,4224]{1,0:T(8,128)(2,1)} %bitcast.6.rows_ref.far_x, bf16[256,1536]{1,0:T(8,128)(2,1)} %get-tuple-element.58.near_grads, bf16[256,1536]{1,0:T(8,128)(2,1)} %get-tuple-element.59.far_grads), custom_call_target="tpu_custom_call" | custom-call | flops 1610612736 | bytes 6291456 | tf_op jit(solution)/shard_map/wide/pallas_call | solution.py:310
  115.1 0.0 collective-permute-start.3
  115.1 6.8 %all-to-all-start.2 = ((bf16[16,16,4224]{2,1,0:T(8,128)(2,1)}), bf16[16,16,4224]{2,1,0:T(8,128)(2,1)}, u32[]{:S(2)}, u32[]{:S(2)}) async-start(bf16[16,16,4224]{2,1,0:T(8,128)(2,1)} %get-tuple-element.74), calls=%async_computation.2 | async-start | bytes 4325376 | tf_op jit(solution)/shard_map/all_to_all | solution.py:54
  121.9 6.4 %down.1 = (bf16[4,96,2048]{2,1,0:T(8,128)(2,1)}, bf16[4,96,2048]{2,1,0:T(8,128)(2,1)}) custom-call(s32[2]{0:T(128)} %pad_add_fusion.where_ref, bf16[256,768]{1,0:T(8,128)(2,1)} %get-tuple-element.60.near_hidden, bf16[256,768]{1,0:T(8,128)(2,1)} %get-tuple-element.61.far_hidden, bf16[256,2048]{1,0:T(8,128)(2,1)} %get-tuple-element.62.near_pick, ...), custom_call_target="tpu_custom_call" | custom-call | flops 1610612736 | bytes 6291456 | tf_op jit(solution)/shard_map/down/pallas_call | solution.py:359
  128.3 8.0 %wide.3 = (bf16[256,1536]{1,0:T(8,128)(2,1)}, bf16[256,1536]{1,0:T(8,128)(2,1)}, bf16[256,1536]{1,0:T(8,128)(2,1)}, bf16[256,1536]{1,0:T(8,128)(2,1)}, bf16[256,1536]{1,0:T(8,128)(2,1)}) custom-call(s32[2]{0:T(128)} %pad_add_fusion.where_ref, bf16[256,4224]{1,0:T(8,128)(2,1)} %bitcast.4.rows_ref.near_x, bf16[256,4224]{1,0:T(8,128)(2,1)} %bitcast.6.rows_ref.far_x, ...), custom_call_target="tpu_custom_call" | custom-call | flops 1610612736 | bytes 6291456 | tf_op jit(solution)/shard_map/wide/pallas_call | solution.py:310
  136.3 0.2 collective-permute-start.7
  136.6 2.2 collective-permute-start.4
  138.7 16.2 %all-to-all-done.2.returned_ref = bf16[16,16,4224]{2,1,0:T(8,128)(2,1)} async-done(((bf16[16,16,4224]{2,1,0:T(8,128)(2,1)}), bf16[16,16,4224]{2,1,0:T(8,128)(2,1)}, u32[]{:S(2)}, u32[]{:S(2)}) %all-to-all-start.2) | async-done | bytes 2162720 | tf_op jit(solution)/shard_map/all_to_all | solution.py:54
  155.0 7.2 %all-to-all-start.3 = ((bf16[16,16,4224]{2,1,0:T(8,128)(2,1)}), bf16[16,16,4224]{2,1,0:T(8,128)(2,1)}, u32[]{:S(2)}, u32[]{:S(2)}) async-start(bf16[16,16,4224]{2,1,0:T(8,128)(2,1)} %get-tuple-element.83), calls=%async_computation.3 | async-start | bytes 4325376 | tf_op jit(solution)/shard_map/all_to_all | solution.py:54
  162.2 1.4 add_convert_fusion.3
  163.7 0.8 collective-permute-start.6
  164.5 1.3 collective-permute-start.5
  165.9 1.3 select_bitcast_fusion.1
  167.2 2.1 collective-permute-start.8
  169.4 14.4 %collective-permute-done.5 = bf16[256,1536]{1,0:T(8,128)(2,1)S(1)} collective-permute-done((bf16[256,1536]{1,0:T(8,128)(2,1)S(1)}, bf16[256,1536]{1,0:T(8,128)(2,1)S(1)}, u32[]{:S(2)}, u32[]{:S(2)}) %collective-permute-start.5) | collective-permute-done | bytes 786464 | tf_op jit(solution)/shard_map/ppermute | solution.py:466
  183.8 7.2 %collective-permute-done.8 = bf16[96,2048]{1,0:T(8,128)(2,1)S(1)} collective-permute-done((bf16[96,2048]{1,0:T(8,128)(2,1)S(1)}, bf16[96,2048]{1,0:T(8,128)(2,1)S(1)}, u32[]{:S(2)}, u32[]{:S(2)}) %collective-permute-start.8) | collective-permute-done | bytes 393248 | tf_op jit(solution)/shard_map/ppermute | solution.py:466
  190.9 1.6 add_convert_fusion.1
  192.5 5.3 %collective-permute-start.9 = (bf16[256,1536]{1,0:T(8,128)(2,1)}, bf16[256,1536]{1,0:T(8,128)(2,1)}, u32[]{:S(2)}, u32[]{:S(2)}) collective-permute-start(bf16[256,1536]{1,0:T(8,128)(2,1)} %get-tuple-element.80), channel_id=1, source_target_pairs={{0,64},{32,96},{64,128},{96,160},{128,192},{160,224},{1,65},{33,97... | collective-permute-start | bytes 2359304 | tf_op jit(solution)/shard_map/ppermute | solution.py:466
  197.8 1.3 collective-permute-start.10
  199.0 1.9 fusion.1
  200.9 0.7 collective-permute-start.14
  201.6 5.9 %collective-permute-start.13 = (bf16[96,2048]{1,0:T(8,128)(2,1)}, bf16[96,2048]{1,0:T(8,128)(2,1)}, u32[]{:S(2)}, u32[]{:S(2)}) collective-permute-start(bf16[96,2048]{1,0:T(8,128)(2,1)} %fusion.1), channel_id=1, source_target_pairs={{0,64},{32,96},{64,128},{96,160},{1,65},{33,97},{65,129},{97,161},... | collective-permute-start | bytes 1179656 | tf_op jit(solution)/shard_map/ppermute | solution.py:466
  207.5 3.1 %collect.1 = bf16[128,4224]{1,0:T(8,128)(2,1)} custom-call(bf16[256,128]{1,0:T(8,128)(2,1)} %get-tuple-element.54.picked_ref, bf16[16,16,4224]{2,1,0:T(8,128)(2,1)} %all-to-all-done.2.returned_ref), custom_call_target="tpu_custom_call" | custom-call | flops 276824064 | bytes 2162688 | tf_op jit(solution)/shard_map/collect/pallas_call | solution.py:408
  210.7 4.5 %collective-permute-done.9 = bf16[256,1536]{1,0:T(8,128)(2,1)} collective-permute-done((bf16[256,1536]{1,0:T(8,128)(2,1)}, bf16[256,1536]{1,0:T(8,128)(2,1)}, u32[]{:S(2)}, u32[]{:S(2)}) %collective-permute-start.9) | collective-permute-done | bytes 786464 | tf_op jit(solution)/shard_map/ppermute | solution.py:466
  215.2 2.8 collective-permute-done.10
  218.0 1.9 add_convert_fusion
  219.8 0.0 copy-start.8
  219.9 1.5 collective-permute-done.13
  221.4 2.4 fusion.2
  223.8 6.2 %collective-permute-start.15 = (bf16[96,2048]{1,0:T(8,128)(2,1)}, bf16[96,2048]{1,0:T(8,128)(2,1)S(1)}, u32[]{:S(2)}, u32[]{:S(2)}) collective-permute-start(bf16[96,2048]{1,0:T(8,128)(2,1)} %get-tuple-element.102), channel_id=1, source_target_pairs={{0,64},{32,96},{64,128},{96,160},{128,192},{160,224},{1,65},{33,97... | collective-permute-start | bytes 1179656 | tf_op jit(solution)/shard_map/ppermute | solution.py:466
  230.0 1.3 collective-permute-start.16
  231.3 3.1 %collective-permute-start.12 = (bf16[256,1536]{1,0:T(8,128)(2,1)S(1)}, bf16[256,1536]{1,0:T(8,128)(2,1)}, u32[]{:S(2)}, u32[]{:S(2)}) collective-permute-start(bf16[256,1536]{1,0:T(8,128)(2,1)S(1)} %add_convert_fusion), channel_id=1, source_target_pairs={{0,16},{1,17},{2,18},{3,19},{4,20},{5,21},{6,22},{7,23},{8,24},{9,... | collective-permute-start | bytes 2359304 | tf_op jit(solution)/shard_map/ppermute | solution.py:556
  234.4 0.6 dynamic_slice.3
  235.6 2.3 collective-permute-start.11
  238.0 4.8 %collective-permute-done.16 = bf16[96,2048]{1,0:T(8,128)(2,1)} collective-permute-done((bf16[96,2048]{1,0:T(8,128)(2,1)S(1)}, bf16[96,2048]{1,0:T(8,128)(2,1)}, u32[]{:S(2)}, u32[]{:S(2)}) %collective-permute-start.16) | collective-permute-done | bytes 393248 | tf_op jit(solution)/shard_map/ppermute | solution.py:466
  242.7 1.3 fusion.4
  244.1 4.4 %collective-permute-start.17 = (bf16[96,2048]{1,0:T(8,128)(2,1)S(1)}, bf16[96,2048]{1,0:T(8,128)(2,1)S(1)}, u32[]{:S(2)}, u32[]{:S(2)}) collective-permute-start(bf16[96,2048]{1,0:T(8,128)(2,1)S(1)} %fusion.4), channel_id=1, source_target_pairs={{0,16},{1,17},{2,18},{3,19},{4,20},{5,21},{6,22},{7,23},{8,24},{9,... | collective-permute-start | bytes 1179656 | tf_op jit(solution)/shard_map/ppermute | solution.py:557
  248.5 5.0 %collective-permute-done.12 = bf16[256,1536]{1,0:T(8,128)(2,1)} collective-permute-done((bf16[256,1536]{1,0:T(8,128)(2,1)S(1)}, bf16[256,1536]{1,0:T(8,128)(2,1)}, u32[]{:S(2)}, u32[]{:S(2)}) %collective-permute-start.12) | collective-permute-done | bytes 786464 | tf_op jit(solution)/shard_map/ppermute | solution.py:556
  253.5 1.2 broadcast_select_fusion
  254.7 0.9 slice_bitcast_fusion
  255.6 2.7 collective-permute-done.17
  258.3 25.0 %collective-permute-done.11.far_ref = bf16[128,4224]{1,0:T(8,128)(2,1)S(1)} collective-permute-done((bf16[128,4224]{1,0:T(8,128)(2,1)}, bf16[128,4224]{1,0:T(8,128)(2,1)S(1)}, u32[]{:S(2)}, u32[]{:S(2)}) %collective-permute-start.11) | collective-permute-done | bytes 1081376 | tf_op jit(solution)/shard_map/ppermute | solution.py:50
  283.3 0.8 select_bitcast_fusion
  284.1 0.3 copy-done.1
  284.4 3.4 %finish.1 = (bf16[128,2048]{1,0:T(8,128)(2,1)}, bf16[128,2048]{1,0:T(8,128)(2,1)}, f32[128,8]{1,0:T(8,128)}) custom-call(s32[1]{0:T(128)} %bitcast.half_ref, s32[128,8]{1,0:T(8,128)} %copy.16.ids_ref, bf16[256,128]{1,0:T(8,128)(2,1)} %get-tuple-element.52.picked_ref, bf16[16,16,4224]{2,1,0:T(8,128)(2,1)} %all-to-all-done.3.returned_ref, ...), custom_call_target="tpu_custom_call" | custom-call | flops 276824064 | bytes 2162688 | tf_op jit(solution)/shard_map/finish/pallas_call | solution.py:447
  287.8 1.5 copy.17
  (23 shorter events, 0.1 us)
Async XLA Ops:
  0.6 53.2 %collective-permute-start.1 = (bf16[128,2048]{1,0:T(8,128)(2,1)}, bf16[128,2048]{1,0:T(8,128)(2,1)S(1)}, u32[]{:S(2)}, u32[]{:S(2)}) collective-permute-start(bf16[128,2048]{1,0:T(8,128)(2,1)} %tokens_ref.1), channel_id=1, source_target_pairs={{0,196},{1,197},{2,198},{3,199},{4,192},{5,193},{6,194},{7,195},{8... | collective-permute-start | bytes 1572872 | tf_op jit(solution)/shard_map/ppermute | solution.py:50
  6.6 47.3 %collective-permute-start.2 = (bf16[128,2048]{1,0:T(8,128)(2,1)}, bf16[128,2048]{1,0:T(8,128)(2,1)S(1)}, u32[]{:S(2)}, u32[]{:S(2)}) collective-permute-start(bf16[128,2048]{1,0:T(8,128)(2,1)} %grads_ref.1), channel_id=1, source_target_pairs={{0,196},{1,197},{2,198},{3,199},{4,192},{5,193},{6,194},{7,195},{8... | collective-permute-start | bytes 1572872 | tf_op jit(solution)/shard_map/ppermute | solution.py:50
  11.6 42.2 %collective-permute-start = (bf16[128,128]{1,0:T(8,128)(2,1)}, bf16[128,128]{1,0:T(8,128)(2,1)S(1)}, u32[]{:S(2)}, u32[]{:S(2)}) collective-permute-start(bf16[128,128]{1,0:T(8,128)(2,1)} %get-tuple-element.53), channel_id=1, source_target_pairs={{0,196},{1,197},{2,198},{3,199},{4,192},{5,193},{6,194},{7,195},{8... | collective-permute-start | bytes 98312 | tf_op jit(solution)/shard_map/ppermute | solution.py:50
  18.2 40.7 %all-to-all-start = ((bf16[16,16,4224]{2,1,0:T(8,128)(2,1)}), bf16[16,16,4224]{2,1,0:T(8,128)(2,1)}, u32[]{:S(2)}, u32[]{:S(2)}) async-start(bf16[16,16,4224]{2,1,0:T(8,128)(2,1)} %bitcast.37), calls=%async_computation | async-start | bytes 4325376 | tf_op jit(solution)/shard_map/all_to_all | solution.py:54
  53.8 0.6 copy-start.7
  53.8 0.8 copy-start.5
  54.6 0.8 copy-start.6
  58.9 36.8 %all-to-all-start.1 = ((bf16[16,16,4224]{2,1,0:T(8,128)(2,1)}), bf16[16,16,4224]{2,1,0:T(8,128)(2,1)}, u32[]{:S(2)}, u32[]{:S(2)}) async-start(bf16[16,16,4224]{2,1,0:T(8,128)(2,1)} %bitcast.36), calls=%async_computation.1 | async-start | bytes 4325376 | tf_op jit(solution)/shard_map/all_to_all | solution.py:54
  115.1 13.2 %collective-permute-start.3 = (bf16[4,256,1536]{2,1,0:T(8,128)(2,1)}, bf16[4,256,1536]{2,1,0:T(8,128)(2,1)}, u32[]{:S(2)}, u32[]{:S(2)}) collective-permute-start(bf16[4,256,1536]{2,1,0:T(8,128)(2,1)} %wide.2), channel_id=1, source_target_pairs={{0,32},{32,0},{64,96},{96,64},{128,160},{160,128},{192,224},{224,1... | collective-permute-start | bytes 9437192 | tf_op jit(solution)/shard_map/ppermute | solution.py:461
  115.1 39.8 %all-to-all-start.2 = ((bf16[16,16,4224]{2,1,0:T(8,128)(2,1)}), bf16[16,16,4224]{2,1,0:T(8,128)(2,1)}, u32[]{:S(2)}, u32[]{:S(2)}) async-start(bf16[16,16,4224]{2,1,0:T(8,128)(2,1)} %get-tuple-element.74), calls=%async_computation.2 | async-start | bytes 4325376 | tf_op jit(solution)/shard_map/all_to_all | solution.py:54
  136.3 29.5 %collective-permute-start.7 = (bf16[4,96,2048]{2,1,0:T(8,128)(2,1)}, bf16[4,96,2048]{2,1,0:T(8,128)(2,1)}, u32[]{:S(2)}, u32[]{:S(2)}) collective-permute-start(bf16[4,96,2048]{2,1,0:T(8,128)(2,1)} %get-tuple-element.70), channel_id=1, source_target_pairs={{0,32},{32,0},{64,96},{96,64},{128,160},{160,128},{192,224},{224,1... | collective-permute-start | bytes 4718600 | tf_op jit(solution)/shard_map/ppermute | solution.py:461
  136.6 25.6 %collective-permute-start.4 = (bf16[256,1536]{1,0:T(8,128)(2,1)}, bf16[256,1536]{1,0:T(8,128)(2,1)}, u32[]{:S(2)}, u32[]{:S(2)}) collective-permute-start(bf16[256,1536]{1,0:T(8,128)(2,1)} %get-tuple-element.67), channel_id=1, source_target_pairs={{0,64},{32,96},{192,128},{224,160},{1,65},{33,97},{193,129},{225,1... | collective-permute-start | bytes 2359304 | tf_op jit(solution)/shard_map/ppermute | solution.py:466
  154.9 7.2 %copy-start.4 = (bf16[256,1536]{1,0:T(8,128)(2,1)S(1)}, bf16[256,1536]{1,0:T(8,128)(2,1)}, u32[]{:S(2)}) copy-start(bf16[256,1536]{1,0:T(8,128)(2,1)} %get-tuple-element.66) | copy-start | bytes 2359300
  155.0 55.7 %all-to-all-start.3 = ((bf16[16,16,4224]{2,1,0:T(8,128)(2,1)}), bf16[16,16,4224]{2,1,0:T(8,128)(2,1)}, u32[]{:S(2)}, u32[]{:S(2)}) async-start(bf16[16,16,4224]{2,1,0:T(8,128)(2,1)} %get-tuple-element.83), calls=%async_computation.3 | async-start | bytes 4325376 | tf_op jit(solution)/shard_map/all_to_all | solution.py:54
  162.2 3.7 %copy-start = (bf16[4,96,2048]{2,1,0:T(8,128)(2,1)S(1)}, bf16[4,96,2048]{2,1,0:T(8,128)(2,1)}, u32[]{:S(2)}) copy-start(bf16[4,96,2048]{2,1,0:T(8,128)(2,1)} %get-tuple-element.68) | copy-start | bytes 4718596
  163.6 27.3 %copy-start.2 = (bf16[256,1536]{1,0:T(8,128)(2,1)S(1)}, bf16[256,1536]{1,0:T(8,128)(2,1)}, u32[]{:S(2)}) copy-start(bf16[256,1536]{1,0:T(8,128)(2,1)} %get-tuple-element.76) | copy-start | bytes 2359300
  163.7 27.3 %copy-start.3 = (bf16[256,1536]{1,0:T(8,128)(2,1)S(1)}, bf16[256,1536]{1,0:T(8,128)(2,1)}, u32[]{:S(2)}) copy-start(bf16[256,1536]{1,0:T(8,128)(2,1)} %get-tuple-element.78) | copy-start | bytes 2359300
  163.7 5.7 %collective-permute-start.6 = (bf16[256,1536]{1,0:T(8,128)(2,1)S(1)}, bf16[256,1536]{1,0:T(8,128)(2,1)S(1)}, u32[]{:S(2)}, u32[]{:S(2)}) collective-permute-start(bf16[256,1536]{1,0:T(8,128)(2,1)S(1)} %add_convert_fusion.3), channel_id=1, source_target_pairs={{192,128},{224,160},{128,64},{160,96},{193,129},{225,161},{129,65}... | collective-permute-start | bytes 2359304 | tf_op jit(solution)/shard_map/ppermute | solution.py:466
  164.5 19.2 %collective-permute-start.5 = (bf16[256,1536]{1,0:T(8,128)(2,1)S(1)}, bf16[256,1536]{1,0:T(8,128)(2,1)S(1)}, u32[]{:S(2)}, u32[]{:S(2)}) collective-permute-start(bf16[256,1536]{1,0:T(8,128)(2,1)S(1)} %add_convert_fusion.3), channel_id=1, source_target_pairs={{0,64},{32,96},{64,128},{96,160},{1,65},{33,97},{65,129},{97,161},... | collective-permute-start | bytes 2359304 | tf_op jit(solution)/shard_map/ppermute | solution.py:466
  167.2 23.7 %collective-permute-start.8 = (bf16[96,2048]{1,0:T(8,128)(2,1)S(1)}, bf16[96,2048]{1,0:T(8,128)(2,1)S(1)}, u32[]{:S(2)}, u32[]{:S(2)}) collective-permute-start(bf16[96,2048]{1,0:T(8,128)(2,1)S(1)} %select_bitcast_fusion.1), channel_id=1, source_target_pairs={{0,64},{32,96},{192,128},{224,160},{1,65},{33,97},{193,129},{225,1... | collective-permute-start | bytes 1179656 | tf_op jit(solution)/shard_map/ppermute | solution.py:466
  192.5 22.7 %collective-permute-start.9 = (bf16[256,1536]{1,0:T(8,128)(2,1)}, bf16[256,1536]{1,0:T(8,128)(2,1)}, u32[]{:S(2)}, u32[]{:S(2)}) collective-permute-start(bf16[256,1536]{1,0:T(8,128)(2,1)} %get-tuple-element.80), channel_id=1, source_target_pairs={{0,64},{32,96},{64,128},{96,160},{128,192},{160,224},{1,65},{33,97... | collective-permute-start | bytes 2359304 | tf_op jit(solution)/shard_map/ppermute | solution.py:466
  197.8 20.2 %collective-permute-start.10 = (bf16[256,1536]{1,0:T(8,128)(2,1)}, bf16[256,1536]{1,0:T(8,128)(2,1)}, u32[]{:S(2)}, u32[]{:S(2)}) collective-permute-start(bf16[256,1536]{1,0:T(8,128)(2,1)} %get-tuple-element.81), channel_id=1, source_target_pairs={{192,128},{224,160},{128,64},{160,96},{64,0},{96,32},{193,129},{22... | collective-permute-start | bytes 2359304 | tf_op jit(solution)/shard_map/ppermute | solution.py:466
  200.9 18.9 %collective-permute-start.14 = (bf16[96,2048]{1,0:T(8,128)(2,1)}, bf16[96,2048]{1,0:T(8,128)(2,1)S(1)}, u32[]{:S(2)}, u32[]{:S(2)}) collective-permute-start(bf16[96,2048]{1,0:T(8,128)(2,1)} %fusion.1), channel_id=1, source_target_pairs={{192,128},{224,160},{128,64},{160,96},{193,129},{225,161},{129,65}... | collective-permute-start | bytes 1179656 | tf_op jit(solution)/shard_map/ppermute | solution.py:466
  201.6 19.8 %collective-permute-start.13 = (bf16[96,2048]{1,0:T(8,128)(2,1)}, bf16[96,2048]{1,0:T(8,128)(2,1)}, u32[]{:S(2)}, u32[]{:S(2)}) collective-permute-start(bf16[96,2048]{1,0:T(8,128)(2,1)} %fusion.1), channel_id=1, source_target_pairs={{0,64},{32,96},{64,128},{96,160},{1,65},{33,97},{65,129},{97,161},... | collective-permute-start | bytes 1179656 | tf_op jit(solution)/shard_map/ppermute | solution.py:466
  219.8 14.5 %copy-start.8 = (s32[32]{0:T(128)S(1)}, s32[32]{0:T(128)}, u32[]{:S(2)}) copy-start(s32[32]{0:T(128)} %param.12) | copy-start | bytes 388
  223.8 14.2 %collective-permute-start.15 = (bf16[96,2048]{1,0:T(8,128)(2,1)}, bf16[96,2048]{1,0:T(8,128)(2,1)S(1)}, u32[]{:S(2)}, u32[]{:S(2)}) collective-permute-start(bf16[96,2048]{1,0:T(8,128)(2,1)} %get-tuple-element.102), channel_id=1, source_target_pairs={{0,64},{32,96},{64,128},{96,160},{128,192},{160,224},{1,65},{33,97... | collective-permute-start | bytes 1179656 | tf_op jit(solution)/shard_map/ppermute | solution.py:466
  230.0 12.7 %collective-permute-start.16 = (bf16[96,2048]{1,0:T(8,128)(2,1)S(1)}, bf16[96,2048]{1,0:T(8,128)(2,1)}, u32[]{:S(2)}, u32[]{:S(2)}) collective-permute-start(bf16[96,2048]{1,0:T(8,128)(2,1)S(1)} %get-tuple-element.103), channel_id=1, source_target_pairs={{192,128},{224,160},{128,64},{160,96},{64,0},{96,32},{193,129},{22... | collective-permute-start | bytes 1179656 | tf_op jit(solution)/shard_map/ppermute | solution.py:466
  231.3 22.2 %collective-permute-start.12 = (bf16[256,1536]{1,0:T(8,128)(2,1)S(1)}, bf16[256,1536]{1,0:T(8,128)(2,1)}, u32[]{:S(2)}, u32[]{:S(2)}) collective-permute-start(bf16[256,1536]{1,0:T(8,128)(2,1)S(1)} %add_convert_fusion), channel_id=1, source_target_pairs={{0,16},{1,17},{2,18},{3,19},{4,20},{5,21},{6,22},{7,23},{8,24},{9,... | collective-permute-start | bytes 2359304 | tf_op jit(solution)/shard_map/ppermute | solution.py:556
  235.6 47.7 %collective-permute-start.11 = (bf16[128,4224]{1,0:T(8,128)(2,1)}, bf16[128,4224]{1,0:T(8,128)(2,1)S(1)}, u32[]{:S(2)}, u32[]{:S(2)}) collective-permute-start(bf16[128,4224]{1,0:T(8,128)(2,1)} %collect.1), channel_id=1, source_target_pairs={{0,196},{1,197},{2,198},{3,199},{4,192},{5,193},{6,194},{7,195},{8... | collective-permute-start | bytes 3244040 | tf_op jit(solution)/shard_map/ppermute | solution.py:50
  244.1 14.2 %collective-permute-start.17 = (bf16[96,2048]{1,0:T(8,128)(2,1)S(1)}, bf16[96,2048]{1,0:T(8,128)(2,1)S(1)}, u32[]{:S(2)}, u32[]{:S(2)}) collective-permute-start(bf16[96,2048]{1,0:T(8,128)(2,1)S(1)} %fusion.4), channel_id=1, source_target_pairs={{0,16},{1,17},{2,18},{3,19},{4,20},{5,21},{6,22},{7,23},{8,24},{9,... | collective-permute-start | bytes 1179656 | tf_op jit(solution)/shard_map/ppermute | solution.py:557
  283.3 1.1 copy-start.1

commit v10 on v8

--- a/solution.py
+++ b/solution.py
@@ -44,7 +44,7 @@
     pairs = []
     for dp in range(lax.axis_size("dp")):
         lo, core = divmod(dp, CORES)
-        other_dp = (lo ^ 1) * CORES + core
+        other_dp = (LO_SIZE - 1 - lo) * CORES + core
         for expert in range(experts):
             pairs.append((dp * experts + expert, other_dp * experts + (expert ^ Y_SIZE)))
     return lax.ppermute(value, BOTH, pairs)

time: 298 us -> 285 us (0.956)
  waiting for transfers between devices: 122 us -> 101 us
  starting transfers between devices: 85.8 us -> 92.7 us
    ppermute x4, waiting for transfers between devices: 58 us -> 33 us  [across(): return lax.ppermute(value, BOTH, pairs)]
    all_to_all x4, starting transfers between devices: 28.5 us -> 51.9 us  [to_plane(): lax.all_to_all(blocks, 'expert', split_axis=0, concat_axis=0, axis_index_...]
    ppermute x10, starting transfers between devices: 37.6 us -> 29.1 us  [move(): return lax.ppermute(value, 'dp', pairs)]
    ppermute x4, starting transfers between devices: 17.3 us -> 10.9 us  [across(): return lax.ppermute(value, BOTH, pairs)]
    all_to_all x4, waiting for transfers between devices: 28.3 us -> 32.4 us  [to_plane(): lax.all_to_all(blocks, 'expert', split_axis=0, concat_axis=0, axis_index_...]
where the time goes in v10:
time: 285 us; the launch traced here: 280 us
  waiting for transfers between devices  101 us (35%)
  starting transfers between devices  92.7 us (33%)
  Pallas kernels  62.2 us (22%)
  other arithmetic  14.7 us (5%)
  local copies, waits for them, and re-layouts  7.44 us (3%)
    all_to_all x4, starting transfers between devices, to_plane(): lax.all_to_all(blocks, 'expert', split_axis=0, concat_axis=0, axis_index_...  51.9 us
    ppermute x4, waiting for transfers between devices, across(): return lax.ppermute(value, BOTH, pairs)  33 us
    all_to_all x4, waiting for transfers between devices, to_plane(): lax.all_to_all(blocks, 'expert', split_axis=0, concat_axis=0, axis_index_...  32.4 us
    ppermute x10, starting transfers between devices, move(): return lax.ppermute(value, 'dp', pairs)  29.1 us
    pallas_call x2, Pallas kernels, run_expert(): pl.pallas_call(expert_kernel, out_shape=(jax.ShapeDtypeStruct((PLANE, MOS...  25.5 us
    ppermute x10, waiting for transfers between devices, move(): return lax.ppermute(value, 'dp', pairs)  21.2 us
    pallas_call x2, Pallas kernels, wide_grads(): pl.pallas_call(functools.partial(wide_kernel, keep, shard), grid_spec=plt...  14.6 us
    ppermute x1, waiting for transfers between devices, on_device(): other_gate_up = lax.ppermute(gate_up_sum, 'expert', swap)  11.1 us
  transfers between devices with their start and end apart: 22, of which 9 were waited for; matrix products, arithmetic and copies ran while one was open for 7% of the time, Pallas kernels for 15%

profile of v10, /device:TPU:16, one launch (start us, length us, event | category | flops | bytes accessed | tf_op | source)
XLA Modules:
  0.0 279.9 jit_solution(4458195628969294789)
XLA Ops:
  0.6 5.9 %collective-permute-start.1 = (bf16[128,2048]{1,0:T(8,128)(2,1)}, bf16[128,2048]{1,0:T(8,128)(2,1)S(1)}, u32[]{:S(2)}, u32[]{:S(2)}) collective-permute-start(bf16[128,2048]{1,0:T(8,128)(2,1)} %tokens_ref.1), channel_id=1, source_target_pairs={{0,196},{1,197},{2,198},{3,199},{4,192},{5,193},{6,194},{7,195},{8... | collective-permute-start | bytes 1572872 | tf_op jit(solution)/shard_map/ppermute | solution.py:50
  6.6 0.1 collective-permute-start.2
  6.7 1.4 copy.16.ids_ref
  8.1 1.4 copy.15.gates_ref
  9.5 2.1 route.1
  11.6 3.1 %collective-permute-start = (bf16[128,128]{1,0:T(8,128)(2,1)}, bf16[128,128]{1,0:T(8,128)(2,1)S(1)}, u32[]{:S(2)}, u32[]{:S(2)}) collective-permute-start(bf16[128,128]{1,0:T(8,128)(2,1)} %get-tuple-element.53), channel_id=1, source_target_pairs={{0,196},{1,197},{2,198},{3,199},{4,192},{5,193},{6,194},{7,195},{8... | collective-permute-start | bytes 98312 | tf_op jit(solution)/shard_map/ppermute | solution.py:50
  14.8 3.5 %fill.2 = (bf16[256,4224]{1,0:T(8,128)(2,1)}, bf16[256,128]{1,0:T(8,128)(2,1)}) custom-call(bf16[128,128]{1,0:T(8,128)(2,1)} %get-tuple-element.49.sides_ref, bf16[128,2048]{1,0:T(8,128)(2,1)} %tokens_ref.1, bf16[128,2048]{1,0:T(8,128)(2,1)} %grads_ref.1), custom_call_target="tpu_custom_call" | custom-call | flops 1000000000 | bytes 4194304 | tf_op jit(solution)/shard_map/fill/pallas_call | solution.py:130
  18.3 7.3 %all-to-all-start = ((bf16[16,16,4224]{2,1,0:T(8,128)(2,1)}), bf16[16,16,4224]{2,1,0:T(8,128)(2,1)}, u32[]{:S(2)}, u32[]{:S(2)}) async-start(bf16[16,16,4224]{2,1,0:T(8,128)(2,1)} %bitcast.37), calls=%async_computation | async-start | bytes 4325376 | tf_op jit(solution)/shard_map/all_to_all | solution.py:54
  25.5 28.3 %collective-permute-done.sides_ref = bf16[128,128]{1,0:T(8,128)(2,1)S(1)} collective-permute-done((bf16[128,128]{1,0:T(8,128)(2,1)}, bf16[128,128]{1,0:T(8,128)(2,1)S(1)}, u32[]{:S(2)}, u32[]{:S(2)}) %collective-permute-start) | collective-permute-done | bytes 32800 | tf_op jit(solution)/shard_map/ppermute | solution.py:50
  53.8 0.0 collective-permute-done.1.tokens_ref
  53.8 0.0 collective-permute-done.2.grads_ref
  53.8 0.6 copy-done.5
  54.4 0.2 copy-done.3
  54.6 0.8 copy-done.4
  55.4 3.5 %fill.3 = (bf16[256,4224]{1,0:T(8,128)(2,1)}, bf16[256,128]{1,0:T(8,128)(2,1)}) custom-call(bf16[128,128]{1,0:T(8,128)(2,1)} %copy-done.5, bf16[128,2048]{1,0:T(8,128)(2,1)} %copy-done.3, bf16[128,2048]{1,0:T(8,128)(2,1)} %copy-done.4), custom_call_target="tpu_custom_call" | custom-call | flops 999999995904 | bytes 4194304 | tf_op jit(solution)/shard_map/fill/pallas_call | solution.py:130
  58.9 0.0 all-to-all-done
  58.9 7.3 %all-to-all-start.1 = ((bf16[16,16,4224]{2,1,0:T(8,128)(2,1)}), bf16[16,16,4224]{2,1,0:T(8,128)(2,1)}, u32[]{:S(2)}, u32[]{:S(2)}) async-start(bf16[16,16,4224]{2,1,0:T(8,128)(2,1)} %bitcast.36), calls=%async_computation.1 | async-start | bytes 4325376 | tf_op jit(solution)/shard_map/all_to_all | solution.py:54
  66.2 0.6 pad_add_fusion.where_ref
  66.8 12.8 %expert.2 = (bf16[16,16,4224]{2,1,0:T(8,128)(2,1)}, bf16[256,768]{1,0:T(8,128)(2,1)}, bf16[256,2048]{1,0:T(8,128)(2,1)}, bf16[256,1536]{1,0:T(8,128)(2,1)}) custom-call(s32[1]{0:T(128)} %bitcast.1.place_ref, bf16[256,4224]{1,0:T(8,128)(2,1)} %bitcast.3.rows_ref.near_x, bf16[2048,768]{1,0:T(8,128)(2,1)} %bitcast.38, bf16[2048,768]{1,0:T(8,128)(2,1)} %bitcast.40, ...), custom_call_target="tpu_custom_call" | custom-call | flops 4831838208 | bytes 9437184 | tf_op jit(solution)/shard_map/expert/pallas_call | solution.py:235
  79.6 16.1 %all-to-all-done.1 = bf16[16,16,4224]{2,1,0:T(8,128)(2,1)} async-done(((bf16[16,16,4224]{2,1,0:T(8,128)(2,1)}), bf16[16,16,4224]{2,1,0:T(8,128)(2,1)}, u32[]{:S(2)}, u32[]{:S(2)}) %all-to-all-start.1) | async-done | bytes 2162720 | tf_op jit(solution)/shard_map/all_to_all | solution.py:54
  95.7 12.7 %expert.3 = (bf16[16,16,4224]{2,1,0:T(8,128)(2,1)}, bf16[256,768]{1,0:T(8,128)(2,1)}, bf16[256,2048]{1,0:T(8,128)(2,1)}, bf16[256,1536]{1,0:T(8,128)(2,1)}) custom-call(s32[1]{0:T(128)} %bitcast.1.place_ref, bf16[256,4224]{1,0:T(8,128)(2,1)} %bitcast.8.rows_ref.far_x, bf16[2048,768]{1,0:T(8,128)(2,1)} %bitcast.39, bf16[2048,768]{1,0:T(8,128)(2,1)} %bitcast.41, ...), custom_call_target="tpu_custom_call" | custom-call | flops 4831838208 | bytes 9437184 | tf_op jit(solution)/shard_map/expert/pallas_call | solution.py:235
  108.5 6.6 %wide.2 = bf16[4,256,1536]{2,1,0:T(8,128)(2,1)} custom-call(s32[2]{0:T(128)} %pad_add_fusion.where_ref, bf16[256,4224]{1,0:T(8,128)(2,1)} %bitcast.3.rows_ref.near_x, bf16[256,4224]{1,0:T(8,128)(2,1)} %bitcast.8.rows_ref.far_x, bf16[256,1536]{1,0:T(8,128)(2,1)} %get-tuple-element.57.near_grads, bf16[256,1536]{1,0:T(8,128)(2,1)} %get-tuple-element.58.far_grads), custom_call_target="tpu_custom_call" | custom-call | flops 1610612736 | bytes 6291456 | tf_op jit(solution)/shard_map/wide/pallas_call | solution.py:310
  115.0 0.0 collective-permute-start.3
  115.0 6.8 %all-to-all-start.2 = ((bf16[16,16,4224]{2,1,0:T(8,128)(2,1)}), bf16[16,16,4224]{2,1,0:T(8,128)(2,1)}, u32[]{:S(2)}, u32[]{:S(2)}) async-start(bf16[16,16,4224]{2,1,0:T(8,128)(2,1)} %get-tuple-element.59), calls=%async_computation.2 | async-start | bytes 4325376 | tf_op jit(solution)/shard_map/all_to_all | solution.py:54
  121.8 6.4 %down.1 = (bf16[4,96,2048]{2,1,0:T(8,128)(2,1)}, bf16[4,96,2048]{2,1,0:T(8,128)(2,1)}) custom-call(s32[2]{0:T(128)} %pad_add_fusion.where_ref, bf16[256,768]{1,0:T(8,128)(2,1)} %get-tuple-element.61.near_hidden, bf16[256,768]{1,0:T(8,128)(2,1)} %get-tuple-element.62.far_hidden, bf16[256,2048]{1,0:T(8,128)(2,1)} %get-tuple-element.63.near_pick, ...), custom_call_target="tpu_custom_call" | custom-call | flops 1610612736 | bytes 6291456 | tf_op jit(solution)/shard_map/down/pallas_call | solution.py:359
  128.2 0.0 collective-permute-done.3.refs_0_
  128.2 8.1 %wide.3 = (bf16[256,1536]{1,0:T(8,128)(2,1)}, bf16[256,1536]{1,0:T(8,128)(2,1)}, bf16[256,1536]{1,0:T(8,128)(2,1)}, bf16[256,1536]{1,0:T(8,128)(2,1)}, bf16[256,1536]{1,0:T(8,128)(2,1)}) custom-call(s32[2]{0:T(128)} %pad_add_fusion.where_ref, bf16[256,4224]{1,0:T(8,128)(2,1)} %bitcast.3.rows_ref.near_x, bf16[256,4224]{1,0:T(8,128)(2,1)} %bitcast.8.rows_ref.far_x, ...), custom_call_target="tpu_custom_call" | custom-call | flops 1610612736 | bytes 6291456 | tf_op jit(solution)/shard_map/wide/pallas_call | solution.py:310
  136.3 0.2 collective-permute-start.8
  136.5 2.2 collective-permute-start.4
  138.7 16.2 %all-to-all-done.2.returned_ref = bf16[16,16,4224]{2,1,0:T(8,128)(2,1)} async-done(((bf16[16,16,4224]{2,1,0:T(8,128)(2,1)}), bf16[16,16,4224]{2,1,0:T(8,128)(2,1)}, u32[]{:S(2)}, u32[]{:S(2)}) %all-to-all-start.2) | async-done | bytes 2162720 | tf_op jit(solution)/shard_map/all_to_all | solution.py:54
  154.9 3.2 %collect.1 = bf16[128,4224]{1,0:T(8,128)(2,1)} custom-call(bf16[256,128]{1,0:T(8,128)(2,1)} %get-tuple-element.69.picked_ref, bf16[16,16,4224]{2,1,0:T(8,128)(2,1)} %all-to-all-done.2.returned_ref), custom_call_target="tpu_custom_call" | custom-call | flops 276824064 | bytes 2162688 | tf_op jit(solution)/shard_map/collect/pallas_call | solution.py:408
  158.0 1.7 collective-permute-start.7
  159.7 2.5 add_convert_fusion.3
  162.2 1.5 collective-permute-start.6
  163.7 2.2 collective-permute-start.5
  165.9 1.3 select_bitcast_fusion.1
  167.3 2.4 collective-permute-start.9
  169.7 30.5 %all-to-all-start.3 = ((bf16[16,16,4224]{2,1,0:T(8,128)(2,1)}), bf16[16,16,4224]{2,1,0:T(8,128)(2,1)}, u32[]{:S(2)}, u32[]{:S(2)}) async-start(bf16[16,16,4224]{2,1,0:T(8,128)(2,1)} %get-tuple-element.60), calls=%async_computation.3 | async-start | bytes 4325376 | tf_op jit(solution)/shard_map/all_to_all | solution.py:54
  200.2 4.7 %collective-permute-done.7.far_ref = bf16[128,4224]{1,0:T(8,128)(2,1)S(1)} collective-permute-done((bf16[128,4224]{1,0:T(8,128)(2,1)}, bf16[128,4224]{1,0:T(8,128)(2,1)S(1)}, u32[]{:S(2)}, u32[]{:S(2)}) %collective-permute-start.7) | collective-permute-done | bytes 1081376 | tf_op jit(solution)/shard_map/ppermute | solution.py:50
  204.9 0.0 collective-permute-done.6
  204.9 1.2 collective-permute-done.9
  206.1 2.2 add_convert_fusion.1
  208.3 4.4 %collective-permute-start.12 = (bf16[256,1536]{1,0:T(8,128)(2,1)S(1)}, bf16[256,1536]{1,0:T(8,128)(2,1)S(1)}, u32[]{:S(2)}, u32[]{:S(2)}) collective-permute-start(bf16[256,1536]{1,0:T(8,128)(2,1)S(1)} %get-tuple-element.85), channel_id=1, source_target_pairs={{0,64},{32,96},{64,128},{96,160},{128,192},{160,224},{1,65},{33,97... | collective-permute-start | bytes 2359304 | tf_op jit(solution)/shard_map/ppermute | solution.py:466
  212.7 1.3 collective-permute-start.13
  214.0 1.1 fusion.4
  215.2 0.8 collective-permute-start.11
  216.0 5.2 %collective-permute-start.10 = (bf16[96,2048]{1,0:T(8,128)(2,1)S(1)}, bf16[96,2048]{1,0:T(8,128)(2,1)S(1)}, u32[]{:S(2)}, u32[]{:S(2)}) collective-permute-start(bf16[96,2048]{1,0:T(8,128)(2,1)S(1)} %fusion.4), channel_id=1, source_target_pairs={{0,64},{32,96},{64,128},{96,160},{1,65},{33,97},{65,129},{97,161},... | collective-permute-start | bytes 1179656 | tf_op jit(solution)/shard_map/ppermute | solution.py:466
  221.2 17.0 %collective-permute-done.10 = bf16[96,2048]{1,0:T(8,128)(2,1)S(1)} collective-permute-done((bf16[96,2048]{1,0:T(8,128)(2,1)S(1)}, bf16[96,2048]{1,0:T(8,128)(2,1)S(1)}, u32[]{:S(2)}, u32[]{:S(2)}) %collective-permute-start.10) | collective-permute-done | bytes 393248 | tf_op jit(solution)/shard_map/ppermute | solution.py:466
  238.2 2.3 fusion.1
  240.5 7.8 %collective-permute-start.15 = (bf16[96,2048]{1,0:T(8,128)(2,1)}, bf16[96,2048]{1,0:T(8,128)(2,1)}, u32[]{:S(2)}, u32[]{:S(2)}) collective-permute-start(bf16[96,2048]{1,0:T(8,128)(2,1)} %get-tuple-element.98), channel_id=1, source_target_pairs={{0,64},{32,96},{64,128},{96,160},{128,192},{160,224},{1,65},{33,97... | collective-permute-start | bytes 1179656 | tf_op jit(solution)/shard_map/ppermute | solution.py:466
  248.3 1.3 collective-permute-start.16
  249.6 0.0 copy-start.6
  249.6 1.2 add_convert_fusion
  250.8 0.6 dynamic_slice.3
  252.0 3.4 %finish.1 = (bf16[128,2048]{1,0:T(8,128)(2,1)}, bf16[128,2048]{1,0:T(8,128)(2,1)}, f32[128,8]{1,0:T(8,128)}) custom-call(s32[1]{0:T(128)} %bitcast.half_ref, s32[128,8]{1,0:T(8,128)} %copy.16.ids_ref, bf16[256,128]{1,0:T(8,128)(2,1)} %get-tuple-element.50.picked_ref, bf16[16,16,4224]{2,1,0:T(8,128)(2,1)} %all-to-all-done.3.returned_ref, ...), custom_call_target="tpu_custom_call" | custom-call | flops 276824064 | bytes 2162688 | tf_op jit(solution)/shard_map/finish/pallas_call | solution.py:447
  255.4 1.5 copy.17
  256.9 3.0 %collective-permute-done.16 = bf16[96,2048]{1,0:T(8,128)(2,1)} collective-permute-done((bf16[96,2048]{1,0:T(8,128)(2,1)S(1)}, bf16[96,2048]{1,0:T(8,128)(2,1)}, u32[]{:S(2)}, u32[]{:S(2)}) %collective-permute-start.16) | collective-permute-done | bytes 393248 | tf_op jit(solution)/shard_map/ppermute | solution.py:466
  260.0 1.5 fusion.3
  261.4 0.6 collective-permute-start.17
  262.0 11.1 %collective-permute-done.14 = bf16[256,1536]{1,0:T(8,128)(2,1)} collective-permute-done((bf16[256,1536]{1,0:T(8,128)(2,1)}, bf16[256,1536]{1,0:T(8,128)(2,1)}, u32[]{:S(2)}, u32[]{:S(2)}) %collective-permute-start.14) | collective-permute-done | bytes 786464 | tf_op jit(solution)/shard_map/ppermute | solution.py:552
  273.1 1.2 broadcast_select_fusion
  274.3 0.9 slice_bitcast_fusion
  275.2 3.8 %collective-permute-done.17 = bf16[96,2048]{1,0:T(8,128)(2,1)S(1)} collective-permute-done((bf16[96,2048]{1,0:T(8,128)(2,1)S(1)}, bf16[96,2048]{1,0:T(8,128)(2,1)S(1)}, u32[]{:S(2)}, u32[]{:S(2)}) %collective-permute-start.17) | collective-permute-done | bytes 393248 | tf_op jit(solution)/shard_map/ppermute | solution.py:553
  279.1 0.8 select_bitcast_fusion
  (19 shorter events, 0.0 us)
Async XLA Ops:
  0.6 53.2 %collective-permute-start.1 = (bf16[128,2048]{1,0:T(8,128)(2,1)}, bf16[128,2048]{1,0:T(8,128)(2,1)S(1)}, u32[]{:S(2)}, u32[]{:S(2)}) collective-permute-start(bf16[128,2048]{1,0:T(8,128)(2,1)} %tokens_ref.1), channel_id=1, source_target_pairs={{0,196},{1,197},{2,198},{3,199},{4,192},{5,193},{6,194},{7,195},{8... | collective-permute-start | bytes 1572872 | tf_op jit(solution)/shard_map/ppermute | solution.py:50
  6.6 47.3 %collective-permute-start.2 = (bf16[128,2048]{1,0:T(8,128)(2,1)}, bf16[128,2048]{1,0:T(8,128)(2,1)S(1)}, u32[]{:S(2)}, u32[]{:S(2)}) collective-permute-start(bf16[128,2048]{1,0:T(8,128)(2,1)} %grads_ref.1), channel_id=1, source_target_pairs={{0,196},{1,197},{2,198},{3,199},{4,192},{5,193},{6,194},{7,195},{8... | collective-permute-start | bytes 1572872 | tf_op jit(solution)/shard_map/ppermute | solution.py:50
  11.6 42.2 %collective-permute-start = (bf16[128,128]{1,0:T(8,128)(2,1)}, bf16[128,128]{1,0:T(8,128)(2,1)S(1)}, u32[]{:S(2)}, u32[]{:S(2)}) collective-permute-start(bf16[128,128]{1,0:T(8,128)(2,1)} %get-tuple-element.53), channel_id=1, source_target_pairs={{0,196},{1,197},{2,198},{3,199},{4,192},{5,193},{6,194},{7,195},{8... | collective-permute-start | bytes 98312 | tf_op jit(solution)/shard_map/ppermute | solution.py:50
  18.3 40.6 %all-to-all-start = ((bf16[16,16,4224]{2,1,0:T(8,128)(2,1)}), bf16[16,16,4224]{2,1,0:T(8,128)(2,1)}, u32[]{:S(2)}, u32[]{:S(2)}) async-start(bf16[16,16,4224]{2,1,0:T(8,128)(2,1)} %bitcast.37), calls=%async_computation | async-start | bytes 4325376 | tf_op jit(solution)/shard_map/all_to_all | solution.py:54
  53.8 0.6 copy-start.5
  53.8 0.8 copy-start.3
  54.6 0.8 copy-start.4
  58.9 36.8 %all-to-all-start.1 = ((bf16[16,16,4224]{2,1,0:T(8,128)(2,1)}), bf16[16,16,4224]{2,1,0:T(8,128)(2,1)}, u32[]{:S(2)}, u32[]{:S(2)}) async-start(bf16[16,16,4224]{2,1,0:T(8,128)(2,1)} %bitcast.36), calls=%async_computation.1 | async-start | bytes 4325376 | tf_op jit(solution)/shard_map/all_to_all | solution.py:54
  115.0 13.2 %collective-permute-start.3 = (bf16[4,256,1536]{2,1,0:T(8,128)(2,1)}, bf16[4,256,1536]{2,1,0:T(8,128)(2,1)}, u32[]{:S(2)}, u32[]{:S(2)}) collective-permute-start(bf16[4,256,1536]{2,1,0:T(8,128)(2,1)} %wide.2), channel_id=1, source_target_pairs={{0,32},{32,0},{64,96},{96,64},{128,160},{160,128},{192,224},{224,1... | collective-permute-start | bytes 9437192 | tf_op jit(solution)/shard_map/ppermute | solution.py:461
  115.0 39.8 %all-to-all-start.2 = ((bf16[16,16,4224]{2,1,0:T(8,128)(2,1)}), bf16[16,16,4224]{2,1,0:T(8,128)(2,1)}, u32[]{:S(2)}, u32[]{:S(2)}) async-start(bf16[16,16,4224]{2,1,0:T(8,128)(2,1)} %get-tuple-element.59), calls=%async_computation.2 | async-start | bytes 4325376 | tf_op jit(solution)/shard_map/all_to_all | solution.py:54
  136.3 29.7 %collective-permute-start.8 = (bf16[4,96,2048]{2,1,0:T(8,128)(2,1)}, bf16[4,96,2048]{2,1,0:T(8,128)(2,1)}, u32[]{:S(2)}, u32[]{:S(2)}) collective-permute-start(bf16[4,96,2048]{2,1,0:T(8,128)(2,1)} %get-tuple-element.74), channel_id=1, source_target_pairs={{0,32},{32,0},{64,96},{96,64},{128,160},{160,128},{192,224},{224,1... | collective-permute-start | bytes 4718600 | tf_op jit(solution)/shard_map/ppermute | solution.py:461
  136.5 23.3 %collective-permute-start.4 = (bf16[256,1536]{1,0:T(8,128)(2,1)}, bf16[256,1536]{1,0:T(8,128)(2,1)}, u32[]{:S(2)}, u32[]{:S(2)}) collective-permute-start(bf16[256,1536]{1,0:T(8,128)(2,1)} %get-tuple-element.68), channel_id=1, source_target_pairs={{0,64},{32,96},{192,128},{224,160},{1,65},{33,97},{193,129},{225,1... | collective-permute-start | bytes 2359304 | tf_op jit(solution)/shard_map/ppermute | solution.py:466
  158.0 7.9 %copy-start = (bf16[4,96,2048]{2,1,0:T(8,128)(2,1)S(1)}, bf16[4,96,2048]{2,1,0:T(8,128)(2,1)}, u32[]{:S(2)}) copy-start(bf16[4,96,2048]{2,1,0:T(8,128)(2,1)} %get-tuple-element.72) | copy-start | bytes 4718596
  158.0 46.8 %collective-permute-start.7 = (bf16[128,4224]{1,0:T(8,128)(2,1)}, bf16[128,4224]{1,0:T(8,128)(2,1)S(1)}, u32[]{:S(2)}, u32[]{:S(2)}) collective-permute-start(bf16[128,4224]{1,0:T(8,128)(2,1)} %collect.1), channel_id=1, source_target_pairs={{0,196},{1,197},{2,198},{3,199},{4,192},{5,193},{6,194},{7,195},{8... | collective-permute-start | bytes 3244040 | tf_op jit(solution)/shard_map/ppermute | solution.py:50
  162.2 42.7 %collective-permute-start.6 = (bf16[256,1536]{1,0:T(8,128)(2,1)}, bf16[256,1536]{1,0:T(8,128)(2,1)}, u32[]{:S(2)}, u32[]{:S(2)}) collective-permute-start(bf16[256,1536]{1,0:T(8,128)(2,1)} %add_convert_fusion.3), channel_id=1, source_target_pairs={{192,128},{224,160},{128,64},{160,96},{193,129},{225,161},{129,65}... | collective-permute-start | bytes 2359304 | tf_op jit(solution)/shard_map/ppermute | solution.py:466
  163.7 41.1 %collective-permute-start.5 = (bf16[256,1536]{1,0:T(8,128)(2,1)}, bf16[256,1536]{1,0:T(8,128)(2,1)}, u32[]{:S(2)}, u32[]{:S(2)}) collective-permute-start(bf16[256,1536]{1,0:T(8,128)(2,1)} %add_convert_fusion.3), channel_id=1, source_target_pairs={{0,64},{32,96},{64,128},{96,160},{1,65},{33,97},{65,129},{97,161},... | collective-permute-start | bytes 2359304 | tf_op jit(solution)/shard_map/ppermute | solution.py:466
  167.3 38.8 %collective-permute-start.9 = (bf16[96,2048]{1,0:T(8,128)(2,1)S(1)}, bf16[96,2048]{1,0:T(8,128)(2,1)S(1)}, u32[]{:S(2)}, u32[]{:S(2)}) collective-permute-start(bf16[96,2048]{1,0:T(8,128)(2,1)S(1)} %select_bitcast_fusion.1), channel_id=1, source_target_pairs={{0,64},{32,96},{192,128},{224,160},{1,65},{33,97},{193,129},{225,1... | collective-permute-start | bytes 1179656 | tf_op jit(solution)/shard_map/ppermute | solution.py:466
  169.7 82.4 %all-to-all-start.3 = ((bf16[16,16,4224]{2,1,0:T(8,128)(2,1)}), bf16[16,16,4224]{2,1,0:T(8,128)(2,1)}, u32[]{:S(2)}, u32[]{:S(2)}) async-start(bf16[16,16,4224]{2,1,0:T(8,128)(2,1)} %get-tuple-element.60), calls=%async_computation.3 | async-start | bytes 4325376 | tf_op jit(solution)/shard_map/all_to_all | solution.py:54
  204.9 3.4 %copy-start.1 = (bf16[128,4224]{1,0:T(8,128)(2,1)}, bf16[128,4224]{1,0:T(8,128)(2,1)S(1)}, u32[]{:S(2)}) copy-start(bf16[128,4224]{1,0:T(8,128)(2,1)S(1)} %collective-permute-done.7.far_ref) | copy-start | bytes 3244036
  208.3 29.9 %collective-permute-start.12 = (bf16[256,1536]{1,0:T(8,128)(2,1)S(1)}, bf16[256,1536]{1,0:T(8,128)(2,1)S(1)}, u32[]{:S(2)}, u32[]{:S(2)}) collective-permute-start(bf16[256,1536]{1,0:T(8,128)(2,1)S(1)} %get-tuple-element.85), channel_id=1, source_target_pairs={{0,64},{32,96},{64,128},{96,160},{128,192},{160,224},{1,65},{33,97... | collective-permute-start | bytes 2359304 | tf_op jit(solution)/shard_map/ppermute | solution.py:466
  212.7 25.5 %collective-permute-start.13 = (bf16[256,1536]{1,0:T(8,128)(2,1)S(1)}, bf16[256,1536]{1,0:T(8,128)(2,1)S(1)}, u32[]{:S(2)}, u32[]{:S(2)}) collective-permute-start(bf16[256,1536]{1,0:T(8,128)(2,1)S(1)} %get-tuple-element.86), channel_id=1, source_target_pairs={{192,128},{224,160},{128,64},{160,96},{64,0},{96,32},{193,129},{22... | collective-permute-start | bytes 2359304 | tf_op jit(solution)/shard_map/ppermute | solution.py:466
  215.2 34.4 %copy-start.2 = (bf16[256,1536]{1,0:T(8,128)(2,1)S(1)}, bf16[256,1536]{1,0:T(8,128)(2,1)}, u32[]{:S(2)}) copy-start(bf16[256,1536]{1,0:T(8,128)(2,1)} %get-tuple-element.79) | copy-start | bytes 2359300
  215.2 6.0 %collective-permute-start.11 = (bf16[96,2048]{1,0:T(8,128)(2,1)S(1)}, bf16[96,2048]{1,0:T(8,128)(2,1)S(1)}, u32[]{:S(2)}, u32[]{:S(2)}) collective-permute-start(bf16[96,2048]{1,0:T(8,128)(2,1)S(1)} %fusion.4), channel_id=1, source_target_pairs={{192,128},{224,160},{128,64},{160,96},{193,129},{225,161},{129,65}... | collective-permute-start | bytes 1179656 | tf_op jit(solution)/shard_map/ppermute | solution.py:466
  216.0 22.2 %collective-permute-start.10 = (bf16[96,2048]{1,0:T(8,128)(2,1)S(1)}, bf16[96,2048]{1,0:T(8,128)(2,1)S(1)}, u32[]{:S(2)}, u32[]{:S(2)}) collective-permute-start(bf16[96,2048]{1,0:T(8,128)(2,1)S(1)} %fusion.4), channel_id=1, source_target_pairs={{0,64},{32,96},{64,128},{96,160},{1,65},{33,97},{65,129},{97,161},... | collective-permute-start | bytes 1179656 | tf_op jit(solution)/shard_map/ppermute | solution.py:466
  240.5 16.5 %collective-permute-start.15 = (bf16[96,2048]{1,0:T(8,128)(2,1)}, bf16[96,2048]{1,0:T(8,128)(2,1)}, u32[]{:S(2)}, u32[]{:S(2)}) collective-permute-start(bf16[96,2048]{1,0:T(8,128)(2,1)} %get-tuple-element.98), channel_id=1, source_target_pairs={{0,64},{32,96},{64,128},{96,160},{128,192},{160,224},{1,65},{33,97... | collective-permute-start | bytes 1179656 | tf_op jit(solution)/shard_map/ppermute | solution.py:466
  248.3 11.7 %collective-permute-start.16 = (bf16[96,2048]{1,0:T(8,128)(2,1)S(1)}, bf16[96,2048]{1,0:T(8,128)(2,1)}, u32[]{:S(2)}, u32[]{:S(2)}) collective-permute-start(bf16[96,2048]{1,0:T(8,128)(2,1)S(1)} %get-tuple-element.99), channel_id=1, source_target_pairs={{192,128},{224,160},{128,64},{160,96},{64,0},{96,32},{193,129},{22... | collective-permute-start | bytes 1179656 | tf_op jit(solution)/shard_map/ppermute | solution.py:466
  249.6 1.2 copy-start.6
  250.8 22.3 %collective-permute-start.14 = (bf16[256,1536]{1,0:T(8,128)(2,1)}, bf16[256,1536]{1,0:T(8,128)(2,1)}, u32[]{:S(2)}, u32[]{:S(2)}) collective-permute-start(bf16[256,1536]{1,0:T(8,128)(2,1)} %add_convert_fusion), channel_id=1, source_target_pairs={{0,16},{1,17},{2,18},{3,19},{4,20},{5,21},{6,22},{7,23},{8,24},{9,... | collective-permute-start | bytes 2359304 | tf_op jit(solution)/shard_map/ppermute | solution.py:552
  261.4 17.6 %collective-permute-start.17 = (bf16[96,2048]{1,0:T(8,128)(2,1)S(1)}, bf16[96,2048]{1,0:T(8,128)(2,1)S(1)}, u32[]{:S(2)}, u32[]{:S(2)}) collective-permute-start(bf16[96,2048]{1,0:T(8,128)(2,1)S(1)} %fusion.3), channel_id=1, source_target_pairs={{0,16},{1,17},{2,18},{3,19},{4,20},{5,21},{6,22},{7,23},{8,24},{9,... | collective-permute-start | bytes 1179656 | tf_op jit(solution)/shard_map/ppermute | solution.py:553

commit v11 on v5

--- a/solution.py
+++ b/solution.py
@@ -120,7 +120,7 @@
         ).astype(BF16)
 
 
-def fill(sides, tokens, grads):
+def fill(sides, tokens, grads, weight):
     rows, width = tokens.shape
     slots = PLANE * MOST
     return pl.pallas_call(
@@ -132,7 +132,7 @@
         in_specs=[WHOLE] * 3,
         out_specs=(WHOLE, WHOLE),
         compiler_params=limits(),
-        cost_estimate=cost(4 * slots * rows * width, 8 * slots * width),
+        cost_estimate=cost(weight, 8 * slots * width),
         name="fill",
     )(sides, tokens, grads)
 
@@ -483,10 +483,9 @@
     far_out_grad = across(out_grad)
     own_sides, far_sides = route(half, expert_ids, route_gates)
     far_sides = across(far_sides)
-    far_tokens, far_sides, own_sides = lax.optimization_barrier((far_tokens, far_sides, own_sides))
-    near_blocks, near_picked = fill(own_sides, tokens, out_grad)
+    near_blocks, near_picked = fill(own_sides, tokens, out_grad, 10**9)
     near_rows = to_plane(near_blocks.reshape(PLANE, MOST, -1)).reshape(PLANE * MOST, -1)
-    far_blocks, far_picked = fill(far_sides, far_tokens, far_out_grad)
+    far_blocks, far_picked = fill(far_sides, far_tokens, far_out_grad, 10**12)
     far_blocks, near_blocks = lax.optimization_barrier((far_blocks, near_blocks))
     far_rows = to_plane(far_blocks.reshape(PLANE, MOST, -1)).reshape(PLANE * MOST, -1)
 

time: 270 us -> 261 us (0.967)
  waiting for transfers between devices: 115 us -> 97.4 us
  local copies, waits for them, and re-layouts: 17.9 us -> 21.1 us
  starting transfers between devices: 70.4 us -> 73.6 us
    all_to_all x4, waiting for transfers between devices: 32.3 us -> 19.2 us  [to_plane(): lax.all_to_all(blocks, 'expert', split_axis=0, concat_axis=0, axis_index_...]
    ppermute x4, waiting for transfers between devices: 36.1 us -> 31.5 us  [across(): return lax.ppermute(value, BOTH, pairs)]
    unnamed x41 -> x45, local copies, waits for them, and re-layouts: 16.4 us -> 19.6 us
  transfers between devices with their start and end apart: 22 -> 22, of which waited for: 11 -> 9; matrix products, arithmetic and copies ran while one was open for 8% -> 8% of each run, Pallas kernels for 8% -> 9%
where the time goes in v11:
time: 261 us; the launch traced here: 258 us
  waiting for transfers between devices  97.4 us (37%)
  starting transfers between devices  73.6 us (28%)
  Pallas kernels  47.9 us (18%)
  local copies, waits for them, and re-layouts  21.1 us (8%)
  other arithmetic  16.9 us (6%)
    ppermute x4, waiting for transfers between devices, across(): return lax.ppermute(value, BOTH, pairs)  31.5 us
    all_to_all x4, starting transfers between devices, to_plane(): lax.all_to_all(blocks, 'expert', split_axis=0, concat_axis=0, axis_index_...  27.8 us
    pallas_call x2, Pallas kernels, run_expert(): pl.pallas_call(expert_kernel, out_shape=(jax.ShapeDtypeStruct((PLANE, MOS...  22.3 us
    ppermute x2, waiting for transfers between devices, line_sum(): lax.ppermute(up, 'dp', neighbours([(0, 1), (1, 2), (2, 3)])).astype(F32)  22.2 us
    unnamed x45, local copies, waits for them, and re-layouts  19.6 us
    all_to_all x4, waiting for transfers between devices, to_plane(): lax.all_to_all(blocks, 'expert', split_axis=0, concat_axis=0, axis_index_...  19.2 us
    pallas_call x2, Pallas kernels, wide_grads(): pl.pallas_call(functools.partial(wide_kernel, taken is not None, shard),...  12.7 us
    ppermute x2, waiting for transfers between devices, line_sum(): lax.ppermute(first, 'dp', neighbours([(0, 1), (3, 2)])).astype(F32)  12.3 us
  transfers between devices with their start and end apart: 22, of which 9 were waited for; matrix products, arithmetic and copies ran while one was open for 8% of the time, Pallas kernels for 9%

profile of v11, /device:TPU:16, one launch (start us, length us, event | category | flops | bytes accessed | tf_op | source)
XLA Modules:
  0.0 258.3 jit_solution(4110656953185147337)
XLA Ops:
  0.6 5.9 %collective-permute-start.1 = (bf16[128,2048]{1,0:T(8,128)(2,1)}, bf16[128,2048]{1,0:T(8,128)(2,1)S(1)}, u32[]{:S(2)}, u32[]{:S(2)}) collective-permute-start(bf16[128,2048]{1,0:T(8,128)(2,1)} %tokens_ref.1), channel_id=1, source_target_pairs={{0,196},{1,197},{2,198},{3,199},{4,192},{5,193},{6,194},{7,195},{8... | collective-permute-start | bytes 1572872 | tf_op jit(solution)/shard_map/ppermute | solution.py:46
  6.7 1.4 copy.16.ids_ref
  8.1 1.4 copy.15.gates_ref
  9.5 2.1 route.1
  11.6 3.1 %collective-permute-start = (bf16[128,128]{1,0:T(8,128)(2,1)}, bf16[128,128]{1,0:T(8,128)(2,1)S(1)}, u32[]{:S(2)}, u32[]{:S(2)}) collective-permute-start(bf16[128,128]{1,0:T(8,128)(2,1)} %get-tuple-element.40), channel_id=1, source_target_pairs={{0,196},{1,197},{2,198},{3,199},{4,192},{5,193},{6,194},{7,195},{8... | collective-permute-start | bytes 98312 | tf_op jit(solution)/shard_map/ppermute | solution.py:46
  14.8 1.0 copy-done.9
  15.8 1.0 copy-done.10
  16.9 0.8 copy-done.11
  17.6 2.3 fill.2
  19.9 7.3 %all-to-all-start = ((bf16[16,16,4224]{2,1,0:T(8,128)(2,1)}), bf16[16,16,4224]{2,1,0:T(8,128)(2,1)}, u32[]{:S(2)}, u32[]{:S(2)}) async-start(bf16[16,16,4224]{2,1,0:T(8,128)(2,1)} %bitcast.2), calls=%async_computation | async-start | bytes 4325376 | tf_op jit(solution)/shard_map/all_to_all | solution.py:50
  27.2 26.7 %collective-permute-done.sides_ref = bf16[128,128]{1,0:T(8,128)(2,1)S(1)} collective-permute-done((bf16[128,128]{1,0:T(8,128)(2,1)}, bf16[128,128]{1,0:T(8,128)(2,1)S(1)}, u32[]{:S(2)}, u32[]{:S(2)}) %collective-permute-start) | collective-permute-done | bytes 32800 | tf_op jit(solution)/shard_map/ppermute | solution.py:46
  53.8 0.9 fill.3
  54.7 1.3 copy-done.3
  56.1 7.3 %all-to-all-start.1 = ((bf16[16,16,4224]{2,1,0:T(8,128)(2,1)}), bf16[16,16,4224]{2,1,0:T(8,128)(2,1)S(1)}, u32[]{:S(2)}, u32[]{:S(2)}) async-start(bf16[16,16,4224]{2,1,0:T(8,128)(2,1)} %bitcast.53), calls=%async_computation.1 | async-start | bytes 4325376 | tf_op jit(solution)/shard_map/all_to_all | solution.py:50
  63.4 11.2 %expert.2 = (bf16[16,16,4224]{2,1,0:T(8,128)(2,1)S(1)}, bf16[256,768]{1,0:T(8,128)(2,1)S(1)}, bf16[256,2048]{1,0:T(8,128)(2,1)S(1)}, bf16[256,1536]{1,0:T(8,128)(2,1)S(1)}) custom-call(s32[1]{0:T(128)} %bitcast.1.place_ref, bf16[256,4224]{1,0:T(8,128)(2,1)} %bitcast.3.rows_ref.near_x, bf16[2048,768]{1,0:T(8,128)(2,1)} %bitcast.54, ...), custom_call_target="tpu_custom_call" | custom-call | flops 4831838208 | bytes 9437184 | tf_op jit(solution)/shard_map/expert/pallas_call | solution.py:230
  74.6 1.4 copy-done.2
  76.0 1.0 copy-done.12
  77.0 0.7 copy-done.14
  77.7 15.1 %all-to-all-done.1 = bf16[16,16,4224]{2,1,0:T(8,128)(2,1)S(1)} async-done(((bf16[16,16,4224]{2,1,0:T(8,128)(2,1)}), bf16[16,16,4224]{2,1,0:T(8,128)(2,1)S(1)}, u32[]{:S(2)}, u32[]{:S(2)}) %all-to-all-start.1) | async-done | bytes 2162720 | tf_op jit(solution)/shard_map/all_to_all | solution.py:50
  92.8 1.3 copy-done
  94.1 11.2 %expert.3 = (bf16[16,16,4224]{2,1,0:T(8,128)(2,1)S(1)}, bf16[256,768]{1,0:T(8,128)(2,1)S(1)}, bf16[256,2048]{1,0:T(8,128)(2,1)S(1)}, bf16[256,1536]{1,0:T(8,128)(2,1)S(1)}) custom-call(s32[1]{0:T(128)} %bitcast.1.place_ref, bf16[256,4224]{1,0:T(8,128)(2,1)} %bitcast.50, bf16[2048,768]{1,0:T(8,128)(2,1)} %bitcast.55, bf16[2048,768]{1,0:T(8,128)(2,1)} %bitcast.57, ...), custom_call_target="tpu_custom_call" | custom-call | flops 4831838208 | bytes 9437184 | tf_op jit(solution)/shard_map/expert/pallas_call | solution.py:230
  105.3 1.3 copy-done.4
  106.6 1.6 copy-done.1
  108.2 5.6 %wide.2 = bf16[4,256,1536]{2,1,0:T(8,128)(2,1)} custom-call(s32[2]{0:T(128)S(1)} %get-tuple-element.82.where_ref, bf16[256,4224]{1,0:T(8,128)(2,1)} %bitcast.3.rows_ref.near_x, bf16[256,4224]{1,0:T(8,128)(2,1)S(1)} %bitcast.52, bf16[256,1536]{1,0:T(8,128)(2,1)S(1)} %get-tuple-element.44.near_grads, bf16[256,1536]{1,0:T(8,128)(2,1)S(1)} %get-tuple-element.45.far_grads), custom_call_target="tpu_custom_call" | custom-call | flops 1610612736 | bytes 6291456 | tf_op jit(solution)/shard_map/wide/pallas_call | solution.py:294
  113.9 4.0 %down.1 = (bf16[4,96,2048]{2,1,0:T(8,128)(2,1)}, bf16[4,96,2048]{2,1,0:T(8,128)(2,1)S(1)}) custom-call(s32[1]{0:T(128)} %bitcast.9.core_ref, bf16[256,768]{1,0:T(8,128)(2,1)S(1)} %copy-done.15, bf16[256,768]{1,0:T(8,128)(2,1)S(1)} %get-tuple-element.51.far_hidden, bf16[256,2048]{1,0:T(8,128)(2,1)S(1)} %copy-done.13, ...), custom_call_target="tpu_custom_call" | custom-call | flops 1610612736 | bytes 6291456 | tf_op jit(solution)/shard_map/down/pallas_call | solution.py:343
  117.8 1.2 copy-done.5
  119.0 0.7 collective-permute-done.3.refs_0_
  119.7 1.7 copy-done.19
  121.4 7.1 %wide.3 = (bf16[4,256,1536]{2,1,0:T(8,128)(2,1)}, bf16[256,1536]{1,0:T(8,128)(2,1)S(1)}) custom-call(s32[2]{0:T(128)S(1)} %get-tuple-element.83.where_ref, bf16[256,4224]{1,0:T(8,128)(2,1)} %bitcast.3.rows_ref.near_x, bf16[256,4224]{1,0:T(8,128)(2,1)} %bitcast.51, bf16[256,1536]{1,0:T(8,128)(2,1)S(1)} %get-tuple-element.44.near_grads, ...), custom_call_target="tpu_custom_call" | custom-call | flops 1610612736 | bytes 6291456 | tf_op jit(solution)/shard_map/wide/pallas_call | solution.py:294
  128.5 0.9 copy-done.7
  129.5 6.2 %all-to-all-start.2 = ((bf16[16,16,4224]{2,1,0:T(8,128)(2,1)}), bf16[16,16,4224]{2,1,0:T(8,128)(2,1)S(1)}, u32[]{:S(2)}, u32[]{:S(2)}) async-start(bf16[16,16,4224]{2,1,0:T(8,128)(2,1)} %copy-done.4), calls=%async_computation.2 | async-start | bytes 4325376 | tf_op jit(solution)/shard_map/all_to_all | solution.py:50
  135.8 3.2 %collective-permute-start.4 = (bf16[256,1536]{1,0:T(8,128)(2,1)S(1)}, bf16[256,1536]{1,0:T(8,128)(2,1)S(1)}, u32[]{:S(2)}, u32[]{:S(2)}) collective-permute-start(bf16[256,1536]{1,0:T(8,128)(2,1)S(1)} %copy-done.8), channel_id=1, source_target_pairs={{0,64},{32,96},{192,128},{224,160},{1,65},{33,97},{193,129},{225,1... | collective-permute-start | bytes 2359304 | tf_op jit(solution)/shard_map/ppermute | solution.py:455
  139.0 2.6 %add_convert_fusion = bf16[4,96,2048]{2,1,0:T(8,128)(2,1)S(1)} fusion(bf16[4,96,2048]{2,1,0:T(8,128)(2,1)} %collective-permute-done.11, bf16[4,96,2048]{2,1,0:T(8,128)(2,1)} %copy-done.5), kind=kLoop, calls=%fused_computation | loop fusion | flops 3145728 | bytes 4718592 | tf_op jit(solution)/shard_map/convert_element_type | solution.py:506
  141.7 0.8 fusion.12
  142.5 2.0 collective-permute-start.12
  144.6 12.3 %collective-permute-done.4 = bf16[256,1536]{1,0:T(8,128)(2,1)S(1)} collective-permute-done((bf16[256,1536]{1,0:T(8,128)(2,1)S(1)}, bf16[256,1536]{1,0:T(8,128)(2,1)S(1)}, u32[]{:S(2)}, u32[]{:S(2)}) %collective-permute-start.4) | collective-permute-done | bytes 786464 | tf_op jit(solution)/shard_map/ppermute | solution.py:455
  156.9 1.5 fusion.1
  158.3 4.4 %collective-permute-start.6 = (bf16[256,1536]{1,0:T(8,128)(2,1)}, bf16[256,1536]{1,0:T(8,128)(2,1)S(1)}, u32[]{:S(2)}, u32[]{:S(2)}) collective-permute-start(bf16[256,1536]{1,0:T(8,128)(2,1)} %get-tuple-element.73), channel_id=1, source_target_pairs={{0,64},{32,96},{64,128},{96,160},{1,65},{33,97},{65,129},{97,161},... | collective-permute-start | bytes 2359304 | tf_op jit(solution)/shard_map/ppermute | solution.py:459
  162.7 1.6 collective-permute-start.8
  164.3 4.2 %all-to-all-done.2.returned_ref = bf16[16,16,4224]{2,1,0:T(8,128)(2,1)S(1)} async-done(((bf16[16,16,4224]{2,1,0:T(8,128)(2,1)}), bf16[16,16,4224]{2,1,0:T(8,128)(2,1)S(1)}, u32[]{:S(2)}, u32[]{:S(2)}) %all-to-all-start.2) | async-done | bytes 2162720 | tf_op jit(solution)/shard_map/all_to_all | solution.py:50
  168.5 6.9 %all-to-all-start.3 = ((bf16[16,16,4224]{2,1,0:T(8,128)(2,1)}), bf16[16,16,4224]{2,1,0:T(8,128)(2,1)}, u32[]{:S(2)}, u32[]{:S(2)}) async-start(bf16[16,16,4224]{2,1,0:T(8,128)(2,1)} %copy-done.2), calls=%async_computation.3 | async-start | bytes 4325376 | tf_op jit(solution)/shard_map/all_to_all | solution.py:50
  175.4 2.3 fusion.6
  177.7 3.9 %collective-permute-start.13 = (bf16[96,2048]{1,0:T(8,128)(2,1)}, bf16[96,2048]{1,0:T(8,128)(2,1)}, u32[]{:S(2)}, u32[]{:S(2)}) collective-permute-start(bf16[96,2048]{1,0:T(8,128)(2,1)} %get-tuple-element.76), channel_id=1, source_target_pairs={{0,64},{32,96},{64,128},{96,160},{1,65},{33,97},{65,129},{97,161},... | collective-permute-start | bytes 1179656 | tf_op jit(solution)/shard_map/ppermute | solution.py:459
  181.7 1.4 collective-permute-start.15
  183.1 3.2 %fusion.3 = (bf16[256,1536]{1,0:T(8,128)(2,1)}, bf16[256,1536]{1,0:T(8,128)(2,1)}) fusion(bf16[256,1536]{1,0:T(8,128)(2,1)S(1)} %collective-permute-done.6, bf16[4,256,1536]{2,1,0:T(8,128)(2,1)} %get-tuple-element.56, s32[]{:T(128)S(6)} %min.23, bf16[256,1536]{1,0:T(8,128)(2,1)} %collective-permute-done.8, s32[]{:T(128)S(6)} %min.24), kind=kLoop, calls=%fused_computation.8 | loop fusion | flops 3145728 | bytes 4718600 | tf_op jit(solution)/shard_map/convert_element_type | solution.py:461
  186.2 1.3 collective-permute-start.9
  187.5 5.5 %collective-permute-start.7 = (bf16[256,1536]{1,0:T(8,128)(2,1)}, bf16[256,1536]{1,0:T(8,128)(2,1)}, u32[]{:S(2)}, u32[]{:S(2)}) collective-permute-start(bf16[256,1536]{1,0:T(8,128)(2,1)} %get-tuple-element.74), channel_id=1, source_target_pairs={{0,64},{32,96},{64,128},{96,160},{128,192},{160,224},{1,65},{33,97... | collective-permute-start | bytes 2359304 | tf_op jit(solution)/shard_map/ppermute | solution.py:463
  193.6 0.8 copy-done.17
  194.4 2.3 fusion.9
  196.7 1.3 collective-permute-start.16
  198.0 5.7 %collective-permute-start.14 = (bf16[96,2048]{1,0:T(8,128)(2,1)}, bf16[96,2048]{1,0:T(8,128)(2,1)}, u32[]{:S(2)}, u32[]{:S(2)}) collective-permute-start(bf16[96,2048]{1,0:T(8,128)(2,1)} %get-tuple-element.78), channel_id=1, source_target_pairs={{0,64},{32,96},{64,128},{96,160},{128,192},{160,224},{1,65},{33,97... | collective-permute-start | bytes 1179656 | tf_op jit(solution)/shard_map/ppermute | solution.py:463
  203.6 5.3 %collective-permute-done.9 = bf16[256,1536]{1,0:T(8,128)(2,1)} collective-permute-done((bf16[256,1536]{1,0:T(8,128)(2,1)}, bf16[256,1536]{1,0:T(8,128)(2,1)}, u32[]{:S(2)}, u32[]{:S(2)}) %collective-permute-start.9) | collective-permute-done | bytes 786464 | tf_op jit(solution)/shard_map/ppermute | solution.py:464
  208.9 22.2 %collective-permute-done.7 = bf16[256,1536]{1,0:T(8,128)(2,1)} collective-permute-done((bf16[256,1536]{1,0:T(8,128)(2,1)}, bf16[256,1536]{1,0:T(8,128)(2,1)}, u32[]{:S(2)}, u32[]{:S(2)}) %collective-permute-start.7) | collective-permute-done | bytes 786464 | tf_op jit(solution)/shard_map/ppermute | solution.py:463
  231.1 1.9 fusion.5
  233.0 3.1 %collective-permute-start.10 = (bf16[256,1536]{1,0:T(8,128)(2,1)S(1)}, bf16[256,1536]{1,0:T(8,128)(2,1)}, u32[]{:S(2)}, u32[]{:S(2)}) collective-permute-start(bf16[256,1536]{1,0:T(8,128)(2,1)S(1)} %fusion.5), channel_id=1, source_target_pairs={{0,16},{1,17},{2,18},{3,19},{4,20},{5,21},{6,22},{7,23},{8,24},{9,... | collective-permute-start | bytes 2359304 | tf_op jit(solution)/shard_map/ppermute | solution.py:520
  236.1 0.6 dynamic_slice.36
  237.3 4.8 %collective-permute-done.5.far_ref = bf16[128,4224]{1,0:T(8,128)(2,1)S(1)} collective-permute-done((bf16[128,4224]{1,0:T(8,128)(2,1)S(1)}, bf16[128,4224]{1,0:T(8,128)(2,1)S(1)}, u32[]{:S(2)}, u32[]{:S(2)}) %collective-permute-start.5) | collective-permute-done | bytes 1081376 | tf_op jit(solution)/shard_map/ppermute | solution.py:46
  242.2 3.0 %finish.1 = (bf16[128,2048]{1,0:T(8,128)(2,1)}, bf16[128,2048]{1,0:T(8,128)(2,1)}, f32[128,8]{1,0:T(8,128)S(1)}) custom-call(s32[1]{0:T(128)} %bitcast.half_ref, s32[128,8]{1,0:T(8,128)S(1)} %copy-done.6, bf16[256,128]{1,0:T(8,128)(2,1)S(1)} %get-tuple-element.37.picked_ref, bf16[16,16,4224]{2,1,0:T(8,128)(2,1)} %all-to-all-done.3.returned_ref, ...), custom_call_target="tpu_custom_call" | custom-call | flops 276824064 | bytes 2162688 | tf_op jit(solution)/shard_map/finish/pallas_call | solution.py:430
  245.2 0.7 copy.17
  245.9 1.4 fusion.11
  247.3 3.1 %collective-permute-start.17 = (bf16[96,2048]{1,0:T(8,128)(2,1)S(1)}, bf16[96,2048]{1,0:T(8,128)(2,1)S(1)}, u32[]{:S(2)}, u32[]{:S(2)}) collective-permute-start(bf16[96,2048]{1,0:T(8,128)(2,1)S(1)} %fusion.11), channel_id=1, source_target_pairs={{0,16},{1,17},{2,18},{3,19},{4,20},{5,21},{6,22},{7,23},{8,24},{9,... | collective-permute-start | bytes 1179656 | tf_op jit(solution)/shard_map/ppermute | solution.py:521
  250.4 0.9 slice_bitcast_fusion
  251.4 6.1 %collective-permute-done.17 = bf16[96,2048]{1,0:T(8,128)(2,1)S(1)} collective-permute-done((bf16[96,2048]{1,0:T(8,128)(2,1)S(1)}, bf16[96,2048]{1,0:T(8,128)(2,1)S(1)}, u32[]{:S(2)}, u32[]{:S(2)}) %collective-permute-start.17) | collective-permute-done | bytes 393248 | tf_op jit(solution)/shard_map/ppermute | solution.py:521
  257.5 0.8 select_bitcast_fusion
  (48 shorter events, 1.1 us)
Async XLA Ops:
  0.6 53.2 %collective-permute-start.1 = (bf16[128,2048]{1,0:T(8,128)(2,1)}, bf16[128,2048]{1,0:T(8,128)(2,1)S(1)}, u32[]{:S(2)}, u32[]{:S(2)}) collective-permute-start(bf16[128,2048]{1,0:T(8,128)(2,1)} %tokens_ref.1), channel_id=1, source_target_pairs={{0,196},{1,197},{2,198},{3,199},{4,192},{5,193},{6,194},{7,195},{8... | collective-permute-start | bytes 1572872 | tf_op jit(solution)/shard_map/ppermute | solution.py:46
  6.6 47.3 %collective-permute-start.2 = (bf16[128,2048]{1,0:T(8,128)(2,1)}, bf16[128,2048]{1,0:T(8,128)(2,1)S(1)}, u32[]{:S(2)}, u32[]{:S(2)}) collective-permute-start(bf16[128,2048]{1,0:T(8,128)(2,1)} %grads_ref.1), channel_id=1, source_target_pairs={{0,196},{1,197},{2,198},{3,199},{4,192},{5,193},{6,194},{7,195},{8... | collective-permute-start | bytes 1572872 | tf_op jit(solution)/shard_map/ppermute | solution.py:46
  11.6 42.2 %collective-permute-start = (bf16[128,128]{1,0:T(8,128)(2,1)}, bf16[128,128]{1,0:T(8,128)(2,1)S(1)}, u32[]{:S(2)}, u32[]{:S(2)}) collective-permute-start(bf16[128,128]{1,0:T(8,128)(2,1)} %get-tuple-element.40), channel_id=1, source_target_pairs={{0,196},{1,197},{2,198},{3,199},{4,192},{5,193},{6,194},{7,195},{8... | collective-permute-start | bytes 98312 | tf_op jit(solution)/shard_map/ppermute | solution.py:46
  14.8 1.0 copy-start.9
  15.8 1.0 copy-start.10
  16.9 0.8 copy-start.11
  19.9 36.2 %all-to-all-start = ((bf16[16,16,4224]{2,1,0:T(8,128)(2,1)}), bf16[16,16,4224]{2,1,0:T(8,128)(2,1)}, u32[]{:S(2)}, u32[]{:S(2)}) async-start(bf16[16,16,4224]{2,1,0:T(8,128)(2,1)} %bitcast.2), calls=%async_computation | async-start | bytes 4325376 | tf_op jit(solution)/shard_map/all_to_all | solution.py:50
  54.7 1.3 copy-start.3
  56.1 36.7 %all-to-all-start.1 = ((bf16[16,16,4224]{2,1,0:T(8,128)(2,1)}), bf16[16,16,4224]{2,1,0:T(8,128)(2,1)S(1)}, u32[]{:S(2)}, u32[]{:S(2)}) async-start(bf16[16,16,4224]{2,1,0:T(8,128)(2,1)} %bitcast.53), calls=%async_computation.1 | async-start | bytes 4325376 | tf_op jit(solution)/shard_map/all_to_all | solution.py:50
  74.6 1.4 copy-start.2
  76.0 1.0 copy-start.12
  77.0 0.7 copy-start.14
  92.8 1.3 copy-start
  105.3 1.3 copy-start.4
  106.6 1.6 copy-start.1
  108.2 5.6 %copy-start.13 = (bf16[256,2048]{1,0:T(8,128)(2,1)S(1)}, bf16[256,2048]{1,0:T(8,128)(2,1)}, u32[]{:S(2)}) copy-start(bf16[256,2048]{1,0:T(8,128)(2,1)} %copy-done.12) | copy-start | bytes 3145732
  108.2 5.6 %copy-start.15 = (bf16[256,768]{1,0:T(8,128)(2,1)S(1)}, bf16[256,768]{1,0:T(8,128)(2,1)}, u32[]{:S(2)}) copy-start(bf16[256,768]{1,0:T(8,128)(2,1)} %copy-done.14) | copy-start | bytes 1179652
  113.8 5.9 %collective-permute-start.3 = (bf16[4,256,1536]{2,1,0:T(8,128)(2,1)}, bf16[4,256,1536]{2,1,0:T(8,128)(2,1)S(1)}, u32[]{:S(2)}, u32[]{:S(2)}) collective-permute-start(bf16[4,256,1536]{2,1,0:T(8,128)(2,1)} %wide.2), channel_id=1, source_target_pairs={{0,32},{32,0},{64,96},{96,64},{128,160},{160,128},{192,224},{224,1... | collective-permute-start | bytes 9437192 | tf_op jit(solution)/shard_map/ppermute | solution.py:446
  117.8 1.2 copy-start.5
  119.7 1.7 copy-start.19
  128.5 0.9 copy-start.7
  129.4 9.6 %collective-permute-start.11 = (bf16[4,96,2048]{2,1,0:T(8,128)(2,1)}, bf16[4,96,2048]{2,1,0:T(8,128)(2,1)}, u32[]{:S(2)}, u32[]{:S(2)}) collective-permute-start(bf16[4,96,2048]{2,1,0:T(8,128)(2,1)} %get-tuple-element.65), channel_id=1, source_target_pairs={{0,32},{32,0},{64,96},{96,64},{128,160},{160,128},{192,224},{224,1... | collective-permute-start | bytes 4718600 | tf_op jit(solution)/shard_map/ppermute | solution.py:446
  129.5 6.3 %copy-start.8 = (bf16[256,1536]{1,0:T(8,128)(2,1)S(1)}, bf16[256,1536]{1,0:T(8,128)(2,1)}, u32[]{:S(2)}) copy-start(bf16[256,1536]{1,0:T(8,128)(2,1)} %copy-done.7) | copy-start | bytes 2359300
  129.5 38.9 %all-to-all-start.2 = ((bf16[16,16,4224]{2,1,0:T(8,128)(2,1)}), bf16[16,16,4224]{2,1,0:T(8,128)(2,1)S(1)}, u32[]{:S(2)}, u32[]{:S(2)}) async-start(bf16[16,16,4224]{2,1,0:T(8,128)(2,1)} %copy-done.4), calls=%async_computation.2 | async-start | bytes 4325376 | tf_op jit(solution)/shard_map/all_to_all | solution.py:50
  135.8 21.1 %collective-permute-start.4 = (bf16[256,1536]{1,0:T(8,128)(2,1)S(1)}, bf16[256,1536]{1,0:T(8,128)(2,1)S(1)}, u32[]{:S(2)}, u32[]{:S(2)}) collective-permute-start(bf16[256,1536]{1,0:T(8,128)(2,1)S(1)} %copy-done.8), channel_id=1, source_target_pairs={{0,64},{32,96},{192,128},{224,160},{1,65},{33,97},{193,129},{225,1... | collective-permute-start | bytes 2359304 | tf_op jit(solution)/shard_map/ppermute | solution.py:455
  139.0 17.8 %copy-start.18 = (bf16[4,256,1536]{2,1,0:T(8,128)(2,1)S(1)}, bf16[4,256,1536]{2,1,0:T(8,128)(2,1)}, u32[]{:S(2)}) copy-start(bf16[4,256,1536]{2,1,0:T(8,128)(2,1)} %get-tuple-element.56) | copy-start | bytes 9437188
  141.7 16.6 %copy-start.16 = (bf16[4,96,2048]{2,1,0:T(8,128)(2,1)}, bf16[4,96,2048]{2,1,0:T(8,128)(2,1)S(1)}, u32[]{:S(2)}) copy-start(bf16[4,96,2048]{2,1,0:T(8,128)(2,1)S(1)} %add_convert_fusion) | copy-start | bytes 4718596
  142.5 32.9 %collective-permute-start.12 = (bf16[96,2048]{1,0:T(8,128)(2,1)}, bf16[96,2048]{1,0:T(8,128)(2,1)}, u32[]{:S(2)}, u32[]{:S(2)}) collective-permute-start(bf16[96,2048]{1,0:T(8,128)(2,1)} %fusion.12), channel_id=1, source_target_pairs={{0,64},{32,96},{192,128},{224,160},{1,65},{33,97},{193,129},{225,1... | collective-permute-start | bytes 1179656 | tf_op jit(solution)/shard_map/ppermute | solution.py:455
  158.3 24.8 %collective-permute-start.6 = (bf16[256,1536]{1,0:T(8,128)(2,1)}, bf16[256,1536]{1,0:T(8,128)(2,1)S(1)}, u32[]{:S(2)}, u32[]{:S(2)}) collective-permute-start(bf16[256,1536]{1,0:T(8,128)(2,1)} %get-tuple-element.73), channel_id=1, source_target_pairs={{0,64},{32,96},{64,128},{96,160},{1,65},{33,97},{65,129},{97,161},... | collective-permute-start | bytes 2359304 | tf_op jit(solution)/shard_map/ppermute | solution.py:459
  162.7 20.3 %collective-permute-start.8 = (bf16[256,1536]{1,0:T(8,128)(2,1)}, bf16[256,1536]{1,0:T(8,128)(2,1)}, u32[]{:S(2)}, u32[]{:S(2)}) collective-permute-start(bf16[256,1536]{1,0:T(8,128)(2,1)} %get-tuple-element.72), channel_id=1, source_target_pairs={{192,128},{224,160},{128,64},{160,96},{193,129},{225,161},{129,65}... | collective-permute-start | bytes 2359304 | tf_op jit(solution)/shard_map/ppermute | solution.py:460
  168.5 68.9 %all-to-all-start.3 = ((bf16[16,16,4224]{2,1,0:T(8,128)(2,1)}), bf16[16,16,4224]{2,1,0:T(8,128)(2,1)}, u32[]{:S(2)}, u32[]{:S(2)}) async-start(bf16[16,16,4224]{2,1,0:T(8,128)(2,1)} %copy-done.2), calls=%async_computation.3 | async-start | bytes 4325376 | tf_op jit(solution)/shard_map/all_to_all | solution.py:50
  177.7 15.9 %collective-permute-start.13 = (bf16[96,2048]{1,0:T(8,128)(2,1)}, bf16[96,2048]{1,0:T(8,128)(2,1)}, u32[]{:S(2)}, u32[]{:S(2)}) collective-permute-start(bf16[96,2048]{1,0:T(8,128)(2,1)} %get-tuple-element.76), channel_id=1, source_target_pairs={{0,64},{32,96},{64,128},{96,160},{1,65},{33,97},{65,129},{97,161},... | collective-permute-start | bytes 1179656 | tf_op jit(solution)/shard_map/ppermute | solution.py:459
  181.7 12.0 %collective-permute-start.15 = (bf16[96,2048]{1,0:T(8,128)(2,1)}, bf16[96,2048]{1,0:T(8,128)(2,1)}, u32[]{:S(2)}, u32[]{:S(2)}) collective-permute-start(bf16[96,2048]{1,0:T(8,128)(2,1)} %get-tuple-element.77), channel_id=1, source_target_pairs={{192,128},{224,160},{128,64},{160,96},{193,129},{225,161},{129,65}... | collective-permute-start | bytes 1179656 | tf_op jit(solution)/shard_map/ppermute | solution.py:460
  186.2 22.7 %collective-permute-start.9 = (bf16[256,1536]{1,0:T(8,128)(2,1)}, bf16[256,1536]{1,0:T(8,128)(2,1)}, u32[]{:S(2)}, u32[]{:S(2)}) collective-permute-start(bf16[256,1536]{1,0:T(8,128)(2,1)} %get-tuple-element.75), channel_id=1, source_target_pairs={{192,128},{224,160},{128,64},{160,96},{64,0},{96,32},{193,129},{22... | collective-permute-start | bytes 2359304 | tf_op jit(solution)/shard_map/ppermute | solution.py:464
  187.5 43.6 %collective-permute-start.7 = (bf16[256,1536]{1,0:T(8,128)(2,1)}, bf16[256,1536]{1,0:T(8,128)(2,1)}, u32[]{:S(2)}, u32[]{:S(2)}) collective-permute-start(bf16[256,1536]{1,0:T(8,128)(2,1)} %get-tuple-element.74), channel_id=1, source_target_pairs={{0,64},{32,96},{64,128},{96,160},{128,192},{160,224},{1,65},{33,97... | collective-permute-start | bytes 2359304 | tf_op jit(solution)/shard_map/ppermute | solution.py:463
  193.0 1.4 copy-start.17
  193.5 48.7 %collective-permute-start.5 = (bf16[128,4224]{1,0:T(8,128)(2,1)S(1)}, bf16[128,4224]{1,0:T(8,128)(2,1)S(1)}, u32[]{:S(2)}, u32[]{:S(2)}) collective-permute-start(bf16[128,4224]{1,0:T(8,128)(2,1)S(1)} %collect.1), channel_id=1, source_target_pairs={{0,196},{1,197},{2,198},{3,199},{4,192},{5,193},{6,194},{7,195},{8... | collective-permute-start | bytes 3244040 | tf_op jit(solution)/shard_map/ppermute | solution.py:46
  196.7 49.2 %collective-permute-start.16 = (bf16[96,2048]{1,0:T(8,128)(2,1)}, bf16[96,2048]{1,0:T(8,128)(2,1)}, u32[]{:S(2)}, u32[]{:S(2)}) collective-permute-start(bf16[96,2048]{1,0:T(8,128)(2,1)} %get-tuple-element.79), channel_id=1, source_target_pairs={{192,128},{224,160},{128,64},{160,96},{64,0},{96,32},{193,129},{22... | collective-permute-start | bytes 1179656 | tf_op jit(solution)/shard_map/ppermute | solution.py:464
  198.0 38.1 %copy-start.20 = (s32[32]{0:T(128)S(1)}, s32[32]{0:T(128)}, u32[]{:S(2)}) copy-start(s32[32]{0:T(128)} %param.12) | copy-start | bytes 388
  198.0 44.2 %copy-start.6 = (s32[128,8]{1,0:T(8,128)S(1)}, s32[128,8]{1,0:T(8,128)}, u32[]{:S(2)}) copy-start(s32[128,8]{1,0:T(8,128)} %copy.16.ids_ref) | copy-start | bytes 12292
  198.0 47.9 %collective-permute-start.14 = (bf16[96,2048]{1,0:T(8,128)(2,1)}, bf16[96,2048]{1,0:T(8,128)(2,1)}, u32[]{:S(2)}, u32[]{:S(2)}) collective-permute-start(bf16[96,2048]{1,0:T(8,128)(2,1)} %get-tuple-element.78), channel_id=1, source_target_pairs={{0,64},{32,96},{64,128},{96,160},{128,192},{160,224},{1,65},{33,97... | collective-permute-start | bytes 1179656 | tf_op jit(solution)/shard_map/ppermute | solution.py:463
  233.0 17.3 %collective-permute-start.10 = (bf16[256,1536]{1,0:T(8,128)(2,1)S(1)}, bf16[256,1536]{1,0:T(8,128)(2,1)}, u32[]{:S(2)}, u32[]{:S(2)}) collective-permute-start(bf16[256,1536]{1,0:T(8,128)(2,1)S(1)} %fusion.5), channel_id=1, source_target_pairs={{0,16},{1,17},{2,18},{3,19},{4,20},{5,21},{6,22},{7,23},{8,24},{9,... | collective-permute-start | bytes 2359304 | tf_op jit(solution)/shard_map/ppermute | solution.py:520
  247.3 10.2 %collective-permute-start.17 = (bf16[96,2048]{1,0:T(8,128)(2,1)S(1)}, bf16[96,2048]{1,0:T(8,128)(2,1)S(1)}, u32[]{:S(2)}, u32[]{:S(2)}) collective-permute-start(bf16[96,2048]{1,0:T(8,128)(2,1)S(1)} %fusion.11), channel_id=1, source_target_pairs={{0,16},{1,17},{2,18},{3,19},{4,20},{5,21},{6,22},{7,23},{8,24},{9,... | collective-permute-start | bytes 1179656 | tf_op jit(solution)/shard_map/ppermute | solution.py:521
